TPU v7x, 32 devices: a whole 2x2x4 slice. The times are simulated.
32 devices in a mesh: dp: 4 (over y, x), seq: 8 (over z, core).
Axes of the slice: x: 2, y: 2, z: 4, core: 2. Of those that a mesh axis runs over, the one named last changes fastest.
Arguments:
- tokens: bfloat16 [4, 4096, 2048], P('dp', 'seq'), may hold values from -6 to 6
- w_query: bfloat16 [2048, 1024], replicated, may hold values from -0.125 to 0.125
- keys: bfloat16 [4, 4096, 1024], P('dp', 'seq'), may hold values from -0.5 to 0.5
- values: bfloat16 [4, 4096, 1024], P('dp', 'seq'), may hold values from -6 to 6
- log_decay: float32 [4, 8, 4096], P('dp', None, 'seq'), may hold values from -0.76640625 to 0, as said below
- regular: float32 [8], replicated, may hold values from 1 to 8
- grad_out: bfloat16 [4, 4096, 1024], P('dp', 'seq'), may hold values from -0.046875 to 0.046875
Outputs:
- mixed: bfloat16 [4, 4096, 1024], P('dp', 'seq')
- query_grad: float32 [1024, 2048], P('dp', 'seq')
Inputs may be any that keep to these rules, and one draw needn't show every extreme that they name: `log_decay`: a head's decay varies from position to position.
All inputs are finite; a program needn't handle non-finite values.
Results may differ from a plain program's by a relative error of at most 0.0049.
Values sent between devices are 32-bit elements; how exact they have to be, the bound alone decides.
No kernel may reach another device: no remote copies, remote signals or barrier semaphores. Data moves between devices by JAX's collectives and lax.ppermute only.
A program may use at most 64 MiB of HBM per device.

v0:
```python
import functools

import jax
import jax.numpy as jnp
from jax import lax
from jax.experimental import pallas as pl
from jax.experimental.pallas import tpu as pltpu
from jax.sharding import PartitionSpec as P

ITERS = 4
SUB = 128
EXTRA = 8


F32 = jnp.float32
BF16 = jnp.bfloat16


def dot(left, right):
    return jnp.dot(left, right, preferred_element_type=F32)


def split(value):
    high = value.astype(BF16)
    low = (value - high.astype(F32)).astype(BF16)
    return high, low


def wide(value, axis=1):
    return jnp.concatenate(split(value), axis=axis)


def lane_shift(value, step):
    lanes = lax.broadcasted_iota(jnp.int32, value.shape, 1)
    return jnp.where(lanes >= step, pltpu.roll(value, step, 1), 0.0), lanes >= step


def cumulative_rows(value):
    step = 1
    while step < value.shape[1]:
        value = value + lane_shift(value, step)[0]
        step *= 2
    return value


def decayed_rows(value, cumulative):
    step = 1
    while step < value.shape[1]:
        earlier, inside = lane_shift(cumulative, step)
        factor = jnp.exp(jnp.where(inside, cumulative - earlier, 0.0))
        value = value + factor * lane_shift(value, step)[0]
        step *= 2
    return value


def decay_tables(decay_ref):
    rows = decay_ref.shape[1]
    offset = jnp.zeros((decay_ref.shape[0], 1), F32)
    local, full = [], []
    for c in range(rows // SUB):
        part = cumulative_rows(decay_ref[:, c * SUB : (c + 1) * SUB])
        local.append(part)
        full.append(part + offset)
        offset = offset + part[:, SUB - 1 : SUB]
    return local, jnp.exp(offset - jnp.concatenate(full, axis=1)), jnp.exp(offset)


def states_kernel(half, per, k, core_ref, keys_ref, values_ref, decay_ref, near_ref, away_ref, table_ref, work_ref):
    rows, dim = keys_ref.shape[0], SUB
    core = core_ref[0]
    local, tails, total = decay_tables(decay_ref)
    work_ref[0] = tails
    work_ref[2] = jnp.broadcast_to(total, tails.shape)
    work_ref[1] = jnp.zeros_like(tails)
    for out, block in ((away_ref, 1 - core), (near_ref, core)):
        for i in range(half):
            head = (block * half + i) * per + k
            column = pl.ds(pl.multiple_of(head * dim, dim), dim)
            key = keys_ref[:, column]
            tail = work_ref[0, pl.ds(head, 1), :]
            key_turned = key.astype(F32).T
            value_turned = values_ref[:, column].astype(F32).T
            work_ref[1, pl.ds(head, 1), :] = jnp.sum(key_turned * key_turned, axis=0, keepdims=True)
            high, low = split(jnp.concatenate([key_turned * tail, value_turned * tail], axis=0))
            out[i, 0 : 2 * dim, :] = dot(high, key) + dot(low, key)
            decay = work_ref[2, pl.ds(head, 1), :][:, 0:SUB]
            out[i, 2 * dim : 2 * dim + EXTRA, :] = jnp.broadcast_to(decay, (EXTRA, dim))
    carry = jnp.zeros_like(total)
    for c in range(rows // SUB):
        lanes = slice(c * SUB, (c + 1) * SUB)
        part = decayed_rows(work_ref[1, :, lanes], local[c]) + jnp.exp(local[c]) * carry
        table_ref[0, :, lanes] = local[c]
        table_ref[1, :, lanes] = part
        carry = part[:, SUB - 1 : SUB]


def local_states(core, keys, values, decay, half, per, k):
    rows, columns = keys.shape
    heads = decay.shape[0]
    dim = columns // heads
    state = jax.ShapeDtypeStruct((half, 2 * dim + EXTRA, dim), F32)
    vmem = pl.BlockSpec(memory_space=pltpu.VMEM)
    return pl.pallas_call(
        functools.partial(states_kernel, half, per, k),
        out_shape=[state, state, jax.ShapeDtypeStruct((2, heads, rows), F32)],
        in_specs=[pl.BlockSpec(memory_space=pltpu.SMEM)] + [vmem] * 3,
        out_specs=[vmem] * 3,
        scratch_shapes=[pltpu.VMEM((3, heads, rows), F32)],
        cost_estimate=pl.CostEstimate(
            flops=16 * rows * dim * dim * half, bytes_accessed=8 * rows * columns, transcendentals=0
        ),
        name="local_states",
    )(core, keys, values, decay)


def solve_kernel(
    first_ref, regular_ref, q_ref, k_ref, v_ref, g_ref, rows_ref, state_ref, *rest
):
    mixed_ref, turned_ref = rest[-2:]
    rows, dim = q_ref.shape
    pieces = range(rows // SUB)
    place = [slice(c * SUB, (c + 1) * SUB) for c in pieces]
    step = pl.program_id(0)
    head = first_ref[0] + step * first_ref[1]
    ridge = regular_ref[head]
    row_at = lax.broadcasted_iota(jnp.int32, (SUB, SUB), 0)
    column_at = lax.broadcasted_iota(jnp.int32, (SUB, SUB), 1)
    lower = row_at >= column_at

    gram = [state_ref[0, 0:dim, :]]
    memory = [state_ref[0, dim : 2 * dim, :]]
    start_trace = jnp.sum(jnp.where(row_at == column_at, gram[0], 0.0), axis=0, keepdims=True)
    start_trace = jnp.sum(start_trace, axis=1, keepdims=True)
    cumulative_row = rows_ref[0, pl.ds(head, 1), :]
    cumulative = [cumulative_row[:, at] for at in place]
    last = [row[:, SUB - 1 : SUB] for row in cumulative]
    whole, offset = [], jnp.zeros((1, 1), F32)
    for c in pieces:
        whole.append(cumulative[c] + offset)
        offset = offset + last[c]
    trace = jnp.exp(jnp.concatenate(whole, axis=1)) * start_trace + rows_ref[1, pl.ds(head, 1), :]
    half = 0.5 * trace
    center = ridge + half
    alphas, gammas = [1.0 / center], []
    for i in range(1, ITERS):
        factor = 0.5 if i == 1 else 0.25
        product = half * alphas[-1]
        alphas.append(1.0 / (center - factor * half * product))
        gammas.append(alphas[-1] * (factor * half * product))
    table = jnp.concatenate(alphas + gammas + [cumulative_row], axis=0).T

    def column(index):
        return [jnp.broadcast_to(table[at, index : index + 1], (SUB, SUB)) for at in place]

    rise = column(2 * ITERS - 1)
    weights = [
        jnp.where(lower, jnp.exp(jnp.where(lower, rise[c] - cumulative[c], 0.0)), 0.0) for c in pieces
    ]
    scale = [jnp.exp(r) for r in rise]

    keys = [k_ref[at, :] for at in place]
    values = [v_ref[at, :] for at in place]
    keys_turned = [key.astype(F32).T for key in keys]
    values_turned = [value.astype(F32).T for value in values]
    for c in pieces[:-1]:
        tail = jnp.exp(last[c] - cumulative[c])
        decay = jnp.exp(last[c])
        both = jnp.concatenate([keys_turned[c] * tail, values_turned[c] * tail], axis=0)
        grown = dot(wide(both), jnp.concatenate([keys[c], keys[c]], axis=0))
        gram.append(decay * gram[-1] + grown[0:dim])
        memory.append(decay * memory[-1] + grown[dim:])
    keys_turned = [key.astype(BF16) for key in keys_turned]
    values_turned = [value.astype(BF16) for value in values_turned]

    def pair(left, right):
        return jnp.concatenate([left, right], axis=0)

    residual = []
    for c in pieces:
        grad = g_ref[place[c], :]
        pulled = scale[c] * dot(jnp.concatenate([grad, grad], axis=1), wide(memory[c], 0))
        score = weights[c] * dot(grad, values_turned[c])
        pulled = pulled + dot(wide(score), pair(keys[c], keys[c]))
        residual.append(pair(q_ref[place[c], :].astype(F32), pulled))

    alpha = column(0)
    change = [pair(alpha[c], alpha[c]) * residual[c] for c in pieces]
    solution = list(change)
    rights = [jnp.concatenate([keys_turned[c], gram[c].astype(BF16)], axis=1) for c in pieces]
    for i in range(1, ITERS):
        alpha, gamma = column(i), column(ITERS + i - 1)
        first = [dot(change[c].astype(BF16), rights[c]) for c in pieces]
        second = [
            dot((first[c][:, 0:SUB] * pair(weights[c], weights[c])).astype(BF16), keys[c]) for c in pieces
        ]
        for c in pieces:
            applied = ridge * change[c] + (pair(scale[c], scale[c]) * first[c][:, SUB:] + second[c])
            residual[c] = residual[c] - applied
            change[c] = pair(alpha[c], alpha[c]) * residual[c] + pair(gamma[c], gamma[c]) * change[c]
            solution[c] = solution[c] + change[c]

    for c in pieces:
        turned_ref[0, :, place[c]] = solution[c][SUB:].T.astype(BF16).astype(F32)
    for c in pieces:
        high, low = split(solution[c][0:SUB])
        memory_high, memory_low = split(memory[c].T)
        right = jnp.concatenate([keys_turned[c], memory_high], axis=1)
        first = dot(jnp.concatenate([high, low], axis=1), pair(right, right))
        second = first[:, SUB:] + dot(high, memory_low)
        score = weights[c] * first[:, 0:SUB]
        output = scale[c] * second + dot(wide(score), pair(values[c], values[c]))
        mixed_ref[place[c], :] = output.astype(BF16)


def solve_heads(first, regular, queries, keys, values, grads, table, states, mixed, after):
    rows, columns = keys.shape
    heads = regular.shape[0]
    dim = columns // heads
    count = states.shape[0]

    def at_head(step, first_ref, regular_ref):
        return (0, first_ref[0] + step * first_ref[1])

    wide_spec = pl.BlockSpec((rows, dim), at_head)
    operands = [queries, keys, values, grads, table, states]
    in_specs = [wide_spec] * 4 + [pl.BlockSpec(table.shape, lambda step, *_: (0, 0, 0))]
    in_specs.append(pl.BlockSpec((1,) + states.shape[1:], lambda step, *_: (step, 0, 0)))
    aliases = {}
    if mixed is not None:
        operands.append(mixed)
        in_specs.append(pl.BlockSpec(memory_space=pl.ANY))
        aliases = {2 + len(operands) - 1: 0}
    if after is not None:
        operands.append(after)
        in_specs.append(pl.BlockSpec(memory_space=pl.ANY))
    return pl.pallas_call(
        solve_kernel,
        out_shape=[
            jax.ShapeDtypeStruct((rows, columns), BF16),
            jax.ShapeDtypeStruct((count, dim, rows), F32),
        ],
        grid_spec=pltpu.PrefetchScalarGridSpec(
            num_scalar_prefetch=2,
            grid=(count,),
            in_specs=in_specs,
            out_specs=[wide_spec, pl.BlockSpec((1, dim, rows), lambda step, *_: (step, 0, 0))],
        ),
        input_output_aliases=aliases,
        cost_estimate=pl.CostEstimate(
            flops=count * 80 * rows * dim * dim, bytes_accessed=count * 14 * rows * dim, transcendentals=0
        ),
        name="solve_heads",
    )(first, regular, *operands)


def pick_kernel(core_ref, tokens_ref, out_ref):
    out_ref[0] = tokens_ref[...].astype(F32)


def pick_columns(core, tokens, blocks):
    rows, width = tokens.shape
    size = width // (2 * blocks)
    return pl.pallas_call(
        pick_kernel,
        out_shape=jax.ShapeDtypeStruct((blocks, rows, size), F32),
        grid_spec=pltpu.PrefetchScalarGridSpec(
            num_scalar_prefetch=1,
            grid=(blocks,),
            in_specs=[pl.BlockSpec((rows, size), lambda z, core_ref: (0, 2 * z + 1 - core_ref[0]))],
            out_specs=pl.BlockSpec((1, rows, size), lambda z, core_ref: (z, 0, 0)),
        ),
        cost_estimate=pl.CostEstimate(flops=0, bytes_accessed=3 * rows * width, transcendentals=0),
        name="pick_columns",
    )(core, tokens)


def narrow_kernel(in_ref, out_ref):
    out_ref[...] = in_ref[...].astype(BF16)


def narrow(blocks):
    spec = pl.BlockSpec((1,) + blocks.shape[1:], lambda z: (z, 0, 0))
    return pl.pallas_call(
        narrow_kernel,
        out_shape=jax.ShapeDtypeStruct(blocks.shape, BF16),
        grid=(blocks.shape[0],),
        in_specs=[spec],
        out_specs=spec,
        cost_estimate=pl.CostEstimate(flops=0, bytes_accessed=6 * blocks.size, transcendentals=0),
        name="narrow",
    )(blocks)


def gradient_kernel(order, place_ref, own0, own1, far0, far1, tokens_ref, other_ref, *rest):
    outs, left_ref = rest[:-1], rest[-1]
    core, group = place_ref[0], place_ref[1]
    half, dim, rows = own0.shape
    middle = dim // 2

    @pl.when(pl.program_id(0) == 0)
    def _():
        for i in range(half):
            near, away = (core * half + i) ^ group, ((1 - core) * half + i) ^ group
            left_ref[near, :, 0:rows] = own0[i].astype(BF16)
            left_ref[away, :, 0:rows] = own1[i].astype(BF16)
            left_ref[near, :, rows:] = far1[i].astype(BF16)
            left_ref[away, :, rows:] = far0[i].astype(BF16)

    left = left_ref[...].reshape(2 * half * dim, 2 * rows)
    result = dot(left, jnp.concatenate([tokens_ref[...], other_ref[0]], axis=0))
    for d in range(2 * half):
        for path in range(2):
            which, index = order[path][d]
            start = d * dim + path * middle
            outs[2 * path + which][index, 0] = result[start : start + middle]


def gradient_blocks(place, own, far, tokens, other, order):
    half, dim, rows = own[0].shape
    blocks, _, size = other.shape
    out = jax.ShapeDtypeStruct((half, blocks, dim // 2, size), F32)
    turned_spec = pl.BlockSpec((half, dim, rows), lambda z, p: (0, 0, 0))
    return pl.pallas_call(
        functools.partial(gradient_kernel, order),
        out_shape=[out] * 4,
        grid_spec=pltpu.PrefetchScalarGridSpec(
            num_scalar_prefetch=1,
            grid=(blocks,),
            in_specs=[turned_spec] * 4
            + [
                pl.BlockSpec((rows, size), lambda z, p: (0, 2 * (p[2] ^ z) + p[0])),
                pl.BlockSpec((1, rows, size), lambda z, p: (p[2] ^ z, 0, 0)),
            ],
            out_specs=[pl.BlockSpec((half, 1, dim // 2, size), lambda z, p: (0, z, 0, 0))] * 4,
            scratch_shapes=[pltpu.VMEM((2 * half, dim, 2 * rows), BF16)],
        ),
        cost_estimate=pl.CostEstimate(
            flops=8 * half * dim * rows * blocks * size,
            bytes_accessed=4 * (4 * half * dim * rows + blocks * rows * size + 2 * half * blocks * dim * size),
            transcendentals=0,
        ),
        name="gradient_blocks",
    )(place, *own, *far, tokens, other)


def bit_order(bits):
    table = []
    for d in range(1 << len(bits)):
        code = 0
        for bit in bits:
            code = 2 * code + ((d >> bit) & 1)
        table.append(divmod(code, 1 << (len(bits) - 1)))
    return table


def per_device(sizes, *arrays):
    return program(sizes, *arrays)


def program(sizes, tokens, w_query, keys, values, log_decay, regular, grad_out):
    groups, steps = sizes["dp"], sizes["seq"]
    chips = steps // 2
    heads = log_decay.shape[1]
    columns = keys.shape[2]
    dim = columns // heads
    per = heads // groups
    half = groups // 2
    tokens, keys, values, grads, decay = tokens[0], keys[0], values[0], grad_out[0], log_decay[0]
    here = lax.axis_index("seq")
    core = here % 2
    core_row = core.reshape(1).astype(jnp.int32)
    partner = [(i, i ^ 1) for i in range(steps)]
    is_first = core == 0

    def decay_of(state):
        return state[:, 2 * dim : 2 * dim + 1, :]

    def join(earlier, later):
        body = lax.broadcasted_iota(jnp.int32, later.shape, 1) < 2 * dim
        return decay_of(later) * earlier + jnp.where(body, later, 0.0)

    locals_, tables = [], []
    for k in range(per):
        near, away, table = local_states(core_row, keys, values, decay, half, per, k)
        locals_.append((near, lax.ppermute(away, "seq", partner)))
        tables.append(table)

    befores = []
    for own, came in locals_:
        chip_state = join(jnp.where(is_first, own, came), jnp.where(is_first, came, own))
        window, before = 0, None
        while window < chips - 1:
            sent = chip_state if before is None else join(before, chip_state)
            shift = 2 * (window + 1)
            pairs = [(i, i + shift) for i in range(steps - shift)]
            came_up = lax.ppermute(sent, "seq", pairs)
            before = came_up if before is None else join(came_up, before)
            window = 2 * window + 1
        befores.append(before)
    starts = []
    for (own, came), before in zip(locals_, befores):
        early = jnp.where(is_first, own, came)
        after = join(before, early)
        mine = jnp.where(is_first, before, after)
        starts.append((mine, lax.ppermute(jnp.where(is_first, after, before), "seq", partner)))

    picked = pick_columns(core_row, tokens, chips)
    other = lax.ppermute(picked, "seq", partner)
    other = narrow(other)
    queries = jnp.dot(tokens, w_query, preferred_element_type=F32).astype(BF16)

    dp_bits = groups.bit_length() - 1
    paths = [list(range(dp_bits)), list(reversed(range(dp_bits)))]
    order = [bit_order(path) for path in paths]
    place = jnp.stack([core, lax.axis_index("dp"), here // 2]).astype(jnp.int32)

    turned, mixed = {}, None

    def solve(k, side, mixed, after):
        block = core if side == 0 else 1 - core
        first = jnp.stack([block * half * per + k, jnp.full_like(core, per)]).astype(jnp.int32)
        mixed, out = solve_heads(
            first, regular, queries, keys, values, grads, tables[k], starts[k][side], mixed, after
        )
        turned[k, side] = (out, lax.ppermute(out, "seq", partner))
        return mixed

    def gradient(k):
        own = [turned[k, side][0] for side in range(2)]
        far = [turned[k, side][1] for side in range(2)]
        return gradient_blocks(place, own, far, tokens, other, order)

    products = []
    for k in range(per):
        mixed = solve(k, 0, mixed, None)
        if k > 0:
            products.append(gradient(k - 1))
        mixed = solve(k, 1, mixed, products[-1][0] if k > 0 else None)
    products.append(gradient(per - 1))

    finished = []
    for blocks in products:
        parts = []
        for index, path in enumerate(paths):
            keep, send = blocks[2 * index], blocks[2 * index + 1]
            for bit in path:
                pairs = [(i, i ^ (1 << bit)) for i in range(groups)]
                total = keep + lax.ppermute(send, "dp", pairs)
                middle = total.shape[0] // 2
                keep, send = total[:middle], total[middle:]
            parts.append(total[0])
        total = jnp.concatenate(parts, axis=1)
        out = total[0]
        for z in range(1, chips):
            out = out + lax.ppermute(total[z], "seq", [(i, i ^ (2 * z)) for i in range(steps)])
        finished.append(out)
    return mixed[None], jnp.concatenate(finished, axis=0)


def solution(mesh):
    sizes = dict(mesh.shape)
    in_specs = (
        P("dp", "seq", None),
        P(),
        P("dp", "seq", None),
        P("dp", "seq", None),
        P("dp", None, "seq"),
        P(),
        P("dp", "seq", None),
    )
    out_specs = (P("dp", "seq", None), P("dp", "seq"))
    return jax.shard_map(
        functools.partial(per_device, sizes),
        mesh=mesh,
        in_specs=in_specs,
        out_specs=out_specs,
        check_vma=False,
    )
```

profile of v0, /device:TPU:0, one launch (start us, length us, event | category | flops | bytes accessed | tf_op | source)
XLA Modules:
  0.0 154.5 jit_solution(11127943119717768323)
XLA Ops:
  0.6 4.0 %local_states.3 = (f32[2,264,128]{2,1,0:T(8,128)}, f32[2,264,128]{2,1,0:T(8,128)}, f32[2,8,512]{2,1,0:T(8,128)}) custom-call(s32[1]{0:T(128)} %bitcast.5.core_ref, bf16[512,1024]{1,0:T(8,128)(2,1)} %bitcast.60, bf16[512,1024]{1,0:T(8,128)(2,1)} %bitcast.66, f32[8,512]{1,0:T(8,128)} %bitcast.80), custom_call_target="tpu_custom_call" | custom-call | flops 268435456 | bytes 4194304 | tf_op jit(solution)/shard_map/local_states/pallas_call | solution.py:103
  5.2 4.0 %local_states.2 = (f32[2,264,128]{2,1,0:T(8,128)}, f32[2,264,128]{2,1,0:T(8,128)}, f32[2,8,512]{2,1,0:T(8,128)}) custom-call(s32[1]{0:T(128)} %bitcast.5.core_ref, bf16[512,1024]{1,0:T(8,128)(2,1)} %bitcast.61, bf16[512,1024]{1,0:T(8,128)(2,1)} %bitcast.67, f32[8,512]{1,0:T(8,128)} %bitcast.81), custom_call_target="tpu_custom_call" | custom-call | flops 268435456 | bytes 4194304 | tf_op jit(solution)/shard_map/local_states/pallas_call | solution.py:103
  9.5 4.9 %collective-permute-start.5 = (f32[2,264,128]{2,1,0:T(8,128)S(1)}, f32[2,264,128]{2,1,0:T(8,128)S(1)}, u32[]{:S(2)}, u32[]{:S(2)}) collective-permute-start(f32[2,264,128]{2,1,0:T(8,128)S(1)} %get-tuple-element.46), channel_id=1, source_target_pairs={{0,2},{1,3},{2,4},{3,5},{4,6},{5,7},{8,10},{9,11},{10,12},{11,13},... | collective-permute-start | bytes 811016 | tf_op jit(solution)/shard_map/ppermute | solution.py:396
  14.4 3.6 %pick_columns.1 = f32[4,512,256]{2,1,0:T(8,128)} custom-call(s32[1]{0:T(128)} %bitcast.5.core_ref, bf16[512,2048]{1,0:T(8,128)(2,1)} %bitcast.72), custom_call_target="tpu_custom_call" | custom-call | bytes 3145728 | tf_op jit(solution)/shard_map/pick_columns/pallas_call | solution.py:263
  18.1 2.2 %collective-permute-done.5 = f32[2,264,128]{2,1,0:T(8,128)S(1)} collective-permute-done((f32[2,264,128]{2,1,0:T(8,128)S(1)}, f32[2,264,128]{2,1,0:T(8,128)S(1)}, u32[]{:S(2)}, u32[]{:S(2)}) %collective-permute-start.5) | collective-permute-done | bytes 270368 | tf_op jit(solution)/shard_map/ppermute | solution.py:396
  20.4 4.4 %collective-permute-start.1 = (f32[2,264,128]{2,1,0:T(8,128)S(1)}, f32[2,264,128]{2,1,0:T(8,128)S(1)}, u32[]{:S(2)}, u32[]{:S(2)}) collective-permute-start(f32[2,264,128]{2,1,0:T(8,128)S(1)} %get-tuple-element.48), channel_id=1, source_target_pairs={{0,2},{1,3},{2,4},{3,5},{4,6},{5,7},{8,10},{9,11},{10,12},{11,13},... | collective-permute-start | bytes 811016 | tf_op jit(solution)/shard_map/ppermute | solution.py:396
  24.8 4.5 %collective-permute-start.6 = (f32[2,264,128]{2,1,0:T(8,128)S(1)}, f32[2,264,128]{2,1,0:T(8,128)S(1)}, u32[]{:S(2)}, u32[]{:S(2)}) collective-permute-start(f32[2,264,128]{2,1,0:T(8,128)S(1)} %get-tuple-element.61), channel_id=1, source_target_pairs={{0,4},{1,5},{2,6},{3,7},{8,12},{9,13},{10,14},{11,15},{16,20},{17,... | collective-permute-start | bytes 811016 | tf_op jit(solution)/shard_map/ppermute | solution.py:396
  29.3 5.5 %convolution_convert_fusion.q_ref = bf16[512,1024]{1,0:T(8,128)(2,1)} fusion(bf16[2048,1024]{1,0:T(8,128)(2,1)} %param.8, bf16[1,512,2048]{2,1,0:T(8,128)(2,1)S(1)} %copy-done), kind=kOutput, calls=%fused_computation | convolution fusion | flops 2148007936 | bytes 7340032 | tf_op jit(solution)/shard_map/dot_general | solution.py:410
  34.9 0.7 pad_add_fusion.3.first_ref
  35.7 0.9 fusion
  36.6 0.6 pad_add_fusion.1.first_ref
  37.2 0.6 pad_add_fusion.first_ref
  37.8 7.3 %collective-permute-start.2 = (f32[2,264,128]{2,1,0:T(8,128)S(1)}, f32[2,264,128]{2,1,0:T(8,128)S(1)}, u32[]{:S(2)}, u32[]{:S(2)}) collective-permute-start(f32[2,264,128]{2,1,0:T(8,128)S(1)} %get-tuple-element.60), channel_id=1, source_target_pairs={{0,4},{1,5},{2,6},{3,7},{8,12},{9,13},{10,14},{11,15},{16,20},{17,... | collective-permute-start | bytes 811016 | tf_op jit(solution)/shard_map/ppermute | solution.py:396
  45.2 7.8 %solve_heads.4 = (bf16[512,1024]{1,0:T(8,128)(2,1)}, f32[2,128,512]{2,1,0:T(8,128)}) custom-call(s32[2]{0:T(128)} %pad_add_fusion.first_ref, f32[8]{0:T(128)} %regular_ref.7, bf16[512,1024]{1,0:T(8,128)(2,1)} %convolution_convert_fusion.q_ref, bf16[512,1024]{1,0:T(8,128)(2,1)} %bitcast.62, bf16[512,1024]{1,0:T(8,128)(2,1)} %bitcast.68, ...), custom_call_target="tpu_custom_call" | custom-call | flops 1342177280 | bytes 1835008 | tf_op jit(solution)/shard_map/solve_heads/pallas_call | solution.py:236
  53.2 0.7 copy-done.12
  53.9 7.8 %solve_heads.5 = (bf16[512,1024]{1,0:T(8,128)(2,1)}, f32[2,128,512]{2,1,0:T(8,128)}) custom-call(s32[2]{0:T(128)} %pad_add_fusion.1.first_ref, f32[8]{0:T(128)} %regular_ref.7, bf16[512,1024]{1,0:T(8,128)(2,1)} %convolution_convert_fusion.q_ref, bf16[512,1024]{1,0:T(8,128)(2,1)} %bitcast.63, ...), custom_call_target="tpu_custom_call", output_to_operand_aliasing={{0}: (8, {})} | custom-call | flops 1342177280 | bytes 1835008 | tf_op jit(solution)/shard_map/solve_heads/pallas_call | solution.py:236
  61.9 0.6 pad_add_fusion.2.first_ref
  62.6 0.8 fusion.2
  63.7 0.6 pad_add_fusion.4.place_ref
  64.3 7.8 %solve_heads.6 = (bf16[512,1024]{1,0:T(8,128)(2,1)}, f32[2,128,512]{2,1,0:T(8,128)}) custom-call(s32[2]{0:T(128)} %pad_add_fusion.2.first_ref, f32[8]{0:T(128)} %regular_ref.7, bf16[512,1024]{1,0:T(8,128)(2,1)} %convolution_convert_fusion.q_ref, bf16[512,1024]{1,0:T(8,128)(2,1)} %bitcast.64, ...), custom_call_target="tpu_custom_call", output_to_operand_aliasing={{0}: (8, {})} | custom-call | flops 1342177280 | bytes 1835008 | tf_op jit(solution)/shard_map/solve_heads/pallas_call | solution.py:236
  72.3 3.6 %narrow.1.other_ref = bf16[4,512,256]{2,1,0:T(8,128)(2,1)} custom-call(f32[4,512,256]{2,1,0:T(8,128)} %collective-permute-done.10.in_ref), custom_call_target="tpu_custom_call" | custom-call | bytes 3145728 | tf_op jit(solution)/shard_map/narrow/pallas_call | solution.py:283
  75.9 0.8 copy-done.7
  76.7 0.8 copy-done.8
  77.5 6.1 %gradient_blocks.2 = (f32[2,4,64,256]{3,2,1,0:T(8,128)}, f32[2,4,64,256]{3,2,1,0:T(8,128)}, f32[2,4,64,256]{3,2,1,0:T(8,128)}, f32[2,4,64,256]{3,2,1,0:T(8,128)}) custom-call(s32[3]{0:T(128)} %pad_add_fusion.4.place_ref, f32[2,128,512]{2,1,0:T(8,128)} %get-tuple-element.33.own0, f32[2,128,512]{2,1,0:T(8,128)} %get-tuple-element.34.own1, ...), custom_call_target="tpu_custom_call" | custom-call | flops 1073741824 | bytes 6291456 | tf_op jit(solution)/shard_map/gradient_blocks/pallas_call | solution.py:323
  83.6 0.7 copy-done.11
  84.3 7.9 %solve_heads.7 = (bf16[512,1024]{1,0:T(8,128)(2,1)}, f32[2,128,512]{2,1,0:T(8,128)}) custom-call(s32[2]{0:T(128)} %pad_add_fusion.3.first_ref, f32[8]{0:T(128)} %regular_ref.7, bf16[512,1024]{1,0:T(8,128)(2,1)} %convolution_convert_fusion.q_ref, bf16[512,1024]{1,0:T(8,128)(2,1)} %bitcast.65, ...), custom_call_target="tpu_custom_call", output_to_operand_aliasing={{0}: (8, {})} | custom-call | flops 1342177280 | bytes 1835008 | tf_op jit(solution)/shard_map/solve_heads/pallas_call | solution.py:236
  92.5 1.5 collective-permute-start.11
  94.0 1.5 collective-permute-start.13
  95.5 0.8 copy-done.9
  96.3 0.8 copy-done.10
  97.1 6.0 %gradient_blocks.3 = (f32[2,4,64,256]{3,2,1,0:T(8,128)}, f32[2,4,64,256]{3,2,1,0:T(8,128)}, f32[2,4,64,256]{3,2,1,0:T(8,128)}, f32[2,4,64,256]{3,2,1,0:T(8,128)}) custom-call(s32[3]{0:T(128)} %pad_add_fusion.4.place_ref, f32[2,128,512]{2,1,0:T(8,128)} %get-tuple-element.40.own0, f32[2,128,512]{2,1,0:T(8,128)} %get-tuple-element.41.own1, ...), custom_call_target="tpu_custom_call" | custom-call | flops 1073741824 | bytes 6291456 | tf_op jit(solution)/shard_map/gradient_blocks/pallas_call | solution.py:323
  103.7 3.8 %collective-permute-done.11 = f32[2,4,64,256]{3,2,1,0:T(8,128)S(1)} collective-permute-done((f32[2,4,64,256]{3,2,1,0:T(8,128)}, f32[2,4,64,256]{3,2,1,0:T(8,128)S(1)}, u32[]{:S(2)}, u32[]{:S(2)}) %collective-permute-start.11) | collective-permute-done | bytes 524320 | tf_op jit(solution)/shard_map/ppermute | solution.py:448
  107.6 1.6 %collective-permute-start.12 = (f32[1,4,64,256]{3,2,1,0:T(8,128)S(1)}, f32[1,4,64,256]{3,2,1,0:T(8,128)S(1)}, u32[]{:S(2)}, u32[]{:S(2)}) collective-permute-start(f32[1,4,64,256]{3,2,1,0:T(8,128)S(1)} %slice.105), channel_id=1, source_target_pairs={{0,16},{8,24},{16,0},{24,8},{1,17},{9,25},{17,1},{25,9},{2,18},{10... | collective-permute-start | bytes 786440 | tf_op jit(solution)/shard_map/ppermute | solution.py:448
  109.8 1.6 %collective-permute-start.14 = (f32[1,4,64,256]{3,2,1,0:T(8,128)S(1)}, f32[1,4,64,256]{3,2,1,0:T(8,128)S(1)}, u32[]{:S(2)}, u32[]{:S(2)}) collective-permute-start(f32[1,4,64,256]{3,2,1,0:T(8,128)S(1)} %slice.107), channel_id=1, source_target_pairs={{0,8},{8,0},{16,24},{24,16},{1,9},{9,1},{17,25},{25,17},{2,10},{10... | collective-permute-start | bytes 786440 | tf_op jit(solution)/shard_map/ppermute | solution.py:448
  111.4 5.5 %collective-permute-done.12 = f32[1,4,64,256]{3,2,1,0:T(8,128)S(1)} collective-permute-done((f32[1,4,64,256]{3,2,1,0:T(8,128)S(1)}, f32[1,4,64,256]{3,2,1,0:T(8,128)S(1)}, u32[]{:S(2)}, u32[]{:S(2)}) %collective-permute-start.12) | collective-permute-done | bytes 262176 | tf_op jit(solution)/shard_map/ppermute | solution.py:448
  116.9 1.8 %collective-permute-done.20 = f32[2,4,64,256]{3,2,1,0:T(8,128)S(1)} collective-permute-done((f32[2,4,64,256]{3,2,1,0:T(8,128)}, f32[2,4,64,256]{3,2,1,0:T(8,128)S(1)}, u32[]{:S(2)}, u32[]{:S(2)}) %collective-permute-start.20) | collective-permute-done | bytes 524320 | tf_op jit(solution)/shard_map/ppermute | solution.py:448
  118.8 1.6 %collective-permute-start.21 = (f32[1,4,64,256]{3,2,1,0:T(8,128)S(1)}, f32[1,4,64,256]{3,2,1,0:T(8,128)S(1)}, u32[]{:S(2)}, u32[]{:S(2)}) collective-permute-start(f32[1,4,64,256]{3,2,1,0:T(8,128)S(1)} %slice.115), channel_id=1, source_target_pairs={{0,16},{8,24},{16,0},{24,8},{1,17},{9,25},{17,1},{25,9},{2,18},{10... | collective-permute-start | bytes 786440 | tf_op jit(solution)/shard_map/ppermute | solution.py:448
  120.4 3.2 %collective-permute-done.14 = f32[1,4,64,256]{3,2,1,0:T(8,128)S(1)} collective-permute-done((f32[1,4,64,256]{3,2,1,0:T(8,128)S(1)}, f32[1,4,64,256]{3,2,1,0:T(8,128)S(1)}, u32[]{:S(2)}, u32[]{:S(2)}) %collective-permute-start.14) | collective-permute-done | bytes 262176 | tf_op jit(solution)/shard_map/ppermute | solution.py:448
  123.7 4.4 %collective-permute-done.22 = f32[2,4,64,256]{3,2,1,0:T(8,128)S(1)} collective-permute-done((f32[2,4,64,256]{3,2,1,0:T(8,128)S(1)}, f32[2,4,64,256]{3,2,1,0:T(8,128)S(1)}, u32[]{:S(2)}, u32[]{:S(2)}) %collective-permute-start.22) | collective-permute-done | bytes 524320 | tf_op jit(solution)/shard_map/ppermute | solution.py:448
  128.2 1.6 %collective-permute-start.23 = (f32[1,4,64,256]{3,2,1,0:T(8,128)S(1)}, f32[1,4,64,256]{3,2,1,0:T(8,128)S(1)}, u32[]{:S(2)}, u32[]{:S(2)}) collective-permute-start(f32[1,4,64,256]{3,2,1,0:T(8,128)S(1)} %slice.117), channel_id=1, source_target_pairs={{0,8},{8,0},{16,24},{24,16},{1,9},{9,1},{17,25},{25,17},{2,10},{10... | collective-permute-start | bytes 786440 | tf_op jit(solution)/shard_map/ppermute | solution.py:448
  129.8 4.6 %collective-permute-start.17 = (f32[128,256]{1,0:T(8,128)S(1)}, f32[128,256]{1,0:T(8,128)S(1)}, u32[]{:S(2)}, u32[]{:S(2)}) collective-permute-start(f32[128,256]{1,0:T(8,128)S(1)} %get-tuple-element.55), channel_id=1, source_target_pairs={{0,6},{1,7},{2,4},{3,5},{4,2},{5,3},{6,0},{7,1},{8,14},{9,15},{10,... | collective-permute-start | bytes 393224 | tf_op jit(solution)/shard_map/ppermute | solution.py:455
  134.4 2.4 %collective-permute-start.16 = (f32[128,256]{1,0:T(8,128)S(1)}, f32[128,256]{1,0:T(8,128)S(1)}, u32[]{:S(2)}, u32[]{:S(2)}) collective-permute-start(f32[128,256]{1,0:T(8,128)S(1)} %get-tuple-element.56), channel_id=1, source_target_pairs={{0,4},{1,5},{2,6},{3,7},{4,0},{5,1},{6,2},{7,3},{8,12},{9,13},{10,... | collective-permute-start | bytes 393224 | tf_op jit(solution)/shard_map/ppermute | solution.py:455
  136.9 2.4 %collective-permute-start.26 = (f32[128,256]{1,0:T(8,128)S(1)}, f32[128,256]{1,0:T(8,128)S(1)}, u32[]{:S(2)}, u32[]{:S(2)}) collective-permute-start(f32[128,256]{1,0:T(8,128)S(1)} %get-tuple-element.58), channel_id=1, source_target_pairs={{0,6},{1,7},{2,4},{3,5},{4,2},{5,3},{6,0},{7,1},{8,14},{9,15},{10,... | collective-permute-start | bytes 393224 | tf_op jit(solution)/shard_map/ppermute | solution.py:455
  139.3 2.4 %collective-permute-start.25 = (f32[128,256]{1,0:T(8,128)S(1)}, f32[128,256]{1,0:T(8,128)S(1)}, u32[]{:S(2)}, u32[]{:S(2)}) collective-permute-start(f32[128,256]{1,0:T(8,128)S(1)} %get-tuple-element.59), channel_id=1, source_target_pairs={{0,4},{1,5},{2,6},{3,7},{4,0},{5,1},{6,2},{7,3},{8,12},{9,13},{10,... | collective-permute-start | bytes 393224 | tf_op jit(solution)/shard_map/ppermute | solution.py:455
  141.7 3.9 %collective-permute-start.24 = (f32[128,256]{1,0:T(8,128)S(1)}, f32[128,256]{1,0:T(8,128)S(1)}, u32[]{:S(2)}, u32[]{:S(2)}) collective-permute-start(f32[128,256]{1,0:T(8,128)S(1)} %get-tuple-element.57), channel_id=1, source_target_pairs={{0,2},{1,3},{2,0},{3,1},{4,6},{5,7},{6,4},{7,5},{8,10},{9,11},{10,... | collective-permute-start | bytes 393224 | tf_op jit(solution)/shard_map/ppermute | solution.py:455
  145.5 5.1 %collective-permute-done.16 = f32[128,256]{1,0:T(8,128)S(1)} collective-permute-done((f32[128,256]{1,0:T(8,128)S(1)}, f32[128,256]{1,0:T(8,128)S(1)}, u32[]{:S(2)}, u32[]{:S(2)}) %collective-permute-start.16) | collective-permute-done | bytes 131104 | tf_op jit(solution)/shard_map/ppermute | solution.py:455
  150.7 3.1 %collective-permute-done.25 = f32[128,256]{1,0:T(8,128)S(1)} collective-permute-done((f32[128,256]{1,0:T(8,128)S(1)}, f32[128,256]{1,0:T(8,128)S(1)}, u32[]{:S(2)}, u32[]{:S(2)}) %collective-permute-start.25) | collective-permute-done | bytes 131104 | tf_op jit(solution)/shard_map/ppermute | solution.py:455
  153.8 0.7 pad_maximum_fusion
  (84 shorter events, 4.2 us)
Async XLA Ops:
  4.7 4.6 %copy-start.3 = (f32[2,264,128]{2,1,0:T(8,128)S(1)}, f32[2,264,128]{2,1,0:T(8,128)}, u32[]{:S(2)}) copy-start(f32[2,264,128]{2,1,0:T(8,128)} %get-tuple-element.28) | copy-start | bytes 811012
  4.7 4.6 %collective-permute-start.4 = (f32[2,264,128]{2,1,0:T(8,128)}, f32[2,264,128]{2,1,0:T(8,128)S(1)}, u32[]{:S(2)}, u32[]{:S(2)}) collective-permute-start(f32[2,264,128]{2,1,0:T(8,128)} %get-tuple-element.29), channel_id=1, source_target_pairs={{0,1},{1,0},{2,3},{3,2},{4,5},{5,4},{6,7},{7,6},{8,9},{9,8},{10,11... | collective-permute-start | bytes 811016 | tf_op jit(solution)/shard_map/ppermute | solution.py:385
  9.2 8.8 %collective-permute-start = (f32[2,264,128]{2,1,0:T(8,128)}, f32[2,264,128]{2,1,0:T(8,128)S(1)}, u32[]{:S(2)}, u32[]{:S(2)}) collective-permute-start(f32[2,264,128]{2,1,0:T(8,128)} %get-tuple-element.26), channel_id=1, source_target_pairs={{0,1},{1,0},{2,3},{3,2},{4,5},{5,4},{6,7},{7,6},{8,9},{9,8},{10,11... | collective-permute-start | bytes 811016 | tf_op jit(solution)/shard_map/ppermute | solution.py:385
  9.5 10.8 %collective-permute-start.5 = (f32[2,264,128]{2,1,0:T(8,128)S(1)}, f32[2,264,128]{2,1,0:T(8,128)S(1)}, u32[]{:S(2)}, u32[]{:S(2)}) collective-permute-start(f32[2,264,128]{2,1,0:T(8,128)S(1)} %get-tuple-element.46), channel_id=1, source_target_pairs={{0,2},{1,3},{2,4},{3,5},{4,6},{5,7},{8,10},{9,11},{10,12},{11,13},... | collective-permute-start | bytes 811016 | tf_op jit(solution)/shard_map/ppermute | solution.py:396
  14.4 3.7 %copy-start.2 = (f32[2,264,128]{2,1,0:T(8,128)S(1)}, f32[2,264,128]{2,1,0:T(8,128)}, u32[]{:S(2)}) copy-start(f32[2,264,128]{2,1,0:T(8,128)} %get-tuple-element.25) | copy-start | bytes 811012
  18.0 11.3 %copy-start = (bf16[1,512,2048]{2,1,0:T(8,128)(2,1)S(1)}, bf16[1,512,2048]{2,1,0:T(8,128)(2,1)}, u32[]{:S(2)}) copy-start(bf16[1,512,2048]{2,1,0:T(8,128)(2,1)} %param.7) | copy-start | bytes 6291460
  18.0 54.3 %collective-permute-start.10 = (f32[4,512,256]{2,1,0:T(8,128)}, f32[4,512,256]{2,1,0:T(8,128)}, u32[]{:S(2)}, u32[]{:S(2)}) collective-permute-start(f32[4,512,256]{2,1,0:T(8,128)} %pick_columns.1), channel_id=1, source_target_pairs={{0,1},{1,0},{2,3},{3,2},{4,5},{5,4},{6,7},{7,6},{8,9},{9,8},{10,11... | collective-permute-start | bytes 6291464 | tf_op jit(solution)/shard_map/ppermute | solution.py:408
  20.4 15.1 %collective-permute-start.1 = (f32[2,264,128]{2,1,0:T(8,128)S(1)}, f32[2,264,128]{2,1,0:T(8,128)S(1)}, u32[]{:S(2)}, u32[]{:S(2)}) collective-permute-start(f32[2,264,128]{2,1,0:T(8,128)S(1)} %get-tuple-element.48), channel_id=1, source_target_pairs={{0,2},{1,3},{2,4},{3,5},{4,6},{5,7},{8,10},{9,11},{10,12},{11,13},... | collective-permute-start | bytes 811016 | tf_op jit(solution)/shard_map/ppermute | solution.py:396
  24.8 10.9 %collective-permute-start.6 = (f32[2,264,128]{2,1,0:T(8,128)S(1)}, f32[2,264,128]{2,1,0:T(8,128)S(1)}, u32[]{:S(2)}, u32[]{:S(2)}) collective-permute-start(f32[2,264,128]{2,1,0:T(8,128)S(1)} %get-tuple-element.61), channel_id=1, source_target_pairs={{0,4},{1,5},{2,6},{3,7},{8,12},{9,13},{10,14},{11,15},{16,20},{17,... | collective-permute-start | bytes 811016 | tf_op jit(solution)/shard_map/ppermute | solution.py:396
  36.6 16.6 %collective-permute-start.7 = (f32[2,264,128]{2,1,0:T(8,128)S(1)}, f32[2,264,128]{2,1,0:T(8,128)S(1)}, u32[]{:S(2)}, u32[]{:S(2)}) collective-permute-start(f32[2,264,128]{2,1,0:T(8,128)S(1)} %get-tuple-element.51), channel_id=1, source_target_pairs={{0,1},{1,0},{2,3},{3,2},{4,5},{5,4},{6,7},{7,6},{8,9},{9,8},{10,11... | collective-permute-start | bytes 811016 | tf_op jit(solution)/shard_map/ppermute | solution.py:405
  37.8 24.8 %collective-permute-start.2 = (f32[2,264,128]{2,1,0:T(8,128)S(1)}, f32[2,264,128]{2,1,0:T(8,128)S(1)}, u32[]{:S(2)}, u32[]{:S(2)}) collective-permute-start(f32[2,264,128]{2,1,0:T(8,128)S(1)} %get-tuple-element.60), channel_id=1, source_target_pairs={{0,4},{1,5},{2,6},{3,7},{8,12},{9,13},{10,14},{11,15},{16,20},{17,... | collective-permute-start | bytes 811016 | tf_op jit(solution)/shard_map/ppermute | solution.py:396
  53.0 23.0 %collective-permute-start.8 = (f32[2,128,512]{2,1,0:T(8,128)}, f32[2,128,512]{2,1,0:T(8,128)S(1)}, u32[]{:S(2)}, u32[]{:S(2)}) collective-permute-start(f32[2,128,512]{2,1,0:T(8,128)} %get-tuple-element.33.own0), channel_id=1, source_target_pairs={{0,1},{1,0},{2,3},{3,2},{4,5},{5,4},{6,7},{7,6},{8,9},{9,8},{10,11... | collective-permute-start | bytes 1572872 | tf_op jit(solution)/shard_map/ppermute | solution.py:425
  53.2 0.7 copy-start.12
  61.7 14.3 %collective-permute-start.9 = (f32[2,128,512]{2,1,0:T(8,128)}, f32[2,128,512]{2,1,0:T(8,128)S(1)}, u32[]{:S(2)}, u32[]{:S(2)}) collective-permute-start(f32[2,128,512]{2,1,0:T(8,128)} %get-tuple-element.34.own1), channel_id=1, source_target_pairs={{0,1},{1,0},{2,3},{3,2},{4,5},{5,4},{6,7},{7,6},{8,9},{9,8},{10,11... | collective-permute-start | bytes 1572872 | tf_op jit(solution)/shard_map/ppermute | solution.py:425
  63.4 20.2 %collective-permute-start.3 = (f32[2,264,128]{2,1,0:T(8,128)S(1)}, f32[2,264,128]{2,1,0:T(8,128)S(1)}, u32[]{:S(2)}, u32[]{:S(2)}) collective-permute-start(f32[2,264,128]{2,1,0:T(8,128)S(1)} %get-tuple-element.53), channel_id=1, source_target_pairs={{0,1},{1,0},{2,3},{3,2},{4,5},{5,4},{6,7},{7,6},{8,9},{9,8},{10,11... | collective-permute-start | bytes 811016 | tf_op jit(solution)/shard_map/ppermute | solution.py:405
  72.0 23.4 %collective-permute-start.18 = (f32[2,128,512]{2,1,0:T(8,128)}, f32[2,128,512]{2,1,0:T(8,128)S(1)}, u32[]{:S(2)}, u32[]{:S(2)}) collective-permute-start(f32[2,128,512]{2,1,0:T(8,128)} %get-tuple-element.40.own0), channel_id=1, source_target_pairs={{0,1},{1,0},{2,3},{3,2},{4,5},{5,4},{6,7},{7,6},{8,9},{9,8},{10,11... | collective-permute-start | bytes 1572872 | tf_op jit(solution)/shard_map/ppermute | solution.py:425
  75.9 0.8 copy-start.7
  76.7 0.8 copy-start.8
  83.6 0.7 copy-start.11
  84.3 9.6 %copy-start.13 = (f32[2,4,64,256]{3,2,1,0:T(8,128)S(1)}, f32[2,4,64,256]{3,2,1,0:T(8,128)}, u32[]{:S(2)}) copy-start(f32[2,4,64,256]{3,2,1,0:T(8,128)} %get-tuple-element.39) | copy-start | bytes 1572868
  92.2 3.3 %collective-permute-start.19 = (f32[2,128,512]{2,1,0:T(8,128)}, f32[2,128,512]{2,1,0:T(8,128)S(1)}, u32[]{:S(2)}, u32[]{:S(2)}) collective-permute-start(f32[2,128,512]{2,1,0:T(8,128)} %get-tuple-element.41.own1), channel_id=1, source_target_pairs={{0,1},{1,0},{2,3},{3,2},{4,5},{5,4},{6,7},{7,6},{8,9},{9,8},{10,11... | collective-permute-start | bytes 1572872 | tf_op jit(solution)/shard_map/ppermute | solution.py:425
  92.5 15.0 %collective-permute-start.11 = (f32[2,4,64,256]{3,2,1,0:T(8,128)}, f32[2,4,64,256]{3,2,1,0:T(8,128)S(1)}, u32[]{:S(2)}, u32[]{:S(2)}) collective-permute-start(f32[2,4,64,256]{3,2,1,0:T(8,128)} %get-tuple-element.37), channel_id=1, source_target_pairs={{0,8},{8,0},{16,24},{24,16},{1,9},{9,1},{17,25},{25,17},{2,10},{10... | collective-permute-start | bytes 1572872 | tf_op jit(solution)/shard_map/ppermute | solution.py:448
  94.0 13.5 %copy-start.1 = (f32[2,4,64,256]{3,2,1,0:T(8,128)S(1)}, f32[2,4,64,256]{3,2,1,0:T(8,128)}, u32[]{:S(2)}) copy-start(f32[2,4,64,256]{3,2,1,0:T(8,128)} %get-tuple-element.35.rest_1_) | copy-start | bytes 1572868
  94.0 15.7 %collective-permute-start.13 = (f32[2,4,64,256]{3,2,1,0:T(8,128)S(1)}, f32[2,4,64,256]{3,2,1,0:T(8,128)S(1)}, u32[]{:S(2)}, u32[]{:S(2)}) collective-permute-start(f32[2,4,64,256]{3,2,1,0:T(8,128)S(1)} %copy-done.13), channel_id=1, source_target_pairs={{0,16},{8,24},{16,0},{24,8},{1,17},{9,25},{17,1},{25,9},{2,18},{10... | collective-permute-start | bytes 1572872 | tf_op jit(solution)/shard_map/ppermute | solution.py:448
  95.5 0.8 copy-start.9
  96.3 0.8 copy-start.10
  103.0 6.1 %copy-start.14 = (f32[2,4,64,256]{3,2,1,0:T(8,128)S(1)}, f32[2,4,64,256]{3,2,1,0:T(8,128)}, u32[]{:S(2)}) copy-start(f32[2,4,64,256]{3,2,1,0:T(8,128)} %get-tuple-element.45) | copy-start | bytes 1572868
  103.0 6.6 %copy-start.4 = (f32[2,4,64,256]{3,2,1,0:T(8,128)S(1)}, f32[2,4,64,256]{3,2,1,0:T(8,128)}, u32[]{:S(2)}) copy-start(f32[2,4,64,256]{3,2,1,0:T(8,128)} %get-tuple-element.38) | copy-start | bytes 1572868
  103.1 15.6 %collective-permute-start.20 = (f32[2,4,64,256]{3,2,1,0:T(8,128)}, f32[2,4,64,256]{3,2,1,0:T(8,128)S(1)}, u32[]{:S(2)}, u32[]{:S(2)}) collective-permute-start(f32[2,4,64,256]{3,2,1,0:T(8,128)} %get-tuple-element.43), channel_id=1, source_target_pairs={{0,8},{8,0},{16,24},{24,16},{1,9},{9,1},{17,25},{25,17},{2,10},{10... | collective-permute-start | bytes 1572872 | tf_op jit(solution)/shard_map/ppermute | solution.py:448
  107.5 11.2 %copy-start.6 = (f32[2,4,64,256]{3,2,1,0:T(8,128)S(1)}, f32[2,4,64,256]{3,2,1,0:T(8,128)}, u32[]{:S(2)}) copy-start(f32[2,4,64,256]{3,2,1,0:T(8,128)} %get-tuple-element.42) | copy-start | bytes 1572868
  107.6 9.2 %collective-permute-start.12 = (f32[1,4,64,256]{3,2,1,0:T(8,128)S(1)}, f32[1,4,64,256]{3,2,1,0:T(8,128)S(1)}, u32[]{:S(2)}, u32[]{:S(2)}) collective-permute-start(f32[1,4,64,256]{3,2,1,0:T(8,128)S(1)} %slice.105), channel_id=1, source_target_pairs={{0,16},{8,24},{16,0},{24,8},{1,17},{9,25},{17,1},{25,9},{2,18},{10... | collective-permute-start | bytes 786440 | tf_op jit(solution)/shard_map/ppermute | solution.py:448
  109.2 18.9 %collective-permute-start.22 = (f32[2,4,64,256]{3,2,1,0:T(8,128)S(1)}, f32[2,4,64,256]{3,2,1,0:T(8,128)S(1)}, u32[]{:S(2)}, u32[]{:S(2)}) collective-permute-start(f32[2,4,64,256]{3,2,1,0:T(8,128)S(1)} %copy-done.14), channel_id=1, source_target_pairs={{0,16},{8,24},{16,0},{24,8},{1,17},{9,25},{17,1},{25,9},{2,18},{10... | collective-permute-start | bytes 1572872 | tf_op jit(solution)/shard_map/ppermute | solution.py:448
  109.8 18.3 %copy-start.5 = (f32[2,4,64,256]{3,2,1,0:T(8,128)S(1)}, f32[2,4,64,256]{3,2,1,0:T(8,128)}, u32[]{:S(2)}) copy-start(f32[2,4,64,256]{3,2,1,0:T(8,128)} %get-tuple-element.44) | copy-start | bytes 1572868
  109.8 13.8 %collective-permute-start.14 = (f32[1,4,64,256]{3,2,1,0:T(8,128)S(1)}, f32[1,4,64,256]{3,2,1,0:T(8,128)S(1)}, u32[]{:S(2)}, u32[]{:S(2)}) collective-permute-start(f32[1,4,64,256]{3,2,1,0:T(8,128)S(1)} %slice.107), channel_id=1, source_target_pairs={{0,8},{8,0},{16,24},{24,16},{1,9},{9,1},{17,25},{25,17},{2,10},{10... | collective-permute-start | bytes 786440 | tf_op jit(solution)/shard_map/ppermute | solution.py:448
  118.8 17.9 %collective-permute-start.21 = (f32[1,4,64,256]{3,2,1,0:T(8,128)S(1)}, f32[1,4,64,256]{3,2,1,0:T(8,128)S(1)}, u32[]{:S(2)}, u32[]{:S(2)}) collective-permute-start(f32[1,4,64,256]{3,2,1,0:T(8,128)S(1)} %slice.115), channel_id=1, source_target_pairs={{0,16},{8,24},{16,0},{24,8},{1,17},{9,25},{17,1},{25,9},{2,18},{10... | collective-permute-start | bytes 786440 | tf_op jit(solution)/shard_map/ppermute | solution.py:448
  128.2 8.6 %collective-permute-start.23 = (f32[1,4,64,256]{3,2,1,0:T(8,128)S(1)}, f32[1,4,64,256]{3,2,1,0:T(8,128)S(1)}, u32[]{:S(2)}, u32[]{:S(2)}) collective-permute-start(f32[1,4,64,256]{3,2,1,0:T(8,128)S(1)} %slice.117), channel_id=1, source_target_pairs={{0,8},{8,0},{16,24},{24,16},{1,9},{9,1},{17,25},{25,17},{2,10},{10... | collective-permute-start | bytes 786440 | tf_op jit(solution)/shard_map/ppermute | solution.py:448
  129.8 11.9 %collective-permute-start.17 = (f32[128,256]{1,0:T(8,128)S(1)}, f32[128,256]{1,0:T(8,128)S(1)}, u32[]{:S(2)}, u32[]{:S(2)}) collective-permute-start(f32[128,256]{1,0:T(8,128)S(1)} %get-tuple-element.55), channel_id=1, source_target_pairs={{0,6},{1,7},{2,4},{3,5},{4,2},{5,3},{6,0},{7,1},{8,14},{9,15},{10,... | collective-permute-start | bytes 393224 | tf_op jit(solution)/shard_map/ppermute | solution.py:455
  134.4 16.3 %collective-permute-start.16 = (f32[128,256]{1,0:T(8,128)S(1)}, f32[128,256]{1,0:T(8,128)S(1)}, u32[]{:S(2)}, u32[]{:S(2)}) collective-permute-start(f32[128,256]{1,0:T(8,128)S(1)} %get-tuple-element.56), channel_id=1, source_target_pairs={{0,4},{1,5},{2,6},{3,7},{4,0},{5,1},{6,2},{7,3},{8,12},{9,13},{10,... | collective-permute-start | bytes 393224 | tf_op jit(solution)/shard_map/ppermute | solution.py:455
  136.7 13.9 %collective-permute-start.15 = (f32[128,256]{1,0:T(8,128)S(1)}, f32[128,256]{1,0:T(8,128)S(1)}, u32[]{:S(2)}, u32[]{:S(2)}) collective-permute-start(f32[128,256]{1,0:T(8,128)S(1)} %get-tuple-element.54), channel_id=1, source_target_pairs={{0,2},{1,3},{2,0},{3,1},{4,6},{5,7},{6,4},{7,5},{8,10},{9,11},{10,... | collective-permute-start | bytes 393224 | tf_op jit(solution)/shard_map/ppermute | solution.py:455
  136.9 13.8 %collective-permute-start.26 = (f32[128,256]{1,0:T(8,128)S(1)}, f32[128,256]{1,0:T(8,128)S(1)}, u32[]{:S(2)}, u32[]{:S(2)}) collective-permute-start(f32[128,256]{1,0:T(8,128)S(1)} %get-tuple-element.58), channel_id=1, source_target_pairs={{0,6},{1,7},{2,4},{3,5},{4,2},{5,3},{6,0},{7,1},{8,14},{9,15},{10,... | collective-permute-start | bytes 393224 | tf_op jit(solution)/shard_map/ppermute | solution.py:455
  139.3 14.5 %collective-permute-start.25 = (f32[128,256]{1,0:T(8,128)S(1)}, f32[128,256]{1,0:T(8,128)S(1)}, u32[]{:S(2)}, u32[]{:S(2)}) collective-permute-start(f32[128,256]{1,0:T(8,128)S(1)} %get-tuple-element.59), channel_id=1, source_target_pairs={{0,4},{1,5},{2,6},{3,7},{4,0},{5,1},{6,2},{7,3},{8,12},{9,13},{10,... | collective-permute-start | bytes 393224 | tf_op jit(solution)/shard_map/ppermute | solution.py:455
  141.7 12.1 %collective-permute-start.24 = (f32[128,256]{1,0:T(8,128)S(1)}, f32[128,256]{1,0:T(8,128)S(1)}, u32[]{:S(2)}, u32[]{:S(2)}) collective-permute-start(f32[128,256]{1,0:T(8,128)S(1)} %get-tuple-element.57), channel_id=1, source_target_pairs={{0,2},{1,3},{2,0},{3,1},{4,6},{5,7},{6,4},{7,5},{8,10},{9,11},{10,... | collective-permute-start | bytes 393224 | tf_op jit(solution)/shard_map/ppermute | solution.py:455
where the time goes:
time: 155 us
  Pallas kernels  58.5 us (38%)
  starting transfers between devices  49 us (32%)
  waiting for transfers between devices  29.3 us (19%)
  other arithmetic  6.47 us (4%)
  matrix products  5.53 us (4%)
  local copies, waits for them, and re-layouts  4.7 us (3%)
    pallas_call x4, Pallas kernels, solve_heads(): pl.pallas_call(solve_kernel, out_shape=[jax.ShapeDtypeStruct((rows, colum...  31.2 us
    ppermute x4, starting transfers between devices, program(): came_up = lax.ppermute(sent, 'seq', pairs)  21.2 us
    ppermute x8, waiting for transfers between devices, program(): total = keep + lax.ppermute(send, 'dp', pairs)  18.8 us
    ppermute x6, starting transfers between devices, program(): lax.ppermute(total[z], 'seq', [(i, i ^ 2 * z) for i in range(steps)])  15.6 us
    pallas_call x2, Pallas kernels, gradient_blocks(): pl.pallas_call(functools.partial(gradient_kernel, order), out_shape=[out]...  12.1 us
    ppermute x8, starting transfers between devices, program(): total = keep + lax.ppermute(send, 'dp', pairs)  10.4 us
    ppermute x6, waiting for transfers between devices, program(): lax.ppermute(total[z], 'seq', [(i, i ^ 2 * z) for i in range(steps)])  8.22 us
    pallas_call x2, Pallas kernels, local_states(): pl.pallas_call(functools.partial(states_kernel, half, per, k), out_shape=...  8.05 us
  transfers between devices with their start and end apart: 27, of which 9 were waited for; matrix products, arithmetic and copies ran while one was open for 7% of the time, Pallas kernels for 35%

commit v1 on v0

--- a/solution.py
+++ b/solution.py
@@ -68,6 +68,8 @@
 def states_kernel(half, per, k, core_ref, keys_ref, values_ref, decay_ref, near_ref, away_ref, table_ref, work_ref):
     rows, dim = keys_ref.shape[0], SUB
     core = core_ref[0]
+    row_at = lax.broadcasted_iota(jnp.int32, (dim, dim), 0)
+    column_at = lax.broadcasted_iota(jnp.int32, (dim, dim), 1)
     local, tails, total = decay_tables(decay_ref)
     work_ref[0] = tails
     work_ref[2] = jnp.broadcast_to(total, tails.shape)
@@ -82,9 +84,18 @@
             value_turned = values_ref[:, column].astype(F32).T
             work_ref[1, pl.ds(head, 1), :] = jnp.sum(key_turned * key_turned, axis=0, keepdims=True)
             high, low = split(jnp.concatenate([key_turned * tail, value_turned * tail], axis=0))
-            out[i, 0 : 2 * dim, :] = dot(high, key) + dot(low, key)
-            decay = work_ref[2, pl.ds(head, 1), :][:, 0:SUB]
-            out[i, 2 * dim : 2 * dim + EXTRA, :] = jnp.broadcast_to(decay, (EXTRA, dim))
+            state = dot(high, key) + dot(low, key)
+            gram = state[0:dim]
+            at, second = i // 2, i % 2
+            out[at, (1 + second) * dim : (2 + second) * dim, :] = state[dim:]
+            out[at, 3 * dim + second : 3 * dim + second + 1, :] = work_ref[2, pl.ds(head, 1), :][:, 0:SUB]
+            if second == 0:
+                first_gram = gram
+            else:
+                out[at, 0:dim, :] = jnp.where(row_at <= column_at, first_gram, gram)
+                diagonal = jnp.sum(jnp.where(row_at == column_at, gram, 0.0), axis=0, keepdims=True)
+                out[at, 3 * dim + 2 : 3 * dim + 3, :] = diagonal
+                out[at, 3 * dim + 3 :, :] = jnp.zeros((EXTRA - 3, dim), F32)
     carry = jnp.zeros_like(total)
     for c in range(rows // SUB):
         lanes = slice(c * SUB, (c + 1) * SUB)
@@ -98,7 +109,7 @@
     rows, columns = keys.shape
     heads = decay.shape[0]
     dim = columns // heads
-    state = jax.ShapeDtypeStruct((half, 2 * dim + EXTRA, dim), F32)
+    state = jax.ShapeDtypeStruct((half // 2, 3 * dim + EXTRA, dim), F32)
     vmem = pl.BlockSpec(memory_space=pltpu.VMEM)
     return pl.pallas_call(
         functools.partial(states_kernel, half, per, k),
@@ -113,22 +124,70 @@
     )(core, keys, values, decay)
 
 
+def join(earlier, later, dim):
+    row_at = lax.broadcasted_iota(jnp.int32, later.shape, 1)
+    column_at = lax.broadcasted_iota(jnp.int32, later.shape, 2)
+    is_first = (row_at < dim) & (row_at <= column_at) | (row_at >= dim) & (row_at < 2 * dim)
+    is_first = is_first | (row_at == 3 * dim)
+    is_decay = (row_at == 3 * dim) | (row_at == 3 * dim + 1)
+    factor = jnp.where(is_first, later[:, 3 * dim : 3 * dim + 1], later[:, 3 * dim + 1 : 3 * dim + 2])
+    return factor * earlier + jnp.where(is_decay, 0.0, later)
+
+
+def chip_kernel(dim, place_ref, own_ref, came_ref, out_ref):
+    is_first = place_ref[0] == 0
+    own, came = own_ref[...], came_ref[...]
+    out_ref[...] = join(jnp.where(is_first, own, came), jnp.where(is_first, came, own), dim)
+
+
+def join_kernel(dim, place_ref, earlier_ref, later_ref, out_ref):
+    out_ref[...] = join(earlier_ref[...], later_ref[...], dim)
+
+
+def start_kernel(dim, place_ref, far_ref, near_ref, own_ref, came_ref, mine_ref, other_ref):
+    is_first = place_ref[0] == 0
+    before = join(far_ref[...], near_ref[...], dim)
+    after = join(before, jnp.where(is_first, own_ref[...], came_ref[...]), dim)
+    mine_ref[...] = jnp.where(is_first, before, after)
+    other_ref[...] = jnp.where(is_first, after, before)
+
+
+def combine(kernel, dim, place, *arrays, outs=1):
+    vmem = pl.BlockSpec(memory_space=pltpu.VMEM)
+    shape = jax.ShapeDtypeStruct(arrays[0].shape, F32)
+    results = pl.pallas_call(
+        functools.partial(kernel, dim),
+        out_shape=[shape] * outs,
+        in_specs=[pl.BlockSpec(memory_space=pltpu.SMEM)] + [vmem] * len(arrays),
+        out_specs=[vmem] * outs,
+        cost_estimate=pl.CostEstimate(
+            flops=0, bytes_accessed=4 * arrays[0].size * (len(arrays) + outs), transcendentals=0
+        ),
+    )(place, *arrays)
+    return results[0] if outs == 1 else results
+
+
 def solve_kernel(
-    first_ref, regular_ref, q_ref, k_ref, v_ref, g_ref, rows_ref, state_ref, *rest
+    head_of, place_ref, regular_ref, q_ref, k_ref, v_ref, g_ref, rows_ref, state_ref, *rest
 ):
     mixed_ref, turned_ref = rest[-2:]
     rows, dim = q_ref.shape
     pieces = range(rows // SUB)
     place = [slice(c * SUB, (c + 1) * SUB) for c in pieces]
     step = pl.program_id(0)
-    head = first_ref[0] + step * first_ref[1]
+    head = head_of(step, place_ref)
     ridge = regular_ref[head]
     row_at = lax.broadcasted_iota(jnp.int32, (SUB, SUB), 0)
     column_at = lax.broadcasted_iota(jnp.int32, (SUB, SUB), 1)
     lower = row_at >= column_at
 
-    gram = [state_ref[0, 0:dim, :]]
-    memory = [state_ref[0, dim : 2 * dim, :]]
+    is_second = lax.rem(step, 2) == 1
+    packed = state_ref[0, 0:dim, :]
+    direct = (row_at > column_at) == is_second
+    start = jnp.where(direct, packed, packed.T)
+    diagonal = state_ref[0, 3 * dim + 2 : 3 * dim + 3, :]
+    gram = [jnp.where((row_at == column_at) & is_second, diagonal, start)]
+    memory = [state_ref[0, pl.ds(pl.multiple_of((1 + lax.rem(step, 2)) * dim, dim), dim), :]]
     start_trace = jnp.sum(jnp.where(row_at == column_at, gram[0], 0.0), axis=0, keepdims=True)
     start_trace = jnp.sum(start_trace, axis=1, keepdims=True)
     cumulative_row = rows_ref[0, pl.ds(head, 1), :]
@@ -212,19 +271,23 @@
         mixed_ref[place[c], :] = output.astype(BF16)
 
 
-def solve_heads(first, regular, queries, keys, values, grads, table, states, mixed, after):
+def solve_heads(place, k, side, per, regular, queries, keys, values, grads, table, states, mixed, after):
     rows, columns = keys.shape
     heads = regular.shape[0]
     dim = columns // heads
-    count = states.shape[0]
-
-    def at_head(step, first_ref, regular_ref):
-        return (0, first_ref[0] + step * first_ref[1])
+    count = 2 * states.shape[0]
+
+    def head_of(step, place_ref):
+        block = place_ref[0] if side == 0 else 1 - place_ref[0]
+        return (block * count + step) * per + k
+
+    def at_head(step, place_ref, regular_ref):
+        return (0, head_of(step, place_ref))
 
     wide_spec = pl.BlockSpec((rows, dim), at_head)
     operands = [queries, keys, values, grads, table, states]
     in_specs = [wide_spec] * 4 + [pl.BlockSpec(table.shape, lambda step, *_: (0, 0, 0))]
-    in_specs.append(pl.BlockSpec((1,) + states.shape[1:], lambda step, *_: (step, 0, 0)))
+    in_specs.append(pl.BlockSpec((1,) + states.shape[1:], lambda step, *_: (step // 2, 0, 0)))
     aliases = {}
     if mixed is not None:
         operands.append(mixed)
@@ -234,7 +297,7 @@
         operands.append(after)
         in_specs.append(pl.BlockSpec(memory_space=pl.ANY))
     return pl.pallas_call(
-        solve_kernel,
+        functools.partial(solve_kernel, head_of),
         out_shape=[
             jax.ShapeDtypeStruct((rows, columns), BF16),
             jax.ShapeDtypeStruct((count, dim, rows), F32),
@@ -250,7 +313,7 @@
             flops=count * 80 * rows * dim * dim, bytes_accessed=count * 14 * rows * dim, transcendentals=0
         ),
         name="solve_heads",
-    )(first, regular, *operands)
+    )(place, regular, *operands)
 
 
 def pick_kernel(core_ref, tokens_ref, out_ref):
@@ -368,43 +431,32 @@
     tokens, keys, values, grads, decay = tokens[0], keys[0], values[0], grad_out[0], log_decay[0]
     here = lax.axis_index("seq")
     core = here % 2
-    core_row = core.reshape(1).astype(jnp.int32)
+    place = jnp.stack([core, lax.axis_index("dp"), here // 2]).astype(jnp.int32)
     partner = [(i, i ^ 1) for i in range(steps)]
-    is_first = core == 0
-
-    def decay_of(state):
-        return state[:, 2 * dim : 2 * dim + 1, :]
-
-    def join(earlier, later):
-        body = lax.broadcasted_iota(jnp.int32, later.shape, 1) < 2 * dim
-        return decay_of(later) * earlier + jnp.where(body, later, 0.0)
 
     locals_, tables = [], []
     for k in range(per):
-        near, away, table = local_states(core_row, keys, values, decay, half, per, k)
+        near, away, table = local_states(place, keys, values, decay, half, per, k)
         locals_.append((near, lax.ppermute(away, "seq", partner)))
         tables.append(table)
 
-    befores = []
+    starts = []
     for own, came in locals_:
-        chip_state = join(jnp.where(is_first, own, came), jnp.where(is_first, came, own))
-        window, before = 0, None
+        chip_state = combine(chip_kernel, dim, place, own, came)
+        window, near, far = 0, None, None
         while window < chips - 1:
-            sent = chip_state if before is None else join(before, chip_state)
+            if far is not None:
+                near = combine(join_kernel, dim, place, far, near)
+            sent = chip_state if near is None else combine(join_kernel, dim, place, near, chip_state)
             shift = 2 * (window + 1)
             pairs = [(i, i + shift) for i in range(steps - shift)]
             came_up = lax.ppermute(sent, "seq", pairs)
-            before = came_up if before is None else join(came_up, before)
+            near, far = (came_up, None) if near is None else (near, came_up)
             window = 2 * window + 1
-        befores.append(before)
-    starts = []
-    for (own, came), before in zip(locals_, befores):
-        early = jnp.where(is_first, own, came)
-        after = join(before, early)
-        mine = jnp.where(is_first, before, after)
-        starts.append((mine, lax.ppermute(jnp.where(is_first, after, before), "seq", partner)))
-
-    picked = pick_columns(core_row, tokens, chips)
+        mine, others = combine(start_kernel, dim, place, far, near, own, came, outs=2)
+        starts.append((mine, lax.ppermute(others, "seq", partner)))
+
+    picked = pick_columns(place, tokens, chips)
     other = lax.ppermute(picked, "seq", partner)
     other = narrow(other)
     queries = jnp.dot(tokens, w_query, preferred_element_type=F32).astype(BF16)
@@ -412,15 +464,12 @@
     dp_bits = groups.bit_length() - 1
     paths = [list(range(dp_bits)), list(reversed(range(dp_bits)))]
     order = [bit_order(path) for path in paths]
-    place = jnp.stack([core, lax.axis_index("dp"), here // 2]).astype(jnp.int32)
 
     turned, mixed = {}, None
 
     def solve(k, side, mixed, after):
-        block = core if side == 0 else 1 - core
-        first = jnp.stack([block * half * per + k, jnp.full_like(core, per)]).astype(jnp.int32)
         mixed, out = solve_heads(
-            first, regular, queries, keys, values, grads, tables[k], starts[k][side], mixed, after
+            place, k, side, per, regular, queries, keys, values, grads, tables[k], starts[k][side], mixed, after
         )
         turned[k, side] = (out, lax.ppermute(out, "seq", partner))
         return mixed

time: 155 us -> 180 us (1.16)
  Pallas kernels: 58.5 us -> 72.2 us
  waiting for transfers between devices: 29.3 us -> 40.8 us
  other arithmetic: 6.47 us -> 1.86 us
  local copies, waits for them, and re-layouts: 4.7 us -> 8.71 us
    pallas_call x4 -> x10, Pallas kernels: 31.2 us -> 44.4 us  [the longest x4 33.3 us: solve_heads(): pl.pallas_call(functools.partial(solve_kernel, head_of), out_shape=[jax.S...]
    ppermute x4, waiting for transfers between devices: 2.34 us -> 10.1 us  [program(): came_up = lax.ppermute(sent, 'seq', pairs)]
    unnamed x30 -> x38, local copies, waits for them, and re-layouts: 4.61 us -> 8.64 us
    another operation x4 -> x0, other arithmetic: 2.56 us -> none  [solve(): jnp.stack([block * half * per + k, jnp.full_like(core, per)])]
    ppermute x6, waiting for transfers between devices: 8.22 us -> 10.3 us  [program(): lax.ppermute(total[z], 'seq', [(i, i ^ 2 * z) for i in range(steps)])]
  transfers between devices with their start and end apart: 27 -> 27, of which waited for: 9 -> 11; matrix products, arithmetic and copies ran while one was open for 7% -> 3% of each run, Pallas kernels for 35% -> 38%
where the time goes in v1:
time: 180 us; the launch traced here: 179 us
  Pallas kernels  72.2 us (40%)
  starting transfers between devices  49.3 us (27%)
  waiting for transfers between devices  40.8 us (23%)
  local copies, waits for them, and re-layouts  8.71 us (5%)
  matrix products  5.51 us (3%)
  other arithmetic  1.86 us (1%)
    pallas_call x4, Pallas kernels, solve_heads(): pl.pallas_call(functools.partial(solve_kernel, head_of), out_shape=[jax.S...  33.3 us
    ppermute x4, starting transfers between devices, program(): came_up = lax.ppermute(sent, 'seq', pairs)  22.7 us
    ppermute x8, waiting for transfers between devices, program(): total = keep + lax.ppermute(send, 'dp', pairs)  18.8 us
    ppermute x6, starting transfers between devices, program(): lax.ppermute(total[z], 'seq', [(i, i ^ 2 * z) for i in range(steps)])  14.4 us
    pallas_call x2, Pallas kernels, gradient_blocks(): pl.pallas_call(functools.partial(gradient_kernel, order), out_shape=[out]...  12.1 us
    pallas_call x6, Pallas kernels, combine(): pl.pallas_call(functools.partial(kernel, dim), out_shape=[shape] * outs,...  11.1 us
    ppermute x8, starting transfers between devices, program(): total = keep + lax.ppermute(send, 'dp', pairs)  10.4 us
    ppermute x6, waiting for transfers between devices, program(): lax.ppermute(total[z], 'seq', [(i, i ^ 2 * z) for i in range(steps)])  10.3 us
  transfers between devices with their start and end apart: 27, of which 11 were waited for; matrix products, arithmetic and copies ran while one was open for 3% of the time, Pallas kernels for 38%

profile of v1, /device:TPU:0, one launch (start us, length us, event | category | flops | bytes accessed | tf_op | source)
XLA Modules:
  0.0 179.4 jit_solution(10697272805099397514)
XLA Ops:
  1.2 4.3 %pick_columns.1 = f32[4,512,256]{2,1,0:T(8,128)} custom-call(s32[3]{0:T(128)} %pad_add_fusion.core_ref.place_ref, bf16[512,2048]{1,0:T(8,128)(2,1)} %bitcast.60), custom_call_target="tpu_custom_call" | custom-call | bytes 3145728 | tf_op jit(solution)/shard_map/pick_columns/pallas_call | solution.py:326
  6.0 4.0 %local_states.3 = (f32[1,392,128]{2,1,0:T(8,128)}, f32[1,392,128]{2,1,0:T(8,128)}, f32[2,8,512]{2,1,0:T(8,128)}) custom-call(s32[3]{0:T(128)} %pad_add_fusion.core_ref.place_ref, bf16[512,1024]{1,0:T(8,128)(2,1)} %bitcast.48, bf16[512,1024]{1,0:T(8,128)(2,1)} %bitcast.54, f32[8,512]{1,0:T(8,128)} %bitcast.68), custom_call_target="tpu_custom_call" | custom-call | flops 268435456 | bytes 4194304 | tf_op jit(solution)/shard_map/local_states/pallas_call | solution.py:114
  10.0 1.6 collective-permute-done.4.came_ref
  12.3 1.8 shard_map.89.later_ref
  14.1 4.6 %collective-permute-start.5 = (f32[1,392,128]{2,1,0:T(8,128)}, f32[1,392,128]{2,1,0:T(8,128)S(1)}, u32[]{:S(2)}, u32[]{:S(2)}) collective-permute-start(f32[1,392,128]{2,1,0:T(8,128)} %shard_map.89.later_ref), channel_id=1, source_target_pairs={{0,2},{1,3},{2,4},{3,5},{4,6},{5,7},{8,10},{9,11},{10,12},{11,13},... | collective-permute-start | bytes 602120 | tf_op jit(solution)/shard_map/ppermute | solution.py:453
  18.7 5.1 %collective-permute-done.5.earlier_ref.near_ref = f32[1,392,128]{2,1,0:T(8,128)S(1)} collective-permute-done((f32[1,392,128]{2,1,0:T(8,128)}, f32[1,392,128]{2,1,0:T(8,128)S(1)}, u32[]{:S(2)}, u32[]{:S(2)}) %collective-permute-start.5) | collective-permute-done | bytes 200736 | tf_op jit(solution)/shard_map/ppermute | solution.py:453
  24.5 1.8 shard_map.90
  26.2 5.3 %collective-permute-start.6 = (f32[1,392,128]{2,1,0:T(8,128)}, f32[1,392,128]{2,1,0:T(8,128)S(1)}, u32[]{:S(2)}, u32[]{:S(2)}) collective-permute-start(f32[1,392,128]{2,1,0:T(8,128)} %shard_map.90), channel_id=1, source_target_pairs={{0,4},{1,5},{2,6},{3,7},{8,12},{9,13},{10,14},{11,15},{16,20},{17,... | collective-permute-start | bytes 602120 | tf_op jit(solution)/shard_map/ppermute | solution.py:453
  31.5 4.0 %local_states.2 = (f32[1,392,128]{2,1,0:T(8,128)}, f32[1,392,128]{2,1,0:T(8,128)}, f32[2,8,512]{2,1,0:T(8,128)}) custom-call(s32[3]{0:T(128)} %pad_add_fusion.core_ref.place_ref, bf16[512,1024]{1,0:T(8,128)(2,1)} %bitcast.49, bf16[512,1024]{1,0:T(8,128)(2,1)} %bitcast.55, f32[8,512]{1,0:T(8,128)} %bitcast.69), custom_call_target="tpu_custom_call" | custom-call | flops 268435456 | bytes 4194304 | tf_op jit(solution)/shard_map/local_states/pallas_call | solution.py:114
  35.8 0.7 copy-done.14
  36.5 2.0 %shard_map.91 = (f32[1,392,128]{2,1,0:T(8,128)}, f32[1,392,128]{2,1,0:T(8,128)}) custom-call(s32[3]{0:T(128)} %pad_add_fusion.core_ref.place_ref, f32[1,392,128]{2,1,0:T(8,128)} %copy-done.14, f32[1,392,128]{2,1,0:T(8,128)} %copy-done.5, f32[1,392,128]{2,1,0:T(8,128)} %get-tuple-element.34.own_ref, f32[1,392,128]{2,1,0:T(8,128)} %copy-done.4), custom_call_target="tpu_custom_call" | custom-call | bytes 1204224 | tf_op jit(solution)/shard_map/pallas_call | solution.py:158
  38.8 5.5 %convolution_convert_fusion.q_ref = bf16[512,1024]{1,0:T(8,128)(2,1)} fusion(bf16[2048,1024]{1,0:T(8,128)(2,1)} %param.8, bf16[1,512,2048]{2,1,0:T(8,128)(2,1)S(1)} %copy-done), kind=kOutput, calls=%fused_computation | convolution fusion | flops 2148007936 | bytes 7340032 | tf_op jit(solution)/shard_map/dot_general | solution.py:462
  45.0 1.7 shard_map.86.later_ref
  46.7 7.4 %collective-permute-start.1 = (f32[1,392,128]{2,1,0:T(8,128)}, f32[1,392,128]{2,1,0:T(8,128)S(1)}, u32[]{:S(2)}, u32[]{:S(2)}) collective-permute-start(f32[1,392,128]{2,1,0:T(8,128)} %shard_map.86.later_ref), channel_id=1, source_target_pairs={{0,2},{1,3},{2,4},{3,5},{4,6},{5,7},{8,10},{9,11},{10,12},{11,13},... | collective-permute-start | bytes 602120 | tf_op jit(solution)/shard_map/ppermute | solution.py:453
  54.1 8.3 %solve_heads.4 = (bf16[512,1024]{1,0:T(8,128)(2,1)}, f32[2,128,512]{2,1,0:T(8,128)}) custom-call(s32[3]{0:T(128)} %pad_add_fusion.core_ref.place_ref, f32[8]{0:T(128)} %regular_ref.7, bf16[512,1024]{1,0:T(8,128)(2,1)} %convolution_convert_fusion.q_ref, bf16[512,1024]{1,0:T(8,128)(2,1)} %bitcast.50, bf16[512,1024]{1,0:T(8,128)(2,1)} %bitcast.56, ...), custom_call_target="tpu_custom_call" | custom-call | flops 1342177280 | bytes 1835008 | tf_op jit(solution)/shard_map/solve_heads/pallas_call | solution.py:299
  63.3 8.3 %solve_heads.5 = (bf16[512,1024]{1,0:T(8,128)(2,1)}, f32[2,128,512]{2,1,0:T(8,128)}) custom-call(s32[3]{0:T(128)} %pad_add_fusion.core_ref.place_ref, f32[8]{0:T(128)} %regular_ref.7, bf16[512,1024]{1,0:T(8,128)(2,1)} %convolution_convert_fusion.q_ref, bf16[512,1024]{1,0:T(8,128)(2,1)} %bitcast.51, ...), custom_call_target="tpu_custom_call", output_to_operand_aliasing={{0}: (8, {})} | custom-call | flops 1342177280 | bytes 1835008 | tf_op jit(solution)/shard_map/solve_heads/pallas_call | solution.py:299
  72.6 1.7 shard_map.87
  74.3 5.3 %collective-permute-start.2 = (f32[1,392,128]{2,1,0:T(8,128)}, f32[1,392,128]{2,1,0:T(8,128)S(1)}, u32[]{:S(2)}, u32[]{:S(2)}) collective-permute-start(f32[1,392,128]{2,1,0:T(8,128)} %shard_map.87), channel_id=1, source_target_pairs={{0,4},{1,5},{2,6},{3,7},{8,12},{9,13},{10,14},{11,15},{16,20},{17,... | collective-permute-start | bytes 602120 | tf_op jit(solution)/shard_map/ppermute | solution.py:453
  79.6 4.8 %collective-permute-done.2.far_ref = f32[1,392,128]{2,1,0:T(8,128)S(1)} collective-permute-done((f32[1,392,128]{2,1,0:T(8,128)}, f32[1,392,128]{2,1,0:T(8,128)S(1)}, u32[]{:S(2)}, u32[]{:S(2)}) %collective-permute-start.2) | collective-permute-done | bytes 200736 | tf_op jit(solution)/shard_map/ppermute | solution.py:453
  85.1 2.1 %shard_map.88 = (f32[1,392,128]{2,1,0:T(8,128)}, f32[1,392,128]{2,1,0:T(8,128)}) custom-call(s32[3]{0:T(128)} %pad_add_fusion.core_ref.place_ref, f32[1,392,128]{2,1,0:T(8,128)} %copy-done.15, f32[1,392,128]{2,1,0:T(8,128)} %copy-done.3, f32[1,392,128]{2,1,0:T(8,128)} %get-tuple-element.29.own_ref, f32[1,392,128]{2,1,0:T(8,128)} %copy-done.2), custom_call_target="tpu_custom_call" | custom-call | bytes 1204224 | tf_op jit(solution)/shard_map/pallas_call | solution.py:158
  87.2 8.3 %solve_heads.6 = (bf16[512,1024]{1,0:T(8,128)(2,1)}, f32[2,128,512]{2,1,0:T(8,128)}) custom-call(s32[3]{0:T(128)} %pad_add_fusion.core_ref.place_ref, f32[8]{0:T(128)} %regular_ref.7, bf16[512,1024]{1,0:T(8,128)(2,1)} %convolution_convert_fusion.q_ref, bf16[512,1024]{1,0:T(8,128)(2,1)} %bitcast.52, ...), custom_call_target="tpu_custom_call", output_to_operand_aliasing={{0}: (8, {})} | custom-call | flops 1342177280 | bytes 1835008 | tf_op jit(solution)/shard_map/solve_heads/pallas_call | solution.py:299
  96.0 3.6 %narrow.1.other_ref = bf16[4,512,256]{2,1,0:T(8,128)(2,1)} custom-call(f32[4,512,256]{2,1,0:T(8,128)} %collective-permute-done.10.in_ref), custom_call_target="tpu_custom_call" | custom-call | bytes 3145728 | tf_op jit(solution)/shard_map/narrow/pallas_call | solution.py:346
  99.6 0.8 copy-done.9
  100.3 0.8 copy-done.11
  101.1 6.1 %gradient_blocks.2 = (f32[2,4,64,256]{3,2,1,0:T(8,128)}, f32[2,4,64,256]{3,2,1,0:T(8,128)}, f32[2,4,64,256]{3,2,1,0:T(8,128)}, f32[2,4,64,256]{3,2,1,0:T(8,128)}) custom-call(s32[3]{0:T(128)} %pad_add_fusion.core_ref.place_ref, f32[2,128,512]{2,1,0:T(8,128)} %get-tuple-element.41.own0, f32[2,128,512]{2,1,0:T(8,128)} %get-tuple-element.42.own1, ...), custom_call_target="tpu_custom_call" | custom-call | flops 1073741824 | bytes 6291456 | tf_op jit(solution)/shard_map/gradient_blocks/pallas_call | solution.py:386
  107.9 8.4 %solve_heads.7 = (bf16[512,1024]{1,0:T(8,128)(2,1)}, f32[2,128,512]{2,1,0:T(8,128)}) custom-call(s32[3]{0:T(128)} %pad_add_fusion.core_ref.place_ref, f32[8]{0:T(128)} %regular_ref.7, bf16[512,1024]{1,0:T(8,128)(2,1)} %convolution_convert_fusion.q_ref, bf16[512,1024]{1,0:T(8,128)(2,1)} %bitcast.53, ...), custom_call_target="tpu_custom_call", output_to_operand_aliasing={{0}: (8, {})} | custom-call | flops 1342177280 | bytes 1835008 | tf_op jit(solution)/shard_map/solve_heads/pallas_call | solution.py:299
  116.3 1.6 collective-permute-start.13
  117.9 1.5 collective-permute-start.11
  119.4 0.8 copy-done.10
  120.2 0.8 copy-done.12
  121.0 6.0 %gradient_blocks.3 = (f32[2,4,64,256]{3,2,1,0:T(8,128)}, f32[2,4,64,256]{3,2,1,0:T(8,128)}, f32[2,4,64,256]{3,2,1,0:T(8,128)}, f32[2,4,64,256]{3,2,1,0:T(8,128)}) custom-call(s32[3]{0:T(128)} %pad_add_fusion.core_ref.place_ref, f32[2,128,512]{2,1,0:T(8,128)} %get-tuple-element.48.own0, f32[2,128,512]{2,1,0:T(8,128)} %get-tuple-element.49.own1, ...), custom_call_target="tpu_custom_call" | custom-call | flops 1073741824 | bytes 6291456 | tf_op jit(solution)/shard_map/gradient_blocks/pallas_call | solution.py:386
  127.6 3.8 %collective-permute-done.13 = f32[2,4,64,256]{3,2,1,0:T(8,128)S(1)} collective-permute-done((f32[2,4,64,256]{3,2,1,0:T(8,128)}, f32[2,4,64,256]{3,2,1,0:T(8,128)S(1)}, u32[]{:S(2)}, u32[]{:S(2)}) %collective-permute-start.13) | collective-permute-done | bytes 524320 | tf_op jit(solution)/shard_map/ppermute | solution.py:497
  131.5 1.6 collective-permute-start.14
  133.7 1.6 collective-permute-start.12
  135.3 5.4 %collective-permute-done.14 = f32[1,4,64,256]{3,2,1,0:T(8,128)S(1)} collective-permute-done((f32[1,4,64,256]{3,2,1,0:T(8,128)S(1)}, f32[1,4,64,256]{3,2,1,0:T(8,128)S(1)}, u32[]{:S(2)}, u32[]{:S(2)}) %collective-permute-start.14) | collective-permute-done | bytes 262176 | tf_op jit(solution)/shard_map/ppermute | solution.py:497
  140.8 1.8 %collective-permute-done.22 = f32[2,4,64,256]{3,2,1,0:T(8,128)S(1)} collective-permute-done((f32[2,4,64,256]{3,2,1,0:T(8,128)}, f32[2,4,64,256]{3,2,1,0:T(8,128)S(1)}, u32[]{:S(2)}, u32[]{:S(2)}) %collective-permute-start.22) | collective-permute-done | bytes 524320 | tf_op jit(solution)/shard_map/ppermute | solution.py:497
  142.7 1.6 collective-permute-start.23
  144.3 3.4 %collective-permute-done.12 = f32[1,4,64,256]{3,2,1,0:T(8,128)S(1)} collective-permute-done((f32[1,4,64,256]{3,2,1,0:T(8,128)S(1)}, f32[1,4,64,256]{3,2,1,0:T(8,128)S(1)}, u32[]{:S(2)}, u32[]{:S(2)}) %collective-permute-start.12) | collective-permute-done | bytes 262176 | tf_op jit(solution)/shard_map/ppermute | solution.py:497
  147.8 4.2 %collective-permute-done.20 = f32[2,4,64,256]{3,2,1,0:T(8,128)S(1)} collective-permute-done((f32[2,4,64,256]{3,2,1,0:T(8,128)S(1)}, f32[2,4,64,256]{3,2,1,0:T(8,128)S(1)}, u32[]{:S(2)}, u32[]{:S(2)}) %collective-permute-start.20) | collective-permute-done | bytes 524320 | tf_op jit(solution)/shard_map/ppermute | solution.py:497
  152.1 1.6 collective-permute-start.21
  153.7 4.0 %collective-permute-start.15 = (f32[128,256]{1,0:T(8,128)S(1)}, f32[128,256]{1,0:T(8,128)S(1)}, u32[]{:S(2)}, u32[]{:S(2)}) collective-permute-start(f32[128,256]{1,0:T(8,128)S(1)} %get-tuple-element.54), channel_id=1, source_target_pairs={{0,2},{1,3},{2,0},{3,1},{4,6},{5,7},{6,4},{7,5},{8,10},{9,11},{10,... | collective-permute-start | bytes 393224 | tf_op jit(solution)/shard_map/ppermute | solution.py:504
  157.7 3.3 %collective-permute-start.16 = (f32[128,256]{1,0:T(8,128)S(1)}, f32[128,256]{1,0:T(8,128)S(1)}, u32[]{:S(2)}, u32[]{:S(2)}) collective-permute-start(f32[128,256]{1,0:T(8,128)S(1)} %get-tuple-element.56), channel_id=1, source_target_pairs={{0,4},{1,5},{2,6},{3,7},{4,0},{5,1},{6,2},{7,3},{8,12},{9,13},{10,... | collective-permute-start | bytes 393224 | tf_op jit(solution)/shard_map/ppermute | solution.py:504
  161.1 1.5 collective-permute-start.24
  162.6 3.3 %collective-permute-start.25 = (f32[128,256]{1,0:T(8,128)S(1)}, f32[128,256]{1,0:T(8,128)S(1)}, u32[]{:S(2)}, u32[]{:S(2)}) collective-permute-start(f32[128,256]{1,0:T(8,128)S(1)} %get-tuple-element.59), channel_id=1, source_target_pairs={{0,4},{1,5},{2,6},{3,7},{4,0},{5,1},{6,2},{7,3},{8,12},{9,13},{10,... | collective-permute-start | bytes 393224 | tf_op jit(solution)/shard_map/ppermute | solution.py:504
  165.9 2.4 %collective-permute-start.26 = (f32[128,256]{1,0:T(8,128)S(1)}, f32[128,256]{1,0:T(8,128)S(1)}, u32[]{:S(2)}, u32[]{:S(2)}) collective-permute-start(f32[128,256]{1,0:T(8,128)S(1)} %get-tuple-element.58), channel_id=1, source_target_pairs={{0,6},{1,7},{2,4},{3,5},{4,2},{5,3},{6,0},{7,1},{8,14},{9,15},{10,... | collective-permute-start | bytes 393224 | tf_op jit(solution)/shard_map/ppermute | solution.py:504
  168.2 2.6 %collective-permute-done.16 = f32[128,256]{1,0:T(8,128)S(1)} collective-permute-done((f32[128,256]{1,0:T(8,128)S(1)}, f32[128,256]{1,0:T(8,128)S(1)}, u32[]{:S(2)}, u32[]{:S(2)}) %collective-permute-start.16) | collective-permute-done | bytes 131104 | tf_op jit(solution)/shard_map/ppermute | solution.py:504
  170.9 7.7 %collective-permute-done.25 = f32[128,256]{1,0:T(8,128)S(1)} collective-permute-done((f32[128,256]{1,0:T(8,128)S(1)}, f32[128,256]{1,0:T(8,128)S(1)}, u32[]{:S(2)}, u32[]{:S(2)}) %collective-permute-start.25) | collective-permute-done | bytes 131104 | tf_op jit(solution)/shard_map/ppermute | solution.py:504
  178.6 0.7 pad_maximum_fusion
  (79 shorter events, 9.2 us)
Async XLA Ops:
  5.5 90.4 %collective-permute-start.10 = (f32[4,512,256]{2,1,0:T(8,128)}, f32[4,512,256]{2,1,0:T(8,128)}, u32[]{:S(2)}, u32[]{:S(2)}) collective-permute-start(f32[4,512,256]{2,1,0:T(8,128)} %pick_columns.1), channel_id=1, source_target_pairs={{0,1},{1,0},{2,3},{3,2},{4,5},{5,4},{6,7},{7,6},{8,9},{9,8},{10,11... | collective-permute-start | bytes 6291464 | tf_op jit(solution)/shard_map/ppermute | solution.py:460
  10.0 28.8 %copy-start = (bf16[1,512,2048]{2,1,0:T(8,128)(2,1)S(1)}, bf16[1,512,2048]{2,1,0:T(8,128)(2,1)}, u32[]{:S(2)}) copy-start(bf16[1,512,2048]{2,1,0:T(8,128)(2,1)} %param.7) | copy-start | bytes 6291460
  10.0 1.7 collective-permute-start.4
  11.6 0.7 copy-start.4
  14.1 9.7 %collective-permute-start.5 = (f32[1,392,128]{2,1,0:T(8,128)}, f32[1,392,128]{2,1,0:T(8,128)S(1)}, u32[]{:S(2)}, u32[]{:S(2)}) collective-permute-start(f32[1,392,128]{2,1,0:T(8,128)} %shard_map.89.later_ref), channel_id=1, source_target_pairs={{0,2},{1,3},{2,4},{3,5},{4,6},{5,7},{8,10},{9,11},{10,12},{11,13},... | collective-permute-start | bytes 602120 | tf_op jit(solution)/shard_map/ppermute | solution.py:453
  23.8 0.7 copy-start.5
  26.2 9.6 %collective-permute-start.6 = (f32[1,392,128]{2,1,0:T(8,128)}, f32[1,392,128]{2,1,0:T(8,128)S(1)}, u32[]{:S(2)}, u32[]{:S(2)}) collective-permute-start(f32[1,392,128]{2,1,0:T(8,128)} %shard_map.90), channel_id=1, source_target_pairs={{0,4},{1,5},{2,6},{3,7},{8,12},{9,13},{10,14},{11,15},{16,20},{17,... | collective-permute-start | bytes 602120 | tf_op jit(solution)/shard_map/ppermute | solution.py:453
  35.5 8.8 %collective-permute-start = (f32[1,392,128]{2,1,0:T(8,128)}, f32[1,392,128]{2,1,0:T(8,128)S(1)}, u32[]{:S(2)}, u32[]{:S(2)}) collective-permute-start(f32[1,392,128]{2,1,0:T(8,128)} %get-tuple-element.30), channel_id=1, source_target_pairs={{0,1},{1,0},{2,3},{3,2},{4,5},{5,4},{6,7},{7,6},{8,9},{9,8},{10,11... | collective-permute-start | bytes 602120 | tf_op jit(solution)/shard_map/ppermute | solution.py:440
  35.8 0.7 copy-start.14
  38.5 24.1 %collective-permute-start.7 = (f32[1,392,128]{2,1,0:T(8,128)}, f32[1,392,128]{2,1,0:T(8,128)S(1)}, u32[]{:S(2)}, u32[]{:S(2)}) collective-permute-start(f32[1,392,128]{2,1,0:T(8,128)} %get-tuple-element.36), channel_id=1, source_target_pairs={{0,1},{1,0},{2,3},{3,2},{4,5},{5,4},{6,7},{7,6},{8,9},{9,8},{10,11... | collective-permute-start | bytes 602120 | tf_op jit(solution)/shard_map/ppermute | solution.py:457
  44.3 0.7 copy-start.2
  46.7 25.2 %collective-permute-start.1 = (f32[1,392,128]{2,1,0:T(8,128)}, f32[1,392,128]{2,1,0:T(8,128)S(1)}, u32[]{:S(2)}, u32[]{:S(2)}) collective-permute-start(f32[1,392,128]{2,1,0:T(8,128)} %shard_map.86.later_ref), channel_id=1, source_target_pairs={{0,2},{1,3},{2,4},{3,5},{4,6},{5,7},{8,10},{9,11},{10,12},{11,13},... | collective-permute-start | bytes 602120 | tf_op jit(solution)/shard_map/ppermute | solution.py:453
  62.4 37.1 %collective-permute-start.8 = (f32[2,128,512]{2,1,0:T(8,128)}, f32[2,128,512]{2,1,0:T(8,128)S(1)}, u32[]{:S(2)}, u32[]{:S(2)}) collective-permute-start(f32[2,128,512]{2,1,0:T(8,128)} %get-tuple-element.41.own0), channel_id=1, source_target_pairs={{0,1},{1,0},{2,3},{3,2},{4,5},{5,4},{6,7},{7,6},{8,9},{9,8},{10,11... | collective-permute-start | bytes 1572872 | tf_op jit(solution)/shard_map/ppermute | solution.py:474
  62.6 0.7 copy-start.13
  71.6 28.0 %collective-permute-start.9 = (f32[2,128,512]{2,1,0:T(8,128)}, f32[2,128,512]{2,1,0:T(8,128)S(1)}, u32[]{:S(2)}, u32[]{:S(2)}) collective-permute-start(f32[2,128,512]{2,1,0:T(8,128)} %get-tuple-element.42.own1), channel_id=1, source_target_pairs={{0,1},{1,0},{2,3},{3,2},{4,5},{5,4},{6,7},{7,6},{8,9},{9,8},{10,11... | collective-permute-start | bytes 1572872 | tf_op jit(solution)/shard_map/ppermute | solution.py:474
  71.9 0.7 copy-start.3
  74.3 10.1 %collective-permute-start.2 = (f32[1,392,128]{2,1,0:T(8,128)}, f32[1,392,128]{2,1,0:T(8,128)S(1)}, u32[]{:S(2)}, u32[]{:S(2)}) collective-permute-start(f32[1,392,128]{2,1,0:T(8,128)} %shard_map.87), channel_id=1, source_target_pairs={{0,4},{1,5},{2,6},{3,7},{8,12},{9,13},{10,14},{11,15},{16,20},{17,... | collective-permute-start | bytes 602120 | tf_op jit(solution)/shard_map/ppermute | solution.py:453
  84.4 0.7 copy-start.15
  87.2 20.0 %collective-permute-start.3 = (f32[1,392,128]{2,1,0:T(8,128)}, f32[1,392,128]{2,1,0:T(8,128)S(1)}, u32[]{:S(2)}, u32[]{:S(2)}) collective-permute-start(f32[1,392,128]{2,1,0:T(8,128)} %get-tuple-element.31), channel_id=1, source_target_pairs={{0,1},{1,0},{2,3},{3,2},{4,5},{5,4},{6,7},{7,6},{8,9},{9,8},{10,11... | collective-permute-start | bytes 602120 | tf_op jit(solution)/shard_map/ppermute | solution.py:457
  95.5 24.0 %collective-permute-start.18 = (f32[2,128,512]{2,1,0:T(8,128)}, f32[2,128,512]{2,1,0:T(8,128)S(1)}, u32[]{:S(2)}, u32[]{:S(2)}) collective-permute-start(f32[2,128,512]{2,1,0:T(8,128)} %get-tuple-element.48.own0), channel_id=1, source_target_pairs={{0,1},{1,0},{2,3},{3,2},{4,5},{5,4},{6,7},{7,6},{8,9},{9,8},{10,11... | collective-permute-start | bytes 1572872 | tf_op jit(solution)/shard_map/ppermute | solution.py:474
  99.5 0.8 copy-start.9
  100.3 0.8 copy-start.11
  107.2 0.7 copy-start.16
  107.9 10.0 %copy-start.17 = (f32[2,4,64,256]{3,2,1,0:T(8,128)S(1)}, f32[2,4,64,256]{3,2,1,0:T(8,128)}, u32[]{:S(2)}) copy-start(f32[2,4,64,256]{3,2,1,0:T(8,128)} %get-tuple-element.45) | copy-start | bytes 1572868
  116.3 3.1 %collective-permute-start.19 = (f32[2,128,512]{2,1,0:T(8,128)}, f32[2,128,512]{2,1,0:T(8,128)S(1)}, u32[]{:S(2)}, u32[]{:S(2)}) collective-permute-start(f32[2,128,512]{2,1,0:T(8,128)} %get-tuple-element.49.own1), channel_id=1, source_target_pairs={{0,1},{1,0},{2,3},{3,2},{4,5},{5,4},{6,7},{7,6},{8,9},{9,8},{10,11... | collective-permute-start | bytes 1572872 | tf_op jit(solution)/shard_map/ppermute | solution.py:474
  116.3 15.1 %collective-permute-start.13 = (f32[2,4,64,256]{3,2,1,0:T(8,128)}, f32[2,4,64,256]{3,2,1,0:T(8,128)S(1)}, u32[]{:S(2)}, u32[]{:S(2)}) collective-permute-start(f32[2,4,64,256]{3,2,1,0:T(8,128)} %get-tuple-element.47), channel_id=1, source_target_pairs={{0,16},{8,24},{16,0},{24,8},{1,17},{9,25},{17,1},{25,9},{2,18},{10... | collective-permute-start | bytes 1572872 | tf_op jit(solution)/shard_map/ppermute | solution.py:497
  117.9 13.5 %copy-start.7 = (f32[2,4,64,256]{3,2,1,0:T(8,128)S(1)}, f32[2,4,64,256]{3,2,1,0:T(8,128)}, u32[]{:S(2)}) copy-start(f32[2,4,64,256]{3,2,1,0:T(8,128)} %get-tuple-element.46) | copy-start | bytes 1572868
  117.9 15.7 %collective-permute-start.11 = (f32[2,4,64,256]{3,2,1,0:T(8,128)S(1)}, f32[2,4,64,256]{3,2,1,0:T(8,128)S(1)}, u32[]{:S(2)}, u32[]{:S(2)}) collective-permute-start(f32[2,4,64,256]{3,2,1,0:T(8,128)S(1)} %copy-done.17), channel_id=1, source_target_pairs={{0,8},{8,0},{16,24},{24,16},{1,9},{9,1},{17,25},{25,17},{2,10},{10... | collective-permute-start | bytes 1572872 | tf_op jit(solution)/shard_map/ppermute | solution.py:497
  119.4 0.8 copy-start.10
  120.2 0.8 copy-start.12
  127.0 6.1 %copy-start.18 = (f32[2,4,64,256]{3,2,1,0:T(8,128)S(1)}, f32[2,4,64,256]{3,2,1,0:T(8,128)}, u32[]{:S(2)}) copy-start(f32[2,4,64,256]{3,2,1,0:T(8,128)} %get-tuple-element.51) | copy-start | bytes 1572868
  127.0 6.6 %copy-start.1 = (f32[2,4,64,256]{3,2,1,0:T(8,128)S(1)}, f32[2,4,64,256]{3,2,1,0:T(8,128)}, u32[]{:S(2)}) copy-start(f32[2,4,64,256]{3,2,1,0:T(8,128)} %get-tuple-element.43.rest_1_) | copy-start | bytes 1572868
  127.0 15.6 %collective-permute-start.22 = (f32[2,4,64,256]{3,2,1,0:T(8,128)}, f32[2,4,64,256]{3,2,1,0:T(8,128)S(1)}, u32[]{:S(2)}, u32[]{:S(2)}) collective-permute-start(f32[2,4,64,256]{3,2,1,0:T(8,128)} %get-tuple-element.53), channel_id=1, source_target_pairs={{0,16},{8,24},{16,0},{24,8},{1,17},{9,25},{17,1},{25,9},{2,18},{10... | collective-permute-start | bytes 1572872 | tf_op jit(solution)/shard_map/ppermute | solution.py:497
  131.5 11.2 %copy-start.8 = (f32[2,4,64,256]{3,2,1,0:T(8,128)S(1)}, f32[2,4,64,256]{3,2,1,0:T(8,128)}, u32[]{:S(2)}) copy-start(f32[2,4,64,256]{3,2,1,0:T(8,128)} %get-tuple-element.52) | copy-start | bytes 1572868
  131.5 9.2 %collective-permute-start.14 = (f32[1,4,64,256]{3,2,1,0:T(8,128)S(1)}, f32[1,4,64,256]{3,2,1,0:T(8,128)S(1)}, u32[]{:S(2)}, u32[]{:S(2)}) collective-permute-start(f32[1,4,64,256]{3,2,1,0:T(8,128)S(1)} %slice.67), channel_id=1, source_target_pairs={{0,8},{8,0},{16,24},{24,16},{1,9},{9,1},{17,25},{25,17},{2,10},{10... | collective-permute-start | bytes 786440 | tf_op jit(solution)/shard_map/ppermute | solution.py:497
  133.1 18.9 %collective-permute-start.20 = (f32[2,4,64,256]{3,2,1,0:T(8,128)S(1)}, f32[2,4,64,256]{3,2,1,0:T(8,128)S(1)}, u32[]{:S(2)}, u32[]{:S(2)}) collective-permute-start(f32[2,4,64,256]{3,2,1,0:T(8,128)S(1)} %copy-done.18), channel_id=1, source_target_pairs={{0,8},{8,0},{16,24},{24,16},{1,9},{9,1},{17,25},{25,17},{2,10},{10... | collective-permute-start | bytes 1572872 | tf_op jit(solution)/shard_map/ppermute | solution.py:497
  133.7 18.3 %copy-start.6 = (f32[2,4,64,256]{3,2,1,0:T(8,128)S(1)}, f32[2,4,64,256]{3,2,1,0:T(8,128)}, u32[]{:S(2)}) copy-start(f32[2,4,64,256]{3,2,1,0:T(8,128)} %get-tuple-element.50) | copy-start | bytes 1572868
  133.7 14.0 %collective-permute-start.12 = (f32[1,4,64,256]{3,2,1,0:T(8,128)S(1)}, f32[1,4,64,256]{3,2,1,0:T(8,128)S(1)}, u32[]{:S(2)}, u32[]{:S(2)}) collective-permute-start(f32[1,4,64,256]{3,2,1,0:T(8,128)S(1)} %slice.65), channel_id=1, source_target_pairs={{0,16},{8,24},{16,0},{24,8},{1,17},{9,25},{17,1},{25,9},{2,18},{10... | collective-permute-start | bytes 786440 | tf_op jit(solution)/shard_map/ppermute | solution.py:497
  142.7 18.2 %collective-permute-start.23 = (f32[1,4,64,256]{3,2,1,0:T(8,128)S(1)}, f32[1,4,64,256]{3,2,1,0:T(8,128)S(1)}, u32[]{:S(2)}, u32[]{:S(2)}) collective-permute-start(f32[1,4,64,256]{3,2,1,0:T(8,128)S(1)} %slice.77), channel_id=1, source_target_pairs={{0,8},{8,0},{16,24},{24,16},{1,9},{9,1},{17,25},{25,17},{2,10},{10... | collective-permute-start | bytes 786440 | tf_op jit(solution)/shard_map/ppermute | solution.py:497
  152.1 8.9 %collective-permute-start.21 = (f32[1,4,64,256]{3,2,1,0:T(8,128)S(1)}, f32[1,4,64,256]{3,2,1,0:T(8,128)S(1)}, u32[]{:S(2)}, u32[]{:S(2)}) collective-permute-start(f32[1,4,64,256]{3,2,1,0:T(8,128)S(1)} %slice.75), channel_id=1, source_target_pairs={{0,16},{8,24},{16,0},{24,8},{1,17},{9,25},{17,1},{25,9},{2,18},{10... | collective-permute-start | bytes 786440 | tf_op jit(solution)/shard_map/ppermute | solution.py:497
  153.7 12.2 %collective-permute-start.15 = (f32[128,256]{1,0:T(8,128)S(1)}, f32[128,256]{1,0:T(8,128)S(1)}, u32[]{:S(2)}, u32[]{:S(2)}) collective-permute-start(f32[128,256]{1,0:T(8,128)S(1)} %get-tuple-element.54), channel_id=1, source_target_pairs={{0,2},{1,3},{2,0},{3,1},{4,6},{5,7},{6,4},{7,5},{8,10},{9,11},{10,... | collective-permute-start | bytes 393224 | tf_op jit(solution)/shard_map/ppermute | solution.py:504
  157.7 13.2 %collective-permute-start.16 = (f32[128,256]{1,0:T(8,128)S(1)}, f32[128,256]{1,0:T(8,128)S(1)}, u32[]{:S(2)}, u32[]{:S(2)}) collective-permute-start(f32[128,256]{1,0:T(8,128)S(1)} %get-tuple-element.56), channel_id=1, source_target_pairs={{0,4},{1,5},{2,6},{3,7},{4,0},{5,1},{6,2},{7,3},{8,12},{9,13},{10,... | collective-permute-start | bytes 393224 | tf_op jit(solution)/shard_map/ppermute | solution.py:504
  161.0 9.9 %collective-permute-start.17 = (f32[128,256]{1,0:T(8,128)S(1)}, f32[128,256]{1,0:T(8,128)S(1)}, u32[]{:S(2)}, u32[]{:S(2)}) collective-permute-start(f32[128,256]{1,0:T(8,128)S(1)} %get-tuple-element.55), channel_id=1, source_target_pairs={{0,6},{1,7},{2,4},{3,5},{4,2},{5,3},{6,0},{7,1},{8,14},{9,15},{10,... | collective-permute-start | bytes 393224 | tf_op jit(solution)/shard_map/ppermute | solution.py:504
  161.1 9.8 %collective-permute-start.24 = (f32[128,256]{1,0:T(8,128)S(1)}, f32[128,256]{1,0:T(8,128)S(1)}, u32[]{:S(2)}, u32[]{:S(2)}) collective-permute-start(f32[128,256]{1,0:T(8,128)S(1)} %get-tuple-element.57), channel_id=1, source_target_pairs={{0,2},{1,3},{2,0},{3,1},{4,6},{5,7},{6,4},{7,5},{8,10},{9,11},{10,... | collective-permute-start | bytes 393224 | tf_op jit(solution)/shard_map/ppermute | solution.py:504
  162.6 16.0 %collective-permute-start.25 = (f32[128,256]{1,0:T(8,128)S(1)}, f32[128,256]{1,0:T(8,128)S(1)}, u32[]{:S(2)}, u32[]{:S(2)}) collective-permute-start(f32[128,256]{1,0:T(8,128)S(1)} %get-tuple-element.59), channel_id=1, source_target_pairs={{0,4},{1,5},{2,6},{3,7},{4,0},{5,1},{6,2},{7,3},{8,12},{9,13},{10,... | collective-permute-start | bytes 393224 | tf_op jit(solution)/shard_map/ppermute | solution.py:504
  165.9 12.7 %collective-permute-start.26 = (f32[128,256]{1,0:T(8,128)S(1)}, f32[128,256]{1,0:T(8,128)S(1)}, u32[]{:S(2)}, u32[]{:S(2)}) collective-permute-start(f32[128,256]{1,0:T(8,128)S(1)} %get-tuple-element.58), channel_id=1, source_target_pairs={{0,6},{1,7},{2,4},{3,5},{4,2},{5,3},{6,0},{7,1},{8,14},{9,15},{10,... | collective-permute-start | bytes 393224 | tf_op jit(solution)/shard_map/ppermute | solution.py:504

commit v2 on v1

--- a/solution.py
+++ b/solution.py
@@ -167,11 +167,9 @@
     return results[0] if outs == 1 else results
 
 
-def solve_kernel(
-    head_of, place_ref, regular_ref, q_ref, k_ref, v_ref, g_ref, rows_ref, state_ref, *rest
-):
-    mixed_ref, turned_ref = rest[-2:]
-    rows, dim = q_ref.shape
+def solve_kernel(is_query, head_of, place_ref, regular_ref, row_ref, k_ref, v_ref, rows_ref, state_ref, *rest):
+    out_ref = rest[-1]
+    rows, dim = row_ref.shape
     pieces = range(rows // SUB)
     place = [slice(c * SUB, (c + 1) * SUB) for c in pieces]
     step = pl.program_id(0)
@@ -217,6 +215,9 @@
     ]
     scale = [jnp.exp(r) for r in rise]
 
+    def twice(value, axis=0):
+        return jnp.concatenate([value, value], axis=axis)
+
     keys = [k_ref[at, :] for at in place]
     values = [v_ref[at, :] for at in place]
     keys_turned = [key.astype(F32).T for key in keys]
@@ -225,53 +226,50 @@
         tail = jnp.exp(last[c] - cumulative[c])
         decay = jnp.exp(last[c])
         both = jnp.concatenate([keys_turned[c] * tail, values_turned[c] * tail], axis=0)
-        grown = dot(wide(both), jnp.concatenate([keys[c], keys[c]], axis=0))
+        grown = dot(wide(both), twice(keys[c]))
         gram.append(decay * gram[-1] + grown[0:dim])
         memory.append(decay * memory[-1] + grown[dim:])
     keys_turned = [key.astype(BF16) for key in keys_turned]
-    values_turned = [value.astype(BF16) for value in values_turned]
-
-    def pair(left, right):
-        return jnp.concatenate([left, right], axis=0)
-
-    residual = []
-    for c in pieces:
-        grad = g_ref[place[c], :]
-        pulled = scale[c] * dot(jnp.concatenate([grad, grad], axis=1), wide(memory[c], 0))
-        score = weights[c] * dot(grad, values_turned[c])
-        pulled = pulled + dot(wide(score), pair(keys[c], keys[c]))
-        residual.append(pair(q_ref[place[c], :].astype(F32), pulled))
+
+    if is_query:
+        residual = [row_ref[at, :].astype(F32) for at in place]
+    else:
+        residual = []
+        for c in pieces:
+            grad = row_ref[place[c], :]
+            pulled = scale[c] * dot(twice(grad, 1), wide(memory[c], 0))
+            score = weights[c] * dot(grad, values_turned[c].astype(BF16))
+            residual.append(pulled + dot(wide(score), twice(keys[c])))
 
     alpha = column(0)
-    change = [pair(alpha[c], alpha[c]) * residual[c] for c in pieces]
+    change = [alpha[c] * residual[c] for c in pieces]
     solution = list(change)
     rights = [jnp.concatenate([keys_turned[c], gram[c].astype(BF16)], axis=1) for c in pieces]
     for i in range(1, ITERS):
         alpha, gamma = column(i), column(ITERS + i - 1)
         first = [dot(change[c].astype(BF16), rights[c]) for c in pieces]
-        second = [
-            dot((first[c][:, 0:SUB] * pair(weights[c], weights[c])).astype(BF16), keys[c]) for c in pieces
-        ]
+        second = [dot((first[c][:, 0:SUB] * weights[c]).astype(BF16), keys[c]) for c in pieces]
         for c in pieces:
-            applied = ridge * change[c] + (pair(scale[c], scale[c]) * first[c][:, SUB:] + second[c])
+            applied = ridge * change[c] + (scale[c] * first[c][:, SUB:] + second[c])
             residual[c] = residual[c] - applied
-            change[c] = pair(alpha[c], alpha[c]) * residual[c] + pair(gamma[c], gamma[c]) * change[c]
+            change[c] = alpha[c] * residual[c] + gamma[c] * change[c]
             solution[c] = solution[c] + change[c]
 
     for c in pieces:
-        turned_ref[0, :, place[c]] = solution[c][SUB:].T.astype(BF16).astype(F32)
-    for c in pieces:
-        high, low = split(solution[c][0:SUB])
+        if not is_query:
+            out_ref[0, :, place[c]] = solution[c].T.astype(BF16).astype(F32)
+            continue
+        high, low = split(solution[c])
         memory_high, memory_low = split(memory[c].T)
         right = jnp.concatenate([keys_turned[c], memory_high], axis=1)
-        first = dot(jnp.concatenate([high, low], axis=1), pair(right, right))
+        first = dot(jnp.concatenate([high, low], axis=1), twice(right))
         second = first[:, SUB:] + dot(high, memory_low)
         score = weights[c] * first[:, 0:SUB]
-        output = scale[c] * second + dot(wide(score), pair(values[c], values[c]))
-        mixed_ref[place[c], :] = output.astype(BF16)
-
-
-def solve_heads(place, k, side, per, regular, queries, keys, values, grads, table, states, mixed, after):
+        output = scale[c] * second + dot(wide(score), twice(values[c]))
+        out_ref[place[c], :] = output.astype(BF16)
+
+
+def solve_heads(is_query, place, k, side, per, regular, sides, keys, values, table, states, mixed, after):
     rows, columns = keys.shape
     heads = regular.shape[0]
     dim = columns // heads
@@ -284,9 +282,9 @@
     def at_head(step, place_ref, regular_ref):
         return (0, head_of(step, place_ref))
 
-    wide_spec = pl.BlockSpec((rows, dim), at_head)
-    operands = [queries, keys, values, grads, table, states]
-    in_specs = [wide_spec] * 4 + [pl.BlockSpec(table.shape, lambda step, *_: (0, 0, 0))]
+    head_spec = pl.BlockSpec((rows, dim), at_head)
+    operands = [sides, keys, values, table, states]
+    in_specs = [head_spec] * 3 + [pl.BlockSpec(table.shape, lambda step, *_: (0, 0, 0))]
     in_specs.append(pl.BlockSpec((1,) + states.shape[1:], lambda step, *_: (step // 2, 0, 0)))
     aliases = {}
     if mixed is not None:
@@ -296,23 +294,22 @@
     if after is not None:
         operands.append(after)
         in_specs.append(pl.BlockSpec(memory_space=pl.ANY))
+    if is_query:
+        shape, spec = jax.ShapeDtypeStruct((rows, columns), BF16), head_spec
+    else:
+        shape = jax.ShapeDtypeStruct((count, dim, rows), F32)
+        spec = pl.BlockSpec((1, dim, rows), lambda step, *_: (step, 0, 0))
     return pl.pallas_call(
-        functools.partial(solve_kernel, head_of),
-        out_shape=[
-            jax.ShapeDtypeStruct((rows, columns), BF16),
-            jax.ShapeDtypeStruct((count, dim, rows), F32),
-        ],
+        functools.partial(solve_kernel, is_query, head_of),
+        out_shape=shape,
         grid_spec=pltpu.PrefetchScalarGridSpec(
-            num_scalar_prefetch=2,
-            grid=(count,),
-            in_specs=in_specs,
-            out_specs=[wide_spec, pl.BlockSpec((1, dim, rows), lambda step, *_: (step, 0, 0))],
+            num_scalar_prefetch=2, grid=(count,), in_specs=in_specs, out_specs=spec
         ),
         input_output_aliases=aliases,
         cost_estimate=pl.CostEstimate(
             flops=count * 80 * rows * dim * dim, bytes_accessed=count * 14 * rows * dim, transcendentals=0
         ),
-        name="solve_heads",
+        name="solve_queries" if is_query else "solve_gradients",
     )(place, regular, *operands)
 
 
@@ -465,14 +462,13 @@
     paths = [list(range(dp_bits)), list(reversed(range(dp_bits)))]
     order = [bit_order(path) for path in paths]
 
-    turned, mixed = {}, None
-
-    def solve(k, side, mixed, after):
-        mixed, out = solve_heads(
-            place, k, side, per, regular, queries, keys, values, grads, tables[k], starts[k][side], mixed, after
+    turned = {}
+
+    def solve(k, side, after):
+        out = solve_heads(
+            False, place, k, side, per, regular, grads, keys, values, tables[k], starts[k][side], None, after
         )
         turned[k, side] = (out, lax.ppermute(out, "seq", partner))
-        return mixed
 
     def gradient(k):
         own = [turned[k, side][0] for side in range(2)]
@@ -481,11 +477,18 @@
 
     products = []
     for k in range(per):
-        mixed = solve(k, 0, mixed, None)
-        if k > 0:
-            products.append(gradient(k - 1))
-        mixed = solve(k, 1, mixed, products[-1][0] if k > 0 else None)
-    products.append(gradient(per - 1))
+        after = products[-1][0] if k > 0 else None
+        solve(k, 0, after)
+        solve(k, 1, after)
+        products.append(gradient(k))
+
+    mixed = None
+    for k in range(per):
+        for side in range(2):
+            after = turned[per - 1, 1][0] if mixed is None else None
+            mixed = solve_heads(
+                True, place, k, side, per, regular, queries, keys, values, tables[k], starts[k][side], mixed, after
+            )
 
     finished = []
     for blocks in products:

time: 180 us -> 197 us (1.094)
  Pallas kernels: 72.2 us -> 92.6 us
  waiting for transfers between devices: 40.8 us -> 36.2 us
    pallas_call x4 -> x8, Pallas kernels: 33.3 us -> 53.5 us  [solve_heads(): pl.pallas_call(functools.partial(solve_kernel, is_query, head_of), out_sh...]
    ppermute x8, waiting for transfers between devices: 18.8 us -> 6.39 us  [program(): total = keep + lax.ppermute(send, 'dp', pairs)]
    ppermute x4, waiting for transfers between devices: 10.1 us -> 17.7 us  [program(): came_up = lax.ppermute(sent, 'seq', pairs)]
    ppermute x8, starting transfers between devices: 10.4 us -> 8.32 us  [program(): total = keep + lax.ppermute(send, 'dp', pairs)]
    unnamed x38 -> x32, local copies, waits for them, and re-layouts: 8.64 us -> 8.45 us
  transfers between devices with their start and end apart: 27 -> 27, of which waited for: 11 -> 8; matrix products, arithmetic and copies ran while one was open for 3% -> 3% of each run, Pallas kernels for 38% -> 45%
where the time goes in v2:
time: 197 us; the launch traced here: 196 us
  Pallas kernels  92.6 us (47%)
  starting transfers between devices  49.6 us (25%)
  waiting for transfers between devices  36.2 us (18%)
  local copies, waits for them, and re-layouts  9.23 us (5%)
  matrix products  5.51 us (3%)
    pallas_call x8, Pallas kernels, solve_heads(): pl.pallas_call(functools.partial(solve_kernel, is_query, head_of), out_sh...  53.5 us
    ppermute x4, starting transfers between devices, program(): came_up = lax.ppermute(sent, 'seq', pairs)  22.9 us
    ppermute x4, waiting for transfers between devices, program(): came_up = lax.ppermute(sent, 'seq', pairs)  17.7 us
    ppermute x6, starting transfers between devices, program(): lax.ppermute(total[z], 'seq', [(i, i ^ 2 * z) for i in range(steps)])  16.3 us
    pallas_call x2, Pallas kernels, gradient_blocks(): pl.pallas_call(functools.partial(gradient_kernel, order), out_shape=[out]...  12.1 us
    pallas_call x6, Pallas kernels, combine(): pl.pallas_call(functools.partial(kernel, dim), out_shape=[shape] * outs,...  11.1 us
    ppermute x6, waiting for transfers between devices, program(): lax.ppermute(total[z], 'seq', [(i, i ^ 2 * z) for i in range(steps)])  10.5 us
    unnamed x32, local copies, waits for them, and re-layouts  8.45 us
  transfers between devices with their start and end apart: 27, of which 8 were waited for; matrix products, arithmetic and copies ran while one was open for 3% of the time, Pallas kernels for 45%

profile of v2, /device:TPU:0, one launch (start us, length us, event | category | flops | bytes accessed | tf_op | source)
XLA Modules:
  0.0 196.0 jit_solution(12987440079118822255)
XLA Ops:
  1.3 4.3 %pick_columns.1 = f32[4,512,256]{2,1,0:T(8,128)} custom-call(s32[3]{0:T(128)} %pad_add_fusion.core_ref.place_ref, bf16[512,2048]{1,0:T(8,128)(2,1)} %bitcast.68), custom_call_target="tpu_custom_call" | custom-call | bytes 3145728 | tf_op jit(solution)/shard_map/pick_columns/pallas_call | solution.py:323
  6.1 4.0 %local_states.3 = (f32[1,392,128]{2,1,0:T(8,128)}, f32[1,392,128]{2,1,0:T(8,128)}, f32[2,8,512]{2,1,0:T(8,128)}) custom-call(s32[3]{0:T(128)} %pad_add_fusion.core_ref.place_ref, bf16[512,1024]{1,0:T(8,128)(2,1)} %bitcast.48, bf16[512,1024]{1,0:T(8,128)(2,1)} %bitcast.58, f32[8,512]{1,0:T(8,128)} %bitcast.72), custom_call_target="tpu_custom_call" | custom-call | flops 268435456 | bytes 4194304 | tf_op jit(solution)/shard_map/local_states/pallas_call | solution.py:114
  10.1 1.6 collective-permute-done.4.came_ref
  12.4 1.8 shard_map.89.later_ref
  14.1 4.6 %collective-permute-start.5 = (f32[1,392,128]{2,1,0:T(8,128)}, f32[1,392,128]{2,1,0:T(8,128)S(1)}, u32[]{:S(2)}, u32[]{:S(2)}) collective-permute-start(f32[1,392,128]{2,1,0:T(8,128)} %shard_map.89.later_ref), channel_id=1, source_target_pairs={{0,2},{1,3},{2,4},{3,5},{4,6},{5,7},{8,10},{9,11},{10,12},{11,13},... | collective-permute-start | bytes 602120 | tf_op jit(solution)/shard_map/ppermute | solution.py:450
  18.8 5.1 %collective-permute-done.5.earlier_ref.near_ref = f32[1,392,128]{2,1,0:T(8,128)S(1)} collective-permute-done((f32[1,392,128]{2,1,0:T(8,128)}, f32[1,392,128]{2,1,0:T(8,128)S(1)}, u32[]{:S(2)}, u32[]{:S(2)}) %collective-permute-start.5) | collective-permute-done | bytes 200736 | tf_op jit(solution)/shard_map/ppermute | solution.py:450
  24.5 1.7 shard_map.90
  26.3 5.3 %collective-permute-start.6 = (f32[1,392,128]{2,1,0:T(8,128)}, f32[1,392,128]{2,1,0:T(8,128)S(1)}, u32[]{:S(2)}, u32[]{:S(2)}) collective-permute-start(f32[1,392,128]{2,1,0:T(8,128)} %shard_map.90), channel_id=1, source_target_pairs={{0,4},{1,5},{2,6},{3,7},{8,12},{9,13},{10,14},{11,15},{16,20},{17,... | collective-permute-start | bytes 602120 | tf_op jit(solution)/shard_map/ppermute | solution.py:450
  31.6 4.3 %collective-permute-done.6.far_ref = f32[1,392,128]{2,1,0:T(8,128)S(1)} collective-permute-done((f32[1,392,128]{2,1,0:T(8,128)}, f32[1,392,128]{2,1,0:T(8,128)S(1)}, u32[]{:S(2)}, u32[]{:S(2)}) %collective-permute-start.6) | collective-permute-done | bytes 200736 | tf_op jit(solution)/shard_map/ppermute | solution.py:450
  36.5 2.1 %shard_map.91 = (f32[1,392,128]{2,1,0:T(8,128)}, f32[1,392,128]{2,1,0:T(8,128)}) custom-call(s32[3]{0:T(128)} %pad_add_fusion.core_ref.place_ref, f32[1,392,128]{2,1,0:T(8,128)} %copy-done.14, f32[1,392,128]{2,1,0:T(8,128)} %copy-done.4, f32[1,392,128]{2,1,0:T(8,128)} %get-tuple-element.26.own_ref, f32[1,392,128]{2,1,0:T(8,128)} %copy-done.3), custom_call_target="tpu_custom_call" | custom-call | bytes 1204224 | tf_op jit(solution)/shard_map/pallas_call | solution.py:158
  38.6 4.0 %local_states.2 = (f32[1,392,128]{2,1,0:T(8,128)}, f32[1,392,128]{2,1,0:T(8,128)}, f32[2,8,512]{2,1,0:T(8,128)}) custom-call(s32[3]{0:T(128)} %pad_add_fusion.core_ref.place_ref, bf16[512,1024]{1,0:T(8,128)(2,1)} %bitcast.49, bf16[512,1024]{1,0:T(8,128)(2,1)} %bitcast.59, f32[8,512]{1,0:T(8,128)} %bitcast.73), custom_call_target="tpu_custom_call" | custom-call | flops 268435456 | bytes 4194304 | tf_op jit(solution)/shard_map/local_states/pallas_call | solution.py:114
  43.1 6.9 %solve_gradients.4.own0 = f32[2,128,512]{2,1,0:T(8,128)} custom-call(s32[3]{0:T(128)} %pad_add_fusion.core_ref.place_ref, f32[8]{0:T(128)} %regular_ref.15, bf16[512,1024]{1,0:T(8,128)(2,1)} %bitcast.74, bf16[512,1024]{1,0:T(8,128)(2,1)} %bitcast.50, bf16[512,1024]{1,0:T(8,128)(2,1)} %bitcast.60, f32[2,8,512]{2,1,0:T(8,128)} %get-tuple-element.25.rows_ref, ...), custom_call_target="tpu_custom_call" | custom-call | flops 1342177280 | bytes 1835008 | tf_op jit(solution)/shard_map/solve_gradients/pallas_call | solution.py:302
  50.7 6.9 %solve_gradients.5.own1 = f32[2,128,512]{2,1,0:T(8,128)} custom-call(s32[3]{0:T(128)} %pad_add_fusion.core_ref.place_ref, f32[8]{0:T(128)} %regular_ref.15, bf16[512,1024]{1,0:T(8,128)(2,1)} %bitcast.75, bf16[512,1024]{1,0:T(8,128)(2,1)} %bitcast.51, bf16[512,1024]{1,0:T(8,128)(2,1)} %bitcast.61, f32[2,8,512]{2,1,0:T(8,128)} %get-tuple-element.25.rows_ref, ...), custom_call_target="tpu_custom_call" | custom-call | flops 1342177280 | bytes 1835008 | tf_op jit(solution)/shard_map/solve_gradients/pallas_call | solution.py:302
  58.9 1.8 shard_map.86.later_ref
  60.6 7.6 %collective-permute-start.1 = (f32[1,392,128]{2,1,0:T(8,128)}, f32[1,392,128]{2,1,0:T(8,128)S(1)}, u32[]{:S(2)}, u32[]{:S(2)}) collective-permute-start(f32[1,392,128]{2,1,0:T(8,128)} %shard_map.86.later_ref), channel_id=1, source_target_pairs={{0,2},{1,3},{2,4},{3,5},{4,6},{5,7},{8,10},{9,11},{10,12},{11,13},... | collective-permute-start | bytes 602120 | tf_op jit(solution)/shard_map/ppermute | solution.py:450
  68.3 4.7 %collective-permute-done.1.earlier_ref.near_ref = f32[1,392,128]{2,1,0:T(8,128)S(1)} collective-permute-done((f32[1,392,128]{2,1,0:T(8,128)}, f32[1,392,128]{2,1,0:T(8,128)S(1)}, u32[]{:S(2)}, u32[]{:S(2)}) %collective-permute-start.1) | collective-permute-done | bytes 200736 | tf_op jit(solution)/shard_map/ppermute | solution.py:450
  73.7 1.7 shard_map.87
  75.4 5.4 %collective-permute-start.2 = (f32[1,392,128]{2,1,0:T(8,128)}, f32[1,392,128]{2,1,0:T(8,128)S(1)}, u32[]{:S(2)}, u32[]{:S(2)}) collective-permute-start(f32[1,392,128]{2,1,0:T(8,128)} %shard_map.87), channel_id=1, source_target_pairs={{0,4},{1,5},{2,6},{3,7},{8,12},{9,13},{10,14},{11,15},{16,20},{17,... | collective-permute-start | bytes 602120 | tf_op jit(solution)/shard_map/ppermute | solution.py:450
  80.8 3.7 %collective-permute-done.2.far_ref = f32[1,392,128]{2,1,0:T(8,128)S(1)} collective-permute-done((f32[1,392,128]{2,1,0:T(8,128)}, f32[1,392,128]{2,1,0:T(8,128)S(1)}, u32[]{:S(2)}, u32[]{:S(2)}) %collective-permute-start.2) | collective-permute-done | bytes 200736 | tf_op jit(solution)/shard_map/ppermute | solution.py:450
  84.5 0.7 copy-done.15
  85.2 2.1 %shard_map.88 = (f32[1,392,128]{2,1,0:T(8,128)}, f32[1,392,128]{2,1,0:T(8,128)}) custom-call(s32[3]{0:T(128)} %pad_add_fusion.core_ref.place_ref, f32[1,392,128]{2,1,0:T(8,128)} %copy-done.15, f32[1,392,128]{2,1,0:T(8,128)} %copy-done.5, f32[1,392,128]{2,1,0:T(8,128)} %get-tuple-element.21.own_ref, f32[1,392,128]{2,1,0:T(8,128)} %copy-done.2), custom_call_target="tpu_custom_call" | custom-call | bytes 1204224 | tf_op jit(solution)/shard_map/pallas_call | solution.py:158
  87.2 1.3 copy-done.1
  88.6 3.6 %narrow.1.other_ref = bf16[4,512,256]{2,1,0:T(8,128)(2,1)} custom-call(f32[4,512,256]{2,1,0:T(8,128)} %copy-done.1), custom_call_target="tpu_custom_call" | custom-call | bytes 3145728 | tf_op jit(solution)/shard_map/narrow/pallas_call | solution.py:343
  92.2 0.8 copy-done.10
  93.0 0.8 copy-done.11
  93.8 6.1 %gradient_blocks.2 = (f32[2,4,64,256]{3,2,1,0:T(8,128)}, f32[2,4,64,256]{3,2,1,0:T(8,128)}, f32[2,4,64,256]{3,2,1,0:T(8,128)}, f32[2,4,64,256]{3,2,1,0:T(8,128)}) custom-call(s32[3]{0:T(128)} %pad_add_fusion.core_ref.place_ref, f32[2,128,512]{2,1,0:T(8,128)} %solve_gradients.4.own0, f32[2,128,512]{2,1,0:T(8,128)} %solve_gradients.5.own1, ...), custom_call_target="tpu_custom_call" | custom-call | flops 1073741824 | bytes 6291456 | tf_op jit(solution)/shard_map/gradient_blocks/pallas_call | solution.py:383
  99.8 1.5 collective-permute-start.13
  101.4 1.5 collective-permute-start.11
  102.9 7.0 %solve_gradients.7.own0 = f32[2,128,512]{2,1,0:T(8,128)} custom-call(s32[3]{0:T(128)} %pad_add_fusion.core_ref.place_ref, f32[8]{0:T(128)} %regular_ref.15, bf16[512,1024]{1,0:T(8,128)(2,1)} %bitcast.76, bf16[512,1024]{1,0:T(8,128)(2,1)} %bitcast.52, bf16[512,1024]{1,0:T(8,128)(2,1)} %bitcast.62, f32[2,8,512]{2,1,0:T(8,128)} %get-tuple-element.20.rows_ref, ...), custom_call_target="tpu_custom_call" | custom-call | flops 1342177280 | bytes 1835008 | tf_op jit(solution)/shard_map/solve_gradients/pallas_call | solution.py:302
  110.5 6.9 %solve_gradients.6.rest_0_.own1 = f32[2,128,512]{2,1,0:T(8,128)} custom-call(s32[3]{0:T(128)} %pad_add_fusion.core_ref.place_ref, f32[8]{0:T(128)} %regular_ref.15, bf16[512,1024]{1,0:T(8,128)(2,1)} %bitcast.77, bf16[512,1024]{1,0:T(8,128)(2,1)} %bitcast.53, bf16[512,1024]{1,0:T(8,128)(2,1)} %bitcast.63, f32[2,8,512]{2,1,0:T(8,128)} %get-tuple-element.20.rows_ref, ...), custom_call_target="tpu_custom_call" | custom-call | flops 1342177280 | bytes 1835008 | tf_op jit(solution)/shard_map/solve_gradients/pallas_call | solution.py:302
  118.0 5.5 %convolution_convert_fusion.row_ref = bf16[512,1024]{1,0:T(8,128)(2,1)} fusion(bf16[2048,1024]{1,0:T(8,128)(2,1)} %param.8, bf16[1,512,2048]{2,1,0:T(8,128)(2,1)S(1)} %copy-done), kind=kOutput, calls=%fused_computation | convolution fusion | flops 2148007936 | bytes 7340032 | tf_op jit(solution)/shard_map/dot_general | solution.py:459
  123.5 6.4 %solve_queries.4.rest_0_ = bf16[512,1024]{1,0:T(8,128)(2,1)} custom-call(s32[3]{0:T(128)} %pad_add_fusion.core_ref.place_ref, f32[8]{0:T(128)} %regular_ref.15, bf16[512,1024]{1,0:T(8,128)(2,1)} %convolution_convert_fusion.row_ref, bf16[512,1024]{1,0:T(8,128)(2,1)} %bitcast.54, bf16[512,1024]{1,0:T(8,128)(2,1)} %bitcast.64, ...), custom_call_target="tpu_custom_call" | custom-call | flops 1342177280 | bytes 1835008 | tf_op jit(solution)/shard_map/solve_queries/pallas_call | solution.py:302
  130.7 6.1 %gradient_blocks.3 = (f32[2,4,64,256]{3,2,1,0:T(8,128)}, f32[2,4,64,256]{3,2,1,0:T(8,128)}, f32[2,4,64,256]{3,2,1,0:T(8,128)}, f32[2,4,64,256]{3,2,1,0:T(8,128)}) custom-call(s32[3]{0:T(128)} %pad_add_fusion.core_ref.place_ref, f32[2,128,512]{2,1,0:T(8,128)} %solve_gradients.7.own0, f32[2,128,512]{2,1,0:T(8,128)} %solve_gradients.6.rest_0_.own1, ...), custom_call_target="tpu_custom_call" | custom-call | flops 1073741824 | bytes 6291456 | tf_op jit(solution)/shard_map/gradient_blocks/pallas_call | solution.py:383
  137.2 6.3 %solve_queries.5.rest_0_ = bf16[512,1024]{1,0:T(8,128)(2,1)} custom-call(s32[3]{0:T(128)} %pad_add_fusion.core_ref.place_ref, f32[8]{0:T(128)} %regular_ref.15, bf16[512,1024]{1,0:T(8,128)(2,1)} %convolution_convert_fusion.row_ref, bf16[512,1024]{1,0:T(8,128)(2,1)} %bitcast.55, bf16[512,1024]{1,0:T(8,128)(2,1)} %bitcast.65, ...), custom_call_target="tpu_custom_call", output_to_operand_aliasing={{}: (7, {})} | custom-call | flops 1342177280 | bytes 1835008 | tf_op jit(solution)/shard_map/solve_queries/pallas_call | solution.py:302
  143.6 6.7 %solve_queries.6.rest_0_ = bf16[512,1024]{1,0:T(8,128)(2,1)} custom-call(s32[3]{0:T(128)} %pad_add_fusion.core_ref.place_ref, f32[8]{0:T(128)} %regular_ref.15, bf16[512,1024]{1,0:T(8,128)(2,1)} %convolution_convert_fusion.row_ref, bf16[512,1024]{1,0:T(8,128)(2,1)} %bitcast.56, bf16[512,1024]{1,0:T(8,128)(2,1)} %bitcast.66, ...), custom_call_target="tpu_custom_call", output_to_operand_aliasing={{}: (7, {})} | custom-call | flops 1342177280 | bytes 1835008 | tf_op jit(solution)/shard_map/solve_queries/pallas_call | solution.py:302
  150.3 0.7 slice.65
  151.0 1.5 collective-permute-start.12
  152.6 1.5 collective-permute-start.20
  154.1 6.3 %solve_queries.7 = bf16[512,1024]{1,0:T(8,128)(2,1)} custom-call(s32[3]{0:T(128)} %pad_add_fusion.core_ref.place_ref, f32[8]{0:T(128)} %regular_ref.15, bf16[512,1024]{1,0:T(8,128)(2,1)} %convolution_convert_fusion.row_ref, bf16[512,1024]{1,0:T(8,128)(2,1)} %bitcast.57, bf16[512,1024]{1,0:T(8,128)(2,1)} %bitcast.67, ...), custom_call_target="tpu_custom_call", output_to_operand_aliasing={{}: (7, {})} | custom-call | flops 1342177280 | bytes 1835008 | tf_op jit(solution)/shard_map/solve_queries/pallas_call | solution.py:302
  161.2 6.4 %collective-permute-done.20 = f32[2,4,64,256]{3,2,1,0:T(8,128)S(1)} collective-permute-done((f32[2,4,64,256]{3,2,1,0:T(8,128)}, f32[2,4,64,256]{3,2,1,0:T(8,128)S(1)}, u32[]{:S(2)}, u32[]{:S(2)}) %collective-permute-start.20) | collective-permute-done | bytes 524320 | tf_op jit(solution)/shard_map/ppermute | solution.py:500
  168.3 5.8 %collective-permute-start.15 = (f32[128,256]{1,0:T(8,128)S(1)}, f32[128,256]{1,0:T(8,128)S(1)}, u32[]{:S(2)}, u32[]{:S(2)}) collective-permute-start(f32[128,256]{1,0:T(8,128)S(1)} %get-tuple-element.38), channel_id=1, source_target_pairs={{0,2},{1,3},{2,0},{3,1},{4,6},{5,7},{6,4},{7,5},{8,10},{9,11},{10,... | collective-permute-start | bytes 393224 | tf_op jit(solution)/shard_map/ppermute | solution.py:507
  174.1 3.3 %collective-permute-start.16 = (f32[128,256]{1,0:T(8,128)S(1)}, f32[128,256]{1,0:T(8,128)S(1)}, u32[]{:S(2)}, u32[]{:S(2)}) collective-permute-start(f32[128,256]{1,0:T(8,128)S(1)} %get-tuple-element.40), channel_id=1, source_target_pairs={{0,4},{1,5},{2,6},{3,7},{4,0},{5,1},{6,2},{7,3},{8,12},{9,13},{10,... | collective-permute-start | bytes 393224 | tf_op jit(solution)/shard_map/ppermute | solution.py:507
  177.5 2.5 %collective-permute-start.24 = (f32[128,256]{1,0:T(8,128)S(1)}, f32[128,256]{1,0:T(8,128)S(1)}, u32[]{:S(2)}, u32[]{:S(2)}) collective-permute-start(f32[128,256]{1,0:T(8,128)S(1)} %get-tuple-element.41), channel_id=1, source_target_pairs={{0,2},{1,3},{2,0},{3,1},{4,6},{5,7},{6,4},{7,5},{8,10},{9,11},{10,... | collective-permute-start | bytes 393224 | tf_op jit(solution)/shard_map/ppermute | solution.py:507
  180.0 3.3 %collective-permute-start.25 = (f32[128,256]{1,0:T(8,128)S(1)}, f32[128,256]{1,0:T(8,128)S(1)}, u32[]{:S(2)}, u32[]{:S(2)}) collective-permute-start(f32[128,256]{1,0:T(8,128)S(1)} %get-tuple-element.43), channel_id=1, source_target_pairs={{0,4},{1,5},{2,6},{3,7},{4,0},{5,1},{6,2},{7,3},{8,12},{9,13},{10,... | collective-permute-start | bytes 393224 | tf_op jit(solution)/shard_map/ppermute | solution.py:507
  183.3 1.5 collective-permute-start.26
  184.7 2.5 %collective-permute-done.16 = f32[128,256]{1,0:T(8,128)S(1)} collective-permute-done((f32[128,256]{1,0:T(8,128)S(1)}, f32[128,256]{1,0:T(8,128)S(1)}, u32[]{:S(2)}, u32[]{:S(2)}) %collective-permute-start.16) | collective-permute-done | bytes 131104 | tf_op jit(solution)/shard_map/ppermute | solution.py:507
  187.3 7.9 %collective-permute-done.25 = f32[128,256]{1,0:T(8,128)S(1)} collective-permute-done((f32[128,256]{1,0:T(8,128)S(1)}, f32[128,256]{1,0:T(8,128)S(1)}, u32[]{:S(2)}, u32[]{:S(2)}) %collective-permute-start.25) | collective-permute-done | bytes 131104 | tf_op jit(solution)/shard_map/ppermute | solution.py:507
  195.3 0.7 pad_maximum_fusion
  (77 shorter events, 10.5 us)
Async XLA Ops:
  5.6 81.6 %collective-permute-start.10 = (f32[4,512,256]{2,1,0:T(8,128)}, f32[4,512,256]{2,1,0:T(8,128)S(1)}, u32[]{:S(2)}, u32[]{:S(2)}) collective-permute-start(f32[4,512,256]{2,1,0:T(8,128)} %pick_columns.1), channel_id=1, source_target_pairs={{0,1},{1,0},{2,3},{3,2},{4,5},{5,4},{6,7},{7,6},{8,9},{9,8},{10,11... | collective-permute-start | bytes 6291464 | tf_op jit(solution)/shard_map/ppermute | solution.py:457
  10.0 1.7 collective-permute-start.4
  11.7 0.7 copy-start.3
  14.1 9.7 %collective-permute-start.5 = (f32[1,392,128]{2,1,0:T(8,128)}, f32[1,392,128]{2,1,0:T(8,128)S(1)}, u32[]{:S(2)}, u32[]{:S(2)}) collective-permute-start(f32[1,392,128]{2,1,0:T(8,128)} %shard_map.89.later_ref), channel_id=1, source_target_pairs={{0,2},{1,3},{2,4},{3,5},{4,6},{5,7},{8,10},{9,11},{10,12},{11,13},... | collective-permute-start | bytes 602120 | tf_op jit(solution)/shard_map/ppermute | solution.py:450
  23.8 0.7 copy-start.4
  26.3 9.6 %collective-permute-start.6 = (f32[1,392,128]{2,1,0:T(8,128)}, f32[1,392,128]{2,1,0:T(8,128)S(1)}, u32[]{:S(2)}, u32[]{:S(2)}) collective-permute-start(f32[1,392,128]{2,1,0:T(8,128)} %shard_map.90), channel_id=1, source_target_pairs={{0,4},{1,5},{2,6},{3,7},{8,12},{9,13},{10,14},{11,15},{16,20},{17,... | collective-permute-start | bytes 602120 | tf_op jit(solution)/shard_map/ppermute | solution.py:450
  35.8 0.7 copy-start.14
  38.6 11.4 %collective-permute-start.7 = (f32[1,392,128]{2,1,0:T(8,128)}, f32[1,392,128]{2,1,0:T(8,128)S(1)}, u32[]{:S(2)}, u32[]{:S(2)}) collective-permute-start(f32[1,392,128]{2,1,0:T(8,128)} %get-tuple-element.28), channel_id=1, source_target_pairs={{0,1},{1,0},{2,3},{3,2},{4,5},{5,4},{6,7},{7,6},{8,9},{9,8},{10,11... | collective-permute-start | bytes 602120 | tf_op jit(solution)/shard_map/ppermute | solution.py:454
  42.6 15.6 %collective-permute-start = (f32[1,392,128]{2,1,0:T(8,128)}, f32[1,392,128]{2,1,0:T(8,128)S(1)}, u32[]{:S(2)}, u32[]{:S(2)}) collective-permute-start(f32[1,392,128]{2,1,0:T(8,128)} %get-tuple-element.22), channel_id=1, source_target_pairs={{0,1},{1,0},{2,3},{3,2},{4,5},{5,4},{6,7},{7,6},{8,9},{9,8},{10,11... | collective-permute-start | bytes 602120 | tf_op jit(solution)/shard_map/ppermute | solution.py:437
  50.0 42.1 %collective-permute-start.8 = (f32[2,128,512]{2,1,0:T(8,128)}, f32[2,128,512]{2,1,0:T(8,128)S(1)}, u32[]{:S(2)}, u32[]{:S(2)}) collective-permute-start(f32[2,128,512]{2,1,0:T(8,128)} %solve_gradients.4.own0), channel_id=1, source_target_pairs={{0,1},{1,0},{2,3},{3,2},{4,5},{5,4},{6,7},{7,6},{8,9},{9,8},{10,11... | collective-permute-start | bytes 1572872 | tf_op jit(solution)/shard_map/ppermute | solution.py:471
  50.0 0.7 copy-start.12
  57.7 34.5 %collective-permute-start.9 = (f32[2,128,512]{2,1,0:T(8,128)}, f32[2,128,512]{2,1,0:T(8,128)S(1)}, u32[]{:S(2)}, u32[]{:S(2)}) collective-permute-start(f32[2,128,512]{2,1,0:T(8,128)} %solve_gradients.5.own1), channel_id=1, source_target_pairs={{0,1},{1,0},{2,3},{3,2},{4,5},{5,4},{6,7},{7,6},{8,9},{9,8},{10,11... | collective-permute-start | bytes 1572872 | tf_op jit(solution)/shard_map/ppermute | solution.py:471
  58.2 0.7 copy-start.2
  60.6 12.3 %collective-permute-start.1 = (f32[1,392,128]{2,1,0:T(8,128)}, f32[1,392,128]{2,1,0:T(8,128)S(1)}, u32[]{:S(2)}, u32[]{:S(2)}) collective-permute-start(f32[1,392,128]{2,1,0:T(8,128)} %shard_map.86.later_ref), channel_id=1, source_target_pairs={{0,2},{1,3},{2,4},{3,5},{4,6},{5,7},{8,10},{9,11},{10,12},{11,13},... | collective-permute-start | bytes 602120 | tf_op jit(solution)/shard_map/ppermute | solution.py:450
  73.0 0.7 copy-start.5
  75.4 9.1 %collective-permute-start.2 = (f32[1,392,128]{2,1,0:T(8,128)}, f32[1,392,128]{2,1,0:T(8,128)S(1)}, u32[]{:S(2)}, u32[]{:S(2)}) collective-permute-start(f32[1,392,128]{2,1,0:T(8,128)} %shard_map.87), channel_id=1, source_target_pairs={{0,4},{1,5},{2,6},{3,7},{8,12},{9,13},{10,14},{11,15},{16,20},{17,... | collective-permute-start | bytes 602120 | tf_op jit(solution)/shard_map/ppermute | solution.py:450
  84.5 0.7 copy-start.15
  87.2 22.6 %collective-permute-start.3 = (f32[1,392,128]{2,1,0:T(8,128)}, f32[1,392,128]{2,1,0:T(8,128)S(1)}, u32[]{:S(2)}, u32[]{:S(2)}) collective-permute-start(f32[1,392,128]{2,1,0:T(8,128)} %get-tuple-element.23), channel_id=1, source_target_pairs={{0,1},{1,0},{2,3},{3,2},{4,5},{5,4},{6,7},{7,6},{8,9},{9,8},{10,11... | collective-permute-start | bytes 602120 | tf_op jit(solution)/shard_map/ppermute | solution.py:454
  87.2 1.3 copy-start.1
  92.2 0.8 copy-start.10
  93.0 0.8 copy-start.11
  99.8 30.1 %collective-permute-start.13 = (f32[2,4,64,256]{3,2,1,0:T(8,128)}, f32[2,4,64,256]{3,2,1,0:T(8,128)S(1)}, u32[]{:S(2)}, u32[]{:S(2)}) collective-permute-start(f32[2,4,64,256]{3,2,1,0:T(8,128)} %get-tuple-element.33), channel_id=1, source_target_pairs={{0,16},{8,24},{16,0},{24,8},{1,17},{9,25},{17,1},{25,9},{2,18},{10... | collective-permute-start | bytes 1572872 | tf_op jit(solution)/shard_map/ppermute | solution.py:500
  101.4 48.9 %collective-permute-start.11 = (f32[2,4,64,256]{3,2,1,0:T(8,128)}, f32[2,4,64,256]{3,2,1,0:T(8,128)S(1)}, u32[]{:S(2)}, u32[]{:S(2)}) collective-permute-start(f32[2,4,64,256]{3,2,1,0:T(8,128)} %get-tuple-element.31), channel_id=1, source_target_pairs={{0,8},{8,0},{16,24},{24,16},{1,9},{9,1},{17,25},{25,17},{2,10},{10... | collective-permute-start | bytes 1572872 | tf_op jit(solution)/shard_map/ppermute | solution.py:500
  109.8 8.2 %copy-start = (bf16[1,512,2048]{2,1,0:T(8,128)(2,1)S(1)}, bf16[1,512,2048]{2,1,0:T(8,128)(2,1)}, u32[]{:S(2)}) copy-start(bf16[1,512,2048]{2,1,0:T(8,128)(2,1)} %param.7) | copy-start | bytes 6291460
  109.8 20.8 %collective-permute-start.18 = (f32[2,128,512]{2,1,0:T(8,128)}, f32[2,128,512]{2,1,0:T(8,128)}, u32[]{:S(2)}, u32[]{:S(2)}) collective-permute-start(f32[2,128,512]{2,1,0:T(8,128)} %solve_gradients.7.own0), channel_id=1, source_target_pairs={{0,1},{1,0},{2,3},{3,2},{4,5},{5,4},{6,7},{7,6},{8,9},{9,8},{10,11... | collective-permute-start | bytes 1572872 | tf_op jit(solution)/shard_map/ppermute | solution.py:471
  109.8 0.7 copy-start.13
  117.5 13.2 %collective-permute-start.19 = (f32[2,128,512]{2,1,0:T(8,128)}, f32[2,128,512]{2,1,0:T(8,128)}, u32[]{:S(2)}, u32[]{:S(2)}) collective-permute-start(f32[2,128,512]{2,1,0:T(8,128)} %solve_gradients.6.rest_0_.own1), channel_id=1, source_target_pairs={{0,1},{1,0},{2,3},{3,2},{4,5},{5,4},{6,7},{7,6},{8,9},{9,8},{10,11... | collective-permute-start | bytes 1572872 | tf_op jit(solution)/shard_map/ppermute | solution.py:471
  123.5 6.5 %copy-start.9 = (f32[2,4,64,256]{3,2,1,0:T(8,128)S(1)}, f32[2,4,64,256]{3,2,1,0:T(8,128)}, u32[]{:S(2)}) copy-start(f32[2,4,64,256]{3,2,1,0:T(8,128)} %get-tuple-element.32) | copy-start | bytes 1572868
  130.0 30.3 %collective-permute-start.14 = (f32[1,4,64,256]{3,2,1,0:T(8,128)S(1)}, f32[1,4,64,256]{3,2,1,0:T(8,128)S(1)}, u32[]{:S(2)}, u32[]{:S(2)}) collective-permute-start(f32[1,4,64,256]{3,2,1,0:T(8,128)S(1)} %slice.67), channel_id=1, source_target_pairs={{0,8},{8,0},{16,24},{24,16},{1,9},{9,1},{17,25},{25,17},{2,10},{10... | collective-permute-start | bytes 786440 | tf_op jit(solution)/shard_map/ppermute | solution.py:500
  136.7 23.7 %collective-permute-start.22 = (f32[2,4,64,256]{3,2,1,0:T(8,128)}, f32[2,4,64,256]{3,2,1,0:T(8,128)S(1)}, u32[]{:S(2)}, u32[]{:S(2)}) collective-permute-start(f32[2,4,64,256]{3,2,1,0:T(8,128)} %get-tuple-element.37), channel_id=1, source_target_pairs={{0,16},{8,24},{16,0},{24,8},{1,17},{9,25},{17,1},{25,9},{2,18},{10... | collective-permute-start | bytes 1572872 | tf_op jit(solution)/shard_map/ppermute | solution.py:500
  143.6 6.7 %copy-start.6 = (f32[2,4,64,256]{3,2,1,0:T(8,128)S(1)}, f32[2,4,64,256]{3,2,1,0:T(8,128)}, u32[]{:S(2)}) copy-start(f32[2,4,64,256]{3,2,1,0:T(8,128)} %get-tuple-element.30.rest_0_) | copy-start | bytes 1572868
  151.0 10.1 %collective-permute-start.12 = (f32[1,4,64,256]{3,2,1,0:T(8,128)}, f32[1,4,64,256]{3,2,1,0:T(8,128)S(1)}, u32[]{:S(2)}, u32[]{:S(2)}) collective-permute-start(f32[1,4,64,256]{3,2,1,0:T(8,128)} %slice.65), channel_id=1, source_target_pairs={{0,16},{8,24},{16,0},{24,8},{1,17},{9,25},{17,1},{25,9},{2,18},{10... | collective-permute-start | bytes 786440 | tf_op jit(solution)/shard_map/ppermute | solution.py:500
  152.6 7.9 %copy-start.8 = (f32[2,4,64,256]{3,2,1,0:T(8,128)S(1)}, f32[2,4,64,256]{3,2,1,0:T(8,128)}, u32[]{:S(2)}) copy-start(f32[2,4,64,256]{3,2,1,0:T(8,128)} %get-tuple-element.36) | copy-start | bytes 1572868
  152.6 15.0 %collective-permute-start.20 = (f32[2,4,64,256]{3,2,1,0:T(8,128)}, f32[2,4,64,256]{3,2,1,0:T(8,128)S(1)}, u32[]{:S(2)}, u32[]{:S(2)}) collective-permute-start(f32[2,4,64,256]{3,2,1,0:T(8,128)} %get-tuple-element.35), channel_id=1, source_target_pairs={{0,8},{8,0},{16,24},{24,16},{1,9},{9,1},{17,25},{25,17},{2,10},{10... | collective-permute-start | bytes 1572872 | tf_op jit(solution)/shard_map/ppermute | solution.py:500
  160.4 7.2 %copy-start.7 = (f32[2,4,64,256]{3,2,1,0:T(8,128)S(1)}, f32[2,4,64,256]{3,2,1,0:T(8,128)}, u32[]{:S(2)}) copy-start(f32[2,4,64,256]{3,2,1,0:T(8,128)} %get-tuple-element.34) | copy-start | bytes 1572868
  160.6 16.8 %collective-permute-start.23 = (f32[1,4,64,256]{3,2,1,0:T(8,128)S(1)}, f32[1,4,64,256]{3,2,1,0:T(8,128)S(1)}, u32[]{:S(2)}, u32[]{:S(2)}) collective-permute-start(f32[1,4,64,256]{3,2,1,0:T(8,128)S(1)} %slice.77), channel_id=1, source_target_pairs={{0,8},{8,0},{16,24},{24,16},{1,9},{9,1},{17,25},{25,17},{2,10},{10... | collective-permute-start | bytes 786440 | tf_op jit(solution)/shard_map/ppermute | solution.py:500
  167.7 9.7 %collective-permute-start.21 = (f32[1,4,64,256]{3,2,1,0:T(8,128)S(1)}, f32[1,4,64,256]{3,2,1,0:T(8,128)S(1)}, u32[]{:S(2)}, u32[]{:S(2)}) collective-permute-start(f32[1,4,64,256]{3,2,1,0:T(8,128)S(1)} %slice.75), channel_id=1, source_target_pairs={{0,16},{8,24},{16,0},{24,8},{1,17},{9,25},{17,1},{25,9},{2,18},{10... | collective-permute-start | bytes 786440 | tf_op jit(solution)/shard_map/ppermute | solution.py:500
  168.3 15.0 %collective-permute-start.15 = (f32[128,256]{1,0:T(8,128)S(1)}, f32[128,256]{1,0:T(8,128)S(1)}, u32[]{:S(2)}, u32[]{:S(2)}) collective-permute-start(f32[128,256]{1,0:T(8,128)S(1)} %get-tuple-element.38), channel_id=1, source_target_pairs={{0,2},{1,3},{2,0},{3,1},{4,6},{5,7},{6,4},{7,5},{8,10},{9,11},{10,... | collective-permute-start | bytes 393224 | tf_op jit(solution)/shard_map/ppermute | solution.py:507
  174.1 13.2 %collective-permute-start.16 = (f32[128,256]{1,0:T(8,128)S(1)}, f32[128,256]{1,0:T(8,128)S(1)}, u32[]{:S(2)}, u32[]{:S(2)}) collective-permute-start(f32[128,256]{1,0:T(8,128)S(1)} %get-tuple-element.40), channel_id=1, source_target_pairs={{0,4},{1,5},{2,6},{3,7},{4,0},{5,1},{6,2},{7,3},{8,12},{9,13},{10,... | collective-permute-start | bytes 393224 | tf_op jit(solution)/shard_map/ppermute | solution.py:507
  177.4 9.9 %collective-permute-start.17 = (f32[128,256]{1,0:T(8,128)S(1)}, f32[128,256]{1,0:T(8,128)S(1)}, u32[]{:S(2)}, u32[]{:S(2)}) collective-permute-start(f32[128,256]{1,0:T(8,128)S(1)} %get-tuple-element.39), channel_id=1, source_target_pairs={{0,6},{1,7},{2,4},{3,5},{4,2},{5,3},{6,0},{7,1},{8,14},{9,15},{10,... | collective-permute-start | bytes 393224 | tf_op jit(solution)/shard_map/ppermute | solution.py:507
  177.5 9.8 %collective-permute-start.24 = (f32[128,256]{1,0:T(8,128)S(1)}, f32[128,256]{1,0:T(8,128)S(1)}, u32[]{:S(2)}, u32[]{:S(2)}) collective-permute-start(f32[128,256]{1,0:T(8,128)S(1)} %get-tuple-element.41), channel_id=1, source_target_pairs={{0,2},{1,3},{2,0},{3,1},{4,6},{5,7},{6,4},{7,5},{8,10},{9,11},{10,... | collective-permute-start | bytes 393224 | tf_op jit(solution)/shard_map/ppermute | solution.py:507
  180.0 15.3 %collective-permute-start.25 = (f32[128,256]{1,0:T(8,128)S(1)}, f32[128,256]{1,0:T(8,128)S(1)}, u32[]{:S(2)}, u32[]{:S(2)}) collective-permute-start(f32[128,256]{1,0:T(8,128)S(1)} %get-tuple-element.43), channel_id=1, source_target_pairs={{0,4},{1,5},{2,6},{3,7},{4,0},{5,1},{6,2},{7,3},{8,12},{9,13},{10,... | collective-permute-start | bytes 393224 | tf_op jit(solution)/shard_map/ppermute | solution.py:507
  183.3 12.0 %collective-permute-start.26 = (f32[128,256]{1,0:T(8,128)S(1)}, f32[128,256]{1,0:T(8,128)S(1)}, u32[]{:S(2)}, u32[]{:S(2)}) collective-permute-start(f32[128,256]{1,0:T(8,128)S(1)} %get-tuple-element.42), channel_id=1, source_target_pairs={{0,6},{1,7},{2,4},{3,5},{4,2},{5,3},{6,0},{7,1},{8,14},{9,15},{10,... | collective-permute-start | bytes 393224 | tf_op jit(solution)/shard_map/ppermute | solution.py:507

commit v3 on v1

--- a/solution.py
+++ b/solution.py
@@ -65,37 +65,38 @@
     return local, jnp.exp(offset - jnp.concatenate(full, axis=1)), jnp.exp(offset)
 
 
-def states_kernel(half, per, k, core_ref, keys_ref, values_ref, decay_ref, near_ref, away_ref, table_ref, work_ref):
+def states_kernel(half, per, place_ref, keys_ref, values_ref, decay_ref, near_ref, away_ref, table_ref, work_ref):
     rows, dim = keys_ref.shape[0], SUB
-    core = core_ref[0]
+    core = place_ref[0]
     row_at = lax.broadcasted_iota(jnp.int32, (dim, dim), 0)
     column_at = lax.broadcasted_iota(jnp.int32, (dim, dim), 1)
     local, tails, total = decay_tables(decay_ref)
     work_ref[0] = tails
     work_ref[2] = jnp.broadcast_to(total, tails.shape)
-    work_ref[1] = jnp.zeros_like(tails)
     for out, block in ((away_ref, 1 - core), (near_ref, core)):
-        for i in range(half):
-            head = (block * half + i) * per + k
-            column = pl.ds(pl.multiple_of(head * dim, dim), dim)
-            key = keys_ref[:, column]
-            tail = work_ref[0, pl.ds(head, 1), :]
-            key_turned = key.astype(F32).T
-            value_turned = values_ref[:, column].astype(F32).T
-            work_ref[1, pl.ds(head, 1), :] = jnp.sum(key_turned * key_turned, axis=0, keepdims=True)
-            high, low = split(jnp.concatenate([key_turned * tail, value_turned * tail], axis=0))
-            state = dot(high, key) + dot(low, key)
-            gram = state[0:dim]
-            at, second = i // 2, i % 2
-            out[at, (1 + second) * dim : (2 + second) * dim, :] = state[dim:]
-            out[at, 3 * dim + second : 3 * dim + second + 1, :] = work_ref[2, pl.ds(head, 1), :][:, 0:SUB]
-            if second == 0:
-                first_gram = gram
-            else:
-                out[at, 0:dim, :] = jnp.where(row_at <= column_at, first_gram, gram)
-                diagonal = jnp.sum(jnp.where(row_at == column_at, gram, 0.0), axis=0, keepdims=True)
-                out[at, 3 * dim + 2 : 3 * dim + 3, :] = diagonal
-                out[at, 3 * dim + 3 :, :] = jnp.zeros((EXTRA - 3, dim), F32)
+        for k in range(per):
+            for i in range(half):
+                head = (block * half + i) * per + k
+                column = pl.ds(pl.multiple_of(head * dim, dim), dim)
+                key = keys_ref[:, column]
+                tail = work_ref[0, pl.ds(head, 1), :]
+                key_turned = key.astype(F32).T
+                value_turned = values_ref[:, column].astype(F32).T
+                work_ref[1, pl.ds(head, 1), :] = jnp.sum(key_turned * key_turned, axis=0, keepdims=True)
+                high, low = split(jnp.concatenate([key_turned * tail, value_turned * tail], axis=0))
+                state = dot(high, key) + dot(low, key)
+                gram = state[0:dim]
+                at, second = i // 2, i % 2
+                out[k, at, (1 + second) * dim : (2 + second) * dim, :] = state[dim:]
+                decay = work_ref[2, pl.ds(head, 1), :][:, 0:SUB]
+                out[k, at, 3 * dim + second : 3 * dim + second + 1, :] = decay
+                if second == 0:
+                    first_gram = gram
+                else:
+                    out[k, at, 0:dim, :] = jnp.where(row_at <= column_at, first_gram, gram)
+                    diagonal = jnp.sum(jnp.where(row_at == column_at, gram, 0.0), axis=0, keepdims=True)
+                    out[k, at, 3 * dim + 2 : 3 * dim + 3, :] = diagonal
+                    out[k, at, 3 * dim + 3 :, :] = jnp.zeros((EXTRA - 3, dim), F32)
     carry = jnp.zeros_like(total)
     for c in range(rows // SUB):
         lanes = slice(c * SUB, (c + 1) * SUB)
@@ -105,23 +106,23 @@
         carry = part[:, SUB - 1 : SUB]
 
 
-def local_states(core, keys, values, decay, half, per, k):
+def local_states(place, keys, values, decay, half, per):
     rows, columns = keys.shape
     heads = decay.shape[0]
     dim = columns // heads
-    state = jax.ShapeDtypeStruct((half // 2, 3 * dim + EXTRA, dim), F32)
+    state = jax.ShapeDtypeStruct((per, half // 2, 3 * dim + EXTRA, dim), F32)
     vmem = pl.BlockSpec(memory_space=pltpu.VMEM)
     return pl.pallas_call(
-        functools.partial(states_kernel, half, per, k),
+        functools.partial(states_kernel, half, per),
         out_shape=[state, state, jax.ShapeDtypeStruct((2, heads, rows), F32)],
         in_specs=[pl.BlockSpec(memory_space=pltpu.SMEM)] + [vmem] * 3,
         out_specs=[vmem] * 3,
         scratch_shapes=[pltpu.VMEM((3, heads, rows), F32)],
         cost_estimate=pl.CostEstimate(
-            flops=16 * rows * dim * dim * half, bytes_accessed=8 * rows * columns, transcendentals=0
+            flops=16 * rows * dim * dim * half * per, bytes_accessed=8 * rows * columns, transcendentals=0
         ),
         name="local_states",
-    )(core, keys, values, decay)
+    )(place, keys, values, decay)
 
 
 def join(earlier, later, dim):
@@ -134,37 +135,35 @@
     return factor * earlier + jnp.where(is_decay, 0.0, later)
 
 
-def chip_kernel(dim, place_ref, own_ref, came_ref, out_ref):
+def chip_kernel(dim, place_ref, own_ref, came_ref, *out_refs):
     is_first = place_ref[0] == 0
-    own, came = own_ref[...], came_ref[...]
-    out_ref[...] = join(jnp.where(is_first, own, came), jnp.where(is_first, came, own), dim)
+    for k, out_ref in enumerate(out_refs):
+        own, came = own_ref[k], came_ref[k]
+        out_ref[...] = join(jnp.where(is_first, own, came), jnp.where(is_first, came, own), dim)
 
 
 def join_kernel(dim, place_ref, earlier_ref, later_ref, out_ref):
     out_ref[...] = join(earlier_ref[...], later_ref[...], dim)
 
 
-def start_kernel(dim, place_ref, far_ref, near_ref, own_ref, came_ref, mine_ref, other_ref):
+def start_kernel(dim, k, place_ref, far_ref, near_ref, own_ref, came_ref, mine_ref, other_ref):
     is_first = place_ref[0] == 0
     before = join(far_ref[...], near_ref[...], dim)
-    after = join(before, jnp.where(is_first, own_ref[...], came_ref[...]), dim)
+    after = join(before, jnp.where(is_first, own_ref[k], came_ref[k]), dim)
     mine_ref[...] = jnp.where(is_first, before, after)
     other_ref[...] = jnp.where(is_first, after, before)
 
 
-def combine(kernel, dim, place, *arrays, outs=1):
-    vmem = pl.BlockSpec(memory_space=pltpu.VMEM)
-    shape = jax.ShapeDtypeStruct(arrays[0].shape, F32)
-    results = pl.pallas_call(
-        functools.partial(kernel, dim),
-        out_shape=[shape] * outs,
-        in_specs=[pl.BlockSpec(memory_space=pltpu.SMEM)] + [vmem] * len(arrays),
-        out_specs=[vmem] * outs,
+def combine(kernel, place, arrays, shape, outs):
+    return pl.pallas_call(
+        kernel,
+        out_shape=[jax.ShapeDtypeStruct(shape, F32)] * outs,
+        in_specs=[pl.BlockSpec(memory_space=pltpu.SMEM)] + [pl.BlockSpec(memory_space=pltpu.VMEM)] * len(arrays),
+        out_specs=[pl.BlockSpec(memory_space=pltpu.VMEM)] * outs,
         cost_estimate=pl.CostEstimate(
-            flops=0, bytes_accessed=4 * arrays[0].size * (len(arrays) + outs), transcendentals=0
+            flops=0, bytes_accessed=8 * sum(a.size for a in arrays), transcendentals=0
         ),
     )(place, *arrays)
-    return results[0] if outs == 1 else results
 
 
 def solve_kernel(
@@ -406,6 +405,30 @@
     )(place, *own, *far, tokens, other)
 
 
+def merge_kernel(count, *refs):
+    sums, outs = refs[: 2 * count], refs[2 * count :]
+    rows = sums[0].shape[2]
+    for z, out in enumerate(outs):
+        for i in range(count):
+            out[i * rows : (i + 1) * rows, :] = sums[2 * i][0, z] + sums[2 * i + 1][0, z]
+
+
+def merge_blocks(sums):
+    _, chips, rows, size = sums[0].shape
+    count = len(sums) // 2
+    vmem = pl.BlockSpec(memory_space=pltpu.VMEM)
+    return pl.pallas_call(
+        functools.partial(merge_kernel, count),
+        out_shape=[jax.ShapeDtypeStruct((count * rows, size), F32)] * chips,
+        in_specs=[vmem] * len(sums),
+        out_specs=[vmem] * chips,
+        cost_estimate=pl.CostEstimate(
+            flops=0, bytes_accessed=6 * sum(a.size for a in sums), transcendentals=0
+        ),
+        name="merge_blocks",
+    )(*sums)
+
+
 def bit_order(bits):
     table = []
     for d in range(1 << len(bits)):
@@ -434,26 +457,27 @@
     place = jnp.stack([core, lax.axis_index("dp"), here // 2]).astype(jnp.int32)
     partner = [(i, i ^ 1) for i in range(steps)]
 
-    locals_, tables = [], []
-    for k in range(per):
-        near, away, table = local_states(place, keys, values, decay, half, per, k)
-        locals_.append((near, lax.ppermute(away, "seq", partner)))
-        tables.append(table)
-
+    own, away, table = local_states(place, keys, values, decay, half, per)
+    came = lax.ppermute(away, "seq", partner)
+    shape = own.shape[1:]
+    chip_states = combine(functools.partial(chip_kernel, dim), place, [own, came], shape, per)
+    joined = functools.partial(join_kernel, dim)
     starts = []
-    for own, came in locals_:
-        chip_state = combine(chip_kernel, dim, place, own, came)
+    for k, chip_state in enumerate(chip_states):
         window, near, far = 0, None, None
         while window < chips - 1:
             if far is not None:
-                near = combine(join_kernel, dim, place, far, near)
-            sent = chip_state if near is None else combine(join_kernel, dim, place, near, chip_state)
+                (near,) = combine(joined, place, [far, near], shape, 1)
+            sent = chip_state
+            if near is not None:
+                (sent,) = combine(joined, place, [near, chip_state], shape, 1)
             shift = 2 * (window + 1)
             pairs = [(i, i + shift) for i in range(steps - shift)]
             came_up = lax.ppermute(sent, "seq", pairs)
             near, far = (came_up, None) if near is None else (near, came_up)
             window = 2 * window + 1
-        mine, others = combine(start_kernel, dim, place, far, near, own, came, outs=2)
+        starting = functools.partial(start_kernel, dim, k)
+        mine, others = combine(starting, place, [far, near, own, came], shape, 2)
         starts.append((mine, lax.ppermute(others, "seq", partner)))
 
     picked = pick_columns(place, tokens, chips)
@@ -469,7 +493,7 @@
 
     def solve(k, side, mixed, after):
         mixed, out = solve_heads(
-            place, k, side, per, regular, queries, keys, values, grads, tables[k], starts[k][side], mixed, after
+            place, k, side, per, regular, queries, keys, values, grads, table, starts[k][side], mixed, after
         )
         turned[k, side] = (out, lax.ppermute(out, "seq", partner))
         return mixed
@@ -489,19 +513,21 @@
 
     finished = []
     for blocks in products:
-        parts = []
+        sums = []
         for index, path in enumerate(paths):
             keep, send = blocks[2 * index], blocks[2 * index + 1]
             for bit in path:
                 pairs = [(i, i ^ (1 << bit)) for i in range(groups)]
-                total = keep + lax.ppermute(send, "dp", pairs)
-                middle = total.shape[0] // 2
-                keep, send = total[:middle], total[middle:]
-            parts.append(total[0])
-        total = jnp.concatenate(parts, axis=1)
-        out = total[0]
-        for z in range(1, chips):
-            out = out + lax.ppermute(total[z], "seq", [(i, i ^ (2 * z)) for i in range(steps)])
+                came = lax.ppermute(send, "dp", pairs)
+                if bit == path[-1]:
+                    sums += [keep, came]
+                else:
+                    total = keep + came
+                    keep, send = jnp.split(total, 2, axis=0)
+        out, *others = merge_blocks(sums)
+        for z, other_block in enumerate(others, 1):
+            pairs = [(i, i ^ (2 * z)) for i in range(steps)]
+            out = out + lax.ppermute(other_block, "seq", pairs)
         finished.append(out)
     return mixed[None], jnp.concatenate(finished, axis=0)
 

time: 180 us -> 179 us (level)
  waiting for transfers between devices: 40.8 us -> 34.6 us
  local copies, waits for them, and re-layouts: 8.71 us -> 12.7 us
    ppermute x16 -> x15, waiting for transfers between devices: 30.7 us -> 21.2 us  [the longest x8 11.9 us: program(): came = lax.ppermute(send, 'dp', pairs)]
    ppermute x4, waiting for transfers between devices: 10.1 us -> 13.4 us  [program(): came_up = lax.ppermute(sent, 'seq', pairs)]
    split x0 -> x4, local copies, waits for them, and re-layouts: none -> 2.99 us  [program(): keep, send = jnp.split(total, 2, axis=0)]
    add x6, other arithmetic: 0.35 us -> 2.16 us  [the longest x2 1.88 us: program(): out = out + lax.ppermute(other_block, 'seq', pairs)]
    unnamed x38 -> x44, local copies, waits for them, and re-layouts: 8.64 us -> 9.66 us
    ppermute x16 -> x15, starting transfers between devices: 24.9 us -> 25 us  [the longest x6 14.2 us: program(): out = out + lax.ppermute(other_block, 'seq', pairs)]
  transfers between devices with their start and end apart: 27 -> 26, of which waited for: 11 -> 8; matrix products, arithmetic and copies ran while one was open for 3% -> 6% of each run, Pallas kernels for 38% -> 38%
where the time goes in v3:
time: 179 us; the launch traced here: 178 us
  Pallas kernels  72 us (40%)
  starting transfers between devices  49.3 us (28%)
  waiting for transfers between devices  34.6 us (19%)
  local copies, waits for them, and re-layouts  12.7 us (7%)
  matrix products  5.61 us (3%)
  other arithmetic  3.47 us (2%)
    pallas_call x4, Pallas kernels, solve_heads(): pl.pallas_call(functools.partial(solve_kernel, head_of), out_shape=[jax.S...  33.3 us
    ppermute x4, starting transfers between devices, program(): came_up = lax.ppermute(sent, 'seq', pairs)  23.2 us
    ppermute x6, starting transfers between devices, program(): out = out + lax.ppermute(other_block, 'seq', pairs)  14.2 us
    ppermute x4, waiting for transfers between devices, program(): came_up = lax.ppermute(sent, 'seq', pairs)  13.4 us
    pallas_call x2, Pallas kernels, gradient_blocks(): pl.pallas_call(functools.partial(gradient_kernel, order), out_shape=[out]...  12.1 us
    ppermute x8, waiting for transfers between devices, program(): came = lax.ppermute(send, 'dp', pairs)  11.9 us
    ppermute x8, starting transfers between devices, program(): came = lax.ppermute(send, 'dp', pairs)  10.3 us
    pallas_call x5, Pallas kernels, combine(): pl.pallas_call(kernel, out_shape=[jax.ShapeDtypeStruct(shape, F32)] * out...  9.86 us
  transfers between devices with their start and end apart: 26, of which 8 were waited for; matrix products, arithmetic and copies ran while one was open for 6% of the time, Pallas kernels for 38%

profile of v3, /device:TPU:0, one launch (start us, length us, event | category | flops | bytes accessed | tf_op | source)
XLA Modules:
  0.0 178.4 jit_solution(9409575484493041957)
XLA Ops:
  1.2 4.9 %local_states.1 = (f32[2,1,392,128]{3,2,1,0:T(8,128)}, f32[2,1,392,128]{3,2,1,0:T(8,128)}, f32[2,8,512]{2,1,0:T(8,128)}) custom-call(s32[3]{0:T(128)} %pad_add_fusion.place_ref.core_ref, bf16[512,1024]{1,0:T(8,128)(2,1)} %bitcast.15, bf16[512,1024]{1,0:T(8,128)(2,1)} %bitcast.20, f32[8,512]{1,0:T(8,128)} %bitcast.30), custom_call_target="tpu_custom_call" | custom-call | flops 536870912 | bytes 4194304 | tf_op jit(solution)/shard_map/local_states/pallas_call | solution.py:115
  6.6 4.3 %pick_columns.1 = f32[4,512,256]{2,1,0:T(8,128)} custom-call(s32[3]{0:T(128)} %pad_add_fusion.place_ref.core_ref, bf16[512,2048]{1,0:T(8,128)(2,1)} %bitcast.12), custom_call_target="tpu_custom_call" | custom-call | bytes 3145728 | tf_op jit(solution)/shard_map/pick_columns/pallas_call | solution.py:325
  10.9 0.7 copy-done.1
  11.7 2.0 %shard_map.86 = (f32[1,392,128]{2,1,0:T(8,128)}, f32[1,392,128]{2,1,0:T(8,128)}) custom-call(s32[3]{0:T(128)} %pad_add_fusion.place_ref.core_ref, f32[2,1,392,128]{3,2,1,0:T(8,128)} %get-tuple-element.36.own_ref, f32[2,1,392,128]{3,2,1,0:T(8,128)} %copy-done.1), custom_call_target="tpu_custom_call" | custom-call | bytes 1605632 | tf_op jit(solution)/shard_map/pallas_call | solution.py:158
  13.7 4.9 %collective-permute-start.4 = (f32[1,392,128]{2,1,0:T(8,128)}, f32[1,392,128]{2,1,0:T(8,128)S(1)}, u32[]{:S(2)}, u32[]{:S(2)}) collective-permute-start(f32[1,392,128]{2,1,0:T(8,128)} %get-tuple-element.41.later_ref), channel_id=1, source_target_pairs={{0,2},{1,3},{2,4},{3,5},{4,6},{5,7},{8,10},{9,11},{10,12},{11,13},... | collective-permute-start | bytes 602120 | tf_op jit(solution)/shard_map/ppermute | solution.py:476
  18.6 4.7 %collective-permute-done.4.earlier_ref.near_ref = f32[1,392,128]{2,1,0:T(8,128)S(1)} collective-permute-done((f32[1,392,128]{2,1,0:T(8,128)}, f32[1,392,128]{2,1,0:T(8,128)S(1)}, u32[]{:S(2)}, u32[]{:S(2)}) %collective-permute-start.4) | collective-permute-done | bytes 200736 | tf_op jit(solution)/shard_map/ppermute | solution.py:476
  24.0 1.7 shard_map.89
  25.8 5.3 %collective-permute-start.5 = (f32[1,392,128]{2,1,0:T(8,128)}, f32[1,392,128]{2,1,0:T(8,128)S(1)}, u32[]{:S(2)}, u32[]{:S(2)}) collective-permute-start(f32[1,392,128]{2,1,0:T(8,128)} %shard_map.89), channel_id=1, source_target_pairs={{0,4},{1,5},{2,6},{3,7},{8,12},{9,13},{10,14},{11,15},{16,20},{17,... | collective-permute-start | bytes 602120 | tf_op jit(solution)/shard_map/ppermute | solution.py:476
  31.1 3.9 %collective-permute-done.5.far_ref = f32[1,392,128]{2,1,0:T(8,128)S(1)} collective-permute-done((f32[1,392,128]{2,1,0:T(8,128)}, f32[1,392,128]{2,1,0:T(8,128)S(1)}, u32[]{:S(2)}, u32[]{:S(2)}) %collective-permute-start.5) | collective-permute-done | bytes 200736 | tf_op jit(solution)/shard_map/ppermute | solution.py:476
  35.7 2.2 %shard_map.90 = (f32[1,392,128]{2,1,0:T(8,128)}, f32[1,392,128]{2,1,0:T(8,128)}) custom-call(s32[3]{0:T(128)} %pad_add_fusion.place_ref.core_ref, f32[1,392,128]{2,1,0:T(8,128)} %copy-done.19, f32[1,392,128]{2,1,0:T(8,128)} %copy-done.4, f32[2,1,392,128]{3,2,1,0:T(8,128)} %get-tuple-element.36.own_ref, f32[2,1,392,128]{3,2,1,0:T(8,128)} %copy-done.1), custom_call_target="tpu_custom_call" | custom-call | bytes 2408448 | tf_op jit(solution)/shard_map/pallas_call | solution.py:158
  37.8 5.6 %convolution_convert_fusion.q_ref = bf16[512,1024]{1,0:T(8,128)(2,1)} fusion(bf16[2048,1024]{1,0:T(8,128)(2,1)} %param.8, bf16[1,512,2048]{2,1,0:T(8,128)(2,1)S(1)} %copy-done), kind=kOutput, calls=%fused_computation | convolution fusion | flops 2148007936 | bytes 7340032 | tf_op jit(solution)/shard_map/dot_general | solution.py:486
  43.4 7.6 %collective-permute-start.1 = (f32[1,392,128]{2,1,0:T(8,128)S(1)}, f32[1,392,128]{2,1,0:T(8,128)S(1)}, u32[]{:S(2)}, u32[]{:S(2)}) collective-permute-start(f32[1,392,128]{2,1,0:T(8,128)S(1)} %copy-done.17), channel_id=1, source_target_pairs={{0,2},{1,3},{2,4},{3,5},{4,6},{5,7},{8,10},{9,11},{10,12},{11,13},... | collective-permute-start | bytes 602120 | tf_op jit(solution)/shard_map/ppermute | solution.py:476
  51.1 8.3 %solve_heads.4 = (bf16[512,1024]{1,0:T(8,128)(2,1)}, f32[2,128,512]{2,1,0:T(8,128)}) custom-call(s32[3]{0:T(128)} %pad_add_fusion.place_ref.core_ref, f32[8]{0:T(128)} %regular_ref.7, bf16[512,1024]{1,0:T(8,128)(2,1)} %convolution_convert_fusion.q_ref, bf16[512,1024]{1,0:T(8,128)(2,1)} %bitcast.16, bf16[512,1024]{1,0:T(8,128)(2,1)} %bitcast.21, ...), custom_call_target="tpu_custom_call" | custom-call | flops 1342177280 | bytes 1835008 | tf_op jit(solution)/shard_map/solve_heads/pallas_call | solution.py:298
  60.2 8.3 %solve_heads.5 = (bf16[512,1024]{1,0:T(8,128)(2,1)}, f32[2,128,512]{2,1,0:T(8,128)}) custom-call(s32[3]{0:T(128)} %pad_add_fusion.place_ref.core_ref, f32[8]{0:T(128)} %regular_ref.7, bf16[512,1024]{1,0:T(8,128)(2,1)} %convolution_convert_fusion.q_ref, bf16[512,1024]{1,0:T(8,128)(2,1)} %bitcast.17, ...), custom_call_target="tpu_custom_call", output_to_operand_aliasing={{0}: (8, {})} | custom-call | flops 1342177280 | bytes 1835008 | tf_op jit(solution)/shard_map/solve_heads/pallas_call | solution.py:298
  69.5 1.7 shard_map.87
  71.3 5.3 %collective-permute-start.2 = (f32[1,392,128]{2,1,0:T(8,128)}, f32[1,392,128]{2,1,0:T(8,128)S(1)}, u32[]{:S(2)}, u32[]{:S(2)}) collective-permute-start(f32[1,392,128]{2,1,0:T(8,128)} %shard_map.87), channel_id=1, source_target_pairs={{0,4},{1,5},{2,6},{3,7},{8,12},{9,13},{10,14},{11,15},{16,20},{17,... | collective-permute-start | bytes 602120 | tf_op jit(solution)/shard_map/ppermute | solution.py:476
  76.6 4.7 %collective-permute-done.2.far_ref = f32[1,392,128]{2,1,0:T(8,128)S(1)} collective-permute-done((f32[1,392,128]{2,1,0:T(8,128)}, f32[1,392,128]{2,1,0:T(8,128)S(1)}, u32[]{:S(2)}, u32[]{:S(2)}) %collective-permute-start.2) | collective-permute-done | bytes 200736 | tf_op jit(solution)/shard_map/ppermute | solution.py:476
  82.0 2.2 %shard_map.88 = (f32[1,392,128]{2,1,0:T(8,128)}, f32[1,392,128]{2,1,0:T(8,128)}) custom-call(s32[3]{0:T(128)} %pad_add_fusion.place_ref.core_ref, f32[1,392,128]{2,1,0:T(8,128)} %copy-done.18, f32[1,392,128]{2,1,0:T(8,128)} %copy-done.3, f32[2,1,392,128]{3,2,1,0:T(8,128)} %get-tuple-element.36.own_ref, f32[2,1,392,128]{3,2,1,0:T(8,128)} %copy-done.1), custom_call_target="tpu_custom_call" | custom-call | bytes 2408448 | tf_op jit(solution)/shard_map/pallas_call | solution.py:158
  84.3 8.3 %solve_heads.6 = (bf16[512,1024]{1,0:T(8,128)(2,1)}, f32[2,128,512]{2,1,0:T(8,128)}) custom-call(s32[3]{0:T(128)} %pad_add_fusion.place_ref.core_ref, f32[8]{0:T(128)} %regular_ref.7, bf16[512,1024]{1,0:T(8,128)(2,1)} %convolution_convert_fusion.q_ref, bf16[512,1024]{1,0:T(8,128)(2,1)} %bitcast.18, ...), custom_call_target="tpu_custom_call", output_to_operand_aliasing={{0}: (8, {})} | custom-call | flops 1342177280 | bytes 1835008 | tf_op jit(solution)/shard_map/solve_heads/pallas_call | solution.py:298
  93.1 3.6 %narrow.1.other_ref = bf16[4,512,256]{2,1,0:T(8,128)(2,1)} custom-call(f32[4,512,256]{2,1,0:T(8,128)} %collective-permute-done.9.in_ref), custom_call_target="tpu_custom_call" | custom-call | bytes 3145728 | tf_op jit(solution)/shard_map/narrow/pallas_call | solution.py:345
  96.7 0.8 copy-done.8
  97.5 0.8 copy-done.10
  98.3 6.1 %gradient_blocks.2 = (f32[2,4,64,256]{3,2,1,0:T(8,128)}, f32[2,4,64,256]{3,2,1,0:T(8,128)}, f32[2,4,64,256]{3,2,1,0:T(8,128)}, f32[2,4,64,256]{3,2,1,0:T(8,128)}) custom-call(s32[3]{0:T(128)} %pad_add_fusion.place_ref.core_ref, f32[2,128,512]{2,1,0:T(8,128)} %get-tuple-element.47.own0, f32[2,128,512]{2,1,0:T(8,128)} %get-tuple-element.48.own1, ...), custom_call_target="tpu_custom_call" | custom-call | flops 1073741824 | bytes 6291456 | tf_op jit(solution)/shard_map/gradient_blocks/pallas_call | solution.py:385
  105.0 8.4 %solve_heads.7 = (bf16[512,1024]{1,0:T(8,128)(2,1)}, f32[2,128,512]{2,1,0:T(8,128)}) custom-call(s32[3]{0:T(128)} %pad_add_fusion.place_ref.core_ref, f32[8]{0:T(128)} %regular_ref.7, bf16[512,1024]{1,0:T(8,128)(2,1)} %convolution_convert_fusion.q_ref, bf16[512,1024]{1,0:T(8,128)(2,1)} %bitcast.19, ...), custom_call_target="tpu_custom_call", output_to_operand_aliasing={{0}: (8, {})} | custom-call | flops 1342177280 | bytes 1835008 | tf_op jit(solution)/shard_map/solve_heads/pallas_call | solution.py:298
  113.5 1.5 collective-permute-start.10
  115.0 1.5 collective-permute-start.12
  116.5 0.8 copy-done.9
  117.4 0.8 copy-done.11
  118.1 6.0 %gradient_blocks.3 = (f32[2,4,64,256]{3,2,1,0:T(8,128)}, f32[2,4,64,256]{3,2,1,0:T(8,128)}, f32[2,4,64,256]{3,2,1,0:T(8,128)}, f32[2,4,64,256]{3,2,1,0:T(8,128)}) custom-call(s32[3]{0:T(128)} %pad_add_fusion.place_ref.core_ref, f32[2,128,512]{2,1,0:T(8,128)} %get-tuple-element.58.own0, f32[2,128,512]{2,1,0:T(8,128)} %get-tuple-element.59.own1, ...), custom_call_target="tpu_custom_call" | custom-call | flops 1073741824 | bytes 6291456 | tf_op jit(solution)/shard_map/gradient_blocks/pallas_call | solution.py:385
  125.5 3.1 %collective-permute-done.10 = f32[2,4,64,256]{3,2,1,0:T(8,128)S(1)} collective-permute-done((f32[2,4,64,256]{3,2,1,0:T(8,128)}, f32[2,4,64,256]{3,2,1,0:T(8,128)S(1)}, u32[]{:S(2)}, u32[]{:S(2)}) %collective-permute-start.10) | collective-permute-done | bytes 524320 | tf_op jit(solution)/shard_map/ppermute | solution.py:521
  128.6 0.8 fusion.2
  129.4 1.5 collective-permute-start.11
  131.7 1.5 collective-permute-start.13
  133.2 6.6 %collective-permute-done.19 = f32[2,4,64,256]{3,2,1,0:T(8,128)S(1)} collective-permute-done((f32[2,4,64,256]{3,2,1,0:T(8,128)}, f32[2,4,64,256]{3,2,1,0:T(8,128)S(1)}, u32[]{:S(2)}, u32[]{:S(2)}) %collective-permute-start.19) | collective-permute-done | bytes 524320 | tf_op jit(solution)/shard_map/ppermute | solution.py:521
  139.9 0.7 fusion.4
  140.6 1.5 collective-permute-start.20
  142.2 0.8 fusion.3
  142.9 1.5 collective-permute-start.22
  144.4 2.2 %collective-permute-done.11.refs_1_ = f32[1,4,64,256]{3,2,1,0:T(8,128)S(1)} collective-permute-done((f32[1,4,64,256]{3,2,1,0:T(8,128)S(1)}, f32[1,4,64,256]{3,2,1,0:T(8,128)S(1)}, u32[]{:S(2)}, u32[]{:S(2)}) %collective-permute-start.11) | collective-permute-done | bytes 262176 | tf_op jit(solution)/shard_map/ppermute | solution.py:521
  147.5 2.0 %merge_blocks.2 = (f32[128,256]{1,0:T(8,128)}, f32[128,256]{1,0:T(8,128)}, f32[128,256]{1,0:T(8,128)}, f32[128,256]{1,0:T(8,128)}) custom-call(f32[1,4,64,256]{3,2,1,0:T(8,128)} %get-tuple-element.71.refs_0_, f32[1,4,64,256]{3,2,1,0:T(8,128)} %copy-done.12, f32[1,4,64,256]{3,2,1,0:T(8,128)} %get-tuple-element.69.refs_2_, f32[1,4,64,256]{3,2,1,0:T(8,128)} %copy-done.14), custom_call_target="tpu_custom_call" | custom-call | bytes 1572864 | tf_op jit(solution)/shard_map/merge_blocks/pallas_call | solution.py:420
  149.5 6.7 %collective-permute-start.16 = (f32[128,256]{1,0:T(8,128)}, f32[128,256]{1,0:T(8,128)S(1)}, u32[]{:S(2)}, u32[]{:S(2)}) collective-permute-start(f32[128,256]{1,0:T(8,128)} %get-tuple-element.57), channel_id=1, source_target_pairs={{0,6},{1,7},{2,4},{3,5},{4,2},{5,3},{6,0},{7,1},{8,14},{9,15},{10,... | collective-permute-start | bytes 393224 | tf_op jit(solution)/shard_map/ppermute | solution.py:530
  157.5 2.0 %merge_blocks.3 = (f32[128,256]{1,0:T(8,128)}, f32[128,256]{1,0:T(8,128)}, f32[128,256]{1,0:T(8,128)}, f32[128,256]{1,0:T(8,128)}) custom-call(f32[1,4,64,256]{3,2,1,0:T(8,128)} %get-tuple-element.75.refs_0_, f32[1,4,64,256]{3,2,1,0:T(8,128)} %copy-done.13, f32[1,4,64,256]{3,2,1,0:T(8,128)} %get-tuple-element.73.refs_2_, f32[1,4,64,256]{3,2,1,0:T(8,128)} %copy-done.15), custom_call_target="tpu_custom_call" | custom-call | bytes 1572864 | tf_op jit(solution)/shard_map/merge_blocks/pallas_call | solution.py:420
  159.5 3.8 %collective-permute-start.25 = (f32[128,256]{1,0:T(8,128)}, f32[128,256]{1,0:T(8,128)S(1)}, u32[]{:S(2)}, u32[]{:S(2)}) collective-permute-start(f32[128,256]{1,0:T(8,128)} %get-tuple-element.67), channel_id=1, source_target_pairs={{0,6},{1,7},{2,4},{3,5},{4,2},{5,3},{6,0},{7,1},{8,14},{9,15},{10,... | collective-permute-start | bytes 393224 | tf_op jit(solution)/shard_map/ppermute | solution.py:530
  163.3 3.2 %collective-permute-start.23 = (f32[128,256]{1,0:T(8,128)}, f32[128,256]{1,0:T(8,128)S(1)}, u32[]{:S(2)}, u32[]{:S(2)}) collective-permute-start(f32[128,256]{1,0:T(8,128)} %get-tuple-element.65), channel_id=1, source_target_pairs={{0,2},{1,3},{2,0},{3,1},{4,6},{5,7},{6,4},{7,5},{8,10},{9,11},{10,... | collective-permute-start | bytes 393224 | tf_op jit(solution)/shard_map/ppermute | solution.py:530
  166.5 5.9 %collective-permute-done.15 = f32[128,256]{1,0:T(8,128)S(1)} collective-permute-done((f32[128,256]{1,0:T(8,128)}, f32[128,256]{1,0:T(8,128)S(1)}, u32[]{:S(2)}, u32[]{:S(2)}) %collective-permute-start.15) | collective-permute-done | bytes 131104 | tf_op jit(solution)/shard_map/ppermute | solution.py:530
  172.4 0.9 add_add_fusion.1
  173.4 3.4 %collective-permute-done.24 = f32[128,256]{1,0:T(8,128)S(1)} collective-permute-done((f32[128,256]{1,0:T(8,128)}, f32[128,256]{1,0:T(8,128)S(1)}, u32[]{:S(2)}, u32[]{:S(2)}) %collective-permute-start.24) | collective-permute-done | bytes 131104 | tf_op jit(solution)/shard_map/ppermute | solution.py:530
  176.7 0.9 add_add_fusion
  (77 shorter events, 11.5 us)
Async XLA Ops:
  6.1 4.8 %collective-permute-start = (f32[2,1,392,128]{3,2,1,0:T(8,128)}, f32[2,1,392,128]{3,2,1,0:T(8,128)S(1)}, u32[]{:S(2)}, u32[]{:S(2)}) collective-permute-start(f32[2,1,392,128]{3,2,1,0:T(8,128)} %get-tuple-element.37), channel_id=1, source_target_pairs={{0,1},{1,0},{2,3},{3,2},{4,5},{5,4},{6,7},{7,6},{8,9},{9,8},{10,11... | collective-permute-start | bytes 1204232 | tf_op jit(solution)/shard_map/ppermute | solution.py:461
  10.9 26.9 %copy-start = (bf16[1,512,2048]{2,1,0:T(8,128)(2,1)S(1)}, bf16[1,512,2048]{2,1,0:T(8,128)(2,1)}, u32[]{:S(2)}) copy-start(bf16[1,512,2048]{2,1,0:T(8,128)(2,1)} %param.7) | copy-start | bytes 6291460
  10.9 82.1 %collective-permute-start.9 = (f32[4,512,256]{2,1,0:T(8,128)}, f32[4,512,256]{2,1,0:T(8,128)}, u32[]{:S(2)}, u32[]{:S(2)}) collective-permute-start(f32[4,512,256]{2,1,0:T(8,128)} %pick_columns.1), channel_id=1, source_target_pairs={{0,1},{1,0},{2,3},{3,2},{4,5},{5,4},{6,7},{7,6},{8,9},{9,8},{10,11... | collective-permute-start | bytes 6291464 | tf_op jit(solution)/shard_map/ppermute | solution.py:484
  10.9 0.8 copy-start.1
  13.7 9.7 %collective-permute-start.4 = (f32[1,392,128]{2,1,0:T(8,128)}, f32[1,392,128]{2,1,0:T(8,128)S(1)}, u32[]{:S(2)}, u32[]{:S(2)}) collective-permute-start(f32[1,392,128]{2,1,0:T(8,128)} %get-tuple-element.41.later_ref), channel_id=1, source_target_pairs={{0,2},{1,3},{2,4},{3,5},{4,6},{5,7},{8,10},{9,11},{10,12},{11,13},... | collective-permute-start | bytes 602120 | tf_op jit(solution)/shard_map/ppermute | solution.py:476
  23.3 0.7 copy-start.4
  25.8 9.2 %collective-permute-start.5 = (f32[1,392,128]{2,1,0:T(8,128)}, f32[1,392,128]{2,1,0:T(8,128)S(1)}, u32[]{:S(2)}, u32[]{:S(2)}) collective-permute-start(f32[1,392,128]{2,1,0:T(8,128)} %shard_map.89), channel_id=1, source_target_pairs={{0,4},{1,5},{2,6},{3,7},{8,12},{9,13},{10,14},{11,15},{16,20},{17,... | collective-permute-start | bytes 602120 | tf_op jit(solution)/shard_map/ppermute | solution.py:476
  35.0 0.7 copy-start.19
  37.8 5.6 %copy-start.17 = (f32[1,392,128]{2,1,0:T(8,128)S(1)}, f32[1,392,128]{2,1,0:T(8,128)}, u32[]{:S(2)}) copy-start(f32[1,392,128]{2,1,0:T(8,128)} %get-tuple-element.38.later_ref) | copy-start | bytes 602116
  37.8 21.7 %collective-permute-start.6 = (f32[1,392,128]{2,1,0:T(8,128)}, f32[1,392,128]{2,1,0:T(8,128)S(1)}, u32[]{:S(2)}, u32[]{:S(2)}) collective-permute-start(f32[1,392,128]{2,1,0:T(8,128)} %get-tuple-element.42), channel_id=1, source_target_pairs={{0,1},{1,0},{2,3},{3,2},{4,5},{5,4},{6,7},{7,6},{8,9},{9,8},{10,11... | collective-permute-start | bytes 602120 | tf_op jit(solution)/shard_map/ppermute | solution.py:481
  43.4 25.4 %collective-permute-start.1 = (f32[1,392,128]{2,1,0:T(8,128)S(1)}, f32[1,392,128]{2,1,0:T(8,128)S(1)}, u32[]{:S(2)}, u32[]{:S(2)}) collective-permute-start(f32[1,392,128]{2,1,0:T(8,128)S(1)} %copy-done.17), channel_id=1, source_target_pairs={{0,2},{1,3},{2,4},{3,5},{4,6},{5,7},{8,10},{9,11},{10,12},{11,13},... | collective-permute-start | bytes 602120 | tf_op jit(solution)/shard_map/ppermute | solution.py:476
  59.4 37.3 %collective-permute-start.7 = (f32[2,128,512]{2,1,0:T(8,128)}, f32[2,128,512]{2,1,0:T(8,128)S(1)}, u32[]{:S(2)}, u32[]{:S(2)}) collective-permute-start(f32[2,128,512]{2,1,0:T(8,128)} %get-tuple-element.47.own0), channel_id=1, source_target_pairs={{0,1},{1,0},{2,3},{3,2},{4,5},{5,4},{6,7},{7,6},{8,9},{9,8},{10,11... | collective-permute-start | bytes 1572872 | tf_op jit(solution)/shard_map/ppermute | solution.py:498
  59.5 0.7 copy-start.16
  68.5 28.2 %collective-permute-start.8 = (f32[2,128,512]{2,1,0:T(8,128)}, f32[2,128,512]{2,1,0:T(8,128)S(1)}, u32[]{:S(2)}, u32[]{:S(2)}) collective-permute-start(f32[2,128,512]{2,1,0:T(8,128)} %get-tuple-element.48.own1), channel_id=1, source_target_pairs={{0,1},{1,0},{2,3},{3,2},{4,5},{5,4},{6,7},{7,6},{8,9},{9,8},{10,11... | collective-permute-start | bytes 1572872 | tf_op jit(solution)/shard_map/ppermute | solution.py:498
  68.8 0.7 copy-start.3
  71.3 10.1 %collective-permute-start.2 = (f32[1,392,128]{2,1,0:T(8,128)}, f32[1,392,128]{2,1,0:T(8,128)S(1)}, u32[]{:S(2)}, u32[]{:S(2)}) collective-permute-start(f32[1,392,128]{2,1,0:T(8,128)} %shard_map.87), channel_id=1, source_target_pairs={{0,4},{1,5},{2,6},{3,7},{8,12},{9,13},{10,14},{11,15},{16,20},{17,... | collective-permute-start | bytes 602120 | tf_op jit(solution)/shard_map/ppermute | solution.py:476
  81.4 0.7 copy-start.18
  84.3 20.1 %collective-permute-start.3 = (f32[1,392,128]{2,1,0:T(8,128)}, f32[1,392,128]{2,1,0:T(8,128)S(1)}, u32[]{:S(2)}, u32[]{:S(2)}) collective-permute-start(f32[1,392,128]{2,1,0:T(8,128)} %get-tuple-element.39), channel_id=1, source_target_pairs={{0,1},{1,0},{2,3},{3,2},{4,5},{5,4},{6,7},{7,6},{8,9},{9,8},{10,11... | collective-permute-start | bytes 602120 | tf_op jit(solution)/shard_map/ppermute | solution.py:481
  92.5 24.0 %collective-permute-start.17 = (f32[2,128,512]{2,1,0:T(8,128)}, f32[2,128,512]{2,1,0:T(8,128)S(1)}, u32[]{:S(2)}, u32[]{:S(2)}) collective-permute-start(f32[2,128,512]{2,1,0:T(8,128)} %get-tuple-element.58.own0), channel_id=1, source_target_pairs={{0,1},{1,0},{2,3},{3,2},{4,5},{5,4},{6,7},{7,6},{8,9},{9,8},{10,11... | collective-permute-start | bytes 1572872 | tf_op jit(solution)/shard_map/ppermute | solution.py:498
  96.7 0.8 copy-start.8
  97.5 0.8 copy-start.10
  104.4 0.7 copy-start.20
  105.0 10.0 %copy-start.21 = (f32[2,4,64,256]{3,2,1,0:T(8,128)S(1)}, f32[2,4,64,256]{3,2,1,0:T(8,128)}, u32[]{:S(2)}) copy-start(f32[2,4,64,256]{3,2,1,0:T(8,128)} %get-tuple-element.53) | copy-start | bytes 1572868
  113.5 3.1 %collective-permute-start.18 = (f32[2,128,512]{2,1,0:T(8,128)}, f32[2,128,512]{2,1,0:T(8,128)S(1)}, u32[]{:S(2)}, u32[]{:S(2)}) collective-permute-start(f32[2,128,512]{2,1,0:T(8,128)} %get-tuple-element.59.own1), channel_id=1, source_target_pairs={{0,1},{1,0},{2,3},{3,2},{4,5},{5,4},{6,7},{7,6},{8,9},{9,8},{10,11... | collective-permute-start | bytes 1572872 | tf_op jit(solution)/shard_map/ppermute | solution.py:498
  113.5 15.1 %collective-permute-start.10 = (f32[2,4,64,256]{3,2,1,0:T(8,128)}, f32[2,4,64,256]{3,2,1,0:T(8,128)S(1)}, u32[]{:S(2)}, u32[]{:S(2)}) collective-permute-start(f32[2,4,64,256]{3,2,1,0:T(8,128)} %get-tuple-element.51), channel_id=1, source_target_pairs={{0,8},{8,0},{16,24},{24,16},{1,9},{9,1},{17,25},{25,17},{2,10},{10... | collective-permute-start | bytes 1572872 | tf_op jit(solution)/shard_map/ppermute | solution.py:521
  115.0 13.5 %copy-start.2 = (f32[2,4,64,256]{3,2,1,0:T(8,128)S(1)}, f32[2,4,64,256]{3,2,1,0:T(8,128)}, u32[]{:S(2)}) copy-start(f32[2,4,64,256]{3,2,1,0:T(8,128)} %get-tuple-element.49.rest_1_) | copy-start | bytes 1572868
  115.0 15.9 %collective-permute-start.12 = (f32[2,4,64,256]{3,2,1,0:T(8,128)S(1)}, f32[2,4,64,256]{3,2,1,0:T(8,128)S(1)}, u32[]{:S(2)}, u32[]{:S(2)}) collective-permute-start(f32[2,4,64,256]{3,2,1,0:T(8,128)S(1)} %copy-done.21), channel_id=1, source_target_pairs={{0,16},{8,24},{16,0},{24,8},{1,17},{9,25},{17,1},{25,9},{2,18},{10... | collective-permute-start | bytes 1572872 | tf_op jit(solution)/shard_map/ppermute | solution.py:521
  116.5 0.8 copy-start.9
  117.4 0.8 copy-start.11
  124.2 6.7 %copy-start.5 = (f32[2,4,64,256]{3,2,1,0:T(8,128)S(1)}, f32[2,4,64,256]{3,2,1,0:T(8,128)}, u32[]{:S(2)}) copy-start(f32[2,4,64,256]{3,2,1,0:T(8,128)} %get-tuple-element.52) | copy-start | bytes 1572868
  124.2 15.6 %collective-permute-start.19 = (f32[2,4,64,256]{3,2,1,0:T(8,128)}, f32[2,4,64,256]{3,2,1,0:T(8,128)S(1)}, u32[]{:S(2)}, u32[]{:S(2)}) collective-permute-start(f32[2,4,64,256]{3,2,1,0:T(8,128)} %get-tuple-element.61), channel_id=1, source_target_pairs={{0,8},{8,0},{16,24},{24,16},{1,9},{9,1},{17,25},{25,17},{2,10},{10... | collective-permute-start | bytes 1572872 | tf_op jit(solution)/shard_map/ppermute | solution.py:521
  124.8 17.3 %collective-permute-start.21 = (f32[2,4,64,256]{3,2,1,0:T(8,128)}, f32[2,4,64,256]{3,2,1,0:T(8,128)S(1)}, u32[]{:S(2)}, u32[]{:S(2)}) collective-permute-start(f32[2,4,64,256]{3,2,1,0:T(8,128)} %get-tuple-element.63), channel_id=1, source_target_pairs={{0,16},{8,24},{16,0},{24,8},{1,17},{9,25},{17,1},{25,9},{2,18},{10... | collective-permute-start | bytes 1572872 | tf_op jit(solution)/shard_map/ppermute | solution.py:521
  128.6 11.2 %copy-start.7 = (f32[2,4,64,256]{3,2,1,0:T(8,128)S(1)}, f32[2,4,64,256]{3,2,1,0:T(8,128)}, u32[]{:S(2)}) copy-start(f32[2,4,64,256]{3,2,1,0:T(8,128)} %get-tuple-element.60) | copy-start | bytes 1572868
  129.4 17.3 %collective-permute-start.11 = (f32[1,4,64,256]{3,2,1,0:T(8,128)S(1)}, f32[1,4,64,256]{3,2,1,0:T(8,128)S(1)}, u32[]{:S(2)}, u32[]{:S(2)}) collective-permute-start(f32[1,4,64,256]{3,2,1,0:T(8,128)S(1)} %get-tuple-element.70), channel_id=1, source_target_pairs={{0,16},{8,24},{16,0},{24,8},{1,17},{9,25},{17,1},{25,9},{2,18},{10... | collective-permute-start | bytes 786440 | tf_op jit(solution)/shard_map/ppermute | solution.py:521
  131.0 11.1 %copy-start.6 = (f32[2,4,64,256]{3,2,1,0:T(8,128)S(1)}, f32[2,4,64,256]{3,2,1,0:T(8,128)}, u32[]{:S(2)}) copy-start(f32[2,4,64,256]{3,2,1,0:T(8,128)} %get-tuple-element.62) | copy-start | bytes 1572868
  131.7 15.0 %collective-permute-start.13 = (f32[1,4,64,256]{3,2,1,0:T(8,128)S(1)}, f32[1,4,64,256]{3,2,1,0:T(8,128)S(1)}, u32[]{:S(2)}, u32[]{:S(2)}) collective-permute-start(f32[1,4,64,256]{3,2,1,0:T(8,128)S(1)} %get-tuple-element.68), channel_id=1, source_target_pairs={{0,8},{8,0},{16,24},{24,16},{1,9},{9,1},{17,25},{25,17},{2,10},{10... | collective-permute-start | bytes 786440 | tf_op jit(solution)/shard_map/ppermute | solution.py:521
  140.6 16.1 %collective-permute-start.20 = (f32[1,4,64,256]{3,2,1,0:T(8,128)S(1)}, f32[1,4,64,256]{3,2,1,0:T(8,128)S(1)}, u32[]{:S(2)}, u32[]{:S(2)}) collective-permute-start(f32[1,4,64,256]{3,2,1,0:T(8,128)S(1)} %get-tuple-element.74), channel_id=1, source_target_pairs={{0,16},{8,24},{16,0},{24,8},{1,17},{9,25},{17,1},{25,9},{2,18},{10... | collective-permute-start | bytes 786440 | tf_op jit(solution)/shard_map/ppermute | solution.py:521
  142.9 13.8 %collective-permute-start.22 = (f32[1,4,64,256]{3,2,1,0:T(8,128)S(1)}, f32[1,4,64,256]{3,2,1,0:T(8,128)S(1)}, u32[]{:S(2)}, u32[]{:S(2)}) collective-permute-start(f32[1,4,64,256]{3,2,1,0:T(8,128)S(1)} %get-tuple-element.72), channel_id=1, source_target_pairs={{0,8},{8,0},{16,24},{24,16},{1,9},{9,1},{17,25},{25,17},{2,10},{10... | collective-permute-start | bytes 786440 | tf_op jit(solution)/shard_map/ppermute | solution.py:521
  146.7 0.7 copy-start.12
  146.7 0.8 copy-start.14
  149.5 13.9 %collective-permute-start.16 = (f32[128,256]{1,0:T(8,128)}, f32[128,256]{1,0:T(8,128)S(1)}, u32[]{:S(2)}, u32[]{:S(2)}) collective-permute-start(f32[128,256]{1,0:T(8,128)} %get-tuple-element.57), channel_id=1, source_target_pairs={{0,6},{1,7},{2,4},{3,5},{4,2},{5,3},{6,0},{7,1},{8,14},{9,15},{10,... | collective-permute-start | bytes 393224 | tf_op jit(solution)/shard_map/ppermute | solution.py:530
  156.1 16.3 %collective-permute-start.15 = (f32[128,256]{1,0:T(8,128)}, f32[128,256]{1,0:T(8,128)S(1)}, u32[]{:S(2)}, u32[]{:S(2)}) collective-permute-start(f32[128,256]{1,0:T(8,128)} %get-tuple-element.56), channel_id=1, source_target_pairs={{0,4},{1,5},{2,6},{3,7},{4,0},{5,1},{6,2},{7,3},{8,12},{9,13},{10,... | collective-permute-start | bytes 393224 | tf_op jit(solution)/shard_map/ppermute | solution.py:530
  156.1 16.3 %collective-permute-start.14 = (f32[128,256]{1,0:T(8,128)}, f32[128,256]{1,0:T(8,128)S(1)}, u32[]{:S(2)}, u32[]{:S(2)}) collective-permute-start(f32[128,256]{1,0:T(8,128)} %get-tuple-element.55), channel_id=1, source_target_pairs={{0,2},{1,3},{2,0},{3,1},{4,6},{5,7},{6,4},{7,5},{8,10},{9,11},{10,... | collective-permute-start | bytes 393224 | tf_op jit(solution)/shard_map/ppermute | solution.py:530
  156.7 0.7 copy-start.13
  156.7 0.8 copy-start.15
  159.5 13.9 %collective-permute-start.25 = (f32[128,256]{1,0:T(8,128)}, f32[128,256]{1,0:T(8,128)S(1)}, u32[]{:S(2)}, u32[]{:S(2)}) collective-permute-start(f32[128,256]{1,0:T(8,128)} %get-tuple-element.67), channel_id=1, source_target_pairs={{0,6},{1,7},{2,4},{3,5},{4,2},{5,3},{6,0},{7,1},{8,14},{9,15},{10,... | collective-permute-start | bytes 393224 | tf_op jit(solution)/shard_map/ppermute | solution.py:530
  163.3 13.4 %collective-permute-start.24 = (f32[128,256]{1,0:T(8,128)}, f32[128,256]{1,0:T(8,128)S(1)}, u32[]{:S(2)}, u32[]{:S(2)}) collective-permute-start(f32[128,256]{1,0:T(8,128)} %get-tuple-element.66), channel_id=1, source_target_pairs={{0,4},{1,5},{2,6},{3,7},{4,0},{5,1},{6,2},{7,3},{8,12},{9,13},{10,... | collective-permute-start | bytes 393224 | tf_op jit(solution)/shard_map/ppermute | solution.py:530
  163.3 13.4 %collective-permute-start.23 = (f32[128,256]{1,0:T(8,128)}, f32[128,256]{1,0:T(8,128)S(1)}, u32[]{:S(2)}, u32[]{:S(2)}) collective-permute-start(f32[128,256]{1,0:T(8,128)} %get-tuple-element.65), channel_id=1, source_target_pairs={{0,2},{1,3},{2,0},{3,1},{4,6},{5,7},{6,4},{7,5},{8,10},{9,11},{10,... | collective-permute-start | bytes 393224 | tf_op jit(solution)/shard_map/ppermute | solution.py:530

commit v4 on v3

--- a/solution.py
+++ b/solution.py
@@ -167,7 +167,7 @@
 
 
 def solve_kernel(
-    head_of, place_ref, regular_ref, q_ref, k_ref, v_ref, g_ref, rows_ref, state_ref, *rest
+    half, head_of, place_ref, regular_ref, q_ref, k_ref, v_ref, g_ref, rows_ref, mine_ref, other_ref, *rest
 ):
     mixed_ref, turned_ref = rest[-2:]
     rows, dim = q_ref.shape
@@ -181,12 +181,18 @@
     lower = row_at >= column_at
 
     is_second = lax.rem(step, 2) == 1
-    packed = state_ref[0, 0:dim, :]
+    is_mine = step < half
+
+    def state(start, size):
+        at = pl.ds(start, size)
+        return jnp.where(is_mine, mine_ref[0, at, :], other_ref[0, at, :])
+
+    packed = state(0, dim)
     direct = (row_at > column_at) == is_second
     start = jnp.where(direct, packed, packed.T)
-    diagonal = state_ref[0, 3 * dim + 2 : 3 * dim + 3, :]
+    diagonal = state(3 * dim, EXTRA)[2:3]
     gram = [jnp.where((row_at == column_at) & is_second, diagonal, start)]
-    memory = [state_ref[0, pl.ds(pl.multiple_of((1 + lax.rem(step, 2)) * dim, dim), dim), :]]
+    memory = [state(pl.multiple_of((1 + lax.rem(step, 2)) * dim, dim), dim)]
     start_trace = jnp.sum(jnp.where(row_at == column_at, gram[0], 0.0), axis=0, keepdims=True)
     start_trace = jnp.sum(start_trace, axis=1, keepdims=True)
     cumulative_row = rows_ref[0, pl.ds(head, 1), :]
@@ -197,14 +203,14 @@
         whole.append(cumulative[c] + offset)
         offset = offset + last[c]
     trace = jnp.exp(jnp.concatenate(whole, axis=1)) * start_trace + rows_ref[1, pl.ds(head, 1), :]
-    half = 0.5 * trace
-    center = ridge + half
+    span = 0.5 * trace
+    center = ridge + span
     alphas, gammas = [1.0 / center], []
     for i in range(1, ITERS):
         factor = 0.5 if i == 1 else 0.25
-        product = half * alphas[-1]
-        alphas.append(1.0 / (center - factor * half * product))
-        gammas.append(alphas[-1] * (factor * half * product))
+        product = span * alphas[-1]
+        alphas.append(1.0 / (center - factor * span * product))
+        gammas.append(alphas[-1] * (factor * span * product))
     table = jnp.concatenate(alphas + gammas + [cumulative_row], axis=0).T
 
     def column(index):
@@ -270,23 +276,25 @@
         mixed_ref[place[c], :] = output.astype(BF16)
 
 
-def solve_heads(place, k, side, per, regular, queries, keys, values, grads, table, states, mixed, after):
+def solve_heads(place, k, per, regular, queries, keys, values, grads, table, mine, other, mixed, after):
     rows, columns = keys.shape
     heads = regular.shape[0]
     dim = columns // heads
-    count = 2 * states.shape[0]
+    half = 2 * mine.shape[0]
+    count = 2 * half
 
     def head_of(step, place_ref):
-        block = place_ref[0] if side == 0 else 1 - place_ref[0]
-        return (block * count + step) * per + k
+        return lax.rem(place_ref[0] * half + step, count) * per + k
 
     def at_head(step, place_ref, regular_ref):
         return (0, head_of(step, place_ref))
 
     wide_spec = pl.BlockSpec((rows, dim), at_head)
-    operands = [queries, keys, values, grads, table, states]
+    operands = [queries, keys, values, grads, table, mine, other]
     in_specs = [wide_spec] * 4 + [pl.BlockSpec(table.shape, lambda step, *_: (0, 0, 0))]
-    in_specs.append(pl.BlockSpec((1,) + states.shape[1:], lambda step, *_: (step // 2, 0, 0)))
+    pair = (1,) + mine.shape[1:]
+    in_specs.append(pl.BlockSpec(pair, lambda step, *_: (jnp.minimum(step, half - 1) // 2, 0, 0)))
+    in_specs.append(pl.BlockSpec(pair, lambda step, *_: (jnp.maximum(step - half, 0) // 2, 0, 0)))
     aliases = {}
     if mixed is not None:
         operands.append(mixed)
@@ -296,7 +304,7 @@
         operands.append(after)
         in_specs.append(pl.BlockSpec(memory_space=pl.ANY))
     return pl.pallas_call(
-        functools.partial(solve_kernel, head_of),
+        functools.partial(solve_kernel, half, head_of),
         out_shape=[
             jax.ShapeDtypeStruct((rows, columns), BF16),
             jax.ShapeDtypeStruct((count, dim, rows), F32),
@@ -353,20 +361,21 @@
     )(blocks)
 
 
-def gradient_kernel(order, place_ref, own0, own1, far0, far1, tokens_ref, other_ref, *rest):
+def gradient_kernel(order, place_ref, own_ref, far_ref, tokens_ref, other_ref, *rest):
     outs, left_ref = rest[:-1], rest[-1]
     core, group = place_ref[0], place_ref[1]
-    half, dim, rows = own0.shape
+    count, dim, rows = own_ref.shape
+    half = count // 2
     middle = dim // 2
 
     @pl.when(pl.program_id(0) == 0)
     def _():
         for i in range(half):
             near, away = (core * half + i) ^ group, ((1 - core) * half + i) ^ group
-            left_ref[near, :, 0:rows] = own0[i].astype(BF16)
-            left_ref[away, :, 0:rows] = own1[i].astype(BF16)
-            left_ref[near, :, rows:] = far1[i].astype(BF16)
-            left_ref[away, :, rows:] = far0[i].astype(BF16)
+            left_ref[near, :, 0:rows] = own_ref[i].astype(BF16)
+            left_ref[away, :, 0:rows] = own_ref[half + i].astype(BF16)
+            left_ref[near, :, rows:] = far_ref[half + i].astype(BF16)
+            left_ref[away, :, rows:] = far_ref[i].astype(BF16)
 
     left = left_ref[...].reshape(2 * half * dim, 2 * rows)
     result = dot(left, jnp.concatenate([tokens_ref[...], other_ref[0]], axis=0))
@@ -378,17 +387,18 @@
 
 
 def gradient_blocks(place, own, far, tokens, other, order):
-    half, dim, rows = own[0].shape
+    count, dim, rows = own.shape
+    half = count // 2
     blocks, _, size = other.shape
     out = jax.ShapeDtypeStruct((half, blocks, dim // 2, size), F32)
-    turned_spec = pl.BlockSpec((half, dim, rows), lambda z, p: (0, 0, 0))
+    turned_spec = pl.BlockSpec((count, dim, rows), lambda z, p: (0, 0, 0))
     return pl.pallas_call(
         functools.partial(gradient_kernel, order),
         out_shape=[out] * 4,
         grid_spec=pltpu.PrefetchScalarGridSpec(
             num_scalar_prefetch=1,
             grid=(blocks,),
-            in_specs=[turned_spec] * 4
+            in_specs=[turned_spec] * 2
             + [
                 pl.BlockSpec((rows, size), lambda z, p: (0, 2 * (p[2] ^ z) + p[0])),
                 pl.BlockSpec((1, rows, size), lambda z, p: (p[2] ^ z, 0, 0)),
@@ -402,7 +412,28 @@
             transcendentals=0,
         ),
         name="gradient_blocks",
-    )(place, *own, *far, tokens, other)
+    )(place, own, far, tokens, other)
+
+
+def sum_kernel(keep_ref, came_ref, keep_out, send_out):
+    out_half = keep_out.shape[0]
+    for i in range(out_half):
+        send_out[i] = keep_ref[out_half + i] + came_ref[out_half + i]
+    for i in range(out_half):
+        keep_out[i] = keep_ref[i] + came_ref[i]
+
+
+def sum_blocks(keep, came):
+    shape = (keep.shape[0] // 2,) + keep.shape[1:]
+    vmem = pl.BlockSpec(memory_space=pltpu.VMEM)
+    return pl.pallas_call(
+        sum_kernel,
+        out_shape=[jax.ShapeDtypeStruct(shape, F32)] * 2,
+        in_specs=[vmem] * 2,
+        out_specs=[vmem] * 2,
+        cost_estimate=pl.CostEstimate(flops=0, bytes_accessed=12 * keep.size, transcendentals=0),
+        name="sum_blocks",
+    )(keep, came)
 
 
 def merge_kernel(count, *refs):
@@ -489,27 +520,14 @@
     paths = [list(range(dp_bits)), list(reversed(range(dp_bits)))]
     order = [bit_order(path) for path in paths]
 
-    turned, mixed = {}, None
-
-    def solve(k, side, mixed, after):
-        mixed, out = solve_heads(
-            place, k, side, per, regular, queries, keys, values, grads, table, starts[k][side], mixed, after
+    products, mixed = [], None
+    for k, (mine, others) in enumerate(starts):
+        after = products[-1][0] if k > 0 else None
+        mixed, turned = solve_heads(
+            place, k, per, regular, queries, keys, values, grads, table, mine, others, mixed, after
         )
-        turned[k, side] = (out, lax.ppermute(out, "seq", partner))
-        return mixed
-
-    def gradient(k):
-        own = [turned[k, side][0] for side in range(2)]
-        far = [turned[k, side][1] for side in range(2)]
-        return gradient_blocks(place, own, far, tokens, other, order)
-
-    products = []
-    for k in range(per):
-        mixed = solve(k, 0, mixed, None)
-        if k > 0:
-            products.append(gradient(k - 1))
-        mixed = solve(k, 1, mixed, products[-1][0] if k > 0 else None)
-    products.append(gradient(per - 1))
+        far = lax.ppermute(turned, "seq", partner)
+        products.append(gradient_blocks(place, turned, far, tokens, other, order))
 
     finished = []
     for blocks in products:
@@ -522,8 +540,7 @@
                 if bit == path[-1]:
                     sums += [keep, came]
                 else:
-                    total = keep + came
-                    keep, send = jnp.split(total, 2, axis=0)
+                    keep, send = sum_blocks(keep, came)
         out, *others = merge_blocks(sums)
         for z, other_block in enumerate(others, 1):
             pairs = [(i, i ^ (2 * z)) for i in range(steps)]

time: 179 us -> 178 us (level)
  waiting for transfers between devices: 34.6 us -> 30.8 us
  Pallas kernels: 72 us -> 75.7 us
    ppermute x8, waiting for transfers between devices: 11.9 us -> 4.71 us  [program(): came = lax.ppermute(send, 'dp', pairs)]
    pallas_call x4 -> x6, Pallas kernels: 33.3 us -> 36.7 us  [the longest x2 28.6 us: solve_heads(): pl.pallas_call(functools.partial(solve_kernel, half, head_of), out_shape=...]
    split x4 -> x0, local copies, waits for them, and re-layouts: 2.99 us -> none  [program(): keep, send = jnp.split(total, 2, axis=0)]
    ppermute x6, waiting for transfers between devices: 9.28 us -> 11.5 us  [program(): out = out + lax.ppermute(other_block, 'seq', pairs)]
    unnamed x44 -> x42, local copies, waits for them, and re-layouts: 9.66 us -> 11.6 us
  transfers between devices with their start and end apart: 26 -> 24, of which waited for: 8 -> 8; matrix products, arithmetic and copies ran while one was open for 6% -> 4% of each run, Pallas kernels for 38% -> 30%
where the time goes in v4:
time: 178 us; the launch traced here: 177 us
  Pallas kernels  75.7 us (43%)
  starting transfers between devices  49.1 us (28%)
  waiting for transfers between devices  30.8 us (17%)
  local copies, waits for them, and re-layouts  11.6 us (7%)
  matrix products  5.51 us (3%)
  other arithmetic  3.26 us (2%)
    pallas_call x2, Pallas kernels, solve_heads(): pl.pallas_call(functools.partial(solve_kernel, half, head_of), out_shape=...  28.6 us
    ppermute x4, starting transfers between devices, program(): came_up = lax.ppermute(sent, 'seq', pairs)  22.7 us
    ppermute x6, starting transfers between devices, program(): out = out + lax.ppermute(other_block, 'seq', pairs)  13.4 us
    ppermute x4, waiting for transfers between devices, program(): came_up = lax.ppermute(sent, 'seq', pairs)  13 us
    pallas_call x2, Pallas kernels, gradient_blocks(): pl.pallas_call(functools.partial(gradient_kernel, order), out_shape=[out]...  12.3 us
    unnamed x42, local copies, waits for them, and re-layouts  11.6 us
    ppermute x8, starting transfers between devices, program(): came = lax.ppermute(send, 'dp', pairs)  11.5 us
    ppermute x6, waiting for transfers between devices, program(): out = out + lax.ppermute(other_block, 'seq', pairs)  11.5 us
  transfers between devices with their start and end apart: 24, of which 8 were waited for; matrix products, arithmetic and copies ran while one was open for 4% of the time, Pallas kernels for 30%

profile of v4, /device:TPU:0, one launch (start us, length us, event | category | flops | bytes accessed | tf_op | source)
XLA Modules:
  0.0 176.8 jit_solution(6264742995812755806)
XLA Ops:
  1.3 4.9 %local_states.1 = (f32[2,1,392,128]{3,2,1,0:T(8,128)}, f32[2,1,392,128]{3,2,1,0:T(8,128)}, f32[2,8,512]{2,1,0:T(8,128)}) custom-call(s32[3]{0:T(128)} %pad_add_fusion.place_ref.core_ref, bf16[512,1024]{1,0:T(8,128)(2,1)} %bitcast.15, bf16[512,1024]{1,0:T(8,128)(2,1)} %bitcast.18, f32[8,512]{1,0:T(8,128)} %bitcast.21), custom_call_target="tpu_custom_call" | custom-call | flops 536870912 | bytes 4194304 | tf_op jit(solution)/shard_map/local_states/pallas_call | solution.py:115
  6.7 1.6 collective-permute-done.came_ref
  9.0 1.9 %shard_map.86 = (f32[1,392,128]{2,1,0:T(8,128)}, f32[1,392,128]{2,1,0:T(8,128)}) custom-call(s32[3]{0:T(128)} %pad_add_fusion.place_ref.core_ref, f32[2,1,392,128]{3,2,1,0:T(8,128)} %get-tuple-element.40.own_ref, f32[2,1,392,128]{3,2,1,0:T(8,128)} %copy-done.1), custom_call_target="tpu_custom_call" | custom-call | bytes 1605632 | tf_op jit(solution)/shard_map/pallas_call | solution.py:158
  10.9 4.8 %collective-permute-start.4 = (f32[1,392,128]{2,1,0:T(8,128)}, f32[1,392,128]{2,1,0:T(8,128)S(1)}, u32[]{:S(2)}, u32[]{:S(2)}) collective-permute-start(f32[1,392,128]{2,1,0:T(8,128)} %get-tuple-element.45.later_ref), channel_id=1, source_target_pairs={{0,2},{1,3},{2,4},{3,5},{4,6},{5,7},{8,10},{9,11},{10,12},{11,13},... | collective-permute-start | bytes 602120 | tf_op jit(solution)/shard_map/ppermute | solution.py:507
  15.7 4.8 %collective-permute-done.4.earlier_ref.near_ref = f32[1,392,128]{2,1,0:T(8,128)S(1)} collective-permute-done((f32[1,392,128]{2,1,0:T(8,128)}, f32[1,392,128]{2,1,0:T(8,128)S(1)}, u32[]{:S(2)}, u32[]{:S(2)}) %collective-permute-start.4) | collective-permute-done | bytes 200736 | tf_op jit(solution)/shard_map/ppermute | solution.py:507
  21.2 1.7 shard_map.89
  23.0 5.3 %collective-permute-start.5 = (f32[1,392,128]{2,1,0:T(8,128)}, f32[1,392,128]{2,1,0:T(8,128)S(1)}, u32[]{:S(2)}, u32[]{:S(2)}) collective-permute-start(f32[1,392,128]{2,1,0:T(8,128)} %shard_map.89), channel_id=1, source_target_pairs={{0,4},{1,5},{2,6},{3,7},{8,12},{9,13},{10,14},{11,15},{16,20},{17,... | collective-permute-start | bytes 602120 | tf_op jit(solution)/shard_map/ppermute | solution.py:507
  28.3 4.4 %pick_columns.1 = f32[4,512,256]{2,1,0:T(8,128)} custom-call(s32[3]{0:T(128)} %pad_add_fusion.place_ref.core_ref, bf16[512,2048]{1,0:T(8,128)(2,1)} %bitcast.12), custom_call_target="tpu_custom_call" | custom-call | bytes 3145728 | tf_op jit(solution)/shard_map/pick_columns/pallas_call | solution.py:333
  33.4 2.2 %shard_map.90 = (f32[1,392,128]{2,1,0:T(8,128)}, f32[1,392,128]{2,1,0:T(8,128)}) custom-call(s32[3]{0:T(128)} %pad_add_fusion.place_ref.core_ref, f32[1,392,128]{2,1,0:T(8,128)} %copy-done.15, f32[1,392,128]{2,1,0:T(8,128)} %copy-done.4, f32[2,1,392,128]{3,2,1,0:T(8,128)} %get-tuple-element.40.own_ref, f32[2,1,392,128]{3,2,1,0:T(8,128)} %copy-done.1), custom_call_target="tpu_custom_call" | custom-call | bytes 2408448 | tf_op jit(solution)/shard_map/pallas_call | solution.py:158
  36.1 5.5 %convolution_convert_fusion.q_ref = bf16[512,1024]{1,0:T(8,128)(2,1)} fusion(bf16[2048,1024]{1,0:T(8,128)(2,1)} %param.8, bf16[1,512,2048]{2,1,0:T(8,128)(2,1)S(1)} %copy-done), kind=kOutput, calls=%fused_computation | convolution fusion | flops 2148007936 | bytes 7340032 | tf_op jit(solution)/shard_map/dot_general | solution.py:517
  42.3 14.3 %solve_heads.2 = (bf16[512,1024]{1,0:T(8,128)(2,1)}, f32[4,128,512]{2,1,0:T(8,128)}) custom-call(s32[3]{0:T(128)} %pad_add_fusion.place_ref.core_ref, f32[8]{0:T(128)} %regular_ref.3, bf16[512,1024]{1,0:T(8,128)(2,1)} %convolution_convert_fusion.q_ref, bf16[512,1024]{1,0:T(8,128)(2,1)} %bitcast.16, bf16[512,1024]{1,0:T(8,128)(2,1)} %bitcast.19, ...), custom_call_target="tpu_custom_call" | custom-call | flops 2684354560 | bytes 3670016 | tf_op jit(solution)/shard_map/solve_heads/pallas_call | solution.py:306
  56.6 7.2 %collective-permute-start.1 = (f32[1,392,128]{2,1,0:T(8,128)S(1)}, f32[1,392,128]{2,1,0:T(8,128)S(1)}, u32[]{:S(2)}, u32[]{:S(2)}) collective-permute-start(f32[1,392,128]{2,1,0:T(8,128)S(1)} %copy-done.14), channel_id=1, source_target_pairs={{0,2},{1,3},{2,4},{3,5},{4,6},{5,7},{8,10},{9,11},{10,12},{11,13},... | collective-permute-start | bytes 602120 | tf_op jit(solution)/shard_map/ppermute | solution.py:507
  63.8 4.4 %collective-permute-done.1.earlier_ref.near_ref = f32[1,392,128]{2,1,0:T(8,128)S(1)} collective-permute-done((f32[1,392,128]{2,1,0:T(8,128)S(1)}, f32[1,392,128]{2,1,0:T(8,128)S(1)}, u32[]{:S(2)}, u32[]{:S(2)}) %collective-permute-start.1) | collective-permute-done | bytes 200736 | tf_op jit(solution)/shard_map/ppermute | solution.py:507
  68.9 1.8 %shard_map.87 = f32[1,392,128]{2,1,0:T(8,128)} custom-call(s32[3]{0:T(128)} %pad_add_fusion.place_ref.core_ref, f32[1,392,128]{2,1,0:T(8,128)} %copy-done.5, f32[1,392,128]{2,1,0:T(8,128)} %get-tuple-element.42.later_ref), custom_call_target="tpu_custom_call" | custom-call | bytes 802816 | tf_op jit(solution)/shard_map/pallas_call | solution.py:158
  70.7 5.4 %collective-permute-start.2 = (f32[1,392,128]{2,1,0:T(8,128)}, f32[1,392,128]{2,1,0:T(8,128)S(1)}, u32[]{:S(2)}, u32[]{:S(2)}) collective-permute-start(f32[1,392,128]{2,1,0:T(8,128)} %shard_map.87), channel_id=1, source_target_pairs={{0,4},{1,5},{2,6},{3,7},{8,12},{9,13},{10,14},{11,15},{16,20},{17,... | collective-permute-start | bytes 602120 | tf_op jit(solution)/shard_map/ppermute | solution.py:507
  76.1 3.7 %collective-permute-done.2.far_ref = f32[1,392,128]{2,1,0:T(8,128)S(1)} collective-permute-done((f32[1,392,128]{2,1,0:T(8,128)}, f32[1,392,128]{2,1,0:T(8,128)S(1)}, u32[]{:S(2)}, u32[]{:S(2)}) %collective-permute-start.2) | collective-permute-done | bytes 200736 | tf_op jit(solution)/shard_map/ppermute | solution.py:507
  80.5 2.2 %shard_map.88 = (f32[1,392,128]{2,1,0:T(8,128)}, f32[1,392,128]{2,1,0:T(8,128)}) custom-call(s32[3]{0:T(128)} %pad_add_fusion.place_ref.core_ref, f32[1,392,128]{2,1,0:T(8,128)} %copy-done.16, f32[1,392,128]{2,1,0:T(8,128)} %copy-done.5, f32[2,1,392,128]{3,2,1,0:T(8,128)} %get-tuple-element.40.own_ref, f32[2,1,392,128]{3,2,1,0:T(8,128)} %copy-done.1), custom_call_target="tpu_custom_call" | custom-call | bytes 2408448 | tf_op jit(solution)/shard_map/pallas_call | solution.py:158
  82.7 3.6 %narrow.1.other_ref = bf16[4,512,256]{2,1,0:T(8,128)(2,1)} custom-call(f32[4,512,256]{2,1,0:T(8,128)} %collective-permute-done.8.in_ref), custom_call_target="tpu_custom_call" | custom-call | bytes 3145728 | tf_op jit(solution)/shard_map/narrow/pallas_call | solution.py:353
  86.3 1.0 copy-done.2
  87.3 6.2 %gradient_blocks.2 = (f32[2,4,64,256]{3,2,1,0:T(8,128)}, f32[2,4,64,256]{3,2,1,0:T(8,128)}, f32[2,4,64,256]{3,2,1,0:T(8,128)}, f32[2,4,64,256]{3,2,1,0:T(8,128)}) custom-call(s32[3]{0:T(128)} %pad_add_fusion.place_ref.core_ref, f32[4,128,512]{2,1,0:T(8,128)} %get-tuple-element.49.own_ref, f32[4,128,512]{2,1,0:T(8,128)} %copy-done.2, ...), custom_call_target="tpu_custom_call" | custom-call | flops 1073741824 | bytes 6291456 | tf_op jit(solution)/shard_map/gradient_blocks/pallas_call | solution.py:395
  94.1 14.3 %solve_heads.3 = (bf16[512,1024]{1,0:T(8,128)(2,1)}, f32[4,128,512]{2,1,0:T(8,128)}) custom-call(s32[3]{0:T(128)} %pad_add_fusion.place_ref.core_ref, f32[8]{0:T(128)} %regular_ref.3, bf16[512,1024]{1,0:T(8,128)(2,1)} %convolution_convert_fusion.q_ref, bf16[512,1024]{1,0:T(8,128)(2,1)} %bitcast.17, ...), custom_call_target="tpu_custom_call", output_to_operand_aliasing={{0}: (9, {})} | custom-call | flops 2684354560 | bytes 3670016 | tf_op jit(solution)/shard_map/solve_heads/pallas_call | solution.py:306
  108.9 1.5 collective-permute-start.9
  110.4 1.5 collective-permute-start.11
  112.0 1.0 copy-done.3
  113.0 6.1 %gradient_blocks.3 = (f32[2,4,64,256]{3,2,1,0:T(8,128)}, f32[2,4,64,256]{3,2,1,0:T(8,128)}, f32[2,4,64,256]{3,2,1,0:T(8,128)}, f32[2,4,64,256]{3,2,1,0:T(8,128)}) custom-call(s32[3]{0:T(128)} %pad_add_fusion.place_ref.core_ref, f32[4,128,512]{2,1,0:T(8,128)} %get-tuple-element.63.own_ref, f32[4,128,512]{2,1,0:T(8,128)} %copy-done.3, ...), custom_call_target="tpu_custom_call" | custom-call | flops 1073741824 | bytes 6291456 | tf_op jit(solution)/shard_map/gradient_blocks/pallas_call | solution.py:395
  119.1 1.0 collective-permute-start.17
  120.1 1.5 collective-permute-start.19
  121.6 2.1 %collective-permute-done.9.came_ref = f32[2,4,64,256]{3,2,1,0:T(8,128)S(1)} collective-permute-done((f32[2,4,64,256]{3,2,1,0:T(8,128)S(1)}, f32[2,4,64,256]{3,2,1,0:T(8,128)S(1)}, u32[]{:S(2)}, u32[]{:S(2)}) %collective-permute-start.9) | collective-permute-done | bytes 524320 | tf_op jit(solution)/shard_map/ppermute | solution.py:539
  124.5 2.0 %sum_blocks.4 = (f32[1,4,64,256]{3,2,1,0:T(8,128)}, f32[1,4,64,256]{3,2,1,0:T(8,128)}) custom-call(f32[2,4,64,256]{3,2,1,0:T(8,128)} %get-tuple-element.50.rest_1_.keep_ref, f32[2,4,64,256]{3,2,1,0:T(8,128)} %copy-done.9), custom_call_target="tpu_custom_call" | custom-call | bytes 1572864 | tf_op jit(solution)/shard_map/sum_blocks/pallas_call | solution.py:429
  126.6 1.5 collective-permute-start.10
  128.1 0.8 copy-done.7
  128.9 2.0 %sum_blocks.5 = (f32[1,4,64,256]{3,2,1,0:T(8,128)}, f32[1,4,64,256]{3,2,1,0:T(8,128)}) custom-call(f32[2,4,64,256]{3,2,1,0:T(8,128)} %get-tuple-element.55.keep_ref, f32[2,4,64,256]{3,2,1,0:T(8,128)} %copy-done.7), custom_call_target="tpu_custom_call" | custom-call | bytes 1572864 | tf_op jit(solution)/shard_map/sum_blocks/pallas_call | solution.py:429
  130.9 1.5 collective-permute-start.12
  132.4 2.6 %collective-permute-done.17.came_ref = f32[2,4,64,256]{3,2,1,0:T(8,128)S(1)} collective-permute-done((f32[2,4,64,256]{3,2,1,0:T(8,128)}, f32[2,4,64,256]{3,2,1,0:T(8,128)S(1)}, u32[]{:S(2)}, u32[]{:S(2)}) %collective-permute-start.17) | collective-permute-done | bytes 524320 | tf_op jit(solution)/shard_map/ppermute | solution.py:539
  135.8 2.0 %sum_blocks.6 = (f32[1,4,64,256]{3,2,1,0:T(8,128)}, f32[1,4,64,256]{3,2,1,0:T(8,128)}) custom-call(f32[2,4,64,256]{3,2,1,0:T(8,128)} %get-tuple-element.64.keep_ref, f32[2,4,64,256]{3,2,1,0:T(8,128)} %copy-done.8), custom_call_target="tpu_custom_call" | custom-call | bytes 1572864 | tf_op jit(solution)/shard_map/sum_blocks/pallas_call | solution.py:429
  137.8 1.5 collective-permute-start.18
  139.3 0.8 copy-done.6
  140.1 2.0 %sum_blocks.7 = (f32[1,4,64,256]{3,2,1,0:T(8,128)}, f32[1,4,64,256]{3,2,1,0:T(8,128)}) custom-call(f32[2,4,64,256]{3,2,1,0:T(8,128)} %get-tuple-element.68.keep_ref, f32[2,4,64,256]{3,2,1,0:T(8,128)} %copy-done.6), custom_call_target="tpu_custom_call" | custom-call | bytes 1572864 | tf_op jit(solution)/shard_map/sum_blocks/pallas_call | solution.py:429
  142.1 1.5 collective-permute-start.20
  144.4 2.0 %merge_blocks.2 = (f32[128,256]{1,0:T(8,128)}, f32[128,256]{1,0:T(8,128)}, f32[128,256]{1,0:T(8,128)}, f32[128,256]{1,0:T(8,128)}) custom-call(f32[1,4,64,256]{3,2,1,0:T(8,128)} %get-tuple-element.53.refs_0_, f32[1,4,64,256]{3,2,1,0:T(8,128)} %copy-done.11, f32[1,4,64,256]{3,2,1,0:T(8,128)} %get-tuple-element.57.refs_2_, f32[1,4,64,256]{3,2,1,0:T(8,128)} %copy-done.13), custom_call_target="tpu_custom_call" | custom-call | bytes 1572864 | tf_op jit(solution)/shard_map/merge_blocks/pallas_call | solution.py:451
  146.4 5.7 %collective-permute-start.13 = (f32[128,256]{1,0:T(8,128)}, f32[128,256]{1,0:T(8,128)S(1)}, u32[]{:S(2)}, u32[]{:S(2)}) collective-permute-start(f32[128,256]{1,0:T(8,128)} %get-tuple-element.60), channel_id=1, source_target_pairs={{0,2},{1,3},{2,0},{3,1},{4,6},{5,7},{6,4},{7,5},{8,10},{9,11},{10,... | collective-permute-start | bytes 393224 | tf_op jit(solution)/shard_map/ppermute | solution.py:547
  152.2 3.3 %collective-permute-start.14 = (f32[128,256]{1,0:T(8,128)}, f32[128,256]{1,0:T(8,128)S(1)}, u32[]{:S(2)}, u32[]{:S(2)}) collective-permute-start(f32[128,256]{1,0:T(8,128)} %get-tuple-element.61), channel_id=1, source_target_pairs={{0,4},{1,5},{2,6},{3,7},{4,0},{5,1},{6,2},{7,3},{8,12},{9,13},{10,... | collective-permute-start | bytes 393224 | tf_op jit(solution)/shard_map/ppermute | solution.py:547
  156.3 2.0 %merge_blocks.3 = (f32[128,256]{1,0:T(8,128)}, f32[128,256]{1,0:T(8,128)}, f32[128,256]{1,0:T(8,128)}, f32[128,256]{1,0:T(8,128)}) custom-call(f32[1,4,64,256]{3,2,1,0:T(8,128)} %get-tuple-element.66.refs_0_, f32[1,4,64,256]{3,2,1,0:T(8,128)} %copy-done.10, f32[1,4,64,256]{3,2,1,0:T(8,128)} %get-tuple-element.70.refs_2_, f32[1,4,64,256]{3,2,1,0:T(8,128)} %copy-done.12), custom_call_target="tpu_custom_call" | custom-call | bytes 1572864 | tf_op jit(solution)/shard_map/merge_blocks/pallas_call | solution.py:451
  158.8 3.8 %collective-permute-start.22 = (f32[128,256]{1,0:T(8,128)}, f32[128,256]{1,0:T(8,128)S(1)}, u32[]{:S(2)}, u32[]{:S(2)}) collective-permute-start(f32[128,256]{1,0:T(8,128)} %get-tuple-element.74), channel_id=1, source_target_pairs={{0,4},{1,5},{2,6},{3,7},{4,0},{5,1},{6,2},{7,3},{8,12},{9,13},{10,... | collective-permute-start | bytes 393224 | tf_op jit(solution)/shard_map/ppermute | solution.py:547
  162.7 2.8 %collective-permute-done.14 = f32[128,256]{1,0:T(8,128)S(1)} collective-permute-done((f32[128,256]{1,0:T(8,128)}, f32[128,256]{1,0:T(8,128)S(1)}, u32[]{:S(2)}, u32[]{:S(2)}) %collective-permute-start.14) | collective-permute-done | bytes 131104 | tf_op jit(solution)/shard_map/ppermute | solution.py:547
  165.5 0.9 add_add_fusion.1
  166.4 8.7 %collective-permute-done.22 = f32[128,256]{1,0:T(8,128)S(1)} collective-permute-done((f32[128,256]{1,0:T(8,128)}, f32[128,256]{1,0:T(8,128)S(1)}, u32[]{:S(2)}, u32[]{:S(2)}) %collective-permute-start.22) | collective-permute-done | bytes 131104 | tf_op jit(solution)/shard_map/ppermute | solution.py:547
  175.1 0.9 add_add_fusion
  (65 shorter events, 11.6 us)
Async XLA Ops:
  6.2 2.1 %collective-permute-start = (f32[2,1,392,128]{3,2,1,0:T(8,128)}, f32[2,1,392,128]{3,2,1,0:T(8,128)S(1)}, u32[]{:S(2)}, u32[]{:S(2)}) collective-permute-start(f32[2,1,392,128]{3,2,1,0:T(8,128)} %get-tuple-element.41), channel_id=1, source_target_pairs={{0,1},{1,0},{2,3},{3,2},{4,5},{5,4},{6,7},{7,6},{8,9},{9,8},{10,11... | collective-permute-start | bytes 1204232 | tf_op jit(solution)/shard_map/ppermute | solution.py:492
  8.2 0.8 copy-start.1
  10.9 9.7 %collective-permute-start.4 = (f32[1,392,128]{2,1,0:T(8,128)}, f32[1,392,128]{2,1,0:T(8,128)S(1)}, u32[]{:S(2)}, u32[]{:S(2)}) collective-permute-start(f32[1,392,128]{2,1,0:T(8,128)} %get-tuple-element.45.later_ref), channel_id=1, source_target_pairs={{0,2},{1,3},{2,4},{3,5},{4,6},{5,7},{8,10},{9,11},{10,12},{11,13},... | collective-permute-start | bytes 602120 | tf_op jit(solution)/shard_map/ppermute | solution.py:507
  20.6 0.7 copy-start.4
  23.0 9.7 %collective-permute-start.5 = (f32[1,392,128]{2,1,0:T(8,128)}, f32[1,392,128]{2,1,0:T(8,128)S(1)}, u32[]{:S(2)}, u32[]{:S(2)}) collective-permute-start(f32[1,392,128]{2,1,0:T(8,128)} %shard_map.89), channel_id=1, source_target_pairs={{0,4},{1,5},{2,6},{3,7},{8,12},{9,13},{10,14},{11,15},{16,20},{17,... | collective-permute-start | bytes 602120 | tf_op jit(solution)/shard_map/ppermute | solution.py:507
  28.3 7.8 %copy-start = (bf16[1,512,2048]{2,1,0:T(8,128)(2,1)S(1)}, bf16[1,512,2048]{2,1,0:T(8,128)(2,1)}, u32[]{:S(2)}) copy-start(bf16[1,512,2048]{2,1,0:T(8,128)(2,1)} %param.7) | copy-start | bytes 6291460
  32.7 50.0 %collective-permute-start.8 = (f32[4,512,256]{2,1,0:T(8,128)}, f32[4,512,256]{2,1,0:T(8,128)}, u32[]{:S(2)}, u32[]{:S(2)}) collective-permute-start(f32[4,512,256]{2,1,0:T(8,128)} %pick_columns.1), channel_id=1, source_target_pairs={{0,1},{1,0},{2,3},{3,2},{4,5},{5,4},{6,7},{7,6},{8,9},{9,8},{10,11... | collective-permute-start | bytes 6291464 | tf_op jit(solution)/shard_map/ppermute | solution.py:515
  32.7 0.7 copy-start.15
  35.6 6.0 %collective-permute-start.6 = (f32[1,392,128]{2,1,0:T(8,128)}, f32[1,392,128]{2,1,0:T(8,128)S(1)}, u32[]{:S(2)}, u32[]{:S(2)}) collective-permute-start(f32[1,392,128]{2,1,0:T(8,128)} %get-tuple-element.47), channel_id=1, source_target_pairs={{0,1},{1,0},{2,3},{3,2},{4,5},{5,4},{6,7},{7,6},{8,9},{9,8},{10,11... | collective-permute-start | bytes 602120 | tf_op jit(solution)/shard_map/ppermute | solution.py:512
  41.6 0.7 copy-start.20
  42.3 14.3 %copy-start.14 = (f32[1,392,128]{2,1,0:T(8,128)S(1)}, f32[1,392,128]{2,1,0:T(8,128)}, u32[]{:S(2)}) copy-start(f32[1,392,128]{2,1,0:T(8,128)} %get-tuple-element.42.later_ref) | copy-start | bytes 602116
  56.6 29.7 %collective-permute-start.7 = (f32[4,128,512]{2,1,0:T(8,128)}, f32[4,128,512]{2,1,0:T(8,128)S(1)}, u32[]{:S(2)}, u32[]{:S(2)}) collective-permute-start(f32[4,128,512]{2,1,0:T(8,128)} %get-tuple-element.49.own_ref), channel_id=1, source_target_pairs={{0,1},{1,0},{2,3},{3,2},{4,5},{5,4},{6,7},{7,6},{8,9},{9,8},{10,11... | collective-permute-start | bytes 3145736 | tf_op jit(solution)/shard_map/ppermute | solution.py:529
  56.6 11.6 %collective-permute-start.1 = (f32[1,392,128]{2,1,0:T(8,128)S(1)}, f32[1,392,128]{2,1,0:T(8,128)S(1)}, u32[]{:S(2)}, u32[]{:S(2)}) collective-permute-start(f32[1,392,128]{2,1,0:T(8,128)S(1)} %copy-done.14), channel_id=1, source_target_pairs={{0,2},{1,3},{2,4},{3,5},{4,6},{5,7},{8,10},{9,11},{10,12},{11,13},... | collective-permute-start | bytes 602120 | tf_op jit(solution)/shard_map/ppermute | solution.py:507
  68.2 0.7 copy-start.5
  70.7 9.1 %collective-permute-start.2 = (f32[1,392,128]{2,1,0:T(8,128)}, f32[1,392,128]{2,1,0:T(8,128)S(1)}, u32[]{:S(2)}, u32[]{:S(2)}) collective-permute-start(f32[1,392,128]{2,1,0:T(8,128)} %shard_map.87), channel_id=1, source_target_pairs={{0,4},{1,5},{2,6},{3,7},{8,12},{9,13},{10,14},{11,15},{16,20},{17,... | collective-permute-start | bytes 602120 | tf_op jit(solution)/shard_map/ppermute | solution.py:507
  79.8 0.7 copy-start.16
  82.7 10.8 %collective-permute-start.3 = (f32[1,392,128]{2,1,0:T(8,128)}, f32[1,392,128]{2,1,0:T(8,128)S(1)}, u32[]{:S(2)}, u32[]{:S(2)}) collective-permute-start(f32[1,392,128]{2,1,0:T(8,128)} %get-tuple-element.44), channel_id=1, source_target_pairs={{0,1},{1,0},{2,3},{3,2},{4,5},{5,4},{6,7},{7,6},{8,9},{9,8},{10,11... | collective-permute-start | bytes 602120 | tf_op jit(solution)/shard_map/ppermute | solution.py:512
  86.3 1.0 copy-start.2
  93.4 0.7 copy-start.19
  94.1 14.8 %copy-start.18 = (f32[2,4,64,256]{3,2,1,0:T(8,128)S(1)}, f32[2,4,64,256]{3,2,1,0:T(8,128)}, u32[]{:S(2)}) copy-start(f32[2,4,64,256]{3,2,1,0:T(8,128)} %get-tuple-element.52) | copy-start | bytes 1572868
  94.1 16.3 %copy-start.17 = (f32[2,4,64,256]{3,2,1,0:T(8,128)S(1)}, f32[2,4,64,256]{3,2,1,0:T(8,128)}, u32[]{:S(2)}) copy-start(f32[2,4,64,256]{3,2,1,0:T(8,128)} %get-tuple-element.56) | copy-start | bytes 1572868
  108.4 3.5 %collective-permute-start.16 = (f32[4,128,512]{2,1,0:T(8,128)}, f32[4,128,512]{2,1,0:T(8,128)S(1)}, u32[]{:S(2)}, u32[]{:S(2)}) collective-permute-start(f32[4,128,512]{2,1,0:T(8,128)} %get-tuple-element.63.own_ref), channel_id=1, source_target_pairs={{0,1},{1,0},{2,3},{3,2},{4,5},{5,4},{6,7},{7,6},{8,9},{9,8},{10,11... | collective-permute-start | bytes 3145736 | tf_op jit(solution)/shard_map/ppermute | solution.py:529
  108.9 14.8 %collective-permute-start.9 = (f32[2,4,64,256]{3,2,1,0:T(8,128)S(1)}, f32[2,4,64,256]{3,2,1,0:T(8,128)S(1)}, u32[]{:S(2)}, u32[]{:S(2)}) collective-permute-start(f32[2,4,64,256]{3,2,1,0:T(8,128)S(1)} %copy-done.18), channel_id=1, source_target_pairs={{0,8},{8,0},{16,24},{24,16},{1,9},{9,1},{17,25},{25,17},{2,10},{10... | collective-permute-start | bytes 1572872 | tf_op jit(solution)/shard_map/ppermute | solution.py:539
  110.4 17.7 %collective-permute-start.11 = (f32[2,4,64,256]{3,2,1,0:T(8,128)S(1)}, f32[2,4,64,256]{3,2,1,0:T(8,128)S(1)}, u32[]{:S(2)}, u32[]{:S(2)}) collective-permute-start(f32[2,4,64,256]{3,2,1,0:T(8,128)S(1)} %copy-done.17), channel_id=1, source_target_pairs={{0,16},{8,24},{16,0},{24,8},{1,17},{9,25},{17,1},{25,9},{2,18},{10... | collective-permute-start | bytes 1572872 | tf_op jit(solution)/shard_map/ppermute | solution.py:539
  111.9 1.0 copy-start.3
  119.1 15.9 %collective-permute-start.17 = (f32[2,4,64,256]{3,2,1,0:T(8,128)}, f32[2,4,64,256]{3,2,1,0:T(8,128)S(1)}, u32[]{:S(2)}, u32[]{:S(2)}) collective-permute-start(f32[2,4,64,256]{3,2,1,0:T(8,128)} %get-tuple-element.65), channel_id=1, source_target_pairs={{0,8},{8,0},{16,24},{24,16},{1,9},{9,1},{17,25},{25,17},{2,10},{10... | collective-permute-start | bytes 1572872 | tf_op jit(solution)/shard_map/ppermute | solution.py:539
  120.1 19.2 %collective-permute-start.19 = (f32[2,4,64,256]{3,2,1,0:T(8,128)}, f32[2,4,64,256]{3,2,1,0:T(8,128)S(1)}, u32[]{:S(2)}, u32[]{:S(2)}) collective-permute-start(f32[2,4,64,256]{3,2,1,0:T(8,128)} %get-tuple-element.69), channel_id=1, source_target_pairs={{0,16},{8,24},{16,0},{24,8},{1,17},{9,25},{17,1},{25,9},{2,18},{10... | collective-permute-start | bytes 1572872 | tf_op jit(solution)/shard_map/ppermute | solution.py:539
  123.7 0.8 copy-start.9
  126.6 17.1 %collective-permute-start.10 = (f32[1,4,64,256]{3,2,1,0:T(8,128)}, f32[1,4,64,256]{3,2,1,0:T(8,128)S(1)}, u32[]{:S(2)}, u32[]{:S(2)}) collective-permute-start(f32[1,4,64,256]{3,2,1,0:T(8,128)} %get-tuple-element.54), channel_id=1, source_target_pairs={{0,16},{8,24},{16,0},{24,8},{1,17},{9,25},{17,1},{25,9},{2,18},{10... | collective-permute-start | bytes 786440 | tf_op jit(solution)/shard_map/ppermute | solution.py:539
  128.1 0.8 copy-start.7
  130.9 12.7 %collective-permute-start.12 = (f32[1,4,64,256]{3,2,1,0:T(8,128)}, f32[1,4,64,256]{3,2,1,0:T(8,128)S(1)}, u32[]{:S(2)}, u32[]{:S(2)}) collective-permute-start(f32[1,4,64,256]{3,2,1,0:T(8,128)} %get-tuple-element.58), channel_id=1, source_target_pairs={{0,8},{8,0},{16,24},{24,16},{1,9},{9,1},{17,25},{25,17},{2,10},{10... | collective-permute-start | bytes 786440 | tf_op jit(solution)/shard_map/ppermute | solution.py:539
  135.0 0.8 copy-start.8
  137.8 17.6 %collective-permute-start.18 = (f32[1,4,64,256]{3,2,1,0:T(8,128)}, f32[1,4,64,256]{3,2,1,0:T(8,128)S(1)}, u32[]{:S(2)}, u32[]{:S(2)}) collective-permute-start(f32[1,4,64,256]{3,2,1,0:T(8,128)} %get-tuple-element.67), channel_id=1, source_target_pairs={{0,16},{8,24},{16,0},{24,8},{1,17},{9,25},{17,1},{25,9},{2,18},{10... | collective-permute-start | bytes 786440 | tf_op jit(solution)/shard_map/ppermute | solution.py:539
  139.3 0.8 copy-start.6
  142.1 13.3 %collective-permute-start.20 = (f32[1,4,64,256]{3,2,1,0:T(8,128)}, f32[1,4,64,256]{3,2,1,0:T(8,128)S(1)}, u32[]{:S(2)}, u32[]{:S(2)}) collective-permute-start(f32[1,4,64,256]{3,2,1,0:T(8,128)} %get-tuple-element.71), channel_id=1, source_target_pairs={{0,8},{8,0},{16,24},{24,16},{1,9},{9,1},{17,25},{25,17},{2,10},{10... | collective-permute-start | bytes 786440 | tf_op jit(solution)/shard_map/ppermute | solution.py:539
  143.6 0.7 copy-start.11
  143.6 0.8 copy-start.13
  146.4 16.2 %collective-permute-start.13 = (f32[128,256]{1,0:T(8,128)}, f32[128,256]{1,0:T(8,128)S(1)}, u32[]{:S(2)}, u32[]{:S(2)}) collective-permute-start(f32[128,256]{1,0:T(8,128)} %get-tuple-element.60), channel_id=1, source_target_pairs={{0,2},{1,3},{2,0},{3,1},{4,6},{5,7},{6,4},{7,5},{8,10},{9,11},{10,... | collective-permute-start | bytes 393224 | tf_op jit(solution)/shard_map/ppermute | solution.py:547
  152.2 13.3 %collective-permute-start.14 = (f32[128,256]{1,0:T(8,128)}, f32[128,256]{1,0:T(8,128)S(1)}, u32[]{:S(2)}, u32[]{:S(2)}) collective-permute-start(f32[128,256]{1,0:T(8,128)} %get-tuple-element.61), channel_id=1, source_target_pairs={{0,4},{1,5},{2,6},{3,7},{4,0},{5,1},{6,2},{7,3},{8,12},{9,13},{10,... | collective-permute-start | bytes 393224 | tf_op jit(solution)/shard_map/ppermute | solution.py:547
  155.4 10.1 %collective-permute-start.15 = (f32[128,256]{1,0:T(8,128)}, f32[128,256]{1,0:T(8,128)S(1)}, u32[]{:S(2)}, u32[]{:S(2)}) collective-permute-start(f32[128,256]{1,0:T(8,128)} %get-tuple-element.62), channel_id=1, source_target_pairs={{0,6},{1,7},{2,4},{3,5},{4,2},{5,3},{6,0},{7,1},{8,14},{9,15},{10,... | collective-permute-start | bytes 393224 | tf_op jit(solution)/shard_map/ppermute | solution.py:547
  155.4 0.7 copy-start.10
  155.4 0.8 copy-start.12
  158.3 8.2 %collective-permute-start.21 = (f32[128,256]{1,0:T(8,128)}, f32[128,256]{1,0:T(8,128)S(1)}, u32[]{:S(2)}, u32[]{:S(2)}) collective-permute-start(f32[128,256]{1,0:T(8,128)} %get-tuple-element.73), channel_id=1, source_target_pairs={{0,2},{1,3},{2,0},{3,1},{4,6},{5,7},{6,4},{7,5},{8,10},{9,11},{10,... | collective-permute-start | bytes 393224 | tf_op jit(solution)/shard_map/ppermute | solution.py:547
  158.8 16.3 %collective-permute-start.22 = (f32[128,256]{1,0:T(8,128)}, f32[128,256]{1,0:T(8,128)S(1)}, u32[]{:S(2)}, u32[]{:S(2)}) collective-permute-start(f32[128,256]{1,0:T(8,128)} %get-tuple-element.74), channel_id=1, source_target_pairs={{0,4},{1,5},{2,6},{3,7},{4,0},{5,1},{6,2},{7,3},{8,12},{9,13},{10,... | collective-permute-start | bytes 393224 | tf_op jit(solution)/shard_map/ppermute | solution.py:547
  162.7 12.4 %collective-permute-start.23 = (f32[128,256]{1,0:T(8,128)}, f32[128,256]{1,0:T(8,128)S(1)}, u32[]{:S(2)}, u32[]{:S(2)}) collective-permute-start(f32[128,256]{1,0:T(8,128)} %get-tuple-element.75), channel_id=1, source_target_pairs={{0,6},{1,7},{2,4},{3,5},{4,2},{5,3},{6,0},{7,1},{8,14},{9,15},{10,... | collective-permute-start | bytes 393224 | tf_op jit(solution)/shard_map/ppermute | solution.py:547

commit v5 on v4

--- a/solution.py
+++ b/solution.py
@@ -14,6 +14,13 @@
 
 F32 = jnp.float32
 BF16 = jnp.bfloat16
+
+
+FULL = pltpu.CompilerParams(vmem_limit_bytes=67_043_328)
+
+
+def whole(array):
+    return pl.BlockSpec(array.shape, lambda *_: (0,) * len(array.shape))
 
 
 def dot(left, right):
@@ -111,13 +118,15 @@
     heads = decay.shape[0]
     dim = columns // heads
     state = jax.ShapeDtypeStruct((per, half // 2, 3 * dim + EXTRA, dim), F32)
-    vmem = pl.BlockSpec(memory_space=pltpu.VMEM)
+    table = jax.ShapeDtypeStruct((2, heads, rows), F32)
     return pl.pallas_call(
         functools.partial(states_kernel, half, per),
-        out_shape=[state, state, jax.ShapeDtypeStruct((2, heads, rows), F32)],
-        in_specs=[pl.BlockSpec(memory_space=pltpu.SMEM)] + [vmem] * 3,
-        out_specs=[vmem] * 3,
+        out_shape=[state, state, table],
+        in_specs=[pl.BlockSpec(memory_space=pltpu.SMEM)] + [whole(a) for a in (keys, values, decay)],
+        out_specs=[whole(state), whole(state), whole(table)],
         scratch_shapes=[pltpu.VMEM((3, heads, rows), F32)],
+        grid=(1,),
+        compiler_params=FULL,
         cost_estimate=pl.CostEstimate(
             flops=16 * rows * dim * dim * half * per, bytes_accessed=8 * rows * columns, transcendentals=0
         ),
@@ -155,11 +164,14 @@
 
 
 def combine(kernel, place, arrays, shape, outs):
+    out = jax.ShapeDtypeStruct(shape, F32)
     return pl.pallas_call(
         kernel,
-        out_shape=[jax.ShapeDtypeStruct(shape, F32)] * outs,
-        in_specs=[pl.BlockSpec(memory_space=pltpu.SMEM)] + [pl.BlockSpec(memory_space=pltpu.VMEM)] * len(arrays),
-        out_specs=[pl.BlockSpec(memory_space=pltpu.VMEM)] * outs,
+        out_shape=[out] * outs,
+        in_specs=[pl.BlockSpec(memory_space=pltpu.SMEM)] + [whole(a) for a in arrays],
+        out_specs=[whole(out)] * outs,
+        grid=(1,),
+        compiler_params=FULL,
         cost_estimate=pl.CostEstimate(
             flops=0, bytes_accessed=8 * sum(a.size for a in arrays), transcendentals=0
         ),
@@ -319,6 +331,7 @@
         cost_estimate=pl.CostEstimate(
             flops=count * 80 * rows * dim * dim, bytes_accessed=count * 14 * rows * dim, transcendentals=0
         ),
+        compiler_params=FULL,
         name="solve_heads",
     )(place, regular, *operands)
 
@@ -340,6 +353,7 @@
             out_specs=pl.BlockSpec((1, rows, size), lambda z, core_ref: (z, 0, 0)),
         ),
         cost_estimate=pl.CostEstimate(flops=0, bytes_accessed=3 * rows * width, transcendentals=0),
+        compiler_params=FULL,
         name="pick_columns",
     )(core, tokens)
 
@@ -357,6 +371,7 @@
         in_specs=[spec],
         out_specs=spec,
         cost_estimate=pl.CostEstimate(flops=0, bytes_accessed=6 * blocks.size, transcendentals=0),
+        compiler_params=FULL,
         name="narrow",
     )(blocks)
 
@@ -411,6 +426,7 @@
             bytes_accessed=4 * (4 * half * dim * rows + blocks * rows * size + 2 * half * blocks * dim * size),
             transcendentals=0,
         ),
+        compiler_params=FULL,
         name="gradient_blocks",
     )(place, own, far, tokens, other)
 
@@ -424,13 +440,14 @@
 
 
 def sum_blocks(keep, came):
-    shape = (keep.shape[0] // 2,) + keep.shape[1:]
-    vmem = pl.BlockSpec(memory_space=pltpu.VMEM)
+    out = jax.ShapeDtypeStruct((keep.shape[0] // 2,) + keep.shape[1:], F32)
     return pl.pallas_call(
         sum_kernel,
-        out_shape=[jax.ShapeDtypeStruct(shape, F32)] * 2,
-        in_specs=[vmem] * 2,
-        out_specs=[vmem] * 2,
+        out_shape=[out] * 2,
+        in_specs=[whole(keep)] * 2,
+        out_specs=[whole(out)] * 2,
+        grid=(1,),
+        compiler_params=FULL,
         cost_estimate=pl.CostEstimate(flops=0, bytes_accessed=12 * keep.size, transcendentals=0),
         name="sum_blocks",
     )(keep, came)
@@ -447,12 +464,14 @@
 def merge_blocks(sums):
     _, chips, rows, size = sums[0].shape
     count = len(sums) // 2
-    vmem = pl.BlockSpec(memory_space=pltpu.VMEM)
+    out = jax.ShapeDtypeStruct((count * rows, size), F32)
     return pl.pallas_call(
         functools.partial(merge_kernel, count),
-        out_shape=[jax.ShapeDtypeStruct((count * rows, size), F32)] * chips,
-        in_specs=[vmem] * len(sums),
-        out_specs=[vmem] * chips,
+        out_shape=[out] * chips,
+        in_specs=[whole(a) for a in sums],
+        out_specs=[whole(out)] * chips,
+        grid=(1,),
+        compiler_params=FULL,
         cost_estimate=pl.CostEstimate(
             flops=0, bytes_accessed=6 * sum(a.size for a in sums), transcendentals=0
         ),

time: 178 us -> 171 us (0.961)
  local copies, waits for them, and re-layouts: 11.6 us -> 0 us
  starting transfers between devices: 49.1 us -> 51.6 us
  waiting for transfers between devices: 30.8 us -> 32.9 us
    unnamed x42 -> x0, local copies, waits for them, and re-layouts: 11.6 us -> none
    ppermute x8, waiting for transfers between devices: 4.71 us -> 7.6 us  [program(): came = lax.ppermute(send, 'dp', pairs)]
    ppermute x4, starting transfers between devices: 22.7 us -> 24.9 us  [program(): came_up = lax.ppermute(sent, 'seq', pairs)]
  transfers between devices with their start and end apart: 24 -> 24, of which waited for: 8 -> 8; matrix products, arithmetic and copies ran while one was open for 4% -> 4% of each run, Pallas kernels for 30% -> 31%
where the time goes in v5:
time: 171 us; the launch traced here: 170 us
  Pallas kernels  75 us (44%)
  starting transfers between devices  51.6 us (30%)
  waiting for transfers between devices  32.9 us (19%)
  matrix products  6.18 us (4%)
  other arithmetic  3.45 us (2%)
    pallas_call x2, Pallas kernels, solve_heads(): pl.pallas_call(functools.partial(solve_kernel, half, head_of), out_shape=...  28.4 us
    ppermute x4, starting transfers between devices, program(): came_up = lax.ppermute(sent, 'seq', pairs)  24.9 us
    ppermute x6, starting transfers between devices, program(): out = out + lax.ppermute(other_block, 'seq', pairs)  13.5 us
    ppermute x6, waiting for transfers between devices, program(): out = out + lax.ppermute(other_block, 'seq', pairs)  12.1 us
    pallas_call x2, Pallas kernels, gradient_blocks(): pl.pallas_call(functools.partial(gradient_kernel, order), out_shape=[out]...  12.1 us
    ppermute x8, starting transfers between devices, program(): came = lax.ppermute(send, 'dp', pairs)  11.7 us
    ppermute x4, waiting for transfers between devices, program(): came_up = lax.ppermute(sent, 'seq', pairs)  11.4 us
    pallas_call x5, Pallas kernels, combine(): pl.pallas_call(kernel, out_shape=[out] * outs, in_specs=[pl.BlockSpec(mem...  9.68 us
  transfers between devices with their start and end apart: 24, of which 8 were waited for; matrix products, arithmetic and copies ran while one was open for 4% of the time, Pallas kernels for 31%

profile of v5, /device:TPU:0, one launch (start us, length us, event | category | flops | bytes accessed | tf_op | source)
XLA Modules:
  0.0 169.8 jit_solution(3408085975755756727)
XLA Ops:
  0.6 0.7 pad_add_fusion.place_ref.core_ref
  1.3 4.9 %local_states.1 = (f32[2,1,392,128]{3,2,1,0:T(8,128)}, f32[2,1,392,128]{3,2,1,0:T(8,128)}, f32[2,8,512]{2,1,0:T(8,128)}) custom-call(s32[3]{0:T(128)} %pad_add_fusion.place_ref.core_ref, bf16[512,1024]{1,0:T(8,128)(2,1)} %bitcast.15, bf16[512,1024]{1,0:T(8,128)(2,1)} %bitcast.18, f32[8,512]{1,0:T(8,128)} %bitcast.21), custom_call_target="tpu_custom_call" | custom-call | flops 536870912 | bytes 4194304 | tf_op jit(solution)/shard_map/local_states/pallas_call | solution.py:122
  6.2 0.5 collective-permute-start
  6.7 1.7 %collective-permute-done.came_ref = f32[2,1,392,128]{3,2,1,0:T(8,128)} collective-permute-done((f32[2,1,392,128]{3,2,1,0:T(8,128)}, f32[2,1,392,128]{3,2,1,0:T(8,128)}, u32[]{:S(2)}, u32[]{:S(2)}) %collective-permute-start) | collective-permute-done | bytes 401440 | tf_op jit(solution)/shard_map/ppermute | solution.py:511
  8.4 1.9 %shard_map.86 = (f32[1,392,128]{2,1,0:T(8,128)}, f32[1,392,128]{2,1,0:T(8,128)}) custom-call(s32[3]{0:T(128)} %pad_add_fusion.place_ref.core_ref, f32[2,1,392,128]{3,2,1,0:T(8,128)} %get-tuple-element.40.own_ref, f32[2,1,392,128]{3,2,1,0:T(8,128)} %collective-permute-done.came_ref), custom_call_target="tpu_custom_call" | custom-call | bytes 1605632 | tf_op jit(solution)/shard_map/pallas_call | solution.py:168
  10.3 5.5 %collective-permute-start.4 = (f32[1,392,128]{2,1,0:T(8,128)}, f32[1,392,128]{2,1,0:T(8,128)}, u32[]{:S(2)}, u32[]{:S(2)}) collective-permute-start(f32[1,392,128]{2,1,0:T(8,128)} %get-tuple-element.45.later_ref), channel_id=1, source_target_pairs={{0,2},{1,3},{2,4},{3,5},{4,6},{5,7},{8,10},{9,11},{10,12},{11,13},... | collective-permute-start | bytes 602120 | tf_op jit(solution)/shard_map/ppermute | solution.py:526
  15.8 4.2 %collective-permute-done.4.earlier_ref.near_ref = f32[1,392,128]{2,1,0:T(8,128)} collective-permute-done((f32[1,392,128]{2,1,0:T(8,128)}, f32[1,392,128]{2,1,0:T(8,128)}, u32[]{:S(2)}, u32[]{:S(2)}) %collective-permute-start.4) | collective-permute-done | bytes 200736 | tf_op jit(solution)/shard_map/ppermute | solution.py:526
  20.0 1.7 %shard_map.89 = f32[1,392,128]{2,1,0:T(8,128)} custom-call(s32[3]{0:T(128)} %pad_add_fusion.place_ref.core_ref, f32[1,392,128]{2,1,0:T(8,128)} %collective-permute-done.4.earlier_ref.near_ref, f32[1,392,128]{2,1,0:T(8,128)} %get-tuple-element.45.later_ref), custom_call_target="tpu_custom_call" | custom-call | bytes 802816 | tf_op jit(solution)/shard_map/pallas_call | solution.py:168
  21.7 6.1 %collective-permute-start.5 = (f32[1,392,128]{2,1,0:T(8,128)}, f32[1,392,128]{2,1,0:T(8,128)}, u32[]{:S(2)}, u32[]{:S(2)}) collective-permute-start(f32[1,392,128]{2,1,0:T(8,128)} %shard_map.89), channel_id=1, source_target_pairs={{0,4},{1,5},{2,6},{3,7},{8,12},{9,13},{10,14},{11,15},{16,20},{17,... | collective-permute-start | bytes 602120 | tf_op jit(solution)/shard_map/ppermute | solution.py:526
  27.8 4.3 %pick_columns.1 = f32[4,512,256]{2,1,0:T(8,128)} custom-call(s32[3]{0:T(128)} %pad_add_fusion.place_ref.core_ref, bf16[512,2048]{1,0:T(8,128)(2,1)} %bitcast.12), custom_call_target="tpu_custom_call" | custom-call | bytes 3145728 | tf_op jit(solution)/shard_map/pick_columns/pallas_call | solution.py:346
  32.1 2.1 %shard_map.90 = (f32[1,392,128]{2,1,0:T(8,128)}, f32[1,392,128]{2,1,0:T(8,128)}) custom-call(s32[3]{0:T(128)} %pad_add_fusion.place_ref.core_ref, f32[1,392,128]{2,1,0:T(8,128)} %collective-permute-done.5.far_ref, f32[1,392,128]{2,1,0:T(8,128)} %collective-permute-done.4.earlier_ref.near_ref, f32[2,1,392,128]{3,2,1,0:T(8,128)} %get-tuple-element.40.own_ref, ...), custom_call_target="tpu_custom_call" | custom-call | bytes 2408448 | tf_op jit(solution)/shard_map/pallas_call | solution.py:168
  34.7 6.2 %convolution_convert_fusion.q_ref = bf16[512,1024]{1,0:T(8,128)(2,1)} fusion(bf16[2048,1024]{1,0:T(8,128)(2,1)} %param.8, bf16[1,512,2048]{2,1,0:T(8,128)(2,1)} %param.7), kind=kOutput, calls=%fused_computation | convolution fusion | flops 2148007936 | bytes 7340032 | tf_op jit(solution)/shard_map/dot_general | solution.py:536
  40.9 14.2 %solve_heads.2 = (bf16[512,1024]{1,0:T(8,128)(2,1)}, f32[4,128,512]{2,1,0:T(8,128)}) custom-call(s32[3]{0:T(128)} %pad_add_fusion.place_ref.core_ref, f32[8]{0:T(128)} %regular_ref.3, bf16[512,1024]{1,0:T(8,128)(2,1)} %convolution_convert_fusion.q_ref, bf16[512,1024]{1,0:T(8,128)(2,1)} %bitcast.16, bf16[512,1024]{1,0:T(8,128)(2,1)} %bitcast.19, ...), custom_call_target="tpu_custom_call" | custom-call | flops 2684354560 | bytes 3670016 | tf_op jit(solution)/shard_map/solve_heads/pallas_call | solution.py:318
  55.1 7.4 %collective-permute-start.1 = (f32[1,392,128]{2,1,0:T(8,128)}, f32[1,392,128]{2,1,0:T(8,128)}, u32[]{:S(2)}, u32[]{:S(2)}) collective-permute-start(f32[1,392,128]{2,1,0:T(8,128)} %get-tuple-element.42.later_ref), channel_id=1, source_target_pairs={{0,2},{1,3},{2,4},{3,5},{4,6},{5,7},{8,10},{9,11},{10,12},{11,13},... | collective-permute-start | bytes 602120 | tf_op jit(solution)/shard_map/ppermute | solution.py:526
  62.5 4.0 %collective-permute-done.1.earlier_ref.near_ref = f32[1,392,128]{2,1,0:T(8,128)} collective-permute-done((f32[1,392,128]{2,1,0:T(8,128)}, f32[1,392,128]{2,1,0:T(8,128)}, u32[]{:S(2)}, u32[]{:S(2)}) %collective-permute-start.1) | collective-permute-done | bytes 200736 | tf_op jit(solution)/shard_map/ppermute | solution.py:526
  66.5 1.7 %shard_map.87 = f32[1,392,128]{2,1,0:T(8,128)} custom-call(s32[3]{0:T(128)} %pad_add_fusion.place_ref.core_ref, f32[1,392,128]{2,1,0:T(8,128)} %collective-permute-done.1.earlier_ref.near_ref, f32[1,392,128]{2,1,0:T(8,128)} %get-tuple-element.42.later_ref), custom_call_target="tpu_custom_call" | custom-call | bytes 802816 | tf_op jit(solution)/shard_map/pallas_call | solution.py:168
  68.3 6.0 %collective-permute-start.2 = (f32[1,392,128]{2,1,0:T(8,128)}, f32[1,392,128]{2,1,0:T(8,128)}, u32[]{:S(2)}, u32[]{:S(2)}) collective-permute-start(f32[1,392,128]{2,1,0:T(8,128)} %shard_map.87), channel_id=1, source_target_pairs={{0,4},{1,5},{2,6},{3,7},{8,12},{9,13},{10,14},{11,15},{16,20},{17,... | collective-permute-start | bytes 602120 | tf_op jit(solution)/shard_map/ppermute | solution.py:526
  74.2 3.2 %collective-permute-done.2.far_ref = f32[1,392,128]{2,1,0:T(8,128)} collective-permute-done((f32[1,392,128]{2,1,0:T(8,128)}, f32[1,392,128]{2,1,0:T(8,128)}, u32[]{:S(2)}, u32[]{:S(2)}) %collective-permute-start.2) | collective-permute-done | bytes 200736 | tf_op jit(solution)/shard_map/ppermute | solution.py:526
  77.5 2.1 %shard_map.88 = (f32[1,392,128]{2,1,0:T(8,128)}, f32[1,392,128]{2,1,0:T(8,128)}) custom-call(s32[3]{0:T(128)} %pad_add_fusion.place_ref.core_ref, f32[1,392,128]{2,1,0:T(8,128)} %collective-permute-done.2.far_ref, f32[1,392,128]{2,1,0:T(8,128)} %collective-permute-done.1.earlier_ref.near_ref, f32[2,1,392,128]{3,2,1,0:T(8,128)} %get-tuple-element.40.own_ref, ...), custom_call_target="tpu_custom_call" | custom-call | bytes 2408448 | tf_op jit(solution)/shard_map/pallas_call | solution.py:168
  79.6 3.6 %narrow.1.other_ref = bf16[4,512,256]{2,1,0:T(8,128)(2,1)} custom-call(f32[4,512,256]{2,1,0:T(8,128)} %collective-permute-done.8.in_ref), custom_call_target="tpu_custom_call" | custom-call | bytes 3145728 | tf_op jit(solution)/shard_map/narrow/pallas_call | solution.py:367
  83.2 6.1 %gradient_blocks.2 = (f32[2,4,64,256]{3,2,1,0:T(8,128)}, f32[2,4,64,256]{3,2,1,0:T(8,128)}, f32[2,4,64,256]{3,2,1,0:T(8,128)}, f32[2,4,64,256]{3,2,1,0:T(8,128)}) custom-call(s32[3]{0:T(128)} %pad_add_fusion.place_ref.core_ref, f32[4,128,512]{2,1,0:T(8,128)} %get-tuple-element.49.own_ref, f32[4,128,512]{2,1,0:T(8,128)} %collective-permute-done.7.far_ref, ...), custom_call_target="tpu_custom_call" | custom-call | flops 1073741824 | bytes 6291456 | tf_op jit(solution)/shard_map/gradient_blocks/pallas_call | solution.py:410
  89.3 14.2 %solve_heads.3 = (bf16[512,1024]{1,0:T(8,128)(2,1)}, f32[4,128,512]{2,1,0:T(8,128)}) custom-call(s32[3]{0:T(128)} %pad_add_fusion.place_ref.core_ref, f32[8]{0:T(128)} %regular_ref.3, bf16[512,1024]{1,0:T(8,128)(2,1)} %convolution_convert_fusion.q_ref, bf16[512,1024]{1,0:T(8,128)(2,1)} %bitcast.17, ...), custom_call_target="tpu_custom_call", output_to_operand_aliasing={{0}: (9, {})} | custom-call | flops 2684354560 | bytes 3670016 | tf_op jit(solution)/shard_map/solve_heads/pallas_call | solution.py:318
  103.9 1.5 collective-permute-start.9
  105.4 1.5 collective-permute-start.11
  107.0 6.0 %gradient_blocks.3 = (f32[2,4,64,256]{3,2,1,0:T(8,128)}, f32[2,4,64,256]{3,2,1,0:T(8,128)}, f32[2,4,64,256]{3,2,1,0:T(8,128)}, f32[2,4,64,256]{3,2,1,0:T(8,128)}) custom-call(s32[3]{0:T(128)} %pad_add_fusion.place_ref.core_ref, f32[4,128,512]{2,1,0:T(8,128)} %get-tuple-element.63.own_ref, f32[4,128,512]{2,1,0:T(8,128)} %collective-permute-done.16.far_ref, ...), custom_call_target="tpu_custom_call" | custom-call | flops 1073741824 | bytes 6291456 | tf_op jit(solution)/shard_map/gradient_blocks/pallas_call | solution.py:410
  113.0 1.1 collective-permute-start.17
  114.1 1.5 collective-permute-start.19
  115.6 3.4 %collective-permute-done.9.came_ref = f32[2,4,64,256]{3,2,1,0:T(8,128)} collective-permute-done((f32[2,4,64,256]{3,2,1,0:T(8,128)}, f32[2,4,64,256]{3,2,1,0:T(8,128)}, u32[]{:S(2)}, u32[]{:S(2)}) %collective-permute-start.9) | collective-permute-done | bytes 524320 | tf_op jit(solution)/shard_map/ppermute | solution.py:558
  119.0 2.0 %sum_blocks.4 = (f32[1,4,64,256]{3,2,1,0:T(8,128)}, f32[1,4,64,256]{3,2,1,0:T(8,128)}) custom-call(f32[2,4,64,256]{3,2,1,0:T(8,128)} %get-tuple-element.50.rest_1_.keep_ref, f32[2,4,64,256]{3,2,1,0:T(8,128)} %collective-permute-done.9.came_ref), custom_call_target="tpu_custom_call" | custom-call | bytes 1572864 | tf_op jit(solution)/shard_map/sum_blocks/pallas_call | solution.py:444
  121.1 1.5 collective-permute-start.10
  122.6 2.0 %sum_blocks.5 = (f32[1,4,64,256]{3,2,1,0:T(8,128)}, f32[1,4,64,256]{3,2,1,0:T(8,128)}) custom-call(f32[2,4,64,256]{3,2,1,0:T(8,128)} %get-tuple-element.55.keep_ref, f32[2,4,64,256]{3,2,1,0:T(8,128)} %collective-permute-done.11.came_ref), custom_call_target="tpu_custom_call" | custom-call | bytes 1572864 | tf_op jit(solution)/shard_map/sum_blocks/pallas_call | solution.py:444
  124.7 1.5 collective-permute-start.12
  126.1 4.1 %collective-permute-done.17.came_ref = f32[2,4,64,256]{3,2,1,0:T(8,128)} collective-permute-done((f32[2,4,64,256]{3,2,1,0:T(8,128)}, f32[2,4,64,256]{3,2,1,0:T(8,128)}, u32[]{:S(2)}, u32[]{:S(2)}) %collective-permute-start.17) | collective-permute-done | bytes 524320 | tf_op jit(solution)/shard_map/ppermute | solution.py:558
  130.3 2.0 %sum_blocks.6 = (f32[1,4,64,256]{3,2,1,0:T(8,128)}, f32[1,4,64,256]{3,2,1,0:T(8,128)}) custom-call(f32[2,4,64,256]{3,2,1,0:T(8,128)} %get-tuple-element.64.keep_ref, f32[2,4,64,256]{3,2,1,0:T(8,128)} %collective-permute-done.17.came_ref), custom_call_target="tpu_custom_call" | custom-call | bytes 1572864 | tf_op jit(solution)/shard_map/sum_blocks/pallas_call | solution.py:444
  132.3 1.5 collective-permute-start.18
  133.8 2.0 %sum_blocks.7 = (f32[1,4,64,256]{3,2,1,0:T(8,128)}, f32[1,4,64,256]{3,2,1,0:T(8,128)}) custom-call(f32[2,4,64,256]{3,2,1,0:T(8,128)} %get-tuple-element.68.keep_ref, f32[2,4,64,256]{3,2,1,0:T(8,128)} %collective-permute-done.19.came_ref), custom_call_target="tpu_custom_call" | custom-call | bytes 1572864 | tf_op jit(solution)/shard_map/sum_blocks/pallas_call | solution.py:444
  135.9 1.5 collective-permute-start.20
  137.4 2.0 %merge_blocks.2 = (f32[128,256]{1,0:T(8,128)}, f32[128,256]{1,0:T(8,128)}, f32[128,256]{1,0:T(8,128)}, f32[128,256]{1,0:T(8,128)}) custom-call(f32[1,4,64,256]{3,2,1,0:T(8,128)} %get-tuple-element.53.refs_0_, f32[1,4,64,256]{3,2,1,0:T(8,128)} %collective-permute-done.10.refs_1_, f32[1,4,64,256]{3,2,1,0:T(8,128)} %get-tuple-element.57.refs_2_, ...), custom_call_target="tpu_custom_call" | custom-call | bytes 1572864 | tf_op jit(solution)/shard_map/merge_blocks/pallas_call | solution.py:468
  139.4 5.7 %collective-permute-start.13 = (f32[128,256]{1,0:T(8,128)}, f32[128,256]{1,0:T(8,128)}, u32[]{:S(2)}, u32[]{:S(2)}) collective-permute-start(f32[128,256]{1,0:T(8,128)} %get-tuple-element.60), channel_id=1, source_target_pairs={{0,2},{1,3},{2,0},{3,1},{4,6},{5,7},{6,4},{7,5},{8,10},{9,11},{10,... | collective-permute-start | bytes 393224 | tf_op jit(solution)/shard_map/ppermute | solution.py:566
  145.1 3.4 %collective-permute-start.14 = (f32[128,256]{1,0:T(8,128)}, f32[128,256]{1,0:T(8,128)}, u32[]{:S(2)}, u32[]{:S(2)}) collective-permute-start(f32[128,256]{1,0:T(8,128)} %get-tuple-element.61), channel_id=1, source_target_pairs={{0,4},{1,5},{2,6},{3,7},{4,0},{5,1},{6,2},{7,3},{8,12},{9,13},{10,... | collective-permute-start | bytes 393224 | tf_op jit(solution)/shard_map/ppermute | solution.py:566
  148.5 2.0 %merge_blocks.3 = (f32[128,256]{1,0:T(8,128)}, f32[128,256]{1,0:T(8,128)}, f32[128,256]{1,0:T(8,128)}, f32[128,256]{1,0:T(8,128)}) custom-call(f32[1,4,64,256]{3,2,1,0:T(8,128)} %get-tuple-element.66.refs_0_, f32[1,4,64,256]{3,2,1,0:T(8,128)} %collective-permute-done.18.refs_1_, f32[1,4,64,256]{3,2,1,0:T(8,128)} %get-tuple-element.70.refs_2_, ...), custom_call_target="tpu_custom_call" | custom-call | bytes 1572864 | tf_op jit(solution)/shard_map/merge_blocks/pallas_call | solution.py:468
  150.5 0.6 collective-permute-start.21
  151.1 3.8 %collective-permute-start.22 = (f32[128,256]{1,0:T(8,128)}, f32[128,256]{1,0:T(8,128)S(1)}, u32[]{:S(2)}, u32[]{:S(2)}) collective-permute-start(f32[128,256]{1,0:T(8,128)} %get-tuple-element.74), channel_id=1, source_target_pairs={{0,4},{1,5},{2,6},{3,7},{4,0},{5,1},{6,2},{7,3},{8,12},{9,13},{10,... | collective-permute-start | bytes 393224 | tf_op jit(solution)/shard_map/ppermute | solution.py:566
  154.9 3.8 %collective-permute-done.14 = f32[128,256]{1,0:T(8,128)} collective-permute-done((f32[128,256]{1,0:T(8,128)}, f32[128,256]{1,0:T(8,128)}, u32[]{:S(2)}, u32[]{:S(2)}) %collective-permute-start.14) | collective-permute-done | bytes 131104 | tf_op jit(solution)/shard_map/ppermute | solution.py:566
  158.7 1.1 add_add_fusion.1
  159.8 8.3 %collective-permute-done.22 = f32[128,256]{1,0:T(8,128)S(1)} collective-permute-done((f32[128,256]{1,0:T(8,128)}, f32[128,256]{1,0:T(8,128)S(1)}, u32[]{:S(2)}, u32[]{:S(2)}) %collective-permute-start.22) | collective-permute-done | bytes 131104 | tf_op jit(solution)/shard_map/ppermute | solution.py:566
  168.2 0.9 add_add_fusion
  169.1 0.7 pad_maximum_fusion
  (23 shorter events, 1.1 us)
Async XLA Ops:
  6.2 2.2 %collective-permute-start = (f32[2,1,392,128]{3,2,1,0:T(8,128)}, f32[2,1,392,128]{3,2,1,0:T(8,128)}, u32[]{:S(2)}, u32[]{:S(2)}) collective-permute-start(f32[2,1,392,128]{3,2,1,0:T(8,128)} %get-tuple-element.41), channel_id=1, source_target_pairs={{0,1},{1,0},{2,3},{3,2},{4,5},{5,4},{6,7},{7,6},{8,9},{9,8},{10,11... | collective-permute-start | bytes 1204232 | tf_op jit(solution)/shard_map/ppermute | solution.py:511
  10.3 9.7 %collective-permute-start.4 = (f32[1,392,128]{2,1,0:T(8,128)}, f32[1,392,128]{2,1,0:T(8,128)}, u32[]{:S(2)}, u32[]{:S(2)}) collective-permute-start(f32[1,392,128]{2,1,0:T(8,128)} %get-tuple-element.45.later_ref), channel_id=1, source_target_pairs={{0,2},{1,3},{2,4},{3,5},{4,6},{5,7},{8,10},{9,11},{10,12},{11,13},... | collective-permute-start | bytes 602120 | tf_op jit(solution)/shard_map/ppermute | solution.py:526
  21.7 10.4 %collective-permute-start.5 = (f32[1,392,128]{2,1,0:T(8,128)}, f32[1,392,128]{2,1,0:T(8,128)}, u32[]{:S(2)}, u32[]{:S(2)}) collective-permute-start(f32[1,392,128]{2,1,0:T(8,128)} %shard_map.89), channel_id=1, source_target_pairs={{0,4},{1,5},{2,6},{3,7},{8,12},{9,13},{10,14},{11,15},{16,20},{17,... | collective-permute-start | bytes 602120 | tf_op jit(solution)/shard_map/ppermute | solution.py:526
  32.1 47.5 %collective-permute-start.8 = (f32[4,512,256]{2,1,0:T(8,128)}, f32[4,512,256]{2,1,0:T(8,128)}, u32[]{:S(2)}, u32[]{:S(2)}) collective-permute-start(f32[4,512,256]{2,1,0:T(8,128)} %pick_columns.1), channel_id=1, source_target_pairs={{0,1},{1,0},{2,3},{3,2},{4,5},{5,4},{6,7},{7,6},{8,9},{9,8},{10,11... | collective-permute-start | bytes 6291464 | tf_op jit(solution)/shard_map/ppermute | solution.py:534
  34.2 6.7 %collective-permute-start.6 = (f32[1,392,128]{2,1,0:T(8,128)}, f32[1,392,128]{2,1,0:T(8,128)}, u32[]{:S(2)}, u32[]{:S(2)}) collective-permute-start(f32[1,392,128]{2,1,0:T(8,128)} %get-tuple-element.47), channel_id=1, source_target_pairs={{0,1},{1,0},{2,3},{3,2},{4,5},{5,4},{6,7},{7,6},{8,9},{9,8},{10,11... | collective-permute-start | bytes 602120 | tf_op jit(solution)/shard_map/ppermute | solution.py:531
  55.1 28.1 %collective-permute-start.7 = (f32[4,128,512]{2,1,0:T(8,128)}, f32[4,128,512]{2,1,0:T(8,128)}, u32[]{:S(2)}, u32[]{:S(2)}) collective-permute-start(f32[4,128,512]{2,1,0:T(8,128)} %get-tuple-element.49.own_ref), channel_id=1, source_target_pairs={{0,1},{1,0},{2,3},{3,2},{4,5},{5,4},{6,7},{7,6},{8,9},{9,8},{10,11... | collective-permute-start | bytes 3145736 | tf_op jit(solution)/shard_map/ppermute | solution.py:548
  55.1 11.4 %collective-permute-start.1 = (f32[1,392,128]{2,1,0:T(8,128)}, f32[1,392,128]{2,1,0:T(8,128)}, u32[]{:S(2)}, u32[]{:S(2)}) collective-permute-start(f32[1,392,128]{2,1,0:T(8,128)} %get-tuple-element.42.later_ref), channel_id=1, source_target_pairs={{0,2},{1,3},{2,4},{3,5},{4,6},{5,7},{8,10},{9,11},{10,12},{11,13},... | collective-permute-start | bytes 602120 | tf_op jit(solution)/shard_map/ppermute | solution.py:526
  68.3 9.2 %collective-permute-start.2 = (f32[1,392,128]{2,1,0:T(8,128)}, f32[1,392,128]{2,1,0:T(8,128)}, u32[]{:S(2)}, u32[]{:S(2)}) collective-permute-start(f32[1,392,128]{2,1,0:T(8,128)} %shard_map.87), channel_id=1, source_target_pairs={{0,4},{1,5},{2,6},{3,7},{8,12},{9,13},{10,14},{11,15},{16,20},{17,... | collective-permute-start | bytes 602120 | tf_op jit(solution)/shard_map/ppermute | solution.py:526
  79.6 9.6 %collective-permute-start.3 = (f32[1,392,128]{2,1,0:T(8,128)}, f32[1,392,128]{2,1,0:T(8,128)}, u32[]{:S(2)}, u32[]{:S(2)}) collective-permute-start(f32[1,392,128]{2,1,0:T(8,128)} %get-tuple-element.44), channel_id=1, source_target_pairs={{0,1},{1,0},{2,3},{3,2},{4,5},{5,4},{6,7},{7,6},{8,9},{9,8},{10,11... | collective-permute-start | bytes 602120 | tf_op jit(solution)/shard_map/ppermute | solution.py:531
  103.4 3.5 %collective-permute-start.16 = (f32[4,128,512]{2,1,0:T(8,128)}, f32[4,128,512]{2,1,0:T(8,128)}, u32[]{:S(2)}, u32[]{:S(2)}) collective-permute-start(f32[4,128,512]{2,1,0:T(8,128)} %get-tuple-element.63.own_ref), channel_id=1, source_target_pairs={{0,1},{1,0},{2,3},{3,2},{4,5},{5,4},{6,7},{7,6},{8,9},{9,8},{10,11... | collective-permute-start | bytes 3145736 | tf_op jit(solution)/shard_map/ppermute | solution.py:548
  103.9 15.1 %collective-permute-start.9 = (f32[2,4,64,256]{3,2,1,0:T(8,128)}, f32[2,4,64,256]{3,2,1,0:T(8,128)}, u32[]{:S(2)}, u32[]{:S(2)}) collective-permute-start(f32[2,4,64,256]{3,2,1,0:T(8,128)} %get-tuple-element.52), channel_id=1, source_target_pairs={{0,8},{8,0},{16,24},{24,16},{1,9},{9,1},{17,25},{25,17},{2,10},{10... | collective-permute-start | bytes 1572872 | tf_op jit(solution)/shard_map/ppermute | solution.py:558
  105.4 17.2 %collective-permute-start.11 = (f32[2,4,64,256]{3,2,1,0:T(8,128)}, f32[2,4,64,256]{3,2,1,0:T(8,128)}, u32[]{:S(2)}, u32[]{:S(2)}) collective-permute-start(f32[2,4,64,256]{3,2,1,0:T(8,128)} %get-tuple-element.56), channel_id=1, source_target_pairs={{0,16},{8,24},{16,0},{24,8},{1,17},{9,25},{17,1},{25,9},{2,18},{10... | collective-permute-start | bytes 1572872 | tf_op jit(solution)/shard_map/ppermute | solution.py:558
  113.0 17.3 %collective-permute-start.17 = (f32[2,4,64,256]{3,2,1,0:T(8,128)}, f32[2,4,64,256]{3,2,1,0:T(8,128)}, u32[]{:S(2)}, u32[]{:S(2)}) collective-permute-start(f32[2,4,64,256]{3,2,1,0:T(8,128)} %get-tuple-element.65), channel_id=1, source_target_pairs={{0,8},{8,0},{16,24},{24,16},{1,9},{9,1},{17,25},{25,17},{2,10},{10... | collective-permute-start | bytes 1572872 | tf_op jit(solution)/shard_map/ppermute | solution.py:558
  114.1 19.7 %collective-permute-start.19 = (f32[2,4,64,256]{3,2,1,0:T(8,128)}, f32[2,4,64,256]{3,2,1,0:T(8,128)}, u32[]{:S(2)}, u32[]{:S(2)}) collective-permute-start(f32[2,4,64,256]{3,2,1,0:T(8,128)} %get-tuple-element.69), channel_id=1, source_target_pairs={{0,16},{8,24},{16,0},{24,8},{1,17},{9,25},{17,1},{25,9},{2,18},{10... | collective-permute-start | bytes 1572872 | tf_op jit(solution)/shard_map/ppermute | solution.py:558
  121.1 16.3 %collective-permute-start.10 = (f32[1,4,64,256]{3,2,1,0:T(8,128)}, f32[1,4,64,256]{3,2,1,0:T(8,128)}, u32[]{:S(2)}, u32[]{:S(2)}) collective-permute-start(f32[1,4,64,256]{3,2,1,0:T(8,128)} %get-tuple-element.54), channel_id=1, source_target_pairs={{0,16},{8,24},{16,0},{24,8},{1,17},{9,25},{17,1},{25,9},{2,18},{10... | collective-permute-start | bytes 786440 | tf_op jit(solution)/shard_map/ppermute | solution.py:558
  124.7 12.7 %collective-permute-start.12 = (f32[1,4,64,256]{3,2,1,0:T(8,128)}, f32[1,4,64,256]{3,2,1,0:T(8,128)}, u32[]{:S(2)}, u32[]{:S(2)}) collective-permute-start(f32[1,4,64,256]{3,2,1,0:T(8,128)} %get-tuple-element.58), channel_id=1, source_target_pairs={{0,8},{8,0},{16,24},{24,16},{1,9},{9,1},{17,25},{25,17},{2,10},{10... | collective-permute-start | bytes 786440 | tf_op jit(solution)/shard_map/ppermute | solution.py:558
  132.3 16.2 %collective-permute-start.18 = (f32[1,4,64,256]{3,2,1,0:T(8,128)}, f32[1,4,64,256]{3,2,1,0:T(8,128)}, u32[]{:S(2)}, u32[]{:S(2)}) collective-permute-start(f32[1,4,64,256]{3,2,1,0:T(8,128)} %get-tuple-element.67), channel_id=1, source_target_pairs={{0,16},{8,24},{16,0},{24,8},{1,17},{9,25},{17,1},{25,9},{2,18},{10... | collective-permute-start | bytes 786440 | tf_op jit(solution)/shard_map/ppermute | solution.py:558
  135.9 12.6 %collective-permute-start.20 = (f32[1,4,64,256]{3,2,1,0:T(8,128)}, f32[1,4,64,256]{3,2,1,0:T(8,128)}, u32[]{:S(2)}, u32[]{:S(2)}) collective-permute-start(f32[1,4,64,256]{3,2,1,0:T(8,128)} %get-tuple-element.71), channel_id=1, source_target_pairs={{0,8},{8,0},{16,24},{24,16},{1,9},{9,1},{17,25},{25,17},{2,10},{10... | collective-permute-start | bytes 786440 | tf_op jit(solution)/shard_map/ppermute | solution.py:558
  139.4 15.5 %collective-permute-start.13 = (f32[128,256]{1,0:T(8,128)}, f32[128,256]{1,0:T(8,128)}, u32[]{:S(2)}, u32[]{:S(2)}) collective-permute-start(f32[128,256]{1,0:T(8,128)} %get-tuple-element.60), channel_id=1, source_target_pairs={{0,2},{1,3},{2,0},{3,1},{4,6},{5,7},{6,4},{7,5},{8,10},{9,11},{10,... | collective-permute-start | bytes 393224 | tf_op jit(solution)/shard_map/ppermute | solution.py:566
  145.1 13.6 %collective-permute-start.14 = (f32[128,256]{1,0:T(8,128)}, f32[128,256]{1,0:T(8,128)}, u32[]{:S(2)}, u32[]{:S(2)}) collective-permute-start(f32[128,256]{1,0:T(8,128)} %get-tuple-element.61), channel_id=1, source_target_pairs={{0,4},{1,5},{2,6},{3,7},{4,0},{5,1},{6,2},{7,3},{8,12},{9,13},{10,... | collective-permute-start | bytes 393224 | tf_op jit(solution)/shard_map/ppermute | solution.py:566
  148.5 10.2 %collective-permute-start.15 = (f32[128,256]{1,0:T(8,128)}, f32[128,256]{1,0:T(8,128)}, u32[]{:S(2)}, u32[]{:S(2)}) collective-permute-start(f32[128,256]{1,0:T(8,128)} %get-tuple-element.62), channel_id=1, source_target_pairs={{0,6},{1,7},{2,4},{3,5},{4,2},{5,3},{6,0},{7,1},{8,14},{9,15},{10,... | collective-permute-start | bytes 393224 | tf_op jit(solution)/shard_map/ppermute | solution.py:566
  150.5 9.3 %collective-permute-start.21 = (f32[128,256]{1,0:T(8,128)}, f32[128,256]{1,0:T(8,128)S(1)}, u32[]{:S(2)}, u32[]{:S(2)}) collective-permute-start(f32[128,256]{1,0:T(8,128)} %get-tuple-element.73), channel_id=1, source_target_pairs={{0,2},{1,3},{2,0},{3,1},{4,6},{5,7},{6,4},{7,5},{8,10},{9,11},{10,... | collective-permute-start | bytes 393224 | tf_op jit(solution)/shard_map/ppermute | solution.py:566
  151.1 17.1 %collective-permute-start.22 = (f32[128,256]{1,0:T(8,128)}, f32[128,256]{1,0:T(8,128)S(1)}, u32[]{:S(2)}, u32[]{:S(2)}) collective-permute-start(f32[128,256]{1,0:T(8,128)} %get-tuple-element.74), channel_id=1, source_target_pairs={{0,4},{1,5},{2,6},{3,7},{4,0},{5,1},{6,2},{7,3},{8,12},{9,13},{10,... | collective-permute-start | bytes 393224 | tf_op jit(solution)/shard_map/ppermute | solution.py:566
  154.9 13.3 %collective-permute-start.23 = (f32[128,256]{1,0:T(8,128)}, f32[128,256]{1,0:T(8,128)S(1)}, u32[]{:S(2)}, u32[]{:S(2)}) collective-permute-start(f32[128,256]{1,0:T(8,128)} %get-tuple-element.75), channel_id=1, source_target_pairs={{0,6},{1,7},{2,4},{3,5},{4,2},{5,3},{6,0},{7,1},{8,14},{9,15},{10,... | collective-permute-start | bytes 393224 | tf_op jit(solution)/shard_map/ppermute | solution.py:566

commit v6 on v5

--- a/solution.py
+++ b/solution.py
@@ -178,11 +178,15 @@
     )(place, *arrays)
 
 
-def solve_kernel(
-    half, head_of, place_ref, regular_ref, q_ref, k_ref, v_ref, g_ref, rows_ref, mine_ref, other_ref, *rest
-):
-    mixed_ref, turned_ref = rest[-2:]
-    rows, dim = q_ref.shape
+def solve_kernel(with_query, with_gradient, bounds, head_of, place_ref, regular_ref, *refs):
+    refs = list(refs)
+    q_ref = refs.pop(0) if with_query else None
+    g_ref = refs.pop(0) if with_gradient else None
+    k_ref, v_ref, rows_ref = refs[:3]
+    state_refs, refs = refs[3 : 3 + len(bounds)], refs[3 + len(bounds) :]
+    turned_ref = refs.pop() if with_gradient else None
+    mixed_ref = refs.pop() if with_query else None
+    rows, dim = k_ref.shape
     pieces = range(rows // SUB)
     place = [slice(c * SUB, (c + 1) * SUB) for c in pieces]
     step = pl.program_id(0)
@@ -193,11 +197,12 @@
     lower = row_at >= column_at
 
     is_second = lax.rem(step, 2) == 1
-    is_mine = step < half
 
     def state(start, size):
         at = pl.ds(start, size)
-        return jnp.where(is_mine, mine_ref[0, at, :], other_ref[0, at, :])
+        if len(state_refs) == 1:
+            return state_refs[0][0, at, :]
+        return jnp.where(step < bounds[1], state_refs[0][0, at, :], state_refs[1][0, at, :])
 
     packed = state(0, dim)
     direct = (row_at > column_at) == is_second
@@ -251,33 +256,41 @@
     def pair(left, right):
         return jnp.concatenate([left, right], axis=0)
 
+    def each(value):
+        return pair(value, value) if with_query and with_gradient else value
+
     residual = []
     for c in pieces:
-        grad = g_ref[place[c], :]
-        pulled = scale[c] * dot(jnp.concatenate([grad, grad], axis=1), wide(memory[c], 0))
-        score = weights[c] * dot(grad, values_turned[c])
-        pulled = pulled + dot(wide(score), pair(keys[c], keys[c]))
-        residual.append(pair(q_ref[place[c], :].astype(F32), pulled))
+        sides = []
+        if with_query:
+            sides.append(q_ref[place[c], :].astype(F32))
+        if with_gradient:
+            grad = g_ref[place[c], :]
+            pulled = scale[c] * dot(jnp.concatenate([grad, grad], axis=1), wide(memory[c], 0))
+            score = weights[c] * dot(grad, values_turned[c])
+            sides.append(pulled + dot(wide(score), pair(keys[c], keys[c])))
+        residual.append(jnp.concatenate(sides, axis=0) if len(sides) > 1 else sides[0])
 
     alpha = column(0)
-    change = [pair(alpha[c], alpha[c]) * residual[c] for c in pieces]
+    change = [each(alpha[c]) * residual[c] for c in pieces]
     solution = list(change)
     rights = [jnp.concatenate([keys_turned[c], gram[c].astype(BF16)], axis=1) for c in pieces]
     for i in range(1, ITERS):
         alpha, gamma = column(i), column(ITERS + i - 1)
         first = [dot(change[c].astype(BF16), rights[c]) for c in pieces]
         second = [
-            dot((first[c][:, 0:SUB] * pair(weights[c], weights[c])).astype(BF16), keys[c]) for c in pieces
+            dot((first[c][:, 0:SUB] * each(weights[c])).astype(BF16), keys[c]) for c in pieces
         ]
         for c in pieces:
-            applied = ridge * change[c] + (pair(scale[c], scale[c]) * first[c][:, SUB:] + second[c])
+            applied = ridge * change[c] + (each(scale[c]) * first[c][:, SUB:] + second[c])
             residual[c] = residual[c] - applied
-            change[c] = pair(alpha[c], alpha[c]) * residual[c] + pair(gamma[c], gamma[c]) * change[c]
+            change[c] = each(alpha[c]) * residual[c] + each(gamma[c]) * change[c]
             solution[c] = solution[c] + change[c]
 
-    for c in pieces:
-        turned_ref[0, :, place[c]] = solution[c][SUB:].T.astype(BF16).astype(F32)
-    for c in pieces:
+    if with_gradient:
+        for c in pieces:
+            turned_ref[0, :, place[c]] = solution[c][-SUB:].T.astype(BF16).astype(F32)
+    for c in pieces if with_query else ():
         high, low = split(solution[c][0:SUB])
         memory_high, memory_low = split(memory[c].T)
         right = jnp.concatenate([keys_turned[c], memory_high], axis=1)
@@ -288,44 +301,53 @@
         mixed_ref[place[c], :] = output.astype(BF16)
 
 
-def solve_heads(place, k, per, regular, queries, keys, values, grads, table, mine, other, mixed, after):
+def solve_heads(place, k, base, per, regular, queries, grads, keys, values, table, states, mixed, after):
     rows, columns = keys.shape
     heads = regular.shape[0]
     dim = columns // heads
-    half = 2 * mine.shape[0]
-    count = 2 * half
+    half = 2 * states[0].shape[0]
+    groups, count = heads // per, half * len(states)
+    with_query, with_gradient = queries is not None, grads is not None
+    bounds = [half * i for i in range(len(states))]
 
     def head_of(step, place_ref):
-        return lax.rem(place_ref[0] * half + step, count) * per + k
+        return lax.rem(place_ref[0] * half + base + step, groups) * per + k
 
     def at_head(step, place_ref, regular_ref):
         return (0, head_of(step, place_ref))
 
     wide_spec = pl.BlockSpec((rows, dim), at_head)
-    operands = [queries, keys, values, grads, table, mine, other]
-    in_specs = [wide_spec] * 4 + [pl.BlockSpec(table.shape, lambda step, *_: (0, 0, 0))]
-    pair = (1,) + mine.shape[1:]
-    in_specs.append(pl.BlockSpec(pair, lambda step, *_: (jnp.minimum(step, half - 1) // 2, 0, 0)))
-    in_specs.append(pl.BlockSpec(pair, lambda step, *_: (jnp.maximum(step - half, 0) // 2, 0, 0)))
+    operands = [a for a in (queries, grads, keys, values) if a is not None]
+    in_specs = [wide_spec] * len(operands)
+    operands.append(table)
+    in_specs.append(whole(table))
+    for bound, state in zip(bounds, states):
+
+        def at_pair(step, *_, bound=bound):
+            return (jnp.clip(step - bound, 0, half - 1) // 2, 0, 0)
+
+        operands.append(state)
+        in_specs.append(pl.BlockSpec((1,) + state.shape[1:], at_pair))
     aliases = {}
-    if mixed is not None:
+    if with_query and mixed is not None:
         operands.append(mixed)
         in_specs.append(pl.BlockSpec(memory_space=pl.ANY))
         aliases = {2 + len(operands) - 1: 0}
     if after is not None:
         operands.append(after)
         in_specs.append(pl.BlockSpec(memory_space=pl.ANY))
-    return pl.pallas_call(
-        functools.partial(solve_kernel, half, head_of),
-        out_shape=[
-            jax.ShapeDtypeStruct((rows, columns), BF16),
-            jax.ShapeDtypeStruct((count, dim, rows), F32),
-        ],
+    shapes, out_specs = [], []
+    if with_query:
+        shapes.append(jax.ShapeDtypeStruct((rows, columns), BF16))
+        out_specs.append(wide_spec)
+    if with_gradient:
+        shapes.append(jax.ShapeDtypeStruct((count, dim, rows), F32))
+        out_specs.append(pl.BlockSpec((1, dim, rows), lambda step, *_: (step, 0, 0)))
+    return pl.pallas_call(
+        functools.partial(solve_kernel, with_query, with_gradient, bounds, head_of),
+        out_shape=shapes,
         grid_spec=pltpu.PrefetchScalarGridSpec(
-            num_scalar_prefetch=2,
-            grid=(count,),
-            in_specs=in_specs,
-            out_specs=[wide_spec, pl.BlockSpec((1, dim, rows), lambda step, *_: (step, 0, 0))],
+            num_scalar_prefetch=2, grid=(count,), in_specs=in_specs, out_specs=out_specs
         ),
         input_output_aliases=aliases,
         cost_estimate=pl.CostEstimate(
@@ -477,6 +499,34 @@
         ),
         name="merge_blocks",
     )(*sums)
+
+
+def finish_kernel(count, *refs):
+    out = refs[-1]
+    rows = refs[0].shape[0]
+    for k in range((len(refs) - 1) // count):
+        total = refs[k * count][...]
+        for ref in refs[k * count + 1 : (k + 1) * count]:
+            total = total + ref[...]
+        out[k * rows : (k + 1) * rows, :] = total
+
+
+def finish(sets):
+    arrays = [a for group in sets for a in group]
+    rows, size = arrays[0].shape
+    out = jax.ShapeDtypeStruct((rows * len(sets), size), F32)
+    return pl.pallas_call(
+        functools.partial(finish_kernel, len(sets[0])),
+        out_shape=out,
+        in_specs=[whole(a) for a in arrays],
+        out_specs=whole(out),
+        grid=(1,),
+        compiler_params=FULL,
+        cost_estimate=pl.CostEstimate(
+            flops=0, bytes_accessed=5 * sum(a.size for a in arrays), transcendentals=0
+        ),
+        name="finish",
+    )(*arrays)
 
 
 def bit_order(bits):
@@ -540,13 +590,23 @@
     order = [bit_order(path) for path in paths]
 
     products, mixed = [], None
-    for k, (mine, others) in enumerate(starts):
+    for k, states in enumerate(starts):
         after = products[-1][0] if k > 0 else None
-        mixed, turned = solve_heads(
-            place, k, per, regular, queries, keys, values, grads, table, mine, others, mixed, after
+        joint = k < per - 1
+        results = solve_heads(
+            place, k, 0, per, regular, queries if joint else None, grads, keys, values, table, states, mixed, after
         )
+        turned = results[-1]
+        if joint:
+            mixed = results[0]
         far = lax.ppermute(turned, "seq", partner)
         products.append(gradient_blocks(place, turned, far, tokens, other, order))
+    for side in range(2):
+        after = products[-1][0] if side == 0 else None
+        (mixed,) = solve_heads(
+            place, per - 1, side * half, per, regular, queries, None, keys, values, table,
+            [starts[-1][side]], mixed, after,
+        )
 
     finished = []
     for blocks in products:
@@ -561,11 +621,11 @@
                 else:
                     keep, send = sum_blocks(keep, came)
         out, *others = merge_blocks(sums)
+        finished.append([out])
         for z, other_block in enumerate(others, 1):
             pairs = [(i, i ^ (2 * z)) for i in range(steps)]
-            out = out + lax.ppermute(other_block, "seq", pairs)
-        finished.append(out)
-    return mixed[None], jnp.concatenate(finished, axis=0)
+            finished[-1].append(lax.ppermute(other_block, "seq", pairs))
+    return mixed[None], finish(finished)
 
 
 def solution(mesh):

time: 171 us -> 169 us (0.988)
  Pallas kernels: 75 us -> 87.3 us
  waiting for transfers between devices: 32.9 us -> 21.4 us
  other arithmetic: 3.45 us -> 0.56 us
    pallas_call x2 -> x5, Pallas kernels: 28.4 us -> 40.5 us  [the longest x4 38.5 us: solve_heads(): pl.pallas_call(functools.partial(solve_kernel, with_query, with_gradient,...]
    ppermute x6, waiting for transfers between devices: 12.1 us -> 0.6 us  [program(): finished[-1].append(lax.ppermute(other_block, 'seq', pairs))]
    add x2 -> x0, other arithmetic: 2.07 us -> none  [program(): out = out + lax.ppermute(other_block, 'seq', pairs)]
  transfers between devices with their start and end apart: 24 -> 24, of which waited for: 8 -> 7; matrix products, arithmetic and copies ran while one was open for 4% -> 4% of each run, Pallas kernels for 31% -> 39%
where the time goes in v6:
time: 169 us; the launch traced here: 168 us
  Pallas kernels  87.3 us (52%)
  starting transfers between devices  51.6 us (31%)
  waiting for transfers between devices  21.4 us (13%)
  matrix products  6.18 us (4%)
    pallas_call x4, Pallas kernels, solve_heads(): pl.pallas_call(functools.partial(solve_kernel, with_query, with_gradient,...  38.5 us
    ppermute x4, starting transfers between devices, program(): came_up = lax.ppermute(sent, 'seq', pairs)  24.9 us
    ppermute x6, starting transfers between devices, program(): finished[-1].append(lax.ppermute(other_block, 'seq', pairs))  13.5 us
    pallas_call x2, Pallas kernels, gradient_blocks(): pl.pallas_call(functools.partial(gradient_kernel, order), out_shape=[out]...  12.2 us
    ppermute x8, starting transfers between devices, program(): came = lax.ppermute(send, 'dp', pairs)  11.6 us
    ppermute x4, waiting for transfers between devices, program(): came_up = lax.ppermute(sent, 'seq', pairs)  11.5 us
    pallas_call x5, Pallas kernels, combine(): pl.pallas_call(kernel, out_shape=[out] * outs, in_specs=[pl.BlockSpec(mem...  9.67 us
    pallas_call x4, Pallas kernels, sum_blocks(): pl.pallas_call(sum_kernel, out_shape=[out] * 2, in_specs=[whole(keep)] *...  8.12 us
  transfers between devices with their start and end apart: 24, of which 7 were waited for; matrix products, arithmetic and copies ran while one was open for 4% of the time, Pallas kernels for 39%

profile of v6, /device:TPU:0, one launch (start us, length us, event | category | flops | bytes accessed | tf_op | source)
XLA Modules:
  0.0 167.7 jit_solution(7680157784051757668)
XLA Ops:
  0.6 0.6 pad_add_fusion.place_ref.core_ref
  1.2 4.9 %local_states.1 = (f32[2,1,392,128]{3,2,1,0:T(8,128)}, f32[2,1,392,128]{3,2,1,0:T(8,128)}, f32[2,8,512]{2,1,0:T(8,128)}) custom-call(s32[3]{0:T(128)} %pad_add_fusion.place_ref.core_ref, bf16[512,1024]{1,0:T(8,128)(2,1)} %bitcast.15, bf16[512,1024]{1,0:T(8,128)(2,1)} %bitcast.20, f32[8,512]{1,0:T(8,128)} %bitcast.26), custom_call_target="tpu_custom_call" | custom-call | flops 536870912 | bytes 4194304 | tf_op jit(solution)/shard_map/local_states/pallas_call | solution.py:122
  6.1 0.5 collective-permute-start
  6.6 1.7 %collective-permute-done.came_ref = f32[2,1,392,128]{3,2,1,0:T(8,128)} collective-permute-done((f32[2,1,392,128]{3,2,1,0:T(8,128)}, f32[2,1,392,128]{3,2,1,0:T(8,128)}, u32[]{:S(2)}, u32[]{:S(2)}) %collective-permute-start) | collective-permute-done | bytes 401440 | tf_op jit(solution)/shard_map/ppermute | solution.py:561
  8.3 1.9 %shard_map.86 = (f32[1,392,128]{2,1,0:T(8,128)}, f32[1,392,128]{2,1,0:T(8,128)}) custom-call(s32[3]{0:T(128)} %pad_add_fusion.place_ref.core_ref, f32[2,1,392,128]{3,2,1,0:T(8,128)} %get-tuple-element.38.own_ref, f32[2,1,392,128]{3,2,1,0:T(8,128)} %collective-permute-done.came_ref), custom_call_target="tpu_custom_call" | custom-call | bytes 1605632 | tf_op jit(solution)/shard_map/pallas_call | solution.py:168
  10.2 5.5 %collective-permute-start.4 = (f32[1,392,128]{2,1,0:T(8,128)}, f32[1,392,128]{2,1,0:T(8,128)}, u32[]{:S(2)}, u32[]{:S(2)}) collective-permute-start(f32[1,392,128]{2,1,0:T(8,128)} %get-tuple-element.43.later_ref), channel_id=1, source_target_pairs={{0,2},{1,3},{2,4},{3,5},{4,6},{5,7},{8,10},{9,11},{10,12},{11,13},... | collective-permute-start | bytes 602120 | tf_op jit(solution)/shard_map/ppermute | solution.py:576
  15.7 4.2 %collective-permute-done.4.earlier_ref.near_ref = f32[1,392,128]{2,1,0:T(8,128)} collective-permute-done((f32[1,392,128]{2,1,0:T(8,128)}, f32[1,392,128]{2,1,0:T(8,128)}, u32[]{:S(2)}, u32[]{:S(2)}) %collective-permute-start.4) | collective-permute-done | bytes 200736 | tf_op jit(solution)/shard_map/ppermute | solution.py:576
  19.9 1.7 %shard_map.89 = f32[1,392,128]{2,1,0:T(8,128)} custom-call(s32[3]{0:T(128)} %pad_add_fusion.place_ref.core_ref, f32[1,392,128]{2,1,0:T(8,128)} %collective-permute-done.4.earlier_ref.near_ref, f32[1,392,128]{2,1,0:T(8,128)} %get-tuple-element.43.later_ref), custom_call_target="tpu_custom_call" | custom-call | bytes 802816 | tf_op jit(solution)/shard_map/pallas_call | solution.py:168
  21.6 6.1 %collective-permute-start.5 = (f32[1,392,128]{2,1,0:T(8,128)}, f32[1,392,128]{2,1,0:T(8,128)}, u32[]{:S(2)}, u32[]{:S(2)}) collective-permute-start(f32[1,392,128]{2,1,0:T(8,128)} %shard_map.89), channel_id=1, source_target_pairs={{0,4},{1,5},{2,6},{3,7},{8,12},{9,13},{10,14},{11,15},{16,20},{17,... | collective-permute-start | bytes 602120 | tf_op jit(solution)/shard_map/ppermute | solution.py:576
  27.7 4.3 %pick_columns.1 = f32[4,512,256]{2,1,0:T(8,128)} custom-call(s32[3]{0:T(128)} %pad_add_fusion.place_ref.core_ref, bf16[512,2048]{1,0:T(8,128)(2,1)} %bitcast.12), custom_call_target="tpu_custom_call" | custom-call | bytes 3145728 | tf_op jit(solution)/shard_map/pick_columns/pallas_call | solution.py:368
  32.0 2.1 %shard_map.90 = (f32[1,392,128]{2,1,0:T(8,128)}, f32[1,392,128]{2,1,0:T(8,128)}) custom-call(s32[3]{0:T(128)} %pad_add_fusion.place_ref.core_ref, f32[1,392,128]{2,1,0:T(8,128)} %collective-permute-done.5.far_ref, f32[1,392,128]{2,1,0:T(8,128)} %collective-permute-done.4.earlier_ref.near_ref, f32[2,1,392,128]{3,2,1,0:T(8,128)} %get-tuple-element.38.own_ref, ...), custom_call_target="tpu_custom_call" | custom-call | bytes 2408448 | tf_op jit(solution)/shard_map/pallas_call | solution.py:168
  34.1 0.5 collective-permute-start.6
  34.6 6.2 %convolution_convert_fusion.refs_0_ = bf16[512,1024]{1,0:T(8,128)(2,1)} fusion(bf16[2048,1024]{1,0:T(8,128)(2,1)} %param.8, bf16[1,512,2048]{2,1,0:T(8,128)(2,1)} %param.7), kind=kOutput, calls=%fused_computation | convolution fusion | flops 2148007936 | bytes 7340032 | tf_op jit(solution)/shard_map/dot_general | solution.py:586
  40.8 14.2 %solve_heads.4 = (bf16[512,1024]{1,0:T(8,128)(2,1)}, f32[4,128,512]{2,1,0:T(8,128)}) custom-call(s32[3]{0:T(128)} %pad_add_fusion.place_ref.core_ref, f32[8]{0:T(128)} %regular_ref.7, bf16[512,1024]{1,0:T(8,128)(2,1)} %convolution_convert_fusion.refs_0_, bf16[512,1024]{1,0:T(8,128)(2,1)} %bitcast.27, bf16[512,1024]{1,0:T(8,128)(2,1)} %bitcast.16, ...), custom_call_target="tpu_custom_call" | custom-call | flops 2684354560 | bytes 3670016 | tf_op jit(solution)/shard_map/solve_heads/pallas_call | solution.py:346
  55.0 7.4 %collective-permute-start.1 = (f32[1,392,128]{2,1,0:T(8,128)}, f32[1,392,128]{2,1,0:T(8,128)}, u32[]{:S(2)}, u32[]{:S(2)}) collective-permute-start(f32[1,392,128]{2,1,0:T(8,128)} %get-tuple-element.40.later_ref), channel_id=1, source_target_pairs={{0,2},{1,3},{2,4},{3,5},{4,6},{5,7},{8,10},{9,11},{10,12},{11,13},... | collective-permute-start | bytes 602120 | tf_op jit(solution)/shard_map/ppermute | solution.py:576
  62.4 4.1 %collective-permute-done.1.earlier_ref.near_ref = f32[1,392,128]{2,1,0:T(8,128)} collective-permute-done((f32[1,392,128]{2,1,0:T(8,128)}, f32[1,392,128]{2,1,0:T(8,128)}, u32[]{:S(2)}, u32[]{:S(2)}) %collective-permute-start.1) | collective-permute-done | bytes 200736 | tf_op jit(solution)/shard_map/ppermute | solution.py:576
  66.4 1.7 %shard_map.87 = f32[1,392,128]{2,1,0:T(8,128)} custom-call(s32[3]{0:T(128)} %pad_add_fusion.place_ref.core_ref, f32[1,392,128]{2,1,0:T(8,128)} %collective-permute-done.1.earlier_ref.near_ref, f32[1,392,128]{2,1,0:T(8,128)} %get-tuple-element.40.later_ref), custom_call_target="tpu_custom_call" | custom-call | bytes 802816 | tf_op jit(solution)/shard_map/pallas_call | solution.py:168
  68.2 6.0 %collective-permute-start.2 = (f32[1,392,128]{2,1,0:T(8,128)}, f32[1,392,128]{2,1,0:T(8,128)}, u32[]{:S(2)}, u32[]{:S(2)}) collective-permute-start(f32[1,392,128]{2,1,0:T(8,128)} %shard_map.87), channel_id=1, source_target_pairs={{0,4},{1,5},{2,6},{3,7},{8,12},{9,13},{10,14},{11,15},{16,20},{17,... | collective-permute-start | bytes 602120 | tf_op jit(solution)/shard_map/ppermute | solution.py:576
  74.1 3.2 %collective-permute-done.2.far_ref = f32[1,392,128]{2,1,0:T(8,128)} collective-permute-done((f32[1,392,128]{2,1,0:T(8,128)}, f32[1,392,128]{2,1,0:T(8,128)}, u32[]{:S(2)}, u32[]{:S(2)}) %collective-permute-start.2) | collective-permute-done | bytes 200736 | tf_op jit(solution)/shard_map/ppermute | solution.py:576
  77.4 2.1 %shard_map.88 = (f32[1,392,128]{2,1,0:T(8,128)}, f32[1,392,128]{2,1,0:T(8,128)}) custom-call(s32[3]{0:T(128)} %pad_add_fusion.place_ref.core_ref, f32[1,392,128]{2,1,0:T(8,128)} %collective-permute-done.2.far_ref, f32[1,392,128]{2,1,0:T(8,128)} %collective-permute-done.1.earlier_ref.near_ref, f32[2,1,392,128]{3,2,1,0:T(8,128)} %get-tuple-element.38.own_ref, ...), custom_call_target="tpu_custom_call" | custom-call | bytes 2408448 | tf_op jit(solution)/shard_map/pallas_call | solution.py:168
  79.5 3.6 %narrow.1.other_ref = bf16[4,512,256]{2,1,0:T(8,128)(2,1)} custom-call(f32[4,512,256]{2,1,0:T(8,128)} %collective-permute-done.8.in_ref), custom_call_target="tpu_custom_call" | custom-call | bytes 3145728 | tf_op jit(solution)/shard_map/narrow/pallas_call | solution.py:389
  83.1 6.2 %gradient_blocks.2 = (f32[2,4,64,256]{3,2,1,0:T(8,128)}, f32[2,4,64,256]{3,2,1,0:T(8,128)}, f32[2,4,64,256]{3,2,1,0:T(8,128)}, f32[2,4,64,256]{3,2,1,0:T(8,128)}) custom-call(s32[3]{0:T(128)} %pad_add_fusion.place_ref.core_ref, f32[4,128,512]{2,1,0:T(8,128)} %get-tuple-element.47.own_ref, f32[4,128,512]{2,1,0:T(8,128)} %collective-permute-done.7.far_ref, ...), custom_call_target="tpu_custom_call" | custom-call | flops 1073741824 | bytes 6291456 | tf_op jit(solution)/shard_map/gradient_blocks/pallas_call | solution.py:432
  89.3 11.7 %solve_heads.5.own_ref = f32[4,128,512]{2,1,0:T(8,128)} custom-call(s32[3]{0:T(128)} %pad_add_fusion.place_ref.core_ref, f32[8]{0:T(128)} %regular_ref.7, bf16[512,1024]{1,0:T(8,128)(2,1)} %bitcast.28, bf16[512,1024]{1,0:T(8,128)(2,1)} %bitcast.17, bf16[512,1024]{1,0:T(8,128)(2,1)} %bitcast.22, f32[2,8,512]{2,1,0:T(8,128)} %get-tuple-element.37.refs_4_.refs_3_, ...), custom_call_target="tpu_custom_call" | custom-call | flops 2684354560 | bytes 3670016 | tf_op jit(solution)/shard_map/solve_heads/pallas_call | solution.py:346
  101.4 1.5 collective-permute-start.10
  102.9 1.5 collective-permute-start.12
  104.4 6.1 %gradient_blocks.3 = (f32[2,4,64,256]{3,2,1,0:T(8,128)}, f32[2,4,64,256]{3,2,1,0:T(8,128)}, f32[2,4,64,256]{3,2,1,0:T(8,128)}, f32[2,4,64,256]{3,2,1,0:T(8,128)}) custom-call(s32[3]{0:T(128)} %pad_add_fusion.place_ref.core_ref, f32[4,128,512]{2,1,0:T(8,128)} %solve_heads.5.own_ref, f32[4,128,512]{2,1,0:T(8,128)} %collective-permute-done.9.far_ref, ...), custom_call_target="tpu_custom_call" | custom-call | flops 1073741824 | bytes 6291456 | tf_op jit(solution)/shard_map/gradient_blocks/pallas_call | solution.py:432
  110.5 1.1 collective-permute-start.17
  111.6 1.5 collective-permute-start.19
  113.1 3.4 %collective-permute-done.10.came_ref = f32[2,4,64,256]{3,2,1,0:T(8,128)} collective-permute-done((f32[2,4,64,256]{3,2,1,0:T(8,128)}, f32[2,4,64,256]{3,2,1,0:T(8,128)}, u32[]{:S(2)}, u32[]{:S(2)}) %collective-permute-start.10) | collective-permute-done | bytes 524320 | tf_op jit(solution)/shard_map/ppermute | solution.py:618
  116.5 2.0 %sum_blocks.4 = (f32[1,4,64,256]{3,2,1,0:T(8,128)}, f32[1,4,64,256]{3,2,1,0:T(8,128)}) custom-call(f32[2,4,64,256]{3,2,1,0:T(8,128)} %get-tuple-element.48.refs_6_.keep_ref, f32[2,4,64,256]{3,2,1,0:T(8,128)} %collective-permute-done.10.came_ref), custom_call_target="tpu_custom_call" | custom-call | bytes 1572864 | tf_op jit(solution)/shard_map/sum_blocks/pallas_call | solution.py:466
  118.5 1.5 collective-permute-start.11
  120.1 2.0 %sum_blocks.5 = (f32[1,4,64,256]{3,2,1,0:T(8,128)}, f32[1,4,64,256]{3,2,1,0:T(8,128)}) custom-call(f32[2,4,64,256]{3,2,1,0:T(8,128)} %get-tuple-element.53.keep_ref, f32[2,4,64,256]{3,2,1,0:T(8,128)} %collective-permute-done.12.came_ref), custom_call_target="tpu_custom_call" | custom-call | bytes 1572864 | tf_op jit(solution)/shard_map/sum_blocks/pallas_call | solution.py:466
  122.1 1.5 collective-permute-start.13
  123.6 4.2 %collective-permute-done.17.came_ref = f32[2,4,64,256]{3,2,1,0:T(8,128)} collective-permute-done((f32[2,4,64,256]{3,2,1,0:T(8,128)}, f32[2,4,64,256]{3,2,1,0:T(8,128)}, u32[]{:S(2)}, u32[]{:S(2)}) %collective-permute-start.17) | collective-permute-done | bytes 524320 | tf_op jit(solution)/shard_map/ppermute | solution.py:618
  127.8 2.0 %sum_blocks.6 = (f32[1,4,64,256]{3,2,1,0:T(8,128)}, f32[1,4,64,256]{3,2,1,0:T(8,128)}) custom-call(f32[2,4,64,256]{3,2,1,0:T(8,128)} %get-tuple-element.49.refs_6_.keep_ref, f32[2,4,64,256]{3,2,1,0:T(8,128)} %collective-permute-done.17.came_ref), custom_call_target="tpu_custom_call" | custom-call | bytes 1572864 | tf_op jit(solution)/shard_map/sum_blocks/pallas_call | solution.py:466
  129.8 1.5 collective-permute-start.18
  131.3 2.0 %sum_blocks.7 = (f32[1,4,64,256]{3,2,1,0:T(8,128)}, f32[1,4,64,256]{3,2,1,0:T(8,128)}) custom-call(f32[2,4,64,256]{3,2,1,0:T(8,128)} %get-tuple-element.64.keep_ref, f32[2,4,64,256]{3,2,1,0:T(8,128)} %collective-permute-done.19.came_ref), custom_call_target="tpu_custom_call" | custom-call | bytes 1572864 | tf_op jit(solution)/shard_map/sum_blocks/pallas_call | solution.py:466
  133.3 1.5 collective-permute-start.20
  134.9 2.0 %merge_blocks.2 = (f32[128,256]{1,0:T(8,128)}, f32[128,256]{1,0:T(8,128)}, f32[128,256]{1,0:T(8,128)}, f32[128,256]{1,0:T(8,128)}) custom-call(f32[1,4,64,256]{3,2,1,0:T(8,128)} %get-tuple-element.51.refs_0_, f32[1,4,64,256]{3,2,1,0:T(8,128)} %collective-permute-done.11.refs_1_, f32[1,4,64,256]{3,2,1,0:T(8,128)} %get-tuple-element.55.refs_2_, ...), custom_call_target="tpu_custom_call" | custom-call | bytes 1572864 | tf_op jit(solution)/shard_map/merge_blocks/pallas_call | solution.py:490
  136.9 5.7 %collective-permute-start.14 = (f32[128,256]{1,0:T(8,128)}, f32[128,256]{1,0:T(8,128)}, u32[]{:S(2)}, u32[]{:S(2)}) collective-permute-start(f32[128,256]{1,0:T(8,128)} %get-tuple-element.58), channel_id=1, source_target_pairs={{0,2},{1,3},{2,0},{3,1},{4,6},{5,7},{6,4},{7,5},{8,10},{9,11},{10,... | collective-permute-start | bytes 393224 | tf_op jit(solution)/shard_map/ppermute | solution.py:627
  142.6 3.4 %collective-permute-start.15 = (f32[128,256]{1,0:T(8,128)}, f32[128,256]{1,0:T(8,128)}, u32[]{:S(2)}, u32[]{:S(2)}) collective-permute-start(f32[128,256]{1,0:T(8,128)} %get-tuple-element.59), channel_id=1, source_target_pairs={{0,4},{1,5},{2,6},{3,7},{4,0},{5,1},{6,2},{7,3},{8,12},{9,13},{10,... | collective-permute-start | bytes 393224 | tf_op jit(solution)/shard_map/ppermute | solution.py:627
  146.0 2.0 %merge_blocks.3 = (f32[128,256]{1,0:T(8,128)}, f32[128,256]{1,0:T(8,128)}, f32[128,256]{1,0:T(8,128)}, f32[128,256]{1,0:T(8,128)}) custom-call(f32[1,4,64,256]{3,2,1,0:T(8,128)} %get-tuple-element.62.refs_0_, f32[1,4,64,256]{3,2,1,0:T(8,128)} %collective-permute-done.18.refs_1_, f32[1,4,64,256]{3,2,1,0:T(8,128)} %get-tuple-element.66.refs_2_, ...), custom_call_target="tpu_custom_call" | custom-call | bytes 1572864 | tf_op jit(solution)/shard_map/merge_blocks/pallas_call | solution.py:490
  148.0 0.6 collective-permute-start.21
  148.5 3.8 %collective-permute-start.22 = (f32[128,256]{1,0:T(8,128)}, f32[128,256]{1,0:T(8,128)}, u32[]{:S(2)}, u32[]{:S(2)}) collective-permute-start(f32[128,256]{1,0:T(8,128)} %get-tuple-element.70), channel_id=1, source_target_pairs={{0,4},{1,5},{2,6},{3,7},{4,0},{5,1},{6,2},{7,3},{8,12},{9,13},{10,... | collective-permute-start | bytes 393224 | tf_op jit(solution)/shard_map/ppermute | solution.py:627
  152.4 6.3 %solve_heads.6.refs_5_ = bf16[512,1024]{1,0:T(8,128)(2,1)} custom-call(s32[3]{0:T(128)} %pad_add_fusion.place_ref.core_ref, f32[8]{0:T(128)} %regular_ref.7, bf16[512,1024]{1,0:T(8,128)(2,1)} %convolution_convert_fusion.refs_0_, bf16[512,1024]{1,0:T(8,128)(2,1)} %bitcast.18, bf16[512,1024]{1,0:T(8,128)(2,1)} %bitcast.23, ...), custom_call_target="tpu_custom_call", output_to_operand_aliasing={{}: (7, {})} | custom-call | flops 1342177280 | bytes 1835008 | tf_op jit(solution)/shard_map/solve_heads/pallas_call | solution.py:346
  158.7 6.3 %solve_heads.7 = bf16[512,1024]{1,0:T(8,128)(2,1)} custom-call(s32[3]{0:T(128)} %pad_add_fusion.place_ref.core_ref, f32[8]{0:T(128)} %regular_ref.7, bf16[512,1024]{1,0:T(8,128)(2,1)} %convolution_convert_fusion.refs_0_, bf16[512,1024]{1,0:T(8,128)(2,1)} %bitcast.19, bf16[512,1024]{1,0:T(8,128)(2,1)} %bitcast.24, ...), custom_call_target="tpu_custom_call", output_to_operand_aliasing={{}: (7, {})} | custom-call | flops 1342177280 | bytes 1835008 | tf_op jit(solution)/shard_map/solve_heads/pallas_call | solution.py:346
  165.1 0.6 collective-permute-done.22.refs_6_
  165.6 2.0 %finish.1 = f32[256,256]{1,0:T(8,128)} custom-call(f32[128,256]{1,0:T(8,128)} %get-tuple-element.57.refs_0_, f32[128,256]{1,0:T(8,128)} %collective-permute-done.14.refs_1_, f32[128,256]{1,0:T(8,128)} %collective-permute-done.15.refs_2_, f32[128,256]{1,0:T(8,128)} %collective-permute-done.16.refs_3_, f32[128,256]{1,0:T(8,128)} %get-tuple-element.68.refs_4_, ...), custom_call_target="tpu_custom_call" | custom-call | bytes 1310720 | tf_op jit(solution)/shard_map/finish/pallas_call | solution.py:518
  (23 shorter events, 0.6 us)
Async XLA Ops:
  6.1 2.2 %collective-permute-start = (f32[2,1,392,128]{3,2,1,0:T(8,128)}, f32[2,1,392,128]{3,2,1,0:T(8,128)}, u32[]{:S(2)}, u32[]{:S(2)}) collective-permute-start(f32[2,1,392,128]{3,2,1,0:T(8,128)} %get-tuple-element.39), channel_id=1, source_target_pairs={{0,1},{1,0},{2,3},{3,2},{4,5},{5,4},{6,7},{7,6},{8,9},{9,8},{10,11... | collective-permute-start | bytes 1204232 | tf_op jit(solution)/shard_map/ppermute | solution.py:561
  10.2 9.7 %collective-permute-start.4 = (f32[1,392,128]{2,1,0:T(8,128)}, f32[1,392,128]{2,1,0:T(8,128)}, u32[]{:S(2)}, u32[]{:S(2)}) collective-permute-start(f32[1,392,128]{2,1,0:T(8,128)} %get-tuple-element.43.later_ref), channel_id=1, source_target_pairs={{0,2},{1,3},{2,4},{3,5},{4,6},{5,7},{8,10},{9,11},{10,12},{11,13},... | collective-permute-start | bytes 602120 | tf_op jit(solution)/shard_map/ppermute | solution.py:576
  21.6 10.4 %collective-permute-start.5 = (f32[1,392,128]{2,1,0:T(8,128)}, f32[1,392,128]{2,1,0:T(8,128)}, u32[]{:S(2)}, u32[]{:S(2)}) collective-permute-start(f32[1,392,128]{2,1,0:T(8,128)} %shard_map.89), channel_id=1, source_target_pairs={{0,4},{1,5},{2,6},{3,7},{8,12},{9,13},{10,14},{11,15},{16,20},{17,... | collective-permute-start | bytes 602120 | tf_op jit(solution)/shard_map/ppermute | solution.py:576
  32.0 47.5 %collective-permute-start.8 = (f32[4,512,256]{2,1,0:T(8,128)}, f32[4,512,256]{2,1,0:T(8,128)}, u32[]{:S(2)}, u32[]{:S(2)}) collective-permute-start(f32[4,512,256]{2,1,0:T(8,128)} %pick_columns.1), channel_id=1, source_target_pairs={{0,1},{1,0},{2,3},{3,2},{4,5},{5,4},{6,7},{7,6},{8,9},{9,8},{10,11... | collective-permute-start | bytes 6291464 | tf_op jit(solution)/shard_map/ppermute | solution.py:584
  34.1 6.7 %collective-permute-start.6 = (f32[1,392,128]{2,1,0:T(8,128)}, f32[1,392,128]{2,1,0:T(8,128)}, u32[]{:S(2)}, u32[]{:S(2)}) collective-permute-start(f32[1,392,128]{2,1,0:T(8,128)} %get-tuple-element.45), channel_id=1, source_target_pairs={{0,1},{1,0},{2,3},{3,2},{4,5},{5,4},{6,7},{7,6},{8,9},{9,8},{10,11... | collective-permute-start | bytes 602120 | tf_op jit(solution)/shard_map/ppermute | solution.py:581
  55.0 28.1 %collective-permute-start.7 = (f32[4,128,512]{2,1,0:T(8,128)}, f32[4,128,512]{2,1,0:T(8,128)}, u32[]{:S(2)}, u32[]{:S(2)}) collective-permute-start(f32[4,128,512]{2,1,0:T(8,128)} %get-tuple-element.47.own_ref), channel_id=1, source_target_pairs={{0,1},{1,0},{2,3},{3,2},{4,5},{5,4},{6,7},{7,6},{8,9},{9,8},{10,11... | collective-permute-start | bytes 3145736 | tf_op jit(solution)/shard_map/ppermute | solution.py:602
  55.0 11.4 %collective-permute-start.1 = (f32[1,392,128]{2,1,0:T(8,128)}, f32[1,392,128]{2,1,0:T(8,128)}, u32[]{:S(2)}, u32[]{:S(2)}) collective-permute-start(f32[1,392,128]{2,1,0:T(8,128)} %get-tuple-element.40.later_ref), channel_id=1, source_target_pairs={{0,2},{1,3},{2,4},{3,5},{4,6},{5,7},{8,10},{9,11},{10,12},{11,13},... | collective-permute-start | bytes 602120 | tf_op jit(solution)/shard_map/ppermute | solution.py:576
  68.2 9.2 %collective-permute-start.2 = (f32[1,392,128]{2,1,0:T(8,128)}, f32[1,392,128]{2,1,0:T(8,128)}, u32[]{:S(2)}, u32[]{:S(2)}) collective-permute-start(f32[1,392,128]{2,1,0:T(8,128)} %shard_map.87), channel_id=1, source_target_pairs={{0,4},{1,5},{2,6},{3,7},{8,12},{9,13},{10,14},{11,15},{16,20},{17,... | collective-permute-start | bytes 602120 | tf_op jit(solution)/shard_map/ppermute | solution.py:576
  79.5 9.7 %collective-permute-start.3 = (f32[1,392,128]{2,1,0:T(8,128)}, f32[1,392,128]{2,1,0:T(8,128)}, u32[]{:S(2)}, u32[]{:S(2)}) collective-permute-start(f32[1,392,128]{2,1,0:T(8,128)} %get-tuple-element.41), channel_id=1, source_target_pairs={{0,1},{1,0},{2,3},{3,2},{4,5},{5,4},{6,7},{7,6},{8,9},{9,8},{10,11... | collective-permute-start | bytes 602120 | tf_op jit(solution)/shard_map/ppermute | solution.py:581
  100.9 3.5 %collective-permute-start.9 = (f32[4,128,512]{2,1,0:T(8,128)}, f32[4,128,512]{2,1,0:T(8,128)}, u32[]{:S(2)}, u32[]{:S(2)}) collective-permute-start(f32[4,128,512]{2,1,0:T(8,128)} %solve_heads.5.own_ref), channel_id=1, source_target_pairs={{0,1},{1,0},{2,3},{3,2},{4,5},{5,4},{6,7},{7,6},{8,9},{9,8},{10,11... | collective-permute-start | bytes 3145736 | tf_op jit(solution)/shard_map/ppermute | solution.py:602
  101.4 15.1 %collective-permute-start.10 = (f32[2,4,64,256]{3,2,1,0:T(8,128)}, f32[2,4,64,256]{3,2,1,0:T(8,128)}, u32[]{:S(2)}, u32[]{:S(2)}) collective-permute-start(f32[2,4,64,256]{3,2,1,0:T(8,128)} %get-tuple-element.50), channel_id=1, source_target_pairs={{0,8},{8,0},{16,24},{24,16},{1,9},{9,1},{17,25},{25,17},{2,10},{10... | collective-permute-start | bytes 1572872 | tf_op jit(solution)/shard_map/ppermute | solution.py:618
  102.9 17.2 %collective-permute-start.12 = (f32[2,4,64,256]{3,2,1,0:T(8,128)}, f32[2,4,64,256]{3,2,1,0:T(8,128)}, u32[]{:S(2)}, u32[]{:S(2)}) collective-permute-start(f32[2,4,64,256]{3,2,1,0:T(8,128)} %get-tuple-element.54), channel_id=1, source_target_pairs={{0,16},{8,24},{16,0},{24,8},{1,17},{9,25},{17,1},{25,9},{2,18},{10... | collective-permute-start | bytes 1572872 | tf_op jit(solution)/shard_map/ppermute | solution.py:618
  110.5 17.2 %collective-permute-start.17 = (f32[2,4,64,256]{3,2,1,0:T(8,128)}, f32[2,4,64,256]{3,2,1,0:T(8,128)}, u32[]{:S(2)}, u32[]{:S(2)}) collective-permute-start(f32[2,4,64,256]{3,2,1,0:T(8,128)} %get-tuple-element.61), channel_id=1, source_target_pairs={{0,8},{8,0},{16,24},{24,16},{1,9},{9,1},{17,25},{25,17},{2,10},{10... | collective-permute-start | bytes 1572872 | tf_op jit(solution)/shard_map/ppermute | solution.py:618
  111.6 19.7 %collective-permute-start.19 = (f32[2,4,64,256]{3,2,1,0:T(8,128)}, f32[2,4,64,256]{3,2,1,0:T(8,128)}, u32[]{:S(2)}, u32[]{:S(2)}) collective-permute-start(f32[2,4,64,256]{3,2,1,0:T(8,128)} %get-tuple-element.65), channel_id=1, source_target_pairs={{0,16},{8,24},{16,0},{24,8},{1,17},{9,25},{17,1},{25,9},{2,18},{10... | collective-permute-start | bytes 1572872 | tf_op jit(solution)/shard_map/ppermute | solution.py:618
  118.5 16.3 %collective-permute-start.11 = (f32[1,4,64,256]{3,2,1,0:T(8,128)}, f32[1,4,64,256]{3,2,1,0:T(8,128)}, u32[]{:S(2)}, u32[]{:S(2)}) collective-permute-start(f32[1,4,64,256]{3,2,1,0:T(8,128)} %get-tuple-element.52), channel_id=1, source_target_pairs={{0,16},{8,24},{16,0},{24,8},{1,17},{9,25},{17,1},{25,9},{2,18},{10... | collective-permute-start | bytes 786440 | tf_op jit(solution)/shard_map/ppermute | solution.py:618
  122.1 12.8 %collective-permute-start.13 = (f32[1,4,64,256]{3,2,1,0:T(8,128)}, f32[1,4,64,256]{3,2,1,0:T(8,128)}, u32[]{:S(2)}, u32[]{:S(2)}) collective-permute-start(f32[1,4,64,256]{3,2,1,0:T(8,128)} %get-tuple-element.56), channel_id=1, source_target_pairs={{0,8},{8,0},{16,24},{24,16},{1,9},{9,1},{17,25},{25,17},{2,10},{10... | collective-permute-start | bytes 786440 | tf_op jit(solution)/shard_map/ppermute | solution.py:618
  129.8 16.2 %collective-permute-start.18 = (f32[1,4,64,256]{3,2,1,0:T(8,128)}, f32[1,4,64,256]{3,2,1,0:T(8,128)}, u32[]{:S(2)}, u32[]{:S(2)}) collective-permute-start(f32[1,4,64,256]{3,2,1,0:T(8,128)} %get-tuple-element.63), channel_id=1, source_target_pairs={{0,16},{8,24},{16,0},{24,8},{1,17},{9,25},{17,1},{25,9},{2,18},{10... | collective-permute-start | bytes 786440 | tf_op jit(solution)/shard_map/ppermute | solution.py:618
  133.3 12.7 %collective-permute-start.20 = (f32[1,4,64,256]{3,2,1,0:T(8,128)}, f32[1,4,64,256]{3,2,1,0:T(8,128)}, u32[]{:S(2)}, u32[]{:S(2)}) collective-permute-start(f32[1,4,64,256]{3,2,1,0:T(8,128)} %get-tuple-element.67), channel_id=1, source_target_pairs={{0,8},{8,0},{16,24},{24,16},{1,9},{9,1},{17,25},{25,17},{2,10},{10... | collective-permute-start | bytes 786440 | tf_op jit(solution)/shard_map/ppermute | solution.py:618
  136.9 15.5 %collective-permute-start.14 = (f32[128,256]{1,0:T(8,128)}, f32[128,256]{1,0:T(8,128)}, u32[]{:S(2)}, u32[]{:S(2)}) collective-permute-start(f32[128,256]{1,0:T(8,128)} %get-tuple-element.58), channel_id=1, source_target_pairs={{0,2},{1,3},{2,0},{3,1},{4,6},{5,7},{6,4},{7,5},{8,10},{9,11},{10,... | collective-permute-start | bytes 393224 | tf_op jit(solution)/shard_map/ppermute | solution.py:627
  142.6 22.4 %collective-permute-start.15 = (f32[128,256]{1,0:T(8,128)}, f32[128,256]{1,0:T(8,128)}, u32[]{:S(2)}, u32[]{:S(2)}) collective-permute-start(f32[128,256]{1,0:T(8,128)} %get-tuple-element.59), channel_id=1, source_target_pairs={{0,4},{1,5},{2,6},{3,7},{4,0},{5,1},{6,2},{7,3},{8,12},{9,13},{10,... | collective-permute-start | bytes 393224 | tf_op jit(solution)/shard_map/ppermute | solution.py:627
  146.0 19.0 %collective-permute-start.16 = (f32[128,256]{1,0:T(8,128)}, f32[128,256]{1,0:T(8,128)}, u32[]{:S(2)}, u32[]{:S(2)}) collective-permute-start(f32[128,256]{1,0:T(8,128)} %get-tuple-element.60), channel_id=1, source_target_pairs={{0,6},{1,7},{2,4},{3,5},{4,2},{5,3},{6,0},{7,1},{8,14},{9,15},{10,... | collective-permute-start | bytes 393224 | tf_op jit(solution)/shard_map/ppermute | solution.py:627
  148.0 17.1 %collective-permute-start.21 = (f32[128,256]{1,0:T(8,128)}, f32[128,256]{1,0:T(8,128)}, u32[]{:S(2)}, u32[]{:S(2)}) collective-permute-start(f32[128,256]{1,0:T(8,128)} %get-tuple-element.69), channel_id=1, source_target_pairs={{0,2},{1,3},{2,0},{3,1},{4,6},{5,7},{6,4},{7,5},{8,10},{9,11},{10,... | collective-permute-start | bytes 393224 | tf_op jit(solution)/shard_map/ppermute | solution.py:627
  148.5 17.1 %collective-permute-start.22 = (f32[128,256]{1,0:T(8,128)}, f32[128,256]{1,0:T(8,128)}, u32[]{:S(2)}, u32[]{:S(2)}) collective-permute-start(f32[128,256]{1,0:T(8,128)} %get-tuple-element.70), channel_id=1, source_target_pairs={{0,4},{1,5},{2,6},{3,7},{4,0},{5,1},{6,2},{7,3},{8,12},{9,13},{10,... | collective-permute-start | bytes 393224 | tf_op jit(solution)/shard_map/ppermute | solution.py:627
  152.4 13.3 %collective-permute-start.23 = (f32[128,256]{1,0:T(8,128)}, f32[128,256]{1,0:T(8,128)}, u32[]{:S(2)}, u32[]{:S(2)}) collective-permute-start(f32[128,256]{1,0:T(8,128)} %get-tuple-element.71), channel_id=1, source_target_pairs={{0,6},{1,7},{2,4},{3,5},{4,2},{5,3},{6,0},{7,1},{8,14},{9,15},{10,... | collective-permute-start | bytes 393224 | tf_op jit(solution)/shard_map/ppermute | solution.py:627

commit v7 on v6

--- a/solution.py
+++ b/solution.py
@@ -151,13 +151,12 @@
         out_ref[...] = join(jnp.where(is_first, own, came), jnp.where(is_first, came, own), dim)
 
 
-def join_kernel(dim, place_ref, earlier_ref, later_ref, out_ref):
-    out_ref[...] = join(earlier_ref[...], later_ref[...], dim)
-
-
-def start_kernel(dim, k, place_ref, far_ref, near_ref, own_ref, came_ref, mine_ref, other_ref):
+def start_kernel(dim, k, place_ref, own_ref, came_ref, *refs):
+    sent_refs, (mine_ref, other_ref) = refs[:-2], refs[-2:]
     is_first = place_ref[0] == 0
-    before = join(far_ref[...], near_ref[...], dim)
+    before = sent_refs[-1][...]
+    for ref in reversed(sent_refs[:-1]):
+        before = join(before, ref[...], dim)
     after = join(before, jnp.where(is_first, own_ref[k], came_ref[k]), dim)
     mine_ref[...] = jnp.where(is_first, before, after)
     other_ref[...] = jnp.where(is_first, after, before)
@@ -453,52 +452,58 @@
     )(place, own, far, tokens, other)
 
 
-def sum_kernel(keep_ref, came_ref, keep_out, send_out):
-    out_half = keep_out.shape[0]
-    for i in range(out_half):
-        send_out[i] = keep_ref[out_half + i] + came_ref[out_half + i]
-    for i in range(out_half):
-        keep_out[i] = keep_ref[i] + came_ref[i]
-
-
-def sum_blocks(keep, came):
-    out = jax.ShapeDtypeStruct((keep.shape[0] // 2,) + keep.shape[1:], F32)
+def sum_kernel(*refs):
+    total = refs[0][...]
+    for ref in refs[1:-1]:
+        total = total + ref[...]
+    refs[-1][...] = total
+
+
+def sum_blocks(arrays, length):
+    out = jax.ShapeDtypeStruct((length,) + arrays[0].shape[1:], F32)
+    spec = pl.BlockSpec(out.shape, lambda _: (1, 0, 0, 0))
     return pl.pallas_call(
         sum_kernel,
-        out_shape=[out] * 2,
-        in_specs=[whole(keep)] * 2,
-        out_specs=[whole(out)] * 2,
+        out_shape=out,
+        in_specs=[spec] * len(arrays),
+        out_specs=whole(out),
         grid=(1,),
         compiler_params=FULL,
-        cost_estimate=pl.CostEstimate(flops=0, bytes_accessed=12 * keep.size, transcendentals=0),
+        cost_estimate=pl.CostEstimate(flops=0, bytes_accessed=12 * out.size // length, transcendentals=0),
         name="sum_blocks",
-    )(keep, came)
-
-
-def merge_kernel(count, *refs):
-    sums, outs = refs[: 2 * count], refs[2 * count :]
+    )(*arrays)
+
+
+def merge_kernel(counts, *refs):
+    sums, outs = refs[: sum(counts)], refs[sum(counts) :]
     rows = sums[0].shape[2]
-    for z, out in enumerate(outs):
-        for i in range(count):
-            out[i * rows : (i + 1) * rows, :] = sums[2 * i][0, z] + sums[2 * i + 1][0, z]
+    at = 0
+    for i, count in enumerate(counts):
+        for z, out in enumerate(outs):
+            total = sums[at][0, z]
+            for ref in sums[at + 1 : at + count]:
+                total = total + ref[0, z]
+            out[i * rows : (i + 1) * rows, :] = total
+        at += count
 
 
 def merge_blocks(sums):
-    _, chips, rows, size = sums[0].shape
-    count = len(sums) // 2
-    out = jax.ShapeDtypeStruct((count * rows, size), F32)
-    return pl.pallas_call(
-        functools.partial(merge_kernel, count),
+    counts = [len(arrays) for arrays in sums]
+    arrays = [a for group in sums for a in group]
+    _, chips, rows, size = arrays[0].shape
+    out = jax.ShapeDtypeStruct((len(counts) * rows, size), F32)
+    return pl.pallas_call(
+        functools.partial(merge_kernel, counts),
         out_shape=[out] * chips,
-        in_specs=[whole(a) for a in sums],
+        in_specs=[pl.BlockSpec((1, chips, rows, size), lambda _: (0, 0, 0, 0))] * len(arrays),
         out_specs=[whole(out)] * chips,
         grid=(1,),
         compiler_params=FULL,
         cost_estimate=pl.CostEstimate(
-            flops=0, bytes_accessed=6 * sum(a.size for a in sums), transcendentals=0
+            flops=0, bytes_accessed=4 * (len(arrays) + 2) * chips * rows * size, transcendentals=0
         ),
         name="merge_blocks",
-    )(*sums)
+    )(*arrays)
 
 
 def finish_kernel(count, *refs):
@@ -561,23 +566,14 @@
     came = lax.ppermute(away, "seq", partner)
     shape = own.shape[1:]
     chip_states = combine(functools.partial(chip_kernel, dim), place, [own, came], shape, per)
-    joined = functools.partial(join_kernel, dim)
     starts = []
     for k, chip_state in enumerate(chip_states):
-        window, near, far = 0, None, None
-        while window < chips - 1:
-            if far is not None:
-                (near,) = combine(joined, place, [far, near], shape, 1)
-            sent = chip_state
-            if near is not None:
-                (sent,) = combine(joined, place, [near, chip_state], shape, 1)
-            shift = 2 * (window + 1)
-            pairs = [(i, i + shift) for i in range(steps - shift)]
-            came_up = lax.ppermute(sent, "seq", pairs)
-            near, far = (came_up, None) if near is None else (near, came_up)
-            window = 2 * window + 1
+        sent = []
+        for z in range(1, chips):
+            pairs = [(i, i + 2 * z) for i in range(steps - 2 * z)]
+            sent.append(lax.ppermute(chip_state, "seq", pairs))
         starting = functools.partial(start_kernel, dim, k)
-        mine, others = combine(starting, place, [far, near, own, came], shape, 2)
+        mine, others = combine(starting, place, [own, came, *sent], shape, 2)
         starts.append((mine, lax.ppermute(others, "seq", partner)))
 
     picked = pick_columns(place, tokens, chips)
@@ -612,14 +608,13 @@
     for blocks in products:
         sums = []
         for index, path in enumerate(paths):
-            keep, send = blocks[2 * index], blocks[2 * index + 1]
+            held, send = [blocks[2 * index]], blocks[2 * index + 1]
             for bit in path:
                 pairs = [(i, i ^ (1 << bit)) for i in range(groups)]
-                came = lax.ppermute(send, "dp", pairs)
-                if bit == path[-1]:
-                    sums += [keep, came]
-                else:
-                    keep, send = sum_blocks(keep, came)
+                held.append(lax.ppermute(send, "dp", pairs))
+                if bit != path[-1]:
+                    send = sum_blocks(held, held[-1].shape[0] // 2)
+            sums.append(held)
         out, *others = merge_blocks(sums)
         finished.append([out])
         for z, other_block in enumerate(others, 1):

time: 169 us -> 165 us (0.976)
  Pallas kernels: 87.3 us -> 83.1 us
    pallas_call x5 -> x3, Pallas kernels: 9.67 us -> 6.23 us  [combine(): pl.pallas_call(kernel, out_shape=[out] * outs, in_specs=[pl.BlockSpec(mem...]
    ppermute x12 -> x14, starting transfers between devices: 36.5 us -> 37.1 us  [the longest x6 25.5 us: program(): sent.append(lax.ppermute(chip_state, 'seq', pairs))]
    ppermute x12 -> x14, waiting for transfers between devices: 19 us -> 19.2 us  [the longest x6 10.5 us: program(): sent.append(lax.ppermute(chip_state, 'seq', pairs))]
  transfers between devices with their start and end apart: 24 -> 26, of which waited for: 7 -> 8; matrix products, arithmetic and copies ran while one was open for 4% -> 4% of each run, Pallas kernels for 39% -> 38%
where the time goes in v7:
time: 165 us; the launch traced here: 164 us
  Pallas kernels  83.1 us (50%)
  starting transfers between devices  52.6 us (32%)
  waiting for transfers between devices  20.9 us (13%)
  matrix products  6.19 us (4%)
    pallas_call x4, Pallas kernels, solve_heads(): pl.pallas_call(functools.partial(solve_kernel, with_query, with_gradient,...  38.5 us
    ppermute x6, starting transfers between devices, program(): sent.append(lax.ppermute(chip_state, 'seq', pairs))  25.5 us
    ppermute x6, starting transfers between devices, program(): finished[-1].append(lax.ppermute(other_block, 'seq', pairs))  13.9 us
    pallas_call x2, Pallas kernels, gradient_blocks(): pl.pallas_call(functools.partial(gradient_kernel, order), out_shape=[out]...  12.2 us
    ppermute x8, starting transfers between devices, program(): held.append(lax.ppermute(send, 'dp', pairs))  11.6 us
    ppermute x6, waiting for transfers between devices, program(): sent.append(lax.ppermute(chip_state, 'seq', pairs))  10.5 us
    ppermute x8, waiting for transfers between devices, program(): held.append(lax.ppermute(send, 'dp', pairs))  8.62 us
    pallas_call x4, Pallas kernels, sum_blocks(): pl.pallas_call(sum_kernel, out_shape=out, in_specs=[spec] * len(arrays),...  7.09 us
  transfers between devices with their start and end apart: 26, of which 8 were waited for; matrix products, arithmetic and copies ran while one was open for 4% of the time, Pallas kernels for 38%

profile of v7, /device:TPU:0, one launch (start us, length us, event | category | flops | bytes accessed | tf_op | source)
XLA Modules:
  0.0 164.2 jit_solution(7497098088841813672)
XLA Ops:
  0.6 0.7 pad_add_fusion.place_ref.core_ref
  1.3 4.9 %local_states.1 = (f32[2,1,392,128]{3,2,1,0:T(8,128)}, f32[2,1,392,128]{3,2,1,0:T(8,128)}, f32[2,8,512]{2,1,0:T(8,128)}) custom-call(s32[3]{0:T(128)} %pad_add_fusion.place_ref.core_ref, bf16[512,1024]{1,0:T(8,128)(2,1)} %bitcast.15, bf16[512,1024]{1,0:T(8,128)(2,1)} %bitcast.20, f32[8,512]{1,0:T(8,128)} %bitcast.26), custom_call_target="tpu_custom_call" | custom-call | flops 536870912 | bytes 4194304 | tf_op jit(solution)/shard_map/local_states/pallas_call | solution.py:122
  6.7 1.7 %collective-permute-done.came_ref = f32[2,1,392,128]{3,2,1,0:T(8,128)} collective-permute-done((f32[2,1,392,128]{3,2,1,0:T(8,128)}, f32[2,1,392,128]{3,2,1,0:T(8,128)}, u32[]{:S(2)}, u32[]{:S(2)}) %collective-permute-start) | collective-permute-done | bytes 401440 | tf_op jit(solution)/shard_map/ppermute | solution.py:566
  8.4 1.9 %shard_map.86 = (f32[1,392,128]{2,1,0:T(8,128)}, f32[1,392,128]{2,1,0:T(8,128)}) custom-call(s32[3]{0:T(128)} %pad_add_fusion.place_ref.core_ref, f32[2,1,392,128]{3,2,1,0:T(8,128)} %get-tuple-element.30.own_ref, f32[2,1,392,128]{3,2,1,0:T(8,128)} %collective-permute-done.came_ref), custom_call_target="tpu_custom_call" | custom-call | bytes 1605632 | tf_op jit(solution)/shard_map/pallas_call | solution.py:167
  10.3 7.5 %collective-permute-start.7 = (f32[1,392,128]{2,1,0:T(8,128)}, f32[1,392,128]{2,1,0:T(8,128)}, u32[]{:S(2)}, u32[]{:S(2)}) collective-permute-start(f32[1,392,128]{2,1,0:T(8,128)} %get-tuple-element.35), channel_id=1, source_target_pairs={{0,6},{1,7},{8,14},{9,15},{16,22},{17,23},{24,30},{25,31}} | collective-permute-start | bytes 602120 | tf_op jit(solution)/shard_map/ppermute | solution.py:574
  17.8 2.0 %collective-permute-start.6 = (f32[1,392,128]{2,1,0:T(8,128)}, f32[1,392,128]{2,1,0:T(8,128)}, u32[]{:S(2)}, u32[]{:S(2)}) collective-permute-start(f32[1,392,128]{2,1,0:T(8,128)} %get-tuple-element.35), channel_id=1, source_target_pairs={{0,4},{1,5},{2,6},{3,7},{8,12},{9,13},{10,14},{11,15},{16,20},{17,... | collective-permute-start | bytes 602120 | tf_op jit(solution)/shard_map/ppermute | solution.py:574
  19.8 2.5 %collective-permute-start.5 = (f32[1,392,128]{2,1,0:T(8,128)}, f32[1,392,128]{2,1,0:T(8,128)}, u32[]{:S(2)}, u32[]{:S(2)}) collective-permute-start(f32[1,392,128]{2,1,0:T(8,128)} %get-tuple-element.35), channel_id=1, source_target_pairs={{0,2},{1,3},{2,4},{3,5},{4,6},{5,7},{8,10},{9,11},{10,12},{11,13},... | collective-permute-start | bytes 602120 | tf_op jit(solution)/shard_map/ppermute | solution.py:574
  22.3 4.3 %pick_columns.1 = f32[4,512,256]{2,1,0:T(8,128)} custom-call(s32[3]{0:T(128)} %pad_add_fusion.place_ref.core_ref, bf16[512,2048]{1,0:T(8,128)(2,1)} %bitcast.12), custom_call_target="tpu_custom_call" | custom-call | bytes 3145728 | tf_op jit(solution)/shard_map/pick_columns/pallas_call | solution.py:367
  26.5 0.7 collective-permute-done.6.refs_1_
  27.2 3.5 %collective-permute-done.5.refs_0_ = f32[1,392,128]{2,1,0:T(8,128)} collective-permute-done((f32[1,392,128]{2,1,0:T(8,128)}, f32[1,392,128]{2,1,0:T(8,128)}, u32[]{:S(2)}, u32[]{:S(2)}) %collective-permute-start.5) | collective-permute-done | bytes 200736 | tf_op jit(solution)/shard_map/ppermute | solution.py:574
  30.7 2.2 %shard_map.88 = (f32[1,392,128]{2,1,0:T(8,128)}, f32[1,392,128]{2,1,0:T(8,128)}) custom-call(s32[3]{0:T(128)} %pad_add_fusion.place_ref.core_ref, f32[2,1,392,128]{3,2,1,0:T(8,128)} %get-tuple-element.30.own_ref, f32[2,1,392,128]{3,2,1,0:T(8,128)} %collective-permute-done.came_ref, f32[1,392,128]{2,1,0:T(8,128)} %collective-permute-done.5.refs_0_, ...), custom_call_target="tpu_custom_call" | custom-call | bytes 2809856 | tf_op jit(solution)/shard_map/pallas_call | solution.py:167
  32.9 6.2 %convolution_convert_fusion.refs_0_ = bf16[512,1024]{1,0:T(8,128)(2,1)} fusion(bf16[2048,1024]{1,0:T(8,128)(2,1)} %param.8, bf16[1,512,2048]{2,1,0:T(8,128)(2,1)} %param.7), kind=kOutput, calls=%fused_computation | convolution fusion | flops 2148007936 | bytes 7340032 | tf_op jit(solution)/shard_map/dot_general | solution.py:582
  39.0 14.2 %solve_heads.4 = (bf16[512,1024]{1,0:T(8,128)(2,1)}, f32[4,128,512]{2,1,0:T(8,128)}) custom-call(s32[3]{0:T(128)} %pad_add_fusion.place_ref.core_ref, f32[8]{0:T(128)} %regular_ref.7, bf16[512,1024]{1,0:T(8,128)(2,1)} %convolution_convert_fusion.refs_0_, bf16[512,1024]{1,0:T(8,128)(2,1)} %bitcast.27, bf16[512,1024]{1,0:T(8,128)(2,1)} %bitcast.16, ...), custom_call_target="tpu_custom_call" | custom-call | flops 2684354560 | bytes 3670016 | tf_op jit(solution)/shard_map/solve_heads/pallas_call | solution.py:345
  53.7 6.9 %collective-permute-start.3 = (f32[1,392,128]{2,1,0:T(8,128)}, f32[1,392,128]{2,1,0:T(8,128)}, u32[]{:S(2)}, u32[]{:S(2)}) collective-permute-start(f32[1,392,128]{2,1,0:T(8,128)} %get-tuple-element.32), channel_id=1, source_target_pairs={{0,6},{1,7},{8,14},{9,15},{16,22},{17,23},{24,30},{25,31}} | collective-permute-start | bytes 602120 | tf_op jit(solution)/shard_map/ppermute | solution.py:574
  60.6 4.7 %collective-permute-start.2 = (f32[1,392,128]{2,1,0:T(8,128)}, f32[1,392,128]{2,1,0:T(8,128)}, u32[]{:S(2)}, u32[]{:S(2)}) collective-permute-start(f32[1,392,128]{2,1,0:T(8,128)} %get-tuple-element.32), channel_id=1, source_target_pairs={{0,4},{1,5},{2,6},{3,7},{8,12},{9,13},{10,14},{11,15},{16,20},{17,... | collective-permute-start | bytes 602120 | tf_op jit(solution)/shard_map/ppermute | solution.py:574
  65.3 2.0 %collective-permute-start.1 = (f32[1,392,128]{2,1,0:T(8,128)}, f32[1,392,128]{2,1,0:T(8,128)}, u32[]{:S(2)}, u32[]{:S(2)}) collective-permute-start(f32[1,392,128]{2,1,0:T(8,128)} %get-tuple-element.32), channel_id=1, source_target_pairs={{0,2},{1,3},{2,4},{3,5},{4,6},{5,7},{8,10},{9,11},{10,12},{11,13},... | collective-permute-start | bytes 602120 | tf_op jit(solution)/shard_map/ppermute | solution.py:574
  67.3 3.0 %collective-permute-done.2.refs_1_ = f32[1,392,128]{2,1,0:T(8,128)} collective-permute-done((f32[1,392,128]{2,1,0:T(8,128)}, f32[1,392,128]{2,1,0:T(8,128)}, u32[]{:S(2)}, u32[]{:S(2)}) %collective-permute-start.2) | collective-permute-done | bytes 200736 | tf_op jit(solution)/shard_map/ppermute | solution.py:574
  70.3 3.4 %collective-permute-done.1.refs_0_ = f32[1,392,128]{2,1,0:T(8,128)} collective-permute-done((f32[1,392,128]{2,1,0:T(8,128)}, f32[1,392,128]{2,1,0:T(8,128)}, u32[]{:S(2)}, u32[]{:S(2)}) %collective-permute-start.1) | collective-permute-done | bytes 200736 | tf_op jit(solution)/shard_map/ppermute | solution.py:574
  73.7 2.2 %shard_map.87 = (f32[1,392,128]{2,1,0:T(8,128)}, f32[1,392,128]{2,1,0:T(8,128)}) custom-call(s32[3]{0:T(128)} %pad_add_fusion.place_ref.core_ref, f32[2,1,392,128]{3,2,1,0:T(8,128)} %get-tuple-element.30.own_ref, f32[2,1,392,128]{3,2,1,0:T(8,128)} %collective-permute-done.came_ref, f32[1,392,128]{2,1,0:T(8,128)} %collective-permute-done.1.refs_0_, ...), custom_call_target="tpu_custom_call" | custom-call | bytes 2809856 | tf_op jit(solution)/shard_map/pallas_call | solution.py:167
  75.8 3.6 %narrow.1.other_ref = bf16[4,512,256]{2,1,0:T(8,128)(2,1)} custom-call(f32[4,512,256]{2,1,0:T(8,128)} %collective-permute-done.10.in_ref), custom_call_target="tpu_custom_call" | custom-call | bytes 3145728 | tf_op jit(solution)/shard_map/narrow/pallas_call | solution.py:388
  79.4 6.1 %gradient_blocks.2 = (f32[2,4,64,256]{3,2,1,0:T(8,128)}, f32[2,4,64,256]{3,2,1,0:T(8,128)}, f32[2,4,64,256]{3,2,1,0:T(8,128)}, f32[2,4,64,256]{3,2,1,0:T(8,128)}) custom-call(s32[3]{0:T(128)} %pad_add_fusion.place_ref.core_ref, f32[4,128,512]{2,1,0:T(8,128)} %get-tuple-element.39.own_ref, f32[4,128,512]{2,1,0:T(8,128)} %collective-permute-done.9.far_ref, ...), custom_call_target="tpu_custom_call" | custom-call | flops 1073741824 | bytes 6291456 | tf_op jit(solution)/shard_map/gradient_blocks/pallas_call | solution.py:431
  85.6 11.6 %solve_heads.5.own_ref = f32[4,128,512]{2,1,0:T(8,128)} custom-call(s32[3]{0:T(128)} %pad_add_fusion.place_ref.core_ref, f32[8]{0:T(128)} %regular_ref.7, bf16[512,1024]{1,0:T(8,128)(2,1)} %bitcast.28, bf16[512,1024]{1,0:T(8,128)(2,1)} %bitcast.17, bf16[512,1024]{1,0:T(8,128)(2,1)} %bitcast.22, f32[2,8,512]{2,1,0:T(8,128)} %get-tuple-element.29.refs_4_.refs_3_, ...), custom_call_target="tpu_custom_call" | custom-call | flops 2684354560 | bytes 3670016 | tf_op jit(solution)/shard_map/solve_heads/pallas_call | solution.py:345
  97.7 1.5 collective-permute-start.12
  99.2 1.5 collective-permute-start.14
  100.7 6.1 %gradient_blocks.3 = (f32[2,4,64,256]{3,2,1,0:T(8,128)}, f32[2,4,64,256]{3,2,1,0:T(8,128)}, f32[2,4,64,256]{3,2,1,0:T(8,128)}, f32[2,4,64,256]{3,2,1,0:T(8,128)}) custom-call(s32[3]{0:T(128)} %pad_add_fusion.place_ref.core_ref, f32[4,128,512]{2,1,0:T(8,128)} %solve_heads.5.own_ref, f32[4,128,512]{2,1,0:T(8,128)} %collective-permute-done.11.far_ref, ...), custom_call_target="tpu_custom_call" | custom-call | flops 1073741824 | bytes 6291456 | tf_op jit(solution)/shard_map/gradient_blocks/pallas_call | solution.py:431
  106.8 1.1 collective-permute-start.19
  107.9 1.5 collective-permute-start.21
  109.5 3.4 %collective-permute-done.12.refs_1_ = f32[2,4,64,256]{3,2,1,0:T(8,128)} collective-permute-done((f32[2,4,64,256]{3,2,1,0:T(8,128)}, f32[2,4,64,256]{3,2,1,0:T(8,128)}, u32[]{:S(2)}, u32[]{:S(2)}) %collective-permute-start.12) | collective-permute-done | bytes 524320 | tf_op jit(solution)/shard_map/ppermute | solution.py:614
  112.8 1.8 %sum_blocks.4 = f32[1,4,64,256]{3,2,1,0:T(8,128)} custom-call(f32[2,4,64,256]{3,2,1,0:T(8,128)} %get-tuple-element.40.refs_6_.refs_0_, f32[2,4,64,256]{3,2,1,0:T(8,128)} %collective-permute-done.12.refs_1_), custom_call_target="tpu_custom_call" | custom-call | bytes 786432 | tf_op jit(solution)/shard_map/sum_blocks/pallas_call | solution.py:465
  114.6 1.5 collective-permute-start.13
  116.1 1.8 %sum_blocks.5 = f32[1,4,64,256]{3,2,1,0:T(8,128)} custom-call(f32[2,4,64,256]{3,2,1,0:T(8,128)} %get-tuple-element.43.refs_0_.refs_3_, f32[2,4,64,256]{3,2,1,0:T(8,128)} %collective-permute-done.14.refs_1_.refs_4_), custom_call_target="tpu_custom_call" | custom-call | bytes 786432 | tf_op jit(solution)/shard_map/sum_blocks/pallas_call | solution.py:465
  117.9 1.5 collective-permute-start.15
  119.4 4.7 %collective-permute-done.19.refs_1_ = f32[2,4,64,256]{3,2,1,0:T(8,128)} collective-permute-done((f32[2,4,64,256]{3,2,1,0:T(8,128)}, f32[2,4,64,256]{3,2,1,0:T(8,128)}, u32[]{:S(2)}, u32[]{:S(2)}) %collective-permute-start.19) | collective-permute-done | bytes 524320 | tf_op jit(solution)/shard_map/ppermute | solution.py:614
  124.1 1.8 %sum_blocks.6 = f32[1,4,64,256]{3,2,1,0:T(8,128)} custom-call(f32[2,4,64,256]{3,2,1,0:T(8,128)} %get-tuple-element.41.refs_6_.refs_0_, f32[2,4,64,256]{3,2,1,0:T(8,128)} %collective-permute-done.19.refs_1_), custom_call_target="tpu_custom_call" | custom-call | bytes 786432 | tf_op jit(solution)/shard_map/sum_blocks/pallas_call | solution.py:465
  125.8 1.5 collective-permute-start.20
  127.4 1.8 %sum_blocks.7 = f32[1,4,64,256]{3,2,1,0:T(8,128)} custom-call(f32[2,4,64,256]{3,2,1,0:T(8,128)} %get-tuple-element.50.refs_0_.refs_3_, f32[2,4,64,256]{3,2,1,0:T(8,128)} %collective-permute-done.21.refs_1_.refs_4_), custom_call_target="tpu_custom_call" | custom-call | bytes 786432 | tf_op jit(solution)/shard_map/sum_blocks/pallas_call | solution.py:465
  129.1 1.5 collective-permute-start.22
  131.2 2.1 %merge_blocks.2 = (f32[128,256]{1,0:T(8,128)}, f32[128,256]{1,0:T(8,128)}, f32[128,256]{1,0:T(8,128)}, f32[128,256]{1,0:T(8,128)}) custom-call(f32[2,4,64,256]{3,2,1,0:T(8,128)} %get-tuple-element.40.refs_6_.refs_0_, f32[2,4,64,256]{3,2,1,0:T(8,128)} %collective-permute-done.12.refs_1_, f32[1,4,64,256]{3,2,1,0:T(8,128)} %collective-permute-done.13.refs_2_, ...), custom_call_target="tpu_custom_call" | custom-call | bytes 2097152 | tf_op jit(solution)/shard_map/merge_blocks/pallas_call | solution.py:495
  133.3 5.4 %collective-permute-start.16 = (f32[128,256]{1,0:T(8,128)}, f32[128,256]{1,0:T(8,128)}, u32[]{:S(2)}, u32[]{:S(2)}) collective-permute-start(f32[128,256]{1,0:T(8,128)} %get-tuple-element.46), channel_id=1, source_target_pairs={{0,2},{1,3},{2,0},{3,1},{4,6},{5,7},{6,4},{7,5},{8,10},{9,11},{10,... | collective-permute-start | bytes 393224 | tf_op jit(solution)/shard_map/ppermute | solution.py:622
  138.7 1.9 %collective-permute-start.17 = (f32[128,256]{1,0:T(8,128)}, f32[128,256]{1,0:T(8,128)}, u32[]{:S(2)}, u32[]{:S(2)}) collective-permute-start(f32[128,256]{1,0:T(8,128)} %get-tuple-element.47), channel_id=1, source_target_pairs={{0,4},{1,5},{2,6},{3,7},{4,0},{5,1},{6,2},{7,3},{8,12},{9,13},{10,... | collective-permute-start | bytes 393224 | tf_op jit(solution)/shard_map/ppermute | solution.py:622
  140.7 1.4 collective-permute-start.18
  142.1 2.2 %merge_blocks.3 = (f32[128,256]{1,0:T(8,128)}, f32[128,256]{1,0:T(8,128)}, f32[128,256]{1,0:T(8,128)}, f32[128,256]{1,0:T(8,128)}) custom-call(f32[2,4,64,256]{3,2,1,0:T(8,128)} %get-tuple-element.41.refs_6_.refs_0_, f32[2,4,64,256]{3,2,1,0:T(8,128)} %collective-permute-done.19.refs_1_, f32[1,4,64,256]{3,2,1,0:T(8,128)} %collective-permute-done.20.refs_2_, ...), custom_call_target="tpu_custom_call" | custom-call | bytes 2097152 | tf_op jit(solution)/shard_map/merge_blocks/pallas_call | solution.py:495
  144.3 0.6 collective-permute-start.23
  144.9 2.4 %collective-permute-start.24 = (f32[128,256]{1,0:T(8,128)}, f32[128,256]{1,0:T(8,128)}, u32[]{:S(2)}, u32[]{:S(2)}) collective-permute-start(f32[128,256]{1,0:T(8,128)} %get-tuple-element.54), channel_id=1, source_target_pairs={{0,4},{1,5},{2,6},{3,7},{4,0},{5,1},{6,2},{7,3},{8,12},{9,13},{10,... | collective-permute-start | bytes 393224 | tf_op jit(solution)/shard_map/ppermute | solution.py:622
  147.2 2.2 %collective-permute-start.25 = (f32[128,256]{1,0:T(8,128)}, f32[128,256]{1,0:T(8,128)}, u32[]{:S(2)}, u32[]{:S(2)}) collective-permute-start(f32[128,256]{1,0:T(8,128)} %get-tuple-element.55), channel_id=1, source_target_pairs={{0,6},{1,7},{2,4},{3,5},{4,2},{5,3},{6,0},{7,1},{8,14},{9,15},{10,... | collective-permute-start | bytes 393224 | tf_op jit(solution)/shard_map/ppermute | solution.py:622
  149.4 6.3 %solve_heads.6.refs_5_ = bf16[512,1024]{1,0:T(8,128)(2,1)} custom-call(s32[3]{0:T(128)} %pad_add_fusion.place_ref.core_ref, f32[8]{0:T(128)} %regular_ref.7, bf16[512,1024]{1,0:T(8,128)(2,1)} %convolution_convert_fusion.refs_0_, bf16[512,1024]{1,0:T(8,128)(2,1)} %bitcast.18, bf16[512,1024]{1,0:T(8,128)(2,1)} %bitcast.23, ...), custom_call_target="tpu_custom_call", output_to_operand_aliasing={{}: (7, {})} | custom-call | flops 1342177280 | bytes 1835008 | tf_op jit(solution)/shard_map/solve_heads/pallas_call | solution.py:345
  155.8 6.3 %solve_heads.7 = bf16[512,1024]{1,0:T(8,128)(2,1)} custom-call(s32[3]{0:T(128)} %pad_add_fusion.place_ref.core_ref, f32[8]{0:T(128)} %regular_ref.7, bf16[512,1024]{1,0:T(8,128)(2,1)} %convolution_convert_fusion.refs_0_, bf16[512,1024]{1,0:T(8,128)(2,1)} %bitcast.19, bf16[512,1024]{1,0:T(8,128)(2,1)} %bitcast.24, ...), custom_call_target="tpu_custom_call", output_to_operand_aliasing={{}: (7, {})} | custom-call | flops 1342177280 | bytes 1835008 | tf_op jit(solution)/shard_map/solve_heads/pallas_call | solution.py:345
  162.1 2.0 %finish.1 = f32[256,256]{1,0:T(8,128)} custom-call(f32[128,256]{1,0:T(8,128)} %get-tuple-element.45.refs_0_, f32[128,256]{1,0:T(8,128)} %collective-permute-done.16.refs_1_, f32[128,256]{1,0:T(8,128)} %collective-permute-done.17.refs_2_, f32[128,256]{1,0:T(8,128)} %collective-permute-done.18.refs_3_, f32[128,256]{1,0:T(8,128)} %get-tuple-element.52.refs_4_, ...), custom_call_target="tpu_custom_call" | custom-call | bytes 1310720 | tf_op jit(solution)/shard_map/finish/pallas_call | solution.py:523
  (25 shorter events, 2.1 us)
Async XLA Ops:
  6.2 2.2 %collective-permute-start = (f32[2,1,392,128]{3,2,1,0:T(8,128)}, f32[2,1,392,128]{3,2,1,0:T(8,128)}, u32[]{:S(2)}, u32[]{:S(2)}) collective-permute-start(f32[2,1,392,128]{3,2,1,0:T(8,128)} %get-tuple-element.31), channel_id=1, source_target_pairs={{0,1},{1,0},{2,3},{3,2},{4,5},{5,4},{6,7},{7,6},{8,9},{9,8},{10,11... | collective-permute-start | bytes 1204232 | tf_op jit(solution)/shard_map/ppermute | solution.py:566
  10.3 16.2 %collective-permute-start.7 = (f32[1,392,128]{2,1,0:T(8,128)}, f32[1,392,128]{2,1,0:T(8,128)}, u32[]{:S(2)}, u32[]{:S(2)}) collective-permute-start(f32[1,392,128]{2,1,0:T(8,128)} %get-tuple-element.35), channel_id=1, source_target_pairs={{0,6},{1,7},{8,14},{9,15},{16,22},{17,23},{24,30},{25,31}} | collective-permute-start | bytes 602120 | tf_op jit(solution)/shard_map/ppermute | solution.py:574
  17.8 9.4 %collective-permute-start.6 = (f32[1,392,128]{2,1,0:T(8,128)}, f32[1,392,128]{2,1,0:T(8,128)}, u32[]{:S(2)}, u32[]{:S(2)}) collective-permute-start(f32[1,392,128]{2,1,0:T(8,128)} %get-tuple-element.35), channel_id=1, source_target_pairs={{0,4},{1,5},{2,6},{3,7},{8,12},{9,13},{10,14},{11,15},{16,20},{17,... | collective-permute-start | bytes 602120 | tf_op jit(solution)/shard_map/ppermute | solution.py:574
  19.8 10.9 %collective-permute-start.5 = (f32[1,392,128]{2,1,0:T(8,128)}, f32[1,392,128]{2,1,0:T(8,128)}, u32[]{:S(2)}, u32[]{:S(2)}) collective-permute-start(f32[1,392,128]{2,1,0:T(8,128)} %get-tuple-element.35), channel_id=1, source_target_pairs={{0,2},{1,3},{2,4},{3,5},{4,6},{5,7},{8,10},{9,11},{10,12},{11,13},... | collective-permute-start | bytes 602120 | tf_op jit(solution)/shard_map/ppermute | solution.py:574
  26.5 49.3 %collective-permute-start.10 = (f32[4,512,256]{2,1,0:T(8,128)}, f32[4,512,256]{2,1,0:T(8,128)}, u32[]{:S(2)}, u32[]{:S(2)}) collective-permute-start(f32[4,512,256]{2,1,0:T(8,128)} %pick_columns.1), channel_id=1, source_target_pairs={{0,1},{1,0},{2,3},{3,2},{4,5},{5,4},{6,7},{7,6},{8,9},{9,8},{10,11... | collective-permute-start | bytes 6291464 | tf_op jit(solution)/shard_map/ppermute | solution.py:580
  32.8 6.2 %collective-permute-start.8 = (f32[1,392,128]{2,1,0:T(8,128)}, f32[1,392,128]{2,1,0:T(8,128)}, u32[]{:S(2)}, u32[]{:S(2)}) collective-permute-start(f32[1,392,128]{2,1,0:T(8,128)} %get-tuple-element.37), channel_id=1, source_target_pairs={{0,1},{1,0},{2,3},{3,2},{4,5},{5,4},{6,7},{7,6},{8,9},{9,8},{10,11... | collective-permute-start | bytes 602120 | tf_op jit(solution)/shard_map/ppermute | solution.py:577
  53.2 26.2 %collective-permute-start.9 = (f32[4,128,512]{2,1,0:T(8,128)}, f32[4,128,512]{2,1,0:T(8,128)}, u32[]{:S(2)}, u32[]{:S(2)}) collective-permute-start(f32[4,128,512]{2,1,0:T(8,128)} %get-tuple-element.39.own_ref), channel_id=1, source_target_pairs={{0,1},{1,0},{2,3},{3,2},{4,5},{5,4},{6,7},{7,6},{8,9},{9,8},{10,11... | collective-permute-start | bytes 3145736 | tf_op jit(solution)/shard_map/ppermute | solution.py:598
  53.7 13.5 %collective-permute-start.3 = (f32[1,392,128]{2,1,0:T(8,128)}, f32[1,392,128]{2,1,0:T(8,128)}, u32[]{:S(2)}, u32[]{:S(2)}) collective-permute-start(f32[1,392,128]{2,1,0:T(8,128)} %get-tuple-element.32), channel_id=1, source_target_pairs={{0,6},{1,7},{8,14},{9,15},{16,22},{17,23},{24,30},{25,31}} | collective-permute-start | bytes 602120 | tf_op jit(solution)/shard_map/ppermute | solution.py:574
  60.6 9.7 %collective-permute-start.2 = (f32[1,392,128]{2,1,0:T(8,128)}, f32[1,392,128]{2,1,0:T(8,128)}, u32[]{:S(2)}, u32[]{:S(2)}) collective-permute-start(f32[1,392,128]{2,1,0:T(8,128)} %get-tuple-element.32), channel_id=1, source_target_pairs={{0,4},{1,5},{2,6},{3,7},{8,12},{9,13},{10,14},{11,15},{16,20},{17,... | collective-permute-start | bytes 602120 | tf_op jit(solution)/shard_map/ppermute | solution.py:574
  65.3 8.4 %collective-permute-start.1 = (f32[1,392,128]{2,1,0:T(8,128)}, f32[1,392,128]{2,1,0:T(8,128)}, u32[]{:S(2)}, u32[]{:S(2)}) collective-permute-start(f32[1,392,128]{2,1,0:T(8,128)} %get-tuple-element.32), channel_id=1, source_target_pairs={{0,2},{1,3},{2,4},{3,5},{4,6},{5,7},{8,10},{9,11},{10,12},{11,13},... | collective-permute-start | bytes 602120 | tf_op jit(solution)/shard_map/ppermute | solution.py:574
  75.8 9.8 %collective-permute-start.4 = (f32[1,392,128]{2,1,0:T(8,128)}, f32[1,392,128]{2,1,0:T(8,128)}, u32[]{:S(2)}, u32[]{:S(2)}) collective-permute-start(f32[1,392,128]{2,1,0:T(8,128)} %get-tuple-element.33), channel_id=1, source_target_pairs={{0,1},{1,0},{2,3},{3,2},{4,5},{5,4},{6,7},{7,6},{8,9},{9,8},{10,11... | collective-permute-start | bytes 602120 | tf_op jit(solution)/shard_map/ppermute | solution.py:577
  97.2 3.5 %collective-permute-start.11 = (f32[4,128,512]{2,1,0:T(8,128)}, f32[4,128,512]{2,1,0:T(8,128)}, u32[]{:S(2)}, u32[]{:S(2)}) collective-permute-start(f32[4,128,512]{2,1,0:T(8,128)} %solve_heads.5.own_ref), channel_id=1, source_target_pairs={{0,1},{1,0},{2,3},{3,2},{4,5},{5,4},{6,7},{7,6},{8,9},{9,8},{10,11... | collective-permute-start | bytes 3145736 | tf_op jit(solution)/shard_map/ppermute | solution.py:598
  97.7 15.1 %collective-permute-start.12 = (f32[2,4,64,256]{3,2,1,0:T(8,128)}, f32[2,4,64,256]{3,2,1,0:T(8,128)}, u32[]{:S(2)}, u32[]{:S(2)}) collective-permute-start(f32[2,4,64,256]{3,2,1,0:T(8,128)} %get-tuple-element.42), channel_id=1, source_target_pairs={{0,8},{8,0},{16,24},{24,16},{1,9},{9,1},{17,25},{25,17},{2,10},{10... | collective-permute-start | bytes 1572872 | tf_op jit(solution)/shard_map/ppermute | solution.py:614
  99.2 16.9 %collective-permute-start.14 = (f32[2,4,64,256]{3,2,1,0:T(8,128)}, f32[2,4,64,256]{3,2,1,0:T(8,128)}, u32[]{:S(2)}, u32[]{:S(2)}) collective-permute-start(f32[2,4,64,256]{3,2,1,0:T(8,128)} %get-tuple-element.44), channel_id=1, source_target_pairs={{0,16},{8,24},{16,0},{24,8},{1,17},{9,25},{17,1},{25,9},{2,18},{10... | collective-permute-start | bytes 1572872 | tf_op jit(solution)/shard_map/ppermute | solution.py:614
  106.8 17.2 %collective-permute-start.19 = (f32[2,4,64,256]{3,2,1,0:T(8,128)}, f32[2,4,64,256]{3,2,1,0:T(8,128)}, u32[]{:S(2)}, u32[]{:S(2)}) collective-permute-start(f32[2,4,64,256]{3,2,1,0:T(8,128)} %get-tuple-element.49), channel_id=1, source_target_pairs={{0,8},{8,0},{16,24},{24,16},{1,9},{9,1},{17,25},{25,17},{2,10},{10... | collective-permute-start | bytes 1572872 | tf_op jit(solution)/shard_map/ppermute | solution.py:614
  107.9 19.4 %collective-permute-start.21 = (f32[2,4,64,256]{3,2,1,0:T(8,128)}, f32[2,4,64,256]{3,2,1,0:T(8,128)}, u32[]{:S(2)}, u32[]{:S(2)}) collective-permute-start(f32[2,4,64,256]{3,2,1,0:T(8,128)} %get-tuple-element.51), channel_id=1, source_target_pairs={{0,16},{8,24},{16,0},{24,8},{1,17},{9,25},{17,1},{25,9},{2,18},{10... | collective-permute-start | bytes 1572872 | tf_op jit(solution)/shard_map/ppermute | solution.py:614
  114.6 16.6 %collective-permute-start.13 = (f32[1,4,64,256]{3,2,1,0:T(8,128)}, f32[1,4,64,256]{3,2,1,0:T(8,128)}, u32[]{:S(2)}, u32[]{:S(2)}) collective-permute-start(f32[1,4,64,256]{3,2,1,0:T(8,128)} %sum_blocks.4), channel_id=1, source_target_pairs={{0,16},{8,24},{16,0},{24,8},{1,17},{9,25},{17,1},{25,9},{2,18},{10... | collective-permute-start | bytes 786440 | tf_op jit(solution)/shard_map/ppermute | solution.py:614
  117.9 13.3 %collective-permute-start.15 = (f32[1,4,64,256]{3,2,1,0:T(8,128)}, f32[1,4,64,256]{3,2,1,0:T(8,128)}, u32[]{:S(2)}, u32[]{:S(2)}) collective-permute-start(f32[1,4,64,256]{3,2,1,0:T(8,128)} %sum_blocks.5), channel_id=1, source_target_pairs={{0,8},{8,0},{16,24},{24,16},{1,9},{9,1},{17,25},{25,17},{2,10},{10... | collective-permute-start | bytes 786440 | tf_op jit(solution)/shard_map/ppermute | solution.py:614
  125.8 16.3 %collective-permute-start.20 = (f32[1,4,64,256]{3,2,1,0:T(8,128)}, f32[1,4,64,256]{3,2,1,0:T(8,128)}, u32[]{:S(2)}, u32[]{:S(2)}) collective-permute-start(f32[1,4,64,256]{3,2,1,0:T(8,128)} %sum_blocks.6), channel_id=1, source_target_pairs={{0,16},{8,24},{16,0},{24,8},{1,17},{9,25},{17,1},{25,9},{2,18},{10... | collective-permute-start | bytes 786440 | tf_op jit(solution)/shard_map/ppermute | solution.py:614
  129.1 13.0 %collective-permute-start.22 = (f32[1,4,64,256]{3,2,1,0:T(8,128)}, f32[1,4,64,256]{3,2,1,0:T(8,128)}, u32[]{:S(2)}, u32[]{:S(2)}) collective-permute-start(f32[1,4,64,256]{3,2,1,0:T(8,128)} %sum_blocks.7), channel_id=1, source_target_pairs={{0,8},{8,0},{16,24},{24,16},{1,9},{9,1},{17,25},{25,17},{2,10},{10... | collective-permute-start | bytes 786440 | tf_op jit(solution)/shard_map/ppermute | solution.py:614
  133.3 13.9 %collective-permute-start.16 = (f32[128,256]{1,0:T(8,128)}, f32[128,256]{1,0:T(8,128)}, u32[]{:S(2)}, u32[]{:S(2)}) collective-permute-start(f32[128,256]{1,0:T(8,128)} %get-tuple-element.46), channel_id=1, source_target_pairs={{0,2},{1,3},{2,0},{3,1},{4,6},{5,7},{6,4},{7,5},{8,10},{9,11},{10,... | collective-permute-start | bytes 393224 | tf_op jit(solution)/shard_map/ppermute | solution.py:622
  138.7 23.4 %collective-permute-start.17 = (f32[128,256]{1,0:T(8,128)}, f32[128,256]{1,0:T(8,128)}, u32[]{:S(2)}, u32[]{:S(2)}) collective-permute-start(f32[128,256]{1,0:T(8,128)} %get-tuple-element.47), channel_id=1, source_target_pairs={{0,4},{1,5},{2,6},{3,7},{4,0},{5,1},{6,2},{7,3},{8,12},{9,13},{10,... | collective-permute-start | bytes 393224 | tf_op jit(solution)/shard_map/ppermute | solution.py:622
  140.7 21.4 %collective-permute-start.18 = (f32[128,256]{1,0:T(8,128)}, f32[128,256]{1,0:T(8,128)}, u32[]{:S(2)}, u32[]{:S(2)}) collective-permute-start(f32[128,256]{1,0:T(8,128)} %get-tuple-element.48), channel_id=1, source_target_pairs={{0,6},{1,7},{2,4},{3,5},{4,2},{5,3},{6,0},{7,1},{8,14},{9,15},{10,... | collective-permute-start | bytes 393224 | tf_op jit(solution)/shard_map/ppermute | solution.py:622
  144.3 17.8 %collective-permute-start.23 = (f32[128,256]{1,0:T(8,128)}, f32[128,256]{1,0:T(8,128)}, u32[]{:S(2)}, u32[]{:S(2)}) collective-permute-start(f32[128,256]{1,0:T(8,128)} %get-tuple-element.53), channel_id=1, source_target_pairs={{0,2},{1,3},{2,0},{3,1},{4,6},{5,7},{6,4},{7,5},{8,10},{9,11},{10,... | collective-permute-start | bytes 393224 | tf_op jit(solution)/shard_map/ppermute | solution.py:622
  144.9 17.3 %collective-permute-start.24 = (f32[128,256]{1,0:T(8,128)}, f32[128,256]{1,0:T(8,128)}, u32[]{:S(2)}, u32[]{:S(2)}) collective-permute-start(f32[128,256]{1,0:T(8,128)} %get-tuple-element.54), channel_id=1, source_target_pairs={{0,4},{1,5},{2,6},{3,7},{4,0},{5,1},{6,2},{7,3},{8,12},{9,13},{10,... | collective-permute-start | bytes 393224 | tf_op jit(solution)/shard_map/ppermute | solution.py:622
  147.2 14.9 %collective-permute-start.25 = (f32[128,256]{1,0:T(8,128)}, f32[128,256]{1,0:T(8,128)}, u32[]{:S(2)}, u32[]{:S(2)}) collective-permute-start(f32[128,256]{1,0:T(8,128)} %get-tuple-element.55), channel_id=1, source_target_pairs={{0,6},{1,7},{2,4},{3,5},{4,2},{5,3},{6,0},{7,1},{8,14},{9,15},{10,... | collective-permute-start | bytes 393224 | tf_op jit(solution)/shard_map/ppermute | solution.py:622

commit v8 on v7

--- a/solution.py
+++ b/solution.py
@@ -379,24 +379,6 @@
     )(core, tokens)
 
 
-def narrow_kernel(in_ref, out_ref):
-    out_ref[...] = in_ref[...].astype(BF16)
-
-
-def narrow(blocks):
-    spec = pl.BlockSpec((1,) + blocks.shape[1:], lambda z: (z, 0, 0))
-    return pl.pallas_call(
-        narrow_kernel,
-        out_shape=jax.ShapeDtypeStruct(blocks.shape, BF16),
-        grid=(blocks.shape[0],),
-        in_specs=[spec],
-        out_specs=spec,
-        cost_estimate=pl.CostEstimate(flops=0, bytes_accessed=6 * blocks.size, transcendentals=0),
-        compiler_params=FULL,
-        name="narrow",
-    )(blocks)
-
-
 def gradient_kernel(order, place_ref, own_ref, far_ref, tokens_ref, other_ref, *rest):
     outs, left_ref = rest[:-1], rest[-1]
     core, group = place_ref[0], place_ref[1]
@@ -414,7 +396,7 @@
             left_ref[away, :, rows:] = far_ref[i].astype(BF16)
 
     left = left_ref[...].reshape(2 * half * dim, 2 * rows)
-    result = dot(left, jnp.concatenate([tokens_ref[...], other_ref[0]], axis=0))
+    result = dot(left, jnp.concatenate([tokens_ref[...], other_ref[0].astype(BF16)], axis=0))
     for d in range(2 * half):
         for path in range(2):
             which, index = order[path][d]
@@ -578,7 +560,6 @@
 
     picked = pick_columns(place, tokens, chips)
     other = lax.ppermute(picked, "seq", partner)
-    other = narrow(other)
     queries = jnp.dot(tokens, w_query, preferred_element_type=F32).astype(BF16)
 
     dp_bits = groups.bit_length() - 1

time: 165 us -> 161 us (0.976)
  Pallas kernels: 83.1 us -> 79.9 us
    pallas_call x1 -> x0, Pallas kernels: 3.61 us -> none  [narrow(): pl.pallas_call(narrow_kernel, out_shape=jax.ShapeDtypeStruct(blocks.shape...]
  transfers between devices with their start and end apart: 26 -> 26, of which waited for: 8 -> 8; matrix products, arithmetic and copies ran while one was open for 4% -> 4% of each run, Pallas kernels for 38% -> 37%
where the time goes in v8:
time: 161 us
  Pallas kernels  79.9 us (50%)
  starting transfers between devices  52.5 us (33%)
  waiting for transfers between devices  20.7 us (13%)
  matrix products  6.19 us (4%)
    pallas_call x4, Pallas kernels, solve_heads(): pl.pallas_call(functools.partial(solve_kernel, with_query, with_gradient,...  38.5 us
    ppermute x6, starting transfers between devices, program(): sent.append(lax.ppermute(chip_state, 'seq', pairs))  25.5 us
    ppermute x6, starting transfers between devices, program(): finished[-1].append(lax.ppermute(other_block, 'seq', pairs))  13.8 us
    pallas_call x2, Pallas kernels, gradient_blocks(): pl.pallas_call(functools.partial(gradient_kernel, order), out_shape=[out]...  12.6 us
    ppermute x8, starting transfers between devices, program(): held.append(lax.ppermute(send, 'dp', pairs))  11.7 us
    ppermute x6, waiting for transfers between devices, program(): sent.append(lax.ppermute(chip_state, 'seq', pairs))  10.5 us
    ppermute x8, waiting for transfers between devices, program(): held.append(lax.ppermute(send, 'dp', pairs))  8.46 us
    pallas_call x4, Pallas kernels, sum_blocks(): pl.pallas_call(sum_kernel, out_shape=out, in_specs=[spec] * len(arrays),...  7.07 us
  transfers between devices with their start and end apart: 26, of which 8 were waited for; matrix products, arithmetic and copies ran while one was open for 4% of the time, Pallas kernels for 37%

profile of v8, /device:TPU:0, one launch (start us, length us, event | category | flops | bytes accessed | tf_op | source)
XLA Modules:
  0.0 160.6 jit_solution(2651045080204144543)
XLA Ops:
  0.6 0.6 pad_add_fusion.place_ref.core_ref
  1.2 4.9 %local_states.1 = (f32[2,1,392,128]{3,2,1,0:T(8,128)}, f32[2,1,392,128]{3,2,1,0:T(8,128)}, f32[2,8,512]{2,1,0:T(8,128)}) custom-call(s32[3]{0:T(128)} %pad_add_fusion.place_ref.core_ref, bf16[512,1024]{1,0:T(8,128)(2,1)} %bitcast.15, bf16[512,1024]{1,0:T(8,128)(2,1)} %bitcast.20, f32[8,512]{1,0:T(8,128)} %bitcast.26), custom_call_target="tpu_custom_call" | custom-call | flops 536870912 | bytes 4194304 | tf_op jit(solution)/shard_map/local_states/pallas_call | solution.py:122
  6.6 1.7 %collective-permute-done.came_ref = f32[2,1,392,128]{3,2,1,0:T(8,128)} collective-permute-done((f32[2,1,392,128]{3,2,1,0:T(8,128)}, f32[2,1,392,128]{3,2,1,0:T(8,128)}, u32[]{:S(2)}, u32[]{:S(2)}) %collective-permute-start) | collective-permute-done | bytes 401440 | tf_op jit(solution)/shard_map/ppermute | solution.py:548
  8.3 1.9 %shard_map.86 = (f32[1,392,128]{2,1,0:T(8,128)}, f32[1,392,128]{2,1,0:T(8,128)}) custom-call(s32[3]{0:T(128)} %pad_add_fusion.place_ref.core_ref, f32[2,1,392,128]{3,2,1,0:T(8,128)} %get-tuple-element.30.own_ref, f32[2,1,392,128]{3,2,1,0:T(8,128)} %collective-permute-done.came_ref), custom_call_target="tpu_custom_call" | custom-call | bytes 1605632 | tf_op jit(solution)/shard_map/pallas_call | solution.py:167
  10.2 7.5 %collective-permute-start.7 = (f32[1,392,128]{2,1,0:T(8,128)}, f32[1,392,128]{2,1,0:T(8,128)}, u32[]{:S(2)}, u32[]{:S(2)}) collective-permute-start(f32[1,392,128]{2,1,0:T(8,128)} %get-tuple-element.35), channel_id=1, source_target_pairs={{0,6},{1,7},{8,14},{9,15},{16,22},{17,23},{24,30},{25,31}} | collective-permute-start | bytes 602120 | tf_op jit(solution)/shard_map/ppermute | solution.py:556
  17.8 2.0 %collective-permute-start.6 = (f32[1,392,128]{2,1,0:T(8,128)}, f32[1,392,128]{2,1,0:T(8,128)}, u32[]{:S(2)}, u32[]{:S(2)}) collective-permute-start(f32[1,392,128]{2,1,0:T(8,128)} %get-tuple-element.35), channel_id=1, source_target_pairs={{0,4},{1,5},{2,6},{3,7},{8,12},{9,13},{10,14},{11,15},{16,20},{17,... | collective-permute-start | bytes 602120 | tf_op jit(solution)/shard_map/ppermute | solution.py:556
  19.7 2.5 %collective-permute-start.5 = (f32[1,392,128]{2,1,0:T(8,128)}, f32[1,392,128]{2,1,0:T(8,128)}, u32[]{:S(2)}, u32[]{:S(2)}) collective-permute-start(f32[1,392,128]{2,1,0:T(8,128)} %get-tuple-element.35), channel_id=1, source_target_pairs={{0,2},{1,3},{2,4},{3,5},{4,6},{5,7},{8,10},{9,11},{10,12},{11,13},... | collective-permute-start | bytes 602120 | tf_op jit(solution)/shard_map/ppermute | solution.py:556
  22.2 4.3 %pick_columns.1 = f32[4,512,256]{2,1,0:T(8,128)} custom-call(s32[3]{0:T(128)} %pad_add_fusion.place_ref.core_ref, bf16[512,2048]{1,0:T(8,128)(2,1)} %bitcast.12), custom_call_target="tpu_custom_call" | custom-call | bytes 3145728 | tf_op jit(solution)/shard_map/pick_columns/pallas_call | solution.py:367
  26.5 0.7 collective-permute-done.6.refs_1_
  27.1 3.5 %collective-permute-done.5.refs_0_ = f32[1,392,128]{2,1,0:T(8,128)} collective-permute-done((f32[1,392,128]{2,1,0:T(8,128)}, f32[1,392,128]{2,1,0:T(8,128)}, u32[]{:S(2)}, u32[]{:S(2)}) %collective-permute-start.5) | collective-permute-done | bytes 200736 | tf_op jit(solution)/shard_map/ppermute | solution.py:556
  30.6 2.2 %shard_map.88 = (f32[1,392,128]{2,1,0:T(8,128)}, f32[1,392,128]{2,1,0:T(8,128)}) custom-call(s32[3]{0:T(128)} %pad_add_fusion.place_ref.core_ref, f32[2,1,392,128]{3,2,1,0:T(8,128)} %get-tuple-element.30.own_ref, f32[2,1,392,128]{3,2,1,0:T(8,128)} %collective-permute-done.came_ref, f32[1,392,128]{2,1,0:T(8,128)} %collective-permute-done.5.refs_0_, ...), custom_call_target="tpu_custom_call" | custom-call | bytes 2809856 | tf_op jit(solution)/shard_map/pallas_call | solution.py:167
  32.8 6.2 %convolution_convert_fusion.refs_0_ = bf16[512,1024]{1,0:T(8,128)(2,1)} fusion(bf16[2048,1024]{1,0:T(8,128)(2,1)} %param.8, bf16[1,512,2048]{2,1,0:T(8,128)(2,1)} %param.7), kind=kOutput, calls=%fused_computation | convolution fusion | flops 2148007936 | bytes 7340032 | tf_op jit(solution)/shard_map/dot_general | solution.py:563
  39.0 14.2 %solve_heads.4 = (bf16[512,1024]{1,0:T(8,128)(2,1)}, f32[4,128,512]{2,1,0:T(8,128)}) custom-call(s32[3]{0:T(128)} %pad_add_fusion.place_ref.core_ref, f32[8]{0:T(128)} %regular_ref.7, bf16[512,1024]{1,0:T(8,128)(2,1)} %convolution_convert_fusion.refs_0_, bf16[512,1024]{1,0:T(8,128)(2,1)} %bitcast.27, bf16[512,1024]{1,0:T(8,128)(2,1)} %bitcast.16, ...), custom_call_target="tpu_custom_call" | custom-call | flops 2684354560 | bytes 3670016 | tf_op jit(solution)/shard_map/solve_heads/pallas_call | solution.py:345
  53.7 6.9 %collective-permute-start.3 = (f32[1,392,128]{2,1,0:T(8,128)}, f32[1,392,128]{2,1,0:T(8,128)}, u32[]{:S(2)}, u32[]{:S(2)}) collective-permute-start(f32[1,392,128]{2,1,0:T(8,128)} %get-tuple-element.32), channel_id=1, source_target_pairs={{0,6},{1,7},{8,14},{9,15},{16,22},{17,23},{24,30},{25,31}} | collective-permute-start | bytes 602120 | tf_op jit(solution)/shard_map/ppermute | solution.py:556
  60.6 4.7 %collective-permute-start.2 = (f32[1,392,128]{2,1,0:T(8,128)}, f32[1,392,128]{2,1,0:T(8,128)}, u32[]{:S(2)}, u32[]{:S(2)}) collective-permute-start(f32[1,392,128]{2,1,0:T(8,128)} %get-tuple-element.32), channel_id=1, source_target_pairs={{0,4},{1,5},{2,6},{3,7},{8,12},{9,13},{10,14},{11,15},{16,20},{17,... | collective-permute-start | bytes 602120 | tf_op jit(solution)/shard_map/ppermute | solution.py:556
  65.2 2.0 %collective-permute-start.1 = (f32[1,392,128]{2,1,0:T(8,128)}, f32[1,392,128]{2,1,0:T(8,128)}, u32[]{:S(2)}, u32[]{:S(2)}) collective-permute-start(f32[1,392,128]{2,1,0:T(8,128)} %get-tuple-element.32), channel_id=1, source_target_pairs={{0,2},{1,3},{2,4},{3,5},{4,6},{5,7},{8,10},{9,11},{10,12},{11,13},... | collective-permute-start | bytes 602120 | tf_op jit(solution)/shard_map/ppermute | solution.py:556
  67.2 3.0 %collective-permute-done.2.refs_1_ = f32[1,392,128]{2,1,0:T(8,128)} collective-permute-done((f32[1,392,128]{2,1,0:T(8,128)}, f32[1,392,128]{2,1,0:T(8,128)}, u32[]{:S(2)}, u32[]{:S(2)}) %collective-permute-start.2) | collective-permute-done | bytes 200736 | tf_op jit(solution)/shard_map/ppermute | solution.py:556
  70.2 3.4 %collective-permute-done.1.refs_0_ = f32[1,392,128]{2,1,0:T(8,128)} collective-permute-done((f32[1,392,128]{2,1,0:T(8,128)}, f32[1,392,128]{2,1,0:T(8,128)}, u32[]{:S(2)}, u32[]{:S(2)}) %collective-permute-start.1) | collective-permute-done | bytes 200736 | tf_op jit(solution)/shard_map/ppermute | solution.py:556
  73.6 2.2 %shard_map.87 = (f32[1,392,128]{2,1,0:T(8,128)}, f32[1,392,128]{2,1,0:T(8,128)}) custom-call(s32[3]{0:T(128)} %pad_add_fusion.place_ref.core_ref, f32[2,1,392,128]{3,2,1,0:T(8,128)} %get-tuple-element.30.own_ref, f32[2,1,392,128]{3,2,1,0:T(8,128)} %collective-permute-done.came_ref, f32[1,392,128]{2,1,0:T(8,128)} %collective-permute-done.1.refs_0_, ...), custom_call_target="tpu_custom_call" | custom-call | bytes 2809856 | tf_op jit(solution)/shard_map/pallas_call | solution.py:167
  75.8 6.3 %gradient_blocks.2 = (f32[2,4,64,256]{3,2,1,0:T(8,128)}, f32[2,4,64,256]{3,2,1,0:T(8,128)}, f32[2,4,64,256]{3,2,1,0:T(8,128)}, f32[2,4,64,256]{3,2,1,0:T(8,128)}) custom-call(s32[3]{0:T(128)} %pad_add_fusion.place_ref.core_ref, f32[4,128,512]{2,1,0:T(8,128)} %get-tuple-element.39.own_ref, f32[4,128,512]{2,1,0:T(8,128)} %collective-permute-done.9.far_ref, ...), custom_call_target="tpu_custom_call" | custom-call | flops 1073741824 | bytes 6291456 | tf_op jit(solution)/shard_map/gradient_blocks/pallas_call | solution.py:413
  82.1 11.6 %solve_heads.5.own_ref = f32[4,128,512]{2,1,0:T(8,128)} custom-call(s32[3]{0:T(128)} %pad_add_fusion.place_ref.core_ref, f32[8]{0:T(128)} %regular_ref.7, bf16[512,1024]{1,0:T(8,128)(2,1)} %bitcast.28, bf16[512,1024]{1,0:T(8,128)(2,1)} %bitcast.17, bf16[512,1024]{1,0:T(8,128)(2,1)} %bitcast.22, f32[2,8,512]{2,1,0:T(8,128)} %get-tuple-element.29.refs_4_.refs_3_, ...), custom_call_target="tpu_custom_call" | custom-call | flops 2684354560 | bytes 3670016 | tf_op jit(solution)/shard_map/solve_heads/pallas_call | solution.py:345
  94.2 1.5 collective-permute-start.12
  95.7 1.5 collective-permute-start.14
  97.2 6.3 %gradient_blocks.3 = (f32[2,4,64,256]{3,2,1,0:T(8,128)}, f32[2,4,64,256]{3,2,1,0:T(8,128)}, f32[2,4,64,256]{3,2,1,0:T(8,128)}, f32[2,4,64,256]{3,2,1,0:T(8,128)}) custom-call(s32[3]{0:T(128)} %pad_add_fusion.place_ref.core_ref, f32[4,128,512]{2,1,0:T(8,128)} %solve_heads.5.own_ref, f32[4,128,512]{2,1,0:T(8,128)} %collective-permute-done.11.far_ref, ...), custom_call_target="tpu_custom_call" | custom-call | flops 1073741824 | bytes 6291456 | tf_op jit(solution)/shard_map/gradient_blocks/pallas_call | solution.py:413
  103.5 1.1 collective-permute-start.19
  104.6 1.5 collective-permute-start.21
  106.1 3.2 %collective-permute-done.12.refs_1_ = f32[2,4,64,256]{3,2,1,0:T(8,128)} collective-permute-done((f32[2,4,64,256]{3,2,1,0:T(8,128)}, f32[2,4,64,256]{3,2,1,0:T(8,128)}, u32[]{:S(2)}, u32[]{:S(2)}) %collective-permute-start.12) | collective-permute-done | bytes 524320 | tf_op jit(solution)/shard_map/ppermute | solution.py:595
  109.3 1.8 %sum_blocks.4 = f32[1,4,64,256]{3,2,1,0:T(8,128)} custom-call(f32[2,4,64,256]{3,2,1,0:T(8,128)} %get-tuple-element.40.refs_6_.refs_0_, f32[2,4,64,256]{3,2,1,0:T(8,128)} %collective-permute-done.12.refs_1_), custom_call_target="tpu_custom_call" | custom-call | bytes 786432 | tf_op jit(solution)/shard_map/sum_blocks/pallas_call | solution.py:447
  111.1 1.5 collective-permute-start.13
  112.6 1.8 %sum_blocks.5 = f32[1,4,64,256]{3,2,1,0:T(8,128)} custom-call(f32[2,4,64,256]{3,2,1,0:T(8,128)} %get-tuple-element.43.refs_0_.refs_3_, f32[2,4,64,256]{3,2,1,0:T(8,128)} %collective-permute-done.14.refs_1_.refs_4_), custom_call_target="tpu_custom_call" | custom-call | bytes 786432 | tf_op jit(solution)/shard_map/sum_blocks/pallas_call | solution.py:447
  114.4 1.5 collective-permute-start.15
  115.9 4.7 %collective-permute-done.19.refs_1_ = f32[2,4,64,256]{3,2,1,0:T(8,128)} collective-permute-done((f32[2,4,64,256]{3,2,1,0:T(8,128)}, f32[2,4,64,256]{3,2,1,0:T(8,128)}, u32[]{:S(2)}, u32[]{:S(2)}) %collective-permute-start.19) | collective-permute-done | bytes 524320 | tf_op jit(solution)/shard_map/ppermute | solution.py:595
  120.6 1.8 %sum_blocks.6 = f32[1,4,64,256]{3,2,1,0:T(8,128)} custom-call(f32[2,4,64,256]{3,2,1,0:T(8,128)} %get-tuple-element.41.refs_6_.refs_0_, f32[2,4,64,256]{3,2,1,0:T(8,128)} %collective-permute-done.19.refs_1_), custom_call_target="tpu_custom_call" | custom-call | bytes 786432 | tf_op jit(solution)/shard_map/sum_blocks/pallas_call | solution.py:447
  122.4 1.5 collective-permute-start.20
  123.9 1.8 %sum_blocks.7 = f32[1,4,64,256]{3,2,1,0:T(8,128)} custom-call(f32[2,4,64,256]{3,2,1,0:T(8,128)} %get-tuple-element.50.refs_0_.refs_3_, f32[2,4,64,256]{3,2,1,0:T(8,128)} %collective-permute-done.21.refs_1_.refs_4_), custom_call_target="tpu_custom_call" | custom-call | bytes 786432 | tf_op jit(solution)/shard_map/sum_blocks/pallas_call | solution.py:447
  125.6 1.5 collective-permute-start.22
  127.1 0.6 collective-permute-done.13.refs_2_
  127.7 2.2 %merge_blocks.2 = (f32[128,256]{1,0:T(8,128)}, f32[128,256]{1,0:T(8,128)}, f32[128,256]{1,0:T(8,128)}, f32[128,256]{1,0:T(8,128)}) custom-call(f32[2,4,64,256]{3,2,1,0:T(8,128)} %get-tuple-element.40.refs_6_.refs_0_, f32[2,4,64,256]{3,2,1,0:T(8,128)} %collective-permute-done.12.refs_1_, f32[1,4,64,256]{3,2,1,0:T(8,128)} %collective-permute-done.13.refs_2_, ...), custom_call_target="tpu_custom_call" | custom-call | bytes 2097152 | tf_op jit(solution)/shard_map/merge_blocks/pallas_call | solution.py:477
  129.8 5.4 %collective-permute-start.16 = (f32[128,256]{1,0:T(8,128)}, f32[128,256]{1,0:T(8,128)}, u32[]{:S(2)}, u32[]{:S(2)}) collective-permute-start(f32[128,256]{1,0:T(8,128)} %get-tuple-element.46), channel_id=1, source_target_pairs={{0,2},{1,3},{2,0},{3,1},{4,6},{5,7},{6,4},{7,5},{8,10},{9,11},{10,... | collective-permute-start | bytes 393224 | tf_op jit(solution)/shard_map/ppermute | solution.py:603
  135.3 1.9 %collective-permute-start.17 = (f32[128,256]{1,0:T(8,128)}, f32[128,256]{1,0:T(8,128)}, u32[]{:S(2)}, u32[]{:S(2)}) collective-permute-start(f32[128,256]{1,0:T(8,128)} %get-tuple-element.47), channel_id=1, source_target_pairs={{0,4},{1,5},{2,6},{3,7},{4,0},{5,1},{6,2},{7,3},{8,12},{9,13},{10,... | collective-permute-start | bytes 393224 | tf_op jit(solution)/shard_map/ppermute | solution.py:603
  137.2 1.4 collective-permute-start.18
  138.6 2.2 %merge_blocks.3 = (f32[128,256]{1,0:T(8,128)}, f32[128,256]{1,0:T(8,128)}, f32[128,256]{1,0:T(8,128)}, f32[128,256]{1,0:T(8,128)}) custom-call(f32[2,4,64,256]{3,2,1,0:T(8,128)} %get-tuple-element.41.refs_6_.refs_0_, f32[2,4,64,256]{3,2,1,0:T(8,128)} %collective-permute-done.19.refs_1_, f32[1,4,64,256]{3,2,1,0:T(8,128)} %collective-permute-done.20.refs_2_, ...), custom_call_target="tpu_custom_call" | custom-call | bytes 2097152 | tf_op jit(solution)/shard_map/merge_blocks/pallas_call | solution.py:477
  140.8 0.6 collective-permute-start.23
  141.4 2.4 %collective-permute-start.24 = (f32[128,256]{1,0:T(8,128)}, f32[128,256]{1,0:T(8,128)}, u32[]{:S(2)}, u32[]{:S(2)}) collective-permute-start(f32[128,256]{1,0:T(8,128)} %get-tuple-element.54), channel_id=1, source_target_pairs={{0,4},{1,5},{2,6},{3,7},{4,0},{5,1},{6,2},{7,3},{8,12},{9,13},{10,... | collective-permute-start | bytes 393224 | tf_op jit(solution)/shard_map/ppermute | solution.py:603
  143.8 2.1 %collective-permute-start.25 = (f32[128,256]{1,0:T(8,128)}, f32[128,256]{1,0:T(8,128)}, u32[]{:S(2)}, u32[]{:S(2)}) collective-permute-start(f32[128,256]{1,0:T(8,128)} %get-tuple-element.55), channel_id=1, source_target_pairs={{0,6},{1,7},{2,4},{3,5},{4,2},{5,3},{6,0},{7,1},{8,14},{9,15},{10,... | collective-permute-start | bytes 393224 | tf_op jit(solution)/shard_map/ppermute | solution.py:603
  145.8 6.3 %solve_heads.6.refs_5_ = bf16[512,1024]{1,0:T(8,128)(2,1)} custom-call(s32[3]{0:T(128)} %pad_add_fusion.place_ref.core_ref, f32[8]{0:T(128)} %regular_ref.7, bf16[512,1024]{1,0:T(8,128)(2,1)} %convolution_convert_fusion.refs_0_, bf16[512,1024]{1,0:T(8,128)(2,1)} %bitcast.18, bf16[512,1024]{1,0:T(8,128)(2,1)} %bitcast.23, ...), custom_call_target="tpu_custom_call", output_to_operand_aliasing={{}: (7, {})} | custom-call | flops 1342177280 | bytes 1835008 | tf_op jit(solution)/shard_map/solve_heads/pallas_call | solution.py:345
  152.2 6.3 %solve_heads.7 = bf16[512,1024]{1,0:T(8,128)(2,1)} custom-call(s32[3]{0:T(128)} %pad_add_fusion.place_ref.core_ref, f32[8]{0:T(128)} %regular_ref.7, bf16[512,1024]{1,0:T(8,128)(2,1)} %convolution_convert_fusion.refs_0_, bf16[512,1024]{1,0:T(8,128)(2,1)} %bitcast.19, bf16[512,1024]{1,0:T(8,128)(2,1)} %bitcast.24, ...), custom_call_target="tpu_custom_call", output_to_operand_aliasing={{}: (7, {})} | custom-call | flops 1342177280 | bytes 1835008 | tf_op jit(solution)/shard_map/solve_heads/pallas_call | solution.py:345
  158.5 2.0 %finish.1 = f32[256,256]{1,0:T(8,128)} custom-call(f32[128,256]{1,0:T(8,128)} %get-tuple-element.45.refs_0_, f32[128,256]{1,0:T(8,128)} %collective-permute-done.16.refs_1_, f32[128,256]{1,0:T(8,128)} %collective-permute-done.17.refs_2_, f32[128,256]{1,0:T(8,128)} %collective-permute-done.18.refs_3_, f32[128,256]{1,0:T(8,128)} %get-tuple-element.52.refs_4_, ...), custom_call_target="tpu_custom_call" | custom-call | bytes 1310720 | tf_op jit(solution)/shard_map/finish/pallas_call | solution.py:505
  (24 shorter events, 1.6 us)
Async XLA Ops:
  6.1 2.2 %collective-permute-start = (f32[2,1,392,128]{3,2,1,0:T(8,128)}, f32[2,1,392,128]{3,2,1,0:T(8,128)}, u32[]{:S(2)}, u32[]{:S(2)}) collective-permute-start(f32[2,1,392,128]{3,2,1,0:T(8,128)} %get-tuple-element.31), channel_id=1, source_target_pairs={{0,1},{1,0},{2,3},{3,2},{4,5},{5,4},{6,7},{7,6},{8,9},{9,8},{10,11... | collective-permute-start | bytes 1204232 | tf_op jit(solution)/shard_map/ppermute | solution.py:548
  10.2 16.2 %collective-permute-start.7 = (f32[1,392,128]{2,1,0:T(8,128)}, f32[1,392,128]{2,1,0:T(8,128)}, u32[]{:S(2)}, u32[]{:S(2)}) collective-permute-start(f32[1,392,128]{2,1,0:T(8,128)} %get-tuple-element.35), channel_id=1, source_target_pairs={{0,6},{1,7},{8,14},{9,15},{16,22},{17,23},{24,30},{25,31}} | collective-permute-start | bytes 602120 | tf_op jit(solution)/shard_map/ppermute | solution.py:556
  17.8 9.4 %collective-permute-start.6 = (f32[1,392,128]{2,1,0:T(8,128)}, f32[1,392,128]{2,1,0:T(8,128)}, u32[]{:S(2)}, u32[]{:S(2)}) collective-permute-start(f32[1,392,128]{2,1,0:T(8,128)} %get-tuple-element.35), channel_id=1, source_target_pairs={{0,4},{1,5},{2,6},{3,7},{8,12},{9,13},{10,14},{11,15},{16,20},{17,... | collective-permute-start | bytes 602120 | tf_op jit(solution)/shard_map/ppermute | solution.py:556
  19.7 10.9 %collective-permute-start.5 = (f32[1,392,128]{2,1,0:T(8,128)}, f32[1,392,128]{2,1,0:T(8,128)}, u32[]{:S(2)}, u32[]{:S(2)}) collective-permute-start(f32[1,392,128]{2,1,0:T(8,128)} %get-tuple-element.35), channel_id=1, source_target_pairs={{0,2},{1,3},{2,4},{3,5},{4,6},{5,7},{8,10},{9,11},{10,12},{11,13},... | collective-permute-start | bytes 602120 | tf_op jit(solution)/shard_map/ppermute | solution.py:556
  26.5 49.3 %collective-permute-start.10 = (f32[4,512,256]{2,1,0:T(8,128)}, f32[4,512,256]{2,1,0:T(8,128)}, u32[]{:S(2)}, u32[]{:S(2)}) collective-permute-start(f32[4,512,256]{2,1,0:T(8,128)} %pick_columns.1), channel_id=1, source_target_pairs={{0,1},{1,0},{2,3},{3,2},{4,5},{5,4},{6,7},{7,6},{8,9},{9,8},{10,11... | collective-permute-start | bytes 6291464 | tf_op jit(solution)/shard_map/ppermute | solution.py:562
  32.8 6.2 %collective-permute-start.8 = (f32[1,392,128]{2,1,0:T(8,128)}, f32[1,392,128]{2,1,0:T(8,128)}, u32[]{:S(2)}, u32[]{:S(2)}) collective-permute-start(f32[1,392,128]{2,1,0:T(8,128)} %get-tuple-element.37), channel_id=1, source_target_pairs={{0,1},{1,0},{2,3},{3,2},{4,5},{5,4},{6,7},{7,6},{8,9},{9,8},{10,11... | collective-permute-start | bytes 602120 | tf_op jit(solution)/shard_map/ppermute | solution.py:559
  53.2 22.6 %collective-permute-start.9 = (f32[4,128,512]{2,1,0:T(8,128)}, f32[4,128,512]{2,1,0:T(8,128)}, u32[]{:S(2)}, u32[]{:S(2)}) collective-permute-start(f32[4,128,512]{2,1,0:T(8,128)} %get-tuple-element.39.own_ref), channel_id=1, source_target_pairs={{0,1},{1,0},{2,3},{3,2},{4,5},{5,4},{6,7},{7,6},{8,9},{9,8},{10,11... | collective-permute-start | bytes 3145736 | tf_op jit(solution)/shard_map/ppermute | solution.py:579
  53.7 13.5 %collective-permute-start.3 = (f32[1,392,128]{2,1,0:T(8,128)}, f32[1,392,128]{2,1,0:T(8,128)}, u32[]{:S(2)}, u32[]{:S(2)}) collective-permute-start(f32[1,392,128]{2,1,0:T(8,128)} %get-tuple-element.32), channel_id=1, source_target_pairs={{0,6},{1,7},{8,14},{9,15},{16,22},{17,23},{24,30},{25,31}} | collective-permute-start | bytes 602120 | tf_op jit(solution)/shard_map/ppermute | solution.py:556
  60.6 9.7 %collective-permute-start.2 = (f32[1,392,128]{2,1,0:T(8,128)}, f32[1,392,128]{2,1,0:T(8,128)}, u32[]{:S(2)}, u32[]{:S(2)}) collective-permute-start(f32[1,392,128]{2,1,0:T(8,128)} %get-tuple-element.32), channel_id=1, source_target_pairs={{0,4},{1,5},{2,6},{3,7},{8,12},{9,13},{10,14},{11,15},{16,20},{17,... | collective-permute-start | bytes 602120 | tf_op jit(solution)/shard_map/ppermute | solution.py:556
  65.2 8.4 %collective-permute-start.1 = (f32[1,392,128]{2,1,0:T(8,128)}, f32[1,392,128]{2,1,0:T(8,128)}, u32[]{:S(2)}, u32[]{:S(2)}) collective-permute-start(f32[1,392,128]{2,1,0:T(8,128)} %get-tuple-element.32), channel_id=1, source_target_pairs={{0,2},{1,3},{2,4},{3,5},{4,6},{5,7},{8,10},{9,11},{10,12},{11,13},... | collective-permute-start | bytes 602120 | tf_op jit(solution)/shard_map/ppermute | solution.py:556
  75.7 6.4 %collective-permute-start.4 = (f32[1,392,128]{2,1,0:T(8,128)}, f32[1,392,128]{2,1,0:T(8,128)}, u32[]{:S(2)}, u32[]{:S(2)}) collective-permute-start(f32[1,392,128]{2,1,0:T(8,128)} %get-tuple-element.33), channel_id=1, source_target_pairs={{0,1},{1,0},{2,3},{3,2},{4,5},{5,4},{6,7},{7,6},{8,9},{9,8},{10,11... | collective-permute-start | bytes 602120 | tf_op jit(solution)/shard_map/ppermute | solution.py:559
  93.7 3.5 %collective-permute-start.11 = (f32[4,128,512]{2,1,0:T(8,128)}, f32[4,128,512]{2,1,0:T(8,128)}, u32[]{:S(2)}, u32[]{:S(2)}) collective-permute-start(f32[4,128,512]{2,1,0:T(8,128)} %solve_heads.5.own_ref), channel_id=1, source_target_pairs={{0,1},{1,0},{2,3},{3,2},{4,5},{5,4},{6,7},{7,6},{8,9},{9,8},{10,11... | collective-permute-start | bytes 3145736 | tf_op jit(solution)/shard_map/ppermute | solution.py:579
  94.2 15.1 %collective-permute-start.12 = (f32[2,4,64,256]{3,2,1,0:T(8,128)}, f32[2,4,64,256]{3,2,1,0:T(8,128)}, u32[]{:S(2)}, u32[]{:S(2)}) collective-permute-start(f32[2,4,64,256]{3,2,1,0:T(8,128)} %get-tuple-element.42), channel_id=1, source_target_pairs={{0,8},{8,0},{16,24},{24,16},{1,9},{9,1},{17,25},{25,17},{2,10},{10... | collective-permute-start | bytes 1572872 | tf_op jit(solution)/shard_map/ppermute | solution.py:595
  95.7 16.9 %collective-permute-start.14 = (f32[2,4,64,256]{3,2,1,0:T(8,128)}, f32[2,4,64,256]{3,2,1,0:T(8,128)}, u32[]{:S(2)}, u32[]{:S(2)}) collective-permute-start(f32[2,4,64,256]{3,2,1,0:T(8,128)} %get-tuple-element.44), channel_id=1, source_target_pairs={{0,16},{8,24},{16,0},{24,8},{1,17},{9,25},{17,1},{25,9},{2,18},{10... | collective-permute-start | bytes 1572872 | tf_op jit(solution)/shard_map/ppermute | solution.py:595
  103.5 17.1 %collective-permute-start.19 = (f32[2,4,64,256]{3,2,1,0:T(8,128)}, f32[2,4,64,256]{3,2,1,0:T(8,128)}, u32[]{:S(2)}, u32[]{:S(2)}) collective-permute-start(f32[2,4,64,256]{3,2,1,0:T(8,128)} %get-tuple-element.49), channel_id=1, source_target_pairs={{0,8},{8,0},{16,24},{24,16},{1,9},{9,1},{17,25},{25,17},{2,10},{10... | collective-permute-start | bytes 1572872 | tf_op jit(solution)/shard_map/ppermute | solution.py:595
  104.6 19.3 %collective-permute-start.21 = (f32[2,4,64,256]{3,2,1,0:T(8,128)}, f32[2,4,64,256]{3,2,1,0:T(8,128)}, u32[]{:S(2)}, u32[]{:S(2)}) collective-permute-start(f32[2,4,64,256]{3,2,1,0:T(8,128)} %get-tuple-element.51), channel_id=1, source_target_pairs={{0,16},{8,24},{16,0},{24,8},{1,17},{9,25},{17,1},{25,9},{2,18},{10... | collective-permute-start | bytes 1572872 | tf_op jit(solution)/shard_map/ppermute | solution.py:595
  111.1 16.6 %collective-permute-start.13 = (f32[1,4,64,256]{3,2,1,0:T(8,128)}, f32[1,4,64,256]{3,2,1,0:T(8,128)}, u32[]{:S(2)}, u32[]{:S(2)}) collective-permute-start(f32[1,4,64,256]{3,2,1,0:T(8,128)} %sum_blocks.4), channel_id=1, source_target_pairs={{0,16},{8,24},{16,0},{24,8},{1,17},{9,25},{17,1},{25,9},{2,18},{10... | collective-permute-start | bytes 786440 | tf_op jit(solution)/shard_map/ppermute | solution.py:595
  114.4 13.3 %collective-permute-start.15 = (f32[1,4,64,256]{3,2,1,0:T(8,128)}, f32[1,4,64,256]{3,2,1,0:T(8,128)}, u32[]{:S(2)}, u32[]{:S(2)}) collective-permute-start(f32[1,4,64,256]{3,2,1,0:T(8,128)} %sum_blocks.5), channel_id=1, source_target_pairs={{0,8},{8,0},{16,24},{24,16},{1,9},{9,1},{17,25},{25,17},{2,10},{10... | collective-permute-start | bytes 786440 | tf_op jit(solution)/shard_map/ppermute | solution.py:595
  122.4 16.3 %collective-permute-start.20 = (f32[1,4,64,256]{3,2,1,0:T(8,128)}, f32[1,4,64,256]{3,2,1,0:T(8,128)}, u32[]{:S(2)}, u32[]{:S(2)}) collective-permute-start(f32[1,4,64,256]{3,2,1,0:T(8,128)} %sum_blocks.6), channel_id=1, source_target_pairs={{0,16},{8,24},{16,0},{24,8},{1,17},{9,25},{17,1},{25,9},{2,18},{10... | collective-permute-start | bytes 786440 | tf_op jit(solution)/shard_map/ppermute | solution.py:595
  125.6 13.0 %collective-permute-start.22 = (f32[1,4,64,256]{3,2,1,0:T(8,128)}, f32[1,4,64,256]{3,2,1,0:T(8,128)}, u32[]{:S(2)}, u32[]{:S(2)}) collective-permute-start(f32[1,4,64,256]{3,2,1,0:T(8,128)} %sum_blocks.7), channel_id=1, source_target_pairs={{0,8},{8,0},{16,24},{24,16},{1,9},{9,1},{17,25},{25,17},{2,10},{10... | collective-permute-start | bytes 786440 | tf_op jit(solution)/shard_map/ppermute | solution.py:595
  129.8 13.9 %collective-permute-start.16 = (f32[128,256]{1,0:T(8,128)}, f32[128,256]{1,0:T(8,128)}, u32[]{:S(2)}, u32[]{:S(2)}) collective-permute-start(f32[128,256]{1,0:T(8,128)} %get-tuple-element.46), channel_id=1, source_target_pairs={{0,2},{1,3},{2,0},{3,1},{4,6},{5,7},{6,4},{7,5},{8,10},{9,11},{10,... | collective-permute-start | bytes 393224 | tf_op jit(solution)/shard_map/ppermute | solution.py:603
  135.3 23.2 %collective-permute-start.17 = (f32[128,256]{1,0:T(8,128)}, f32[128,256]{1,0:T(8,128)}, u32[]{:S(2)}, u32[]{:S(2)}) collective-permute-start(f32[128,256]{1,0:T(8,128)} %get-tuple-element.47), channel_id=1, source_target_pairs={{0,4},{1,5},{2,6},{3,7},{4,0},{5,1},{6,2},{7,3},{8,12},{9,13},{10,... | collective-permute-start | bytes 393224 | tf_op jit(solution)/shard_map/ppermute | solution.py:603
  137.2 21.3 %collective-permute-start.18 = (f32[128,256]{1,0:T(8,128)}, f32[128,256]{1,0:T(8,128)}, u32[]{:S(2)}, u32[]{:S(2)}) collective-permute-start(f32[128,256]{1,0:T(8,128)} %get-tuple-element.48), channel_id=1, source_target_pairs={{0,6},{1,7},{2,4},{3,5},{4,2},{5,3},{6,0},{7,1},{8,14},{9,15},{10,... | collective-permute-start | bytes 393224 | tf_op jit(solution)/shard_map/ppermute | solution.py:603
  140.8 17.7 %collective-permute-start.23 = (f32[128,256]{1,0:T(8,128)}, f32[128,256]{1,0:T(8,128)}, u32[]{:S(2)}, u32[]{:S(2)}) collective-permute-start(f32[128,256]{1,0:T(8,128)} %get-tuple-element.53), channel_id=1, source_target_pairs={{0,2},{1,3},{2,0},{3,1},{4,6},{5,7},{6,4},{7,5},{8,10},{9,11},{10,... | collective-permute-start | bytes 393224 | tf_op jit(solution)/shard_map/ppermute | solution.py:603
  141.4 17.1 %collective-permute-start.24 = (f32[128,256]{1,0:T(8,128)}, f32[128,256]{1,0:T(8,128)}, u32[]{:S(2)}, u32[]{:S(2)}) collective-permute-start(f32[128,256]{1,0:T(8,128)} %get-tuple-element.54), channel_id=1, source_target_pairs={{0,4},{1,5},{2,6},{3,7},{4,0},{5,1},{6,2},{7,3},{8,12},{9,13},{10,... | collective-permute-start | bytes 393224 | tf_op jit(solution)/shard_map/ppermute | solution.py:603
  143.8 14.8 %collective-permute-start.25 = (f32[128,256]{1,0:T(8,128)}, f32[128,256]{1,0:T(8,128)}, u32[]{:S(2)}, u32[]{:S(2)}) collective-permute-start(f32[128,256]{1,0:T(8,128)} %get-tuple-element.55), channel_id=1, source_target_pairs={{0,6},{1,7},{2,4},{3,5},{4,2},{5,3},{6,0},{7,1},{8,14},{9,15},{10,... | collective-permute-start | bytes 393224 | tf_op jit(solution)/shard_map/ppermute | solution.py:603

commit v9 on v8

--- a/solution.py
+++ b/solution.py
@@ -434,24 +434,31 @@
     )(place, own, far, tokens, other)
 
 
-def sum_kernel(*refs):
-    total = refs[0][...]
-    for ref in refs[1:-1]:
-        total = total + ref[...]
-    refs[-1][...] = total
-
-
-def sum_blocks(arrays, length):
+def sum_kernel(counts, *refs):
+    arrays, outs = refs[: sum(counts)], refs[sum(counts) :]
+    at = 0
+    for count, out in zip(counts, outs):
+        total = arrays[at][...]
+        for ref in arrays[at + 1 : at + count]:
+            total = total + ref[...]
+        out[...] = total
+        at += count
+
+
+def sum_blocks(sums, length):
+    counts = [len(arrays) for arrays in sums]
+    arrays = [a for group in sums for a in group]
     out = jax.ShapeDtypeStruct((length,) + arrays[0].shape[1:], F32)
-    spec = pl.BlockSpec(out.shape, lambda _: (1, 0, 0, 0))
-    return pl.pallas_call(
-        sum_kernel,
-        out_shape=out,
-        in_specs=[spec] * len(arrays),
-        out_specs=whole(out),
+    return pl.pallas_call(
+        functools.partial(sum_kernel, counts),
+        out_shape=[out] * len(sums),
+        in_specs=[pl.BlockSpec(out.shape, lambda _: (1, 0, 0, 0))] * len(arrays),
+        out_specs=[whole(out)] * len(sums),
         grid=(1,),
         compiler_params=FULL,
-        cost_estimate=pl.CostEstimate(flops=0, bytes_accessed=12 * out.size // length, transcendentals=0),
+        cost_estimate=pl.CostEstimate(
+            flops=0, bytes_accessed=4 * (len(arrays) + 2) * out.size, transcendentals=0
+        ),
         name="sum_blocks",
     )(*arrays)
 
@@ -587,15 +594,13 @@
 
     finished = []
     for blocks in products:
-        sums = []
-        for index, path in enumerate(paths):
-            held, send = [blocks[2 * index]], blocks[2 * index + 1]
-            for bit in path:
-                pairs = [(i, i ^ (1 << bit)) for i in range(groups)]
-                held.append(lax.ppermute(send, "dp", pairs))
-                if bit != path[-1]:
-                    send = sum_blocks(held, held[-1].shape[0] // 2)
-            sums.append(held)
+        sums, sends = [[blocks[0]], [blocks[2]]], [blocks[1], blocks[3]]
+        for stage in range(dp_bits):
+            for index, path in enumerate(paths):
+                pairs = [(i, i ^ (1 << path[stage])) for i in range(groups)]
+                sums[index].append(lax.ppermute(sends[index], "dp", pairs))
+            if stage < dp_bits - 1:
+                sends = sum_blocks(sums, sends[0].shape[0] // 2)
         out, *others = merge_blocks(sums)
         finished.append([out])
         for z, other_block in enumerate(others, 1):

time: 161 us -> 162 us (level)
  waiting for transfers between devices: 20.7 us -> 25.6 us
  Pallas kernels: 79.9 us -> 76.9 us
  starting transfers between devices: 52.5 us -> 50.7 us
    ppermute x8, waiting for transfers between devices: 8.46 us -> 13.4 us  [program(): sums[index].append(lax.ppermute(sends[index], 'dp', pairs))]
    pallas_call x4 -> x2, Pallas kernels: 7.07 us -> 4.01 us  [sum_blocks(): pl.pallas_call(functools.partial(sum_kernel, counts), out_shape=[out] * l...]
    ppermute x8, starting transfers between devices: 11.7 us -> 9.76 us  [program(): sums[index].append(lax.ppermute(sends[index], 'dp', pairs))]
  transfers between devices with their start and end apart: 26 -> 26, of which waited for: 8 -> 10; matrix products, arithmetic and copies ran while one was open for 4% -> 4% of each run, Pallas kernels for 37% -> 35%
where the time goes in v9:
time: 162 us; the launch traced here: 161 us
  Pallas kernels  76.9 us (47%)
  starting transfers between devices  50.7 us (31%)
  waiting for transfers between devices  25.6 us (16%)
  matrix products  6.18 us (4%)
    pallas_call x4, Pallas kernels, solve_heads(): pl.pallas_call(functools.partial(solve_kernel, with_query, with_gradient,...  38.5 us
    ppermute x6, starting transfers between devices, program(): sent.append(lax.ppermute(chip_state, 'seq', pairs))  25.5 us
    ppermute x6, starting transfers between devices, program(): finished[-1].append(lax.ppermute(other_block, 'seq', pairs))  13.9 us
    ppermute x8, waiting for transfers between devices, program(): sums[index].append(lax.ppermute(sends[index], 'dp', pairs))  13.4 us
    pallas_call x2, Pallas kernels, gradient_blocks(): pl.pallas_call(functools.partial(gradient_kernel, order), out_shape=[out]...  12.6 us
    ppermute x6, waiting for transfers between devices, program(): sent.append(lax.ppermute(chip_state, 'seq', pairs))  10.5 us
    ppermute x8, starting transfers between devices, program(): sums[index].append(lax.ppermute(sends[index], 'dp', pairs))  9.76 us
    pallas_call x3, Pallas kernels, combine(): pl.pallas_call(kernel, out_shape=[out] * outs, in_specs=[pl.BlockSpec(mem...  6.23 us
  transfers between devices with their start and end apart: 26, of which 10 were waited for; matrix products, arithmetic and copies ran while one was open for 4% of the time, Pallas kernels for 35%

profile of v9, /device:TPU:0, one launch (start us, length us, event | category | flops | bytes accessed | tf_op | source)
XLA Modules:
  0.0 160.7 jit_solution(5743439384788245033)
XLA Ops:
  0.6 0.7 pad_add_fusion.place_ref.core_ref
  1.3 4.9 %local_states.1 = (f32[2,1,392,128]{3,2,1,0:T(8,128)}, f32[2,1,392,128]{3,2,1,0:T(8,128)}, f32[2,8,512]{2,1,0:T(8,128)}) custom-call(s32[3]{0:T(128)} %pad_add_fusion.place_ref.core_ref, bf16[512,1024]{1,0:T(8,128)(2,1)} %bitcast.15, bf16[512,1024]{1,0:T(8,128)(2,1)} %bitcast.20, f32[8,512]{1,0:T(8,128)} %bitcast.26), custom_call_target="tpu_custom_call" | custom-call | flops 536870912 | bytes 4194304 | tf_op jit(solution)/shard_map/local_states/pallas_call | solution.py:122
  6.7 1.7 %collective-permute-done.came_ref = f32[2,1,392,128]{3,2,1,0:T(8,128)} collective-permute-done((f32[2,1,392,128]{3,2,1,0:T(8,128)}, f32[2,1,392,128]{3,2,1,0:T(8,128)}, u32[]{:S(2)}, u32[]{:S(2)}) %collective-permute-start) | collective-permute-done | bytes 401440 | tf_op jit(solution)/shard_map/ppermute | solution.py:555
  8.4 1.9 %shard_map.86 = (f32[1,392,128]{2,1,0:T(8,128)}, f32[1,392,128]{2,1,0:T(8,128)}) custom-call(s32[3]{0:T(128)} %pad_add_fusion.place_ref.core_ref, f32[2,1,392,128]{3,2,1,0:T(8,128)} %get-tuple-element.34.own_ref, f32[2,1,392,128]{3,2,1,0:T(8,128)} %collective-permute-done.came_ref), custom_call_target="tpu_custom_call" | custom-call | bytes 1605632 | tf_op jit(solution)/shard_map/pallas_call | solution.py:167
  10.3 7.5 %collective-permute-start.7 = (f32[1,392,128]{2,1,0:T(8,128)}, f32[1,392,128]{2,1,0:T(8,128)}, u32[]{:S(2)}, u32[]{:S(2)}) collective-permute-start(f32[1,392,128]{2,1,0:T(8,128)} %get-tuple-element.39), channel_id=1, source_target_pairs={{0,6},{1,7},{8,14},{9,15},{16,22},{17,23},{24,30},{25,31}} | collective-permute-start | bytes 602120 | tf_op jit(solution)/shard_map/ppermute | solution.py:563
  17.8 2.0 %collective-permute-start.6 = (f32[1,392,128]{2,1,0:T(8,128)}, f32[1,392,128]{2,1,0:T(8,128)}, u32[]{:S(2)}, u32[]{:S(2)}) collective-permute-start(f32[1,392,128]{2,1,0:T(8,128)} %get-tuple-element.39), channel_id=1, source_target_pairs={{0,4},{1,5},{2,6},{3,7},{8,12},{9,13},{10,14},{11,15},{16,20},{17,... | collective-permute-start | bytes 602120 | tf_op jit(solution)/shard_map/ppermute | solution.py:563
  19.8 2.5 %collective-permute-start.5 = (f32[1,392,128]{2,1,0:T(8,128)}, f32[1,392,128]{2,1,0:T(8,128)}, u32[]{:S(2)}, u32[]{:S(2)}) collective-permute-start(f32[1,392,128]{2,1,0:T(8,128)} %get-tuple-element.39), channel_id=1, source_target_pairs={{0,2},{1,3},{2,4},{3,5},{4,6},{5,7},{8,10},{9,11},{10,12},{11,13},... | collective-permute-start | bytes 602120 | tf_op jit(solution)/shard_map/ppermute | solution.py:563
  22.3 4.3 %pick_columns.1 = f32[4,512,256]{2,1,0:T(8,128)} custom-call(s32[3]{0:T(128)} %pad_add_fusion.place_ref.core_ref, bf16[512,2048]{1,0:T(8,128)(2,1)} %bitcast.12), custom_call_target="tpu_custom_call" | custom-call | bytes 3145728 | tf_op jit(solution)/shard_map/pick_columns/pallas_call | solution.py:367
  26.6 0.6 collective-permute-done.6.refs_1_
  27.2 3.5 %collective-permute-done.5.refs_0_ = f32[1,392,128]{2,1,0:T(8,128)} collective-permute-done((f32[1,392,128]{2,1,0:T(8,128)}, f32[1,392,128]{2,1,0:T(8,128)}, u32[]{:S(2)}, u32[]{:S(2)}) %collective-permute-start.5) | collective-permute-done | bytes 200736 | tf_op jit(solution)/shard_map/ppermute | solution.py:563
  30.7 2.2 %shard_map.88 = (f32[1,392,128]{2,1,0:T(8,128)}, f32[1,392,128]{2,1,0:T(8,128)}) custom-call(s32[3]{0:T(128)} %pad_add_fusion.place_ref.core_ref, f32[2,1,392,128]{3,2,1,0:T(8,128)} %get-tuple-element.34.own_ref, f32[2,1,392,128]{3,2,1,0:T(8,128)} %collective-permute-done.came_ref, f32[1,392,128]{2,1,0:T(8,128)} %collective-permute-done.5.refs_0_, ...), custom_call_target="tpu_custom_call" | custom-call | bytes 2809856 | tf_op jit(solution)/shard_map/pallas_call | solution.py:167
  32.9 6.2 %convolution_convert_fusion.refs_0_ = bf16[512,1024]{1,0:T(8,128)(2,1)} fusion(bf16[2048,1024]{1,0:T(8,128)(2,1)} %param.8, bf16[1,512,2048]{2,1,0:T(8,128)(2,1)} %param.7), kind=kOutput, calls=%fused_computation | convolution fusion | flops 2148007936 | bytes 7340032 | tf_op jit(solution)/shard_map/dot_general | solution.py:570
  39.0 14.2 %solve_heads.4 = (bf16[512,1024]{1,0:T(8,128)(2,1)}, f32[4,128,512]{2,1,0:T(8,128)}) custom-call(s32[3]{0:T(128)} %pad_add_fusion.place_ref.core_ref, f32[8]{0:T(128)} %regular_ref.7, bf16[512,1024]{1,0:T(8,128)(2,1)} %convolution_convert_fusion.refs_0_, bf16[512,1024]{1,0:T(8,128)(2,1)} %bitcast.27, bf16[512,1024]{1,0:T(8,128)(2,1)} %bitcast.16, ...), custom_call_target="tpu_custom_call" | custom-call | flops 2684354560 | bytes 3670016 | tf_op jit(solution)/shard_map/solve_heads/pallas_call | solution.py:345
  53.7 6.9 %collective-permute-start.3 = (f32[1,392,128]{2,1,0:T(8,128)}, f32[1,392,128]{2,1,0:T(8,128)}, u32[]{:S(2)}, u32[]{:S(2)}) collective-permute-start(f32[1,392,128]{2,1,0:T(8,128)} %get-tuple-element.36), channel_id=1, source_target_pairs={{0,6},{1,7},{8,14},{9,15},{16,22},{17,23},{24,30},{25,31}} | collective-permute-start | bytes 602120 | tf_op jit(solution)/shard_map/ppermute | solution.py:563
  60.6 4.7 %collective-permute-start.2 = (f32[1,392,128]{2,1,0:T(8,128)}, f32[1,392,128]{2,1,0:T(8,128)}, u32[]{:S(2)}, u32[]{:S(2)}) collective-permute-start(f32[1,392,128]{2,1,0:T(8,128)} %get-tuple-element.36), channel_id=1, source_target_pairs={{0,4},{1,5},{2,6},{3,7},{8,12},{9,13},{10,14},{11,15},{16,20},{17,... | collective-permute-start | bytes 602120 | tf_op jit(solution)/shard_map/ppermute | solution.py:563
  65.3 2.0 %collective-permute-start.1 = (f32[1,392,128]{2,1,0:T(8,128)}, f32[1,392,128]{2,1,0:T(8,128)}, u32[]{:S(2)}, u32[]{:S(2)}) collective-permute-start(f32[1,392,128]{2,1,0:T(8,128)} %get-tuple-element.36), channel_id=1, source_target_pairs={{0,2},{1,3},{2,4},{3,5},{4,6},{5,7},{8,10},{9,11},{10,12},{11,13},... | collective-permute-start | bytes 602120 | tf_op jit(solution)/shard_map/ppermute | solution.py:563
  67.3 3.0 %collective-permute-done.2.refs_1_ = f32[1,392,128]{2,1,0:T(8,128)} collective-permute-done((f32[1,392,128]{2,1,0:T(8,128)}, f32[1,392,128]{2,1,0:T(8,128)}, u32[]{:S(2)}, u32[]{:S(2)}) %collective-permute-start.2) | collective-permute-done | bytes 200736 | tf_op jit(solution)/shard_map/ppermute | solution.py:563
  70.3 3.4 %collective-permute-done.1.refs_0_ = f32[1,392,128]{2,1,0:T(8,128)} collective-permute-done((f32[1,392,128]{2,1,0:T(8,128)}, f32[1,392,128]{2,1,0:T(8,128)}, u32[]{:S(2)}, u32[]{:S(2)}) %collective-permute-start.1) | collective-permute-done | bytes 200736 | tf_op jit(solution)/shard_map/ppermute | solution.py:563
  73.6 2.2 %shard_map.87 = (f32[1,392,128]{2,1,0:T(8,128)}, f32[1,392,128]{2,1,0:T(8,128)}) custom-call(s32[3]{0:T(128)} %pad_add_fusion.place_ref.core_ref, f32[2,1,392,128]{3,2,1,0:T(8,128)} %get-tuple-element.34.own_ref, f32[2,1,392,128]{3,2,1,0:T(8,128)} %collective-permute-done.came_ref, f32[1,392,128]{2,1,0:T(8,128)} %collective-permute-done.1.refs_0_, ...), custom_call_target="tpu_custom_call" | custom-call | bytes 2809856 | tf_op jit(solution)/shard_map/pallas_call | solution.py:167
  75.8 6.4 %gradient_blocks.2 = (f32[2,4,64,256]{3,2,1,0:T(8,128)}, f32[2,4,64,256]{3,2,1,0:T(8,128)}, f32[2,4,64,256]{3,2,1,0:T(8,128)}, f32[2,4,64,256]{3,2,1,0:T(8,128)}) custom-call(s32[3]{0:T(128)} %pad_add_fusion.place_ref.core_ref, f32[4,128,512]{2,1,0:T(8,128)} %get-tuple-element.43.own_ref, f32[4,128,512]{2,1,0:T(8,128)} %collective-permute-done.9.far_ref, ...), custom_call_target="tpu_custom_call" | custom-call | flops 1073741824 | bytes 6291456 | tf_op jit(solution)/shard_map/gradient_blocks/pallas_call | solution.py:413
  82.2 11.6 %solve_heads.5.own_ref = f32[4,128,512]{2,1,0:T(8,128)} custom-call(s32[3]{0:T(128)} %pad_add_fusion.place_ref.core_ref, f32[8]{0:T(128)} %regular_ref.7, bf16[512,1024]{1,0:T(8,128)(2,1)} %bitcast.28, bf16[512,1024]{1,0:T(8,128)(2,1)} %bitcast.17, bf16[512,1024]{1,0:T(8,128)(2,1)} %bitcast.22, f32[2,8,512]{2,1,0:T(8,128)} %get-tuple-element.33.refs_4_.refs_3_, ...), custom_call_target="tpu_custom_call" | custom-call | flops 2684354560 | bytes 3670016 | tf_op jit(solution)/shard_map/solve_heads/pallas_call | solution.py:345
  94.3 1.5 collective-permute-start.12
  95.8 1.5 collective-permute-start.13
  97.3 6.3 %gradient_blocks.3 = (f32[2,4,64,256]{3,2,1,0:T(8,128)}, f32[2,4,64,256]{3,2,1,0:T(8,128)}, f32[2,4,64,256]{3,2,1,0:T(8,128)}, f32[2,4,64,256]{3,2,1,0:T(8,128)}) custom-call(s32[3]{0:T(128)} %pad_add_fusion.place_ref.core_ref, f32[4,128,512]{2,1,0:T(8,128)} %solve_heads.5.own_ref, f32[4,128,512]{2,1,0:T(8,128)} %collective-permute-done.11.far_ref, ...), custom_call_target="tpu_custom_call" | custom-call | flops 1073741824 | bytes 6291456 | tf_op jit(solution)/shard_map/gradient_blocks/pallas_call | solution.py:413
  103.6 1.1 collective-permute-start.19
  104.7 1.5 collective-permute-start.20
  106.2 3.2 %collective-permute-done.12.refs_1_ = f32[2,4,64,256]{3,2,1,0:T(8,128)} collective-permute-done((f32[2,4,64,256]{3,2,1,0:T(8,128)}, f32[2,4,64,256]{3,2,1,0:T(8,128)}, u32[]{:S(2)}, u32[]{:S(2)}) %collective-permute-start.12) | collective-permute-done | bytes 524320 | tf_op jit(solution)/shard_map/ppermute | solution.py:601
  109.4 1.5 collective-permute-done.13.refs_3_.refs_4_
  110.9 2.0 %sum_blocks.2 = (f32[1,4,64,256]{3,2,1,0:T(8,128)}, f32[1,4,64,256]{3,2,1,0:T(8,128)}) custom-call(f32[2,4,64,256]{3,2,1,0:T(8,128)} %get-tuple-element.44.refs_6_.refs_0_, f32[2,4,64,256]{3,2,1,0:T(8,128)} %collective-permute-done.12.refs_1_, f32[2,4,64,256]{3,2,1,0:T(8,128)} %get-tuple-element.47.refs_2_.refs_3_, ...), custom_call_target="tpu_custom_call" | custom-call | bytes 1572864 | tf_op jit(solution)/shard_map/sum_blocks/pallas_call | solution.py:452
  112.9 1.5 collective-permute-start.14
  114.4 0.5 collective-permute-start.15
  115.0 5.7 %collective-permute-done.19.refs_1_ = f32[2,4,64,256]{3,2,1,0:T(8,128)} collective-permute-done((f32[2,4,64,256]{3,2,1,0:T(8,128)}, f32[2,4,64,256]{3,2,1,0:T(8,128)}, u32[]{:S(2)}, u32[]{:S(2)}) %collective-permute-start.19) | collective-permute-done | bytes 524320 | tf_op jit(solution)/shard_map/ppermute | solution.py:601
  120.7 1.5 collective-permute-done.20.refs_3_.refs_4_
  122.2 2.0 %sum_blocks.3 = (f32[1,4,64,256]{3,2,1,0:T(8,128)}, f32[1,4,64,256]{3,2,1,0:T(8,128)}) custom-call(f32[2,4,64,256]{3,2,1,0:T(8,128)} %get-tuple-element.45.refs_6_.refs_0_, f32[2,4,64,256]{3,2,1,0:T(8,128)} %collective-permute-done.19.refs_1_, f32[2,4,64,256]{3,2,1,0:T(8,128)} %get-tuple-element.56.refs_2_.refs_3_, ...), custom_call_target="tpu_custom_call" | custom-call | bytes 1572864 | tf_op jit(solution)/shard_map/sum_blocks/pallas_call | solution.py:452
  124.2 1.5 collective-permute-start.21
  125.7 0.5 collective-permute-start.22
  126.2 1.5 collective-permute-done.14.refs_2_
  127.8 2.1 %merge_blocks.2 = (f32[128,256]{1,0:T(8,128)}, f32[128,256]{1,0:T(8,128)}, f32[128,256]{1,0:T(8,128)}, f32[128,256]{1,0:T(8,128)}) custom-call(f32[2,4,64,256]{3,2,1,0:T(8,128)} %get-tuple-element.44.refs_6_.refs_0_, f32[2,4,64,256]{3,2,1,0:T(8,128)} %collective-permute-done.12.refs_1_, f32[1,4,64,256]{3,2,1,0:T(8,128)} %collective-permute-done.14.refs_2_, ...), custom_call_target="tpu_custom_call" | custom-call | bytes 2097152 | tf_op jit(solution)/shard_map/merge_blocks/pallas_call | solution.py:484
  129.9 5.4 %collective-permute-start.16 = (f32[128,256]{1,0:T(8,128)}, f32[128,256]{1,0:T(8,128)}, u32[]{:S(2)}, u32[]{:S(2)}) collective-permute-start(f32[128,256]{1,0:T(8,128)} %get-tuple-element.52), channel_id=1, source_target_pairs={{0,2},{1,3},{2,0},{3,1},{4,6},{5,7},{6,4},{7,5},{8,10},{9,11},{10,... | collective-permute-start | bytes 393224 | tf_op jit(solution)/shard_map/ppermute | solution.py:608
  135.3 1.9 %collective-permute-start.17 = (f32[128,256]{1,0:T(8,128)}, f32[128,256]{1,0:T(8,128)}, u32[]{:S(2)}, u32[]{:S(2)}) collective-permute-start(f32[128,256]{1,0:T(8,128)} %get-tuple-element.53), channel_id=1, source_target_pairs={{0,4},{1,5},{2,6},{3,7},{4,0},{5,1},{6,2},{7,3},{8,12},{9,13},{10,... | collective-permute-start | bytes 393224 | tf_op jit(solution)/shard_map/ppermute | solution.py:608
  137.3 1.4 collective-permute-start.18
  138.7 2.2 %merge_blocks.3 = (f32[128,256]{1,0:T(8,128)}, f32[128,256]{1,0:T(8,128)}, f32[128,256]{1,0:T(8,128)}, f32[128,256]{1,0:T(8,128)}) custom-call(f32[2,4,64,256]{3,2,1,0:T(8,128)} %get-tuple-element.45.refs_6_.refs_0_, f32[2,4,64,256]{3,2,1,0:T(8,128)} %collective-permute-done.19.refs_1_, f32[1,4,64,256]{3,2,1,0:T(8,128)} %collective-permute-done.21.refs_2_, ...), custom_call_target="tpu_custom_call" | custom-call | bytes 2097152 | tf_op jit(solution)/shard_map/merge_blocks/pallas_call | solution.py:484
  140.9 0.6 collective-permute-start.23
  141.5 2.4 %collective-permute-start.24 = (f32[128,256]{1,0:T(8,128)}, f32[128,256]{1,0:T(8,128)}, u32[]{:S(2)}, u32[]{:S(2)}) collective-permute-start(f32[128,256]{1,0:T(8,128)} %get-tuple-element.62), channel_id=1, source_target_pairs={{0,4},{1,5},{2,6},{3,7},{4,0},{5,1},{6,2},{7,3},{8,12},{9,13},{10,... | collective-permute-start | bytes 393224 | tf_op jit(solution)/shard_map/ppermute | solution.py:608
  143.8 2.2 %collective-permute-start.25 = (f32[128,256]{1,0:T(8,128)}, f32[128,256]{1,0:T(8,128)}, u32[]{:S(2)}, u32[]{:S(2)}) collective-permute-start(f32[128,256]{1,0:T(8,128)} %get-tuple-element.63), channel_id=1, source_target_pairs={{0,6},{1,7},{2,4},{3,5},{4,2},{5,3},{6,0},{7,1},{8,14},{9,15},{10,... | collective-permute-start | bytes 393224 | tf_op jit(solution)/shard_map/ppermute | solution.py:608
  146.0 6.3 %solve_heads.6.refs_5_ = bf16[512,1024]{1,0:T(8,128)(2,1)} custom-call(s32[3]{0:T(128)} %pad_add_fusion.place_ref.core_ref, f32[8]{0:T(128)} %regular_ref.7, bf16[512,1024]{1,0:T(8,128)(2,1)} %convolution_convert_fusion.refs_0_, bf16[512,1024]{1,0:T(8,128)(2,1)} %bitcast.18, bf16[512,1024]{1,0:T(8,128)(2,1)} %bitcast.23, ...), custom_call_target="tpu_custom_call", output_to_operand_aliasing={{}: (7, {})} | custom-call | flops 1342177280 | bytes 1835008 | tf_op jit(solution)/shard_map/solve_heads/pallas_call | solution.py:345
  152.3 6.3 %solve_heads.7 = bf16[512,1024]{1,0:T(8,128)(2,1)} custom-call(s32[3]{0:T(128)} %pad_add_fusion.place_ref.core_ref, f32[8]{0:T(128)} %regular_ref.7, bf16[512,1024]{1,0:T(8,128)(2,1)} %convolution_convert_fusion.refs_0_, bf16[512,1024]{1,0:T(8,128)(2,1)} %bitcast.19, bf16[512,1024]{1,0:T(8,128)(2,1)} %bitcast.24, ...), custom_call_target="tpu_custom_call", output_to_operand_aliasing={{}: (7, {})} | custom-call | flops 1342177280 | bytes 1835008 | tf_op jit(solution)/shard_map/solve_heads/pallas_call | solution.py:345
  158.7 2.0 %finish.1 = f32[256,256]{1,0:T(8,128)} custom-call(f32[128,256]{1,0:T(8,128)} %get-tuple-element.51.refs_0_, f32[128,256]{1,0:T(8,128)} %collective-permute-done.16.refs_1_, f32[128,256]{1,0:T(8,128)} %collective-permute-done.17.refs_2_, f32[128,256]{1,0:T(8,128)} %collective-permute-done.18.refs_3_, f32[128,256]{1,0:T(8,128)} %get-tuple-element.60.refs_4_, ...), custom_call_target="tpu_custom_call" | custom-call | bytes 1310720 | tf_op jit(solution)/shard_map/finish/pallas_call | solution.py:512
  (22 shorter events, 1.6 us)
Async XLA Ops:
  6.2 2.2 %collective-permute-start = (f32[2,1,392,128]{3,2,1,0:T(8,128)}, f32[2,1,392,128]{3,2,1,0:T(8,128)}, u32[]{:S(2)}, u32[]{:S(2)}) collective-permute-start(f32[2,1,392,128]{3,2,1,0:T(8,128)} %get-tuple-element.35), channel_id=1, source_target_pairs={{0,1},{1,0},{2,3},{3,2},{4,5},{5,4},{6,7},{7,6},{8,9},{9,8},{10,11... | collective-permute-start | bytes 1204232 | tf_op jit(solution)/shard_map/ppermute | solution.py:555
  10.3 16.3 %collective-permute-start.7 = (f32[1,392,128]{2,1,0:T(8,128)}, f32[1,392,128]{2,1,0:T(8,128)}, u32[]{:S(2)}, u32[]{:S(2)}) collective-permute-start(f32[1,392,128]{2,1,0:T(8,128)} %get-tuple-element.39), channel_id=1, source_target_pairs={{0,6},{1,7},{8,14},{9,15},{16,22},{17,23},{24,30},{25,31}} | collective-permute-start | bytes 602120 | tf_op jit(solution)/shard_map/ppermute | solution.py:563
  17.8 9.4 %collective-permute-start.6 = (f32[1,392,128]{2,1,0:T(8,128)}, f32[1,392,128]{2,1,0:T(8,128)}, u32[]{:S(2)}, u32[]{:S(2)}) collective-permute-start(f32[1,392,128]{2,1,0:T(8,128)} %get-tuple-element.39), channel_id=1, source_target_pairs={{0,4},{1,5},{2,6},{3,7},{8,12},{9,13},{10,14},{11,15},{16,20},{17,... | collective-permute-start | bytes 602120 | tf_op jit(solution)/shard_map/ppermute | solution.py:563
  19.8 10.9 %collective-permute-start.5 = (f32[1,392,128]{2,1,0:T(8,128)}, f32[1,392,128]{2,1,0:T(8,128)}, u32[]{:S(2)}, u32[]{:S(2)}) collective-permute-start(f32[1,392,128]{2,1,0:T(8,128)} %get-tuple-element.39), channel_id=1, source_target_pairs={{0,2},{1,3},{2,4},{3,5},{4,6},{5,7},{8,10},{9,11},{10,12},{11,13},... | collective-permute-start | bytes 602120 | tf_op jit(solution)/shard_map/ppermute | solution.py:563
  26.6 49.2 %collective-permute-start.10 = (f32[4,512,256]{2,1,0:T(8,128)}, f32[4,512,256]{2,1,0:T(8,128)}, u32[]{:S(2)}, u32[]{:S(2)}) collective-permute-start(f32[4,512,256]{2,1,0:T(8,128)} %pick_columns.1), channel_id=1, source_target_pairs={{0,1},{1,0},{2,3},{3,2},{4,5},{5,4},{6,7},{7,6},{8,9},{9,8},{10,11... | collective-permute-start | bytes 6291464 | tf_op jit(solution)/shard_map/ppermute | solution.py:569
  32.8 6.2 %collective-permute-start.8 = (f32[1,392,128]{2,1,0:T(8,128)}, f32[1,392,128]{2,1,0:T(8,128)}, u32[]{:S(2)}, u32[]{:S(2)}) collective-permute-start(f32[1,392,128]{2,1,0:T(8,128)} %get-tuple-element.41), channel_id=1, source_target_pairs={{0,1},{1,0},{2,3},{3,2},{4,5},{5,4},{6,7},{7,6},{8,9},{9,8},{10,11... | collective-permute-start | bytes 602120 | tf_op jit(solution)/shard_map/ppermute | solution.py:566
  53.2 22.6 %collective-permute-start.9 = (f32[4,128,512]{2,1,0:T(8,128)}, f32[4,128,512]{2,1,0:T(8,128)}, u32[]{:S(2)}, u32[]{:S(2)}) collective-permute-start(f32[4,128,512]{2,1,0:T(8,128)} %get-tuple-element.43.own_ref), channel_id=1, source_target_pairs={{0,1},{1,0},{2,3},{3,2},{4,5},{5,4},{6,7},{7,6},{8,9},{9,8},{10,11... | collective-permute-start | bytes 3145736 | tf_op jit(solution)/shard_map/ppermute | solution.py:586
  53.7 13.5 %collective-permute-start.3 = (f32[1,392,128]{2,1,0:T(8,128)}, f32[1,392,128]{2,1,0:T(8,128)}, u32[]{:S(2)}, u32[]{:S(2)}) collective-permute-start(f32[1,392,128]{2,1,0:T(8,128)} %get-tuple-element.36), channel_id=1, source_target_pairs={{0,6},{1,7},{8,14},{9,15},{16,22},{17,23},{24,30},{25,31}} | collective-permute-start | bytes 602120 | tf_op jit(solution)/shard_map/ppermute | solution.py:563
  60.6 9.7 %collective-permute-start.2 = (f32[1,392,128]{2,1,0:T(8,128)}, f32[1,392,128]{2,1,0:T(8,128)}, u32[]{:S(2)}, u32[]{:S(2)}) collective-permute-start(f32[1,392,128]{2,1,0:T(8,128)} %get-tuple-element.36), channel_id=1, source_target_pairs={{0,4},{1,5},{2,6},{3,7},{8,12},{9,13},{10,14},{11,15},{16,20},{17,... | collective-permute-start | bytes 602120 | tf_op jit(solution)/shard_map/ppermute | solution.py:563
  65.3 8.4 %collective-permute-start.1 = (f32[1,392,128]{2,1,0:T(8,128)}, f32[1,392,128]{2,1,0:T(8,128)}, u32[]{:S(2)}, u32[]{:S(2)}) collective-permute-start(f32[1,392,128]{2,1,0:T(8,128)} %get-tuple-element.36), channel_id=1, source_target_pairs={{0,2},{1,3},{2,4},{3,5},{4,6},{5,7},{8,10},{9,11},{10,12},{11,13},... | collective-permute-start | bytes 602120 | tf_op jit(solution)/shard_map/ppermute | solution.py:563
  75.8 6.4 %collective-permute-start.4 = (f32[1,392,128]{2,1,0:T(8,128)}, f32[1,392,128]{2,1,0:T(8,128)}, u32[]{:S(2)}, u32[]{:S(2)}) collective-permute-start(f32[1,392,128]{2,1,0:T(8,128)} %get-tuple-element.37), channel_id=1, source_target_pairs={{0,1},{1,0},{2,3},{3,2},{4,5},{5,4},{6,7},{7,6},{8,9},{9,8},{10,11... | collective-permute-start | bytes 602120 | tf_op jit(solution)/shard_map/ppermute | solution.py:566
  93.8 3.5 %collective-permute-start.11 = (f32[4,128,512]{2,1,0:T(8,128)}, f32[4,128,512]{2,1,0:T(8,128)}, u32[]{:S(2)}, u32[]{:S(2)}) collective-permute-start(f32[4,128,512]{2,1,0:T(8,128)} %solve_heads.5.own_ref), channel_id=1, source_target_pairs={{0,1},{1,0},{2,3},{3,2},{4,5},{5,4},{6,7},{7,6},{8,9},{9,8},{10,11... | collective-permute-start | bytes 3145736 | tf_op jit(solution)/shard_map/ppermute | solution.py:586
  94.3 15.1 %collective-permute-start.12 = (f32[2,4,64,256]{3,2,1,0:T(8,128)}, f32[2,4,64,256]{3,2,1,0:T(8,128)}, u32[]{:S(2)}, u32[]{:S(2)}) collective-permute-start(f32[2,4,64,256]{3,2,1,0:T(8,128)} %get-tuple-element.46), channel_id=1, source_target_pairs={{0,8},{8,0},{16,24},{24,16},{1,9},{9,1},{17,25},{25,17},{2,10},{10... | collective-permute-start | bytes 1572872 | tf_op jit(solution)/shard_map/ppermute | solution.py:601
  95.8 15.1 %collective-permute-start.13 = (f32[2,4,64,256]{3,2,1,0:T(8,128)}, f32[2,4,64,256]{3,2,1,0:T(8,128)}, u32[]{:S(2)}, u32[]{:S(2)}) collective-permute-start(f32[2,4,64,256]{3,2,1,0:T(8,128)} %get-tuple-element.48), channel_id=1, source_target_pairs={{0,16},{8,24},{16,0},{24,8},{1,17},{9,25},{17,1},{25,9},{2,18},{10... | collective-permute-start | bytes 1572872 | tf_op jit(solution)/shard_map/ppermute | solution.py:601
  103.6 17.1 %collective-permute-start.19 = (f32[2,4,64,256]{3,2,1,0:T(8,128)}, f32[2,4,64,256]{3,2,1,0:T(8,128)}, u32[]{:S(2)}, u32[]{:S(2)}) collective-permute-start(f32[2,4,64,256]{3,2,1,0:T(8,128)} %get-tuple-element.55), channel_id=1, source_target_pairs={{0,8},{8,0},{16,24},{24,16},{1,9},{9,1},{17,25},{25,17},{2,10},{10... | collective-permute-start | bytes 1572872 | tf_op jit(solution)/shard_map/ppermute | solution.py:601
  104.7 17.4 %collective-permute-start.20 = (f32[2,4,64,256]{3,2,1,0:T(8,128)}, f32[2,4,64,256]{3,2,1,0:T(8,128)}, u32[]{:S(2)}, u32[]{:S(2)}) collective-permute-start(f32[2,4,64,256]{3,2,1,0:T(8,128)} %get-tuple-element.57), channel_id=1, source_target_pairs={{0,16},{8,24},{16,0},{24,8},{1,17},{9,25},{17,1},{25,9},{2,18},{10... | collective-permute-start | bytes 1572872 | tf_op jit(solution)/shard_map/ppermute | solution.py:601
  112.9 14.9 %collective-permute-start.14 = (f32[1,4,64,256]{3,2,1,0:T(8,128)}, f32[1,4,64,256]{3,2,1,0:T(8,128)}, u32[]{:S(2)}, u32[]{:S(2)}) collective-permute-start(f32[1,4,64,256]{3,2,1,0:T(8,128)} %get-tuple-element.49), channel_id=1, source_target_pairs={{0,16},{8,24},{16,0},{24,8},{1,17},{9,25},{17,1},{25,9},{2,18},{10... | collective-permute-start | bytes 786440 | tf_op jit(solution)/shard_map/ppermute | solution.py:601
  114.4 13.3 %collective-permute-start.15 = (f32[1,4,64,256]{3,2,1,0:T(8,128)}, f32[1,4,64,256]{3,2,1,0:T(8,128)}, u32[]{:S(2)}, u32[]{:S(2)}) collective-permute-start(f32[1,4,64,256]{3,2,1,0:T(8,128)} %get-tuple-element.50), channel_id=1, source_target_pairs={{0,8},{8,0},{16,24},{24,16},{1,9},{9,1},{17,25},{25,17},{2,10},{10... | collective-permute-start | bytes 786440 | tf_op jit(solution)/shard_map/ppermute | solution.py:601
  124.2 14.5 %collective-permute-start.21 = (f32[1,4,64,256]{3,2,1,0:T(8,128)}, f32[1,4,64,256]{3,2,1,0:T(8,128)}, u32[]{:S(2)}, u32[]{:S(2)}) collective-permute-start(f32[1,4,64,256]{3,2,1,0:T(8,128)} %get-tuple-element.58), channel_id=1, source_target_pairs={{0,16},{8,24},{16,0},{24,8},{1,17},{9,25},{17,1},{25,9},{2,18},{10... | collective-permute-start | bytes 786440 | tf_op jit(solution)/shard_map/ppermute | solution.py:601
  125.7 13.0 %collective-permute-start.22 = (f32[1,4,64,256]{3,2,1,0:T(8,128)}, f32[1,4,64,256]{3,2,1,0:T(8,128)}, u32[]{:S(2)}, u32[]{:S(2)}) collective-permute-start(f32[1,4,64,256]{3,2,1,0:T(8,128)} %get-tuple-element.59), channel_id=1, source_target_pairs={{0,8},{8,0},{16,24},{24,16},{1,9},{9,1},{17,25},{25,17},{2,10},{10... | collective-permute-start | bytes 786440 | tf_op jit(solution)/shard_map/ppermute | solution.py:601
  129.9 13.9 %collective-permute-start.16 = (f32[128,256]{1,0:T(8,128)}, f32[128,256]{1,0:T(8,128)}, u32[]{:S(2)}, u32[]{:S(2)}) collective-permute-start(f32[128,256]{1,0:T(8,128)} %get-tuple-element.52), channel_id=1, source_target_pairs={{0,2},{1,3},{2,0},{3,1},{4,6},{5,7},{6,4},{7,5},{8,10},{9,11},{10,... | collective-permute-start | bytes 393224 | tf_op jit(solution)/shard_map/ppermute | solution.py:608
  135.3 23.3 %collective-permute-start.17 = (f32[128,256]{1,0:T(8,128)}, f32[128,256]{1,0:T(8,128)}, u32[]{:S(2)}, u32[]{:S(2)}) collective-permute-start(f32[128,256]{1,0:T(8,128)} %get-tuple-element.53), channel_id=1, source_target_pairs={{0,4},{1,5},{2,6},{3,7},{4,0},{5,1},{6,2},{7,3},{8,12},{9,13},{10,... | collective-permute-start | bytes 393224 | tf_op jit(solution)/shard_map/ppermute | solution.py:608
  137.3 21.4 %collective-permute-start.18 = (f32[128,256]{1,0:T(8,128)}, f32[128,256]{1,0:T(8,128)}, u32[]{:S(2)}, u32[]{:S(2)}) collective-permute-start(f32[128,256]{1,0:T(8,128)} %get-tuple-element.54), channel_id=1, source_target_pairs={{0,6},{1,7},{2,4},{3,5},{4,2},{5,3},{6,0},{7,1},{8,14},{9,15},{10,... | collective-permute-start | bytes 393224 | tf_op jit(solution)/shard_map/ppermute | solution.py:608
  140.9 17.8 %collective-permute-start.23 = (f32[128,256]{1,0:T(8,128)}, f32[128,256]{1,0:T(8,128)}, u32[]{:S(2)}, u32[]{:S(2)}) collective-permute-start(f32[128,256]{1,0:T(8,128)} %get-tuple-element.61), channel_id=1, source_target_pairs={{0,2},{1,3},{2,0},{3,1},{4,6},{5,7},{6,4},{7,5},{8,10},{9,11},{10,... | collective-permute-start | bytes 393224 | tf_op jit(solution)/shard_map/ppermute | solution.py:608
  141.5 17.2 %collective-permute-start.24 = (f32[128,256]{1,0:T(8,128)}, f32[128,256]{1,0:T(8,128)}, u32[]{:S(2)}, u32[]{:S(2)}) collective-permute-start(f32[128,256]{1,0:T(8,128)} %get-tuple-element.62), channel_id=1, source_target_pairs={{0,4},{1,5},{2,6},{3,7},{4,0},{5,1},{6,2},{7,3},{8,12},{9,13},{10,... | collective-permute-start | bytes 393224 | tf_op jit(solution)/shard_map/ppermute | solution.py:608
  143.8 14.8 %collective-permute-start.25 = (f32[128,256]{1,0:T(8,128)}, f32[128,256]{1,0:T(8,128)}, u32[]{:S(2)}, u32[]{:S(2)}) collective-permute-start(f32[128,256]{1,0:T(8,128)} %get-tuple-element.63), channel_id=1, source_target_pairs={{0,6},{1,7},{2,4},{3,5},{4,2},{5,3},{6,0},{7,1},{8,14},{9,15},{10,... | collective-permute-start | bytes 393224 | tf_op jit(solution)/shard_map/ppermute | solution.py:608

commit v10 on v9

--- a/solution.py
+++ b/solution.py
@@ -72,38 +72,51 @@
     return local, jnp.exp(offset - jnp.concatenate(full, axis=1)), jnp.exp(offset)
 
 
-def states_kernel(half, per, place_ref, keys_ref, values_ref, decay_ref, near_ref, away_ref, table_ref, work_ref):
-    rows, dim = keys_ref.shape[0], SUB
-    core = place_ref[0]
+def states_kernel(half, per, keys_hbm, values_hbm, decay_ref, near_ref, away_ref, table_ref, work_ref, held_ref, done):
+    rows, dim = keys_hbm.shape[0], SUB
+    core = lax.axis_index("seq") % 2
+    copies = []
+    for slot in range(2 * half):
+        block = 1 - core if slot < half else core
+        group = block * half + slot % half
+        column = pl.ds(pl.multiple_of(group * per * dim, per * dim), per * dim)
+        for which, source in enumerate((keys_hbm, values_hbm)):
+            target = held_ref.at[which, slot]
+            copies.append(pltpu.make_async_copy(source.at[:, column], target, done.at[which, slot]))
+            copies[-1].start()
     row_at = lax.broadcasted_iota(jnp.int32, (dim, dim), 0)
     column_at = lax.broadcasted_iota(jnp.int32, (dim, dim), 1)
     local, tails, total = decay_tables(decay_ref)
     work_ref[0] = tails
     work_ref[2] = jnp.broadcast_to(total, tails.shape)
-    for out, block in ((away_ref, 1 - core), (near_ref, core)):
+    first_gram = {}
+    for slot in range(2 * half):
+        out, block = (away_ref, 1 - core) if slot < half else (near_ref, core)
+        i = slot % half
+        copies[2 * slot].wait()
+        copies[2 * slot + 1].wait()
         for k in range(per):
-            for i in range(half):
-                head = (block * half + i) * per + k
-                column = pl.ds(pl.multiple_of(head * dim, dim), dim)
-                key = keys_ref[:, column]
-                tail = work_ref[0, pl.ds(head, 1), :]
-                key_turned = key.astype(F32).T
-                value_turned = values_ref[:, column].astype(F32).T
-                work_ref[1, pl.ds(head, 1), :] = jnp.sum(key_turned * key_turned, axis=0, keepdims=True)
-                high, low = split(jnp.concatenate([key_turned * tail, value_turned * tail], axis=0))
-                state = dot(high, key) + dot(low, key)
-                gram = state[0:dim]
-                at, second = i // 2, i % 2
-                out[k, at, (1 + second) * dim : (2 + second) * dim, :] = state[dim:]
-                decay = work_ref[2, pl.ds(head, 1), :][:, 0:SUB]
-                out[k, at, 3 * dim + second : 3 * dim + second + 1, :] = decay
-                if second == 0:
-                    first_gram = gram
-                else:
-                    out[k, at, 0:dim, :] = jnp.where(row_at <= column_at, first_gram, gram)
-                    diagonal = jnp.sum(jnp.where(row_at == column_at, gram, 0.0), axis=0, keepdims=True)
-                    out[k, at, 3 * dim + 2 : 3 * dim + 3, :] = diagonal
-                    out[k, at, 3 * dim + 3 :, :] = jnp.zeros((EXTRA - 3, dim), F32)
+            head = (block * half + i) * per + k
+            column = slice(k * dim, (k + 1) * dim)
+            key = held_ref[0, slot, :, column]
+            tail = work_ref[0, pl.ds(head, 1), :]
+            key_turned = key.astype(F32).T
+            value_turned = held_ref[1, slot, :, column].astype(F32).T
+            work_ref[1, pl.ds(head, 1), :] = jnp.sum(key_turned * key_turned, axis=0, keepdims=True)
+            high, low = split(jnp.concatenate([key_turned * tail, value_turned * tail], axis=0))
+            state = dot(high, key) + dot(low, key)
+            gram = state[0:dim]
+            at, second = i // 2, i % 2
+            out[k, at, (1 + second) * dim : (2 + second) * dim, :] = state[dim:]
+            decay = work_ref[2, pl.ds(head, 1), :][:, 0:SUB]
+            out[k, at, 3 * dim + second : 3 * dim + second + 1, :] = decay
+            if second == 0:
+                first_gram[k] = gram
+            else:
+                out[k, at, 0:dim, :] = jnp.where(row_at <= column_at, first_gram[k], gram)
+                diagonal = jnp.sum(jnp.where(row_at == column_at, gram, 0.0), axis=0, keepdims=True)
+                out[k, at, 3 * dim + 2 : 3 * dim + 3, :] = diagonal
+                out[k, at, 3 * dim + 3 :, :] = jnp.zeros((EXTRA - 3, dim), F32)
     carry = jnp.zeros_like(total)
     for c in range(rows // SUB):
         lanes = slice(c * SUB, (c + 1) * SUB)
@@ -113,7 +126,7 @@
         carry = part[:, SUB - 1 : SUB]
 
 
-def local_states(place, keys, values, decay, half, per):
+def local_states(keys, values, decay, half, per):
     rows, columns = keys.shape
     heads = decay.shape[0]
     dim = columns // heads
@@ -122,16 +135,20 @@
     return pl.pallas_call(
         functools.partial(states_kernel, half, per),
         out_shape=[state, state, table],
-        in_specs=[pl.BlockSpec(memory_space=pltpu.SMEM)] + [whole(a) for a in (keys, values, decay)],
+        in_specs=[pl.BlockSpec(memory_space=pl.ANY)] * 2 + [whole(decay)],
         out_specs=[whole(state), whole(state), whole(table)],
-        scratch_shapes=[pltpu.VMEM((3, heads, rows), F32)],
+        scratch_shapes=[
+            pltpu.VMEM((3, heads, rows), F32),
+            pltpu.VMEM((2, 2 * half, rows, per * dim), keys.dtype),
+            pltpu.SemaphoreType.DMA((2, 2 * half)),
+        ],
         grid=(1,),
         compiler_params=FULL,
         cost_estimate=pl.CostEstimate(
             flops=16 * rows * dim * dim * half * per, bytes_accessed=8 * rows * columns, transcendentals=0
         ),
         name="local_states",
-    )(place, keys, values, decay)
+    )(keys, values, decay)
 
 
 def join(earlier, later, dim):
@@ -144,16 +161,16 @@
     return factor * earlier + jnp.where(is_decay, 0.0, later)
 
 
-def chip_kernel(dim, place_ref, own_ref, came_ref, *out_refs):
-    is_first = place_ref[0] == 0
+def chip_kernel(dim, own_ref, came_ref, *out_refs):
+    is_first = lax.axis_index("seq") % 2 == 0
     for k, out_ref in enumerate(out_refs):
         own, came = own_ref[k], came_ref[k]
         out_ref[...] = join(jnp.where(is_first, own, came), jnp.where(is_first, came, own), dim)
 
 
-def start_kernel(dim, k, place_ref, own_ref, came_ref, *refs):
+def start_kernel(dim, k, own_ref, came_ref, *refs):
     sent_refs, (mine_ref, other_ref) = refs[:-2], refs[-2:]
-    is_first = place_ref[0] == 0
+    is_first = lax.axis_index("seq") % 2 == 0
     before = sent_refs[-1][...]
     for ref in reversed(sent_refs[:-1]):
         before = join(before, ref[...], dim)
@@ -162,19 +179,19 @@
     other_ref[...] = jnp.where(is_first, after, before)
 
 
-def combine(kernel, place, arrays, shape, outs):
+def combine(kernel, arrays, shape, outs):
     out = jax.ShapeDtypeStruct(shape, F32)
     return pl.pallas_call(
         kernel,
         out_shape=[out] * outs,
-        in_specs=[pl.BlockSpec(memory_space=pltpu.SMEM)] + [whole(a) for a in arrays],
+        in_specs=[whole(a) for a in arrays],
         out_specs=[whole(out)] * outs,
         grid=(1,),
         compiler_params=FULL,
         cost_estimate=pl.CostEstimate(
             flops=0, bytes_accessed=8 * sum(a.size for a in arrays), transcendentals=0
         ),
-    )(place, *arrays)
+    )(*arrays)
 
 
 def solve_kernel(with_query, with_gradient, bounds, head_of, place_ref, regular_ref, *refs):
@@ -551,10 +568,10 @@
     place = jnp.stack([core, lax.axis_index("dp"), here // 2]).astype(jnp.int32)
     partner = [(i, i ^ 1) for i in range(steps)]
 
-    own, away, table = local_states(place, keys, values, decay, half, per)
+    own, away, table = local_states(keys, values, decay, half, per)
     came = lax.ppermute(away, "seq", partner)
     shape = own.shape[1:]
-    chip_states = combine(functools.partial(chip_kernel, dim), place, [own, came], shape, per)
+    chip_states = combine(functools.partial(chip_kernel, dim), [own, came], shape, per)
     starts = []
     for k, chip_state in enumerate(chip_states):
         sent = []
@@ -562,7 +579,7 @@
             pairs = [(i, i + 2 * z) for i in range(steps - 2 * z)]
             sent.append(lax.ppermute(chip_state, "seq", pairs))
         starting = functools.partial(start_kernel, dim, k)
-        mine, others = combine(starting, place, [own, came, *sent], shape, 2)
+        mine, others = combine(starting, [own, came, *sent], shape, 2)
         starts.append((mine, lax.ppermute(others, "seq", partner)))
 
     picked = pick_columns(place, tokens, chips)

time: 162 us -> 161 us (level)
  transfers between devices with their start and end apart: 26 -> 26, of which waited for: 10 -> 9; matrix products, arithmetic and copies ran while one was open for 4% -> 4% of each run, Pallas kernels for 35% -> 35%
where the time goes in v10:
time: 161 us; the launch traced here: 160 us
  Pallas kernels  77.1 us (48%)
  starting transfers between devices  50.7 us (31%)
  waiting for transfers between devices  25 us (16%)
  matrix products  6.18 us (4%)
    pallas_call x4, Pallas kernels, solve_heads(): pl.pallas_call(functools.partial(solve_kernel, with_query, with_gradient,...  38.5 us
    ppermute x6, starting transfers between devices, program(): sent.append(lax.ppermute(chip_state, 'seq', pairs))  25.5 us
    ppermute x6, starting transfers between devices, program(): finished[-1].append(lax.ppermute(other_block, 'seq', pairs))  13.9 us
    ppermute x8, waiting for transfers between devices, program(): sums[index].append(lax.ppermute(sends[index], 'dp', pairs))  13.4 us
    pallas_call x2, Pallas kernels, gradient_blocks(): pl.pallas_call(functools.partial(gradient_kernel, order), out_shape=[out]...  12.6 us
    ppermute x6, waiting for transfers between devices, program(): sent.append(lax.ppermute(chip_state, 'seq', pairs))  9.84 us
    ppermute x8, starting transfers between devices, program(): sums[index].append(lax.ppermute(sends[index], 'dp', pairs))  9.74 us
    pallas_call x3, Pallas kernels, combine(): pl.pallas_call(kernel, out_shape=[out] * outs, in_specs=[whole(a) for a i...  6.21 us
  transfers between devices with their start and end apart: 26, of which 9 were waited for; matrix products, arithmetic and copies ran while one was open for 4% of the time, Pallas kernels for 35%

profile of v10, /device:TPU:0, one launch (start us, length us, event | category | flops | bytes accessed | tf_op | source)
XLA Modules:
  0.0 160.4 jit_solution(11351410776702833789)
XLA Ops:
  0.6 5.2 %local_states.1 = (f32[2,1,392,128]{3,2,1,0:T(8,128)}, f32[2,1,392,128]{3,2,1,0:T(8,128)}, f32[2,8,512]{2,1,0:T(8,128)}) custom-call(bf16[512,1024]{1,0:T(8,128)(2,1)} %bitcast.15, bf16[512,1024]{1,0:T(8,128)(2,1)} %bitcast.20, f32[8,512]{1,0:T(8,128)} %bitcast.26), custom_call_target="tpu_custom_call" | custom-call | flops 536870912 | bytes 4194304 | tf_op jit(solution)/shard_map/local_states/pallas_call | solution.py:135
  5.8 0.6 collective-permute-start
  6.4 1.7 %collective-permute-done.came_ref = f32[2,1,392,128]{3,2,1,0:T(8,128)} collective-permute-done((f32[2,1,392,128]{3,2,1,0:T(8,128)}, f32[2,1,392,128]{3,2,1,0:T(8,128)}, u32[]{:S(2)}, u32[]{:S(2)}) %collective-permute-start) | collective-permute-done | bytes 401440 | tf_op jit(solution)/shard_map/ppermute | solution.py:572
  8.1 1.9 %shard_map.86 = (f32[1,392,128]{2,1,0:T(8,128)}, f32[1,392,128]{2,1,0:T(8,128)}) custom-call(f32[2,1,392,128]{3,2,1,0:T(8,128)} %get-tuple-element.34.own_ref, f32[2,1,392,128]{3,2,1,0:T(8,128)} %collective-permute-done.came_ref), custom_call_target="tpu_custom_call" | custom-call | bytes 1605632 | tf_op jit(solution)/shard_map/pallas_call | solution.py:184
  10.0 7.5 %collective-permute-start.7 = (f32[1,392,128]{2,1,0:T(8,128)}, f32[1,392,128]{2,1,0:T(8,128)}, u32[]{:S(2)}, u32[]{:S(2)}) collective-permute-start(f32[1,392,128]{2,1,0:T(8,128)} %get-tuple-element.39), channel_id=1, source_target_pairs={{0,6},{1,7},{8,14},{9,15},{16,22},{17,23},{24,30},{25,31}} | collective-permute-start | bytes 602120 | tf_op jit(solution)/shard_map/ppermute | solution.py:580
  17.5 2.0 %collective-permute-start.6 = (f32[1,392,128]{2,1,0:T(8,128)}, f32[1,392,128]{2,1,0:T(8,128)}, u32[]{:S(2)}, u32[]{:S(2)}) collective-permute-start(f32[1,392,128]{2,1,0:T(8,128)} %get-tuple-element.39), channel_id=1, source_target_pairs={{0,4},{1,5},{2,6},{3,7},{8,12},{9,13},{10,14},{11,15},{16,20},{17,... | collective-permute-start | bytes 602120 | tf_op jit(solution)/shard_map/ppermute | solution.py:580
  19.5 2.5 %collective-permute-start.5 = (f32[1,392,128]{2,1,0:T(8,128)}, f32[1,392,128]{2,1,0:T(8,128)}, u32[]{:S(2)}, u32[]{:S(2)}) collective-permute-start(f32[1,392,128]{2,1,0:T(8,128)} %get-tuple-element.39), channel_id=1, source_target_pairs={{0,2},{1,3},{2,4},{3,5},{4,6},{5,7},{8,10},{9,11},{10,12},{11,13},... | collective-permute-start | bytes 602120 | tf_op jit(solution)/shard_map/ppermute | solution.py:580
  22.0 0.7 pad_add_fusion.place_ref.core_ref
  22.6 4.3 %pick_columns.1 = f32[4,512,256]{2,1,0:T(8,128)} custom-call(s32[3]{0:T(128)} %pad_add_fusion.place_ref.core_ref, bf16[512,2048]{1,0:T(8,128)(2,1)} %bitcast.12), custom_call_target="tpu_custom_call" | custom-call | bytes 3145728 | tf_op jit(solution)/shard_map/pick_columns/pallas_call | solution.py:384
  26.9 3.5 %collective-permute-done.5.refs_0_ = f32[1,392,128]{2,1,0:T(8,128)} collective-permute-done((f32[1,392,128]{2,1,0:T(8,128)}, f32[1,392,128]{2,1,0:T(8,128)}, u32[]{:S(2)}, u32[]{:S(2)}) %collective-permute-start.5) | collective-permute-done | bytes 200736 | tf_op jit(solution)/shard_map/ppermute | solution.py:580
  30.4 2.1 %shard_map.88 = (f32[1,392,128]{2,1,0:T(8,128)}, f32[1,392,128]{2,1,0:T(8,128)}) custom-call(f32[2,1,392,128]{3,2,1,0:T(8,128)} %get-tuple-element.34.own_ref, f32[2,1,392,128]{3,2,1,0:T(8,128)} %collective-permute-done.came_ref, f32[1,392,128]{2,1,0:T(8,128)} %collective-permute-done.5.refs_0_, f32[1,392,128]{2,1,0:T(8,128)} %collective-permute-done.6.refs_1_, ...), custom_call_target="tpu_custom_call" | custom-call | bytes 2809856 | tf_op jit(solution)/shard_map/pallas_call | solution.py:184
  32.5 6.2 %convolution_convert_fusion.refs_0_ = bf16[512,1024]{1,0:T(8,128)(2,1)} fusion(bf16[2048,1024]{1,0:T(8,128)(2,1)} %param.8, bf16[1,512,2048]{2,1,0:T(8,128)(2,1)} %param.7), kind=kOutput, calls=%fused_computation | convolution fusion | flops 2148007936 | bytes 7340032 | tf_op jit(solution)/shard_map/dot_general | solution.py:587
  38.7 14.2 %solve_heads.4 = (bf16[512,1024]{1,0:T(8,128)(2,1)}, f32[4,128,512]{2,1,0:T(8,128)}) custom-call(s32[3]{0:T(128)} %pad_add_fusion.place_ref.core_ref, f32[8]{0:T(128)} %regular_ref.7, bf16[512,1024]{1,0:T(8,128)(2,1)} %convolution_convert_fusion.refs_0_, bf16[512,1024]{1,0:T(8,128)(2,1)} %bitcast.27, bf16[512,1024]{1,0:T(8,128)(2,1)} %bitcast.16, ...), custom_call_target="tpu_custom_call" | custom-call | flops 2684354560 | bytes 3670016 | tf_op jit(solution)/shard_map/solve_heads/pallas_call | solution.py:362
  53.4 6.9 %collective-permute-start.3 = (f32[1,392,128]{2,1,0:T(8,128)}, f32[1,392,128]{2,1,0:T(8,128)}, u32[]{:S(2)}, u32[]{:S(2)}) collective-permute-start(f32[1,392,128]{2,1,0:T(8,128)} %get-tuple-element.36), channel_id=1, source_target_pairs={{0,6},{1,7},{8,14},{9,15},{16,22},{17,23},{24,30},{25,31}} | collective-permute-start | bytes 602120 | tf_op jit(solution)/shard_map/ppermute | solution.py:580
  60.3 4.7 %collective-permute-start.2 = (f32[1,392,128]{2,1,0:T(8,128)}, f32[1,392,128]{2,1,0:T(8,128)}, u32[]{:S(2)}, u32[]{:S(2)}) collective-permute-start(f32[1,392,128]{2,1,0:T(8,128)} %get-tuple-element.36), channel_id=1, source_target_pairs={{0,4},{1,5},{2,6},{3,7},{8,12},{9,13},{10,14},{11,15},{16,20},{17,... | collective-permute-start | bytes 602120 | tf_op jit(solution)/shard_map/ppermute | solution.py:580
  65.0 2.0 %collective-permute-start.1 = (f32[1,392,128]{2,1,0:T(8,128)}, f32[1,392,128]{2,1,0:T(8,128)}, u32[]{:S(2)}, u32[]{:S(2)}) collective-permute-start(f32[1,392,128]{2,1,0:T(8,128)} %get-tuple-element.36), channel_id=1, source_target_pairs={{0,2},{1,3},{2,4},{3,5},{4,6},{5,7},{8,10},{9,11},{10,12},{11,13},... | collective-permute-start | bytes 602120 | tf_op jit(solution)/shard_map/ppermute | solution.py:580
  66.9 3.0 %collective-permute-done.2.refs_1_ = f32[1,392,128]{2,1,0:T(8,128)} collective-permute-done((f32[1,392,128]{2,1,0:T(8,128)}, f32[1,392,128]{2,1,0:T(8,128)}, u32[]{:S(2)}, u32[]{:S(2)}) %collective-permute-start.2) | collective-permute-done | bytes 200736 | tf_op jit(solution)/shard_map/ppermute | solution.py:580
  70.0 3.4 %collective-permute-done.1.refs_0_ = f32[1,392,128]{2,1,0:T(8,128)} collective-permute-done((f32[1,392,128]{2,1,0:T(8,128)}, f32[1,392,128]{2,1,0:T(8,128)}, u32[]{:S(2)}, u32[]{:S(2)}) %collective-permute-start.1) | collective-permute-done | bytes 200736 | tf_op jit(solution)/shard_map/ppermute | solution.py:580
  73.3 2.1 %shard_map.87 = (f32[1,392,128]{2,1,0:T(8,128)}, f32[1,392,128]{2,1,0:T(8,128)}) custom-call(f32[2,1,392,128]{3,2,1,0:T(8,128)} %get-tuple-element.34.own_ref, f32[2,1,392,128]{3,2,1,0:T(8,128)} %collective-permute-done.came_ref, f32[1,392,128]{2,1,0:T(8,128)} %collective-permute-done.1.refs_0_, f32[1,392,128]{2,1,0:T(8,128)} %collective-permute-done.2.refs_1_, ...), custom_call_target="tpu_custom_call" | custom-call | bytes 2809856 | tf_op jit(solution)/shard_map/pallas_call | solution.py:184
  75.5 6.4 %gradient_blocks.2 = (f32[2,4,64,256]{3,2,1,0:T(8,128)}, f32[2,4,64,256]{3,2,1,0:T(8,128)}, f32[2,4,64,256]{3,2,1,0:T(8,128)}, f32[2,4,64,256]{3,2,1,0:T(8,128)}) custom-call(s32[3]{0:T(128)} %pad_add_fusion.place_ref.core_ref, f32[4,128,512]{2,1,0:T(8,128)} %get-tuple-element.43.own_ref, f32[4,128,512]{2,1,0:T(8,128)} %collective-permute-done.9.far_ref, ...), custom_call_target="tpu_custom_call" | custom-call | flops 1073741824 | bytes 6291456 | tf_op jit(solution)/shard_map/gradient_blocks/pallas_call | solution.py:430
  81.9 11.6 %solve_heads.5.own_ref = f32[4,128,512]{2,1,0:T(8,128)} custom-call(s32[3]{0:T(128)} %pad_add_fusion.place_ref.core_ref, f32[8]{0:T(128)} %regular_ref.7, bf16[512,1024]{1,0:T(8,128)(2,1)} %bitcast.28, bf16[512,1024]{1,0:T(8,128)(2,1)} %bitcast.17, bf16[512,1024]{1,0:T(8,128)(2,1)} %bitcast.22, f32[2,8,512]{2,1,0:T(8,128)} %get-tuple-element.33.refs_4_.refs_3_, ...), custom_call_target="tpu_custom_call" | custom-call | flops 2684354560 | bytes 3670016 | tf_op jit(solution)/shard_map/solve_heads/pallas_call | solution.py:362
  94.0 1.5 collective-permute-start.12
  95.5 1.5 collective-permute-start.13
  97.0 6.3 %gradient_blocks.3 = (f32[2,4,64,256]{3,2,1,0:T(8,128)}, f32[2,4,64,256]{3,2,1,0:T(8,128)}, f32[2,4,64,256]{3,2,1,0:T(8,128)}, f32[2,4,64,256]{3,2,1,0:T(8,128)}) custom-call(s32[3]{0:T(128)} %pad_add_fusion.place_ref.core_ref, f32[4,128,512]{2,1,0:T(8,128)} %solve_heads.5.own_ref, f32[4,128,512]{2,1,0:T(8,128)} %collective-permute-done.11.far_ref, ...), custom_call_target="tpu_custom_call" | custom-call | flops 1073741824 | bytes 6291456 | tf_op jit(solution)/shard_map/gradient_blocks/pallas_call | solution.py:430
  103.3 1.1 collective-permute-start.19
  104.4 1.5 collective-permute-start.20
  105.9 3.2 %collective-permute-done.12.refs_1_ = f32[2,4,64,256]{3,2,1,0:T(8,128)} collective-permute-done((f32[2,4,64,256]{3,2,1,0:T(8,128)}, f32[2,4,64,256]{3,2,1,0:T(8,128)}, u32[]{:S(2)}, u32[]{:S(2)}) %collective-permute-start.12) | collective-permute-done | bytes 524320 | tf_op jit(solution)/shard_map/ppermute | solution.py:618
  109.1 1.5 collective-permute-done.13.refs_3_.refs_4_
  110.6 2.0 %sum_blocks.2 = (f32[1,4,64,256]{3,2,1,0:T(8,128)}, f32[1,4,64,256]{3,2,1,0:T(8,128)}) custom-call(f32[2,4,64,256]{3,2,1,0:T(8,128)} %get-tuple-element.44.refs_6_.refs_0_, f32[2,4,64,256]{3,2,1,0:T(8,128)} %collective-permute-done.12.refs_1_, f32[2,4,64,256]{3,2,1,0:T(8,128)} %get-tuple-element.47.refs_2_.refs_3_, ...), custom_call_target="tpu_custom_call" | custom-call | bytes 1572864 | tf_op jit(solution)/shard_map/sum_blocks/pallas_call | solution.py:469
  112.6 1.5 collective-permute-start.14
  114.1 0.5 collective-permute-start.15
  114.7 5.7 %collective-permute-done.19.refs_1_ = f32[2,4,64,256]{3,2,1,0:T(8,128)} collective-permute-done((f32[2,4,64,256]{3,2,1,0:T(8,128)}, f32[2,4,64,256]{3,2,1,0:T(8,128)}, u32[]{:S(2)}, u32[]{:S(2)}) %collective-permute-start.19) | collective-permute-done | bytes 524320 | tf_op jit(solution)/shard_map/ppermute | solution.py:618
  120.3 1.5 collective-permute-done.20.refs_3_.refs_4_
  121.8 2.0 %sum_blocks.3 = (f32[1,4,64,256]{3,2,1,0:T(8,128)}, f32[1,4,64,256]{3,2,1,0:T(8,128)}) custom-call(f32[2,4,64,256]{3,2,1,0:T(8,128)} %get-tuple-element.45.refs_6_.refs_0_, f32[2,4,64,256]{3,2,1,0:T(8,128)} %collective-permute-done.19.refs_1_, f32[2,4,64,256]{3,2,1,0:T(8,128)} %get-tuple-element.56.refs_2_.refs_3_, ...), custom_call_target="tpu_custom_call" | custom-call | bytes 1572864 | tf_op jit(solution)/shard_map/sum_blocks/pallas_call | solution.py:469
  123.8 1.5 collective-permute-start.21
  125.4 0.5 collective-permute-start.22
  125.9 1.6 collective-permute-done.14.refs_2_
  127.5 2.1 %merge_blocks.2 = (f32[128,256]{1,0:T(8,128)}, f32[128,256]{1,0:T(8,128)}, f32[128,256]{1,0:T(8,128)}, f32[128,256]{1,0:T(8,128)}) custom-call(f32[2,4,64,256]{3,2,1,0:T(8,128)} %get-tuple-element.44.refs_6_.refs_0_, f32[2,4,64,256]{3,2,1,0:T(8,128)} %collective-permute-done.12.refs_1_, f32[1,4,64,256]{3,2,1,0:T(8,128)} %collective-permute-done.14.refs_2_, ...), custom_call_target="tpu_custom_call" | custom-call | bytes 2097152 | tf_op jit(solution)/shard_map/merge_blocks/pallas_call | solution.py:501
  129.6 5.4 %collective-permute-start.16 = (f32[128,256]{1,0:T(8,128)}, f32[128,256]{1,0:T(8,128)}, u32[]{:S(2)}, u32[]{:S(2)}) collective-permute-start(f32[128,256]{1,0:T(8,128)} %get-tuple-element.52), channel_id=1, source_target_pairs={{0,2},{1,3},{2,0},{3,1},{4,6},{5,7},{6,4},{7,5},{8,10},{9,11},{10,... | collective-permute-start | bytes 393224 | tf_op jit(solution)/shard_map/ppermute | solution.py:625
  135.0 1.9 %collective-permute-start.17 = (f32[128,256]{1,0:T(8,128)}, f32[128,256]{1,0:T(8,128)}, u32[]{:S(2)}, u32[]{:S(2)}) collective-permute-start(f32[128,256]{1,0:T(8,128)} %get-tuple-element.53), channel_id=1, source_target_pairs={{0,4},{1,5},{2,6},{3,7},{4,0},{5,1},{6,2},{7,3},{8,12},{9,13},{10,... | collective-permute-start | bytes 393224 | tf_op jit(solution)/shard_map/ppermute | solution.py:625
  136.9 1.4 collective-permute-start.18
  138.4 2.2 %merge_blocks.3 = (f32[128,256]{1,0:T(8,128)}, f32[128,256]{1,0:T(8,128)}, f32[128,256]{1,0:T(8,128)}, f32[128,256]{1,0:T(8,128)}) custom-call(f32[2,4,64,256]{3,2,1,0:T(8,128)} %get-tuple-element.45.refs_6_.refs_0_, f32[2,4,64,256]{3,2,1,0:T(8,128)} %collective-permute-done.19.refs_1_, f32[1,4,64,256]{3,2,1,0:T(8,128)} %collective-permute-done.21.refs_2_, ...), custom_call_target="tpu_custom_call" | custom-call | bytes 2097152 | tf_op jit(solution)/shard_map/merge_blocks/pallas_call | solution.py:501
  140.6 0.6 collective-permute-start.23
  141.1 2.4 %collective-permute-start.24 = (f32[128,256]{1,0:T(8,128)}, f32[128,256]{1,0:T(8,128)}, u32[]{:S(2)}, u32[]{:S(2)}) collective-permute-start(f32[128,256]{1,0:T(8,128)} %get-tuple-element.62), channel_id=1, source_target_pairs={{0,4},{1,5},{2,6},{3,7},{4,0},{5,1},{6,2},{7,3},{8,12},{9,13},{10,... | collective-permute-start | bytes 393224 | tf_op jit(solution)/shard_map/ppermute | solution.py:625
  143.5 2.2 %collective-permute-start.25 = (f32[128,256]{1,0:T(8,128)}, f32[128,256]{1,0:T(8,128)}, u32[]{:S(2)}, u32[]{:S(2)}) collective-permute-start(f32[128,256]{1,0:T(8,128)} %get-tuple-element.63), channel_id=1, source_target_pairs={{0,6},{1,7},{2,4},{3,5},{4,2},{5,3},{6,0},{7,1},{8,14},{9,15},{10,... | collective-permute-start | bytes 393224 | tf_op jit(solution)/shard_map/ppermute | solution.py:625
  145.7 6.3 %solve_heads.6.refs_5_ = bf16[512,1024]{1,0:T(8,128)(2,1)} custom-call(s32[3]{0:T(128)} %pad_add_fusion.place_ref.core_ref, f32[8]{0:T(128)} %regular_ref.7, bf16[512,1024]{1,0:T(8,128)(2,1)} %convolution_convert_fusion.refs_0_, bf16[512,1024]{1,0:T(8,128)(2,1)} %bitcast.18, bf16[512,1024]{1,0:T(8,128)(2,1)} %bitcast.23, ...), custom_call_target="tpu_custom_call", output_to_operand_aliasing={{}: (7, {})} | custom-call | flops 1342177280 | bytes 1835008 | tf_op jit(solution)/shard_map/solve_heads/pallas_call | solution.py:362
  152.0 6.3 %solve_heads.7 = bf16[512,1024]{1,0:T(8,128)(2,1)} custom-call(s32[3]{0:T(128)} %pad_add_fusion.place_ref.core_ref, f32[8]{0:T(128)} %regular_ref.7, bf16[512,1024]{1,0:T(8,128)(2,1)} %convolution_convert_fusion.refs_0_, bf16[512,1024]{1,0:T(8,128)(2,1)} %bitcast.19, bf16[512,1024]{1,0:T(8,128)(2,1)} %bitcast.24, ...), custom_call_target="tpu_custom_call", output_to_operand_aliasing={{}: (7, {})} | custom-call | flops 1342177280 | bytes 1835008 | tf_op jit(solution)/shard_map/solve_heads/pallas_call | solution.py:362
  158.4 2.0 %finish.1 = f32[256,256]{1,0:T(8,128)} custom-call(f32[128,256]{1,0:T(8,128)} %get-tuple-element.51.refs_0_, f32[128,256]{1,0:T(8,128)} %collective-permute-done.16.refs_1_, f32[128,256]{1,0:T(8,128)} %collective-permute-done.17.refs_2_, f32[128,256]{1,0:T(8,128)} %collective-permute-done.18.refs_3_, f32[128,256]{1,0:T(8,128)} %get-tuple-element.60.refs_4_, ...), custom_call_target="tpu_custom_call" | custom-call | bytes 1310720 | tf_op jit(solution)/shard_map/finish/pallas_call | solution.py:529
  (22 shorter events, 1.1 us)
Async XLA Ops:
  5.8 2.3 %collective-permute-start = (f32[2,1,392,128]{3,2,1,0:T(8,128)}, f32[2,1,392,128]{3,2,1,0:T(8,128)}, u32[]{:S(2)}, u32[]{:S(2)}) collective-permute-start(f32[2,1,392,128]{3,2,1,0:T(8,128)} %get-tuple-element.35), channel_id=1, source_target_pairs={{0,1},{1,0},{2,3},{3,2},{4,5},{5,4},{6,7},{7,6},{8,9},{9,8},{10,11... | collective-permute-start | bytes 1204232 | tf_op jit(solution)/shard_map/ppermute | solution.py:572
  10.0 16.9 %collective-permute-start.7 = (f32[1,392,128]{2,1,0:T(8,128)}, f32[1,392,128]{2,1,0:T(8,128)}, u32[]{:S(2)}, u32[]{:S(2)}) collective-permute-start(f32[1,392,128]{2,1,0:T(8,128)} %get-tuple-element.39), channel_id=1, source_target_pairs={{0,6},{1,7},{8,14},{9,15},{16,22},{17,23},{24,30},{25,31}} | collective-permute-start | bytes 602120 | tf_op jit(solution)/shard_map/ppermute | solution.py:580
  17.5 9.4 %collective-permute-start.6 = (f32[1,392,128]{2,1,0:T(8,128)}, f32[1,392,128]{2,1,0:T(8,128)}, u32[]{:S(2)}, u32[]{:S(2)}) collective-permute-start(f32[1,392,128]{2,1,0:T(8,128)} %get-tuple-element.39), channel_id=1, source_target_pairs={{0,4},{1,5},{2,6},{3,7},{8,12},{9,13},{10,14},{11,15},{16,20},{17,... | collective-permute-start | bytes 602120 | tf_op jit(solution)/shard_map/ppermute | solution.py:580
  19.5 10.9 %collective-permute-start.5 = (f32[1,392,128]{2,1,0:T(8,128)}, f32[1,392,128]{2,1,0:T(8,128)}, u32[]{:S(2)}, u32[]{:S(2)}) collective-permute-start(f32[1,392,128]{2,1,0:T(8,128)} %get-tuple-element.39), channel_id=1, source_target_pairs={{0,2},{1,3},{2,4},{3,5},{4,6},{5,7},{8,10},{9,11},{10,12},{11,13},... | collective-permute-start | bytes 602120 | tf_op jit(solution)/shard_map/ppermute | solution.py:580
  26.9 48.6 %collective-permute-start.10 = (f32[4,512,256]{2,1,0:T(8,128)}, f32[4,512,256]{2,1,0:T(8,128)}, u32[]{:S(2)}, u32[]{:S(2)}) collective-permute-start(f32[4,512,256]{2,1,0:T(8,128)} %pick_columns.1), channel_id=1, source_target_pairs={{0,1},{1,0},{2,3},{3,2},{4,5},{5,4},{6,7},{7,6},{8,9},{9,8},{10,11... | collective-permute-start | bytes 6291464 | tf_op jit(solution)/shard_map/ppermute | solution.py:586
  32.5 6.2 %collective-permute-start.8 = (f32[1,392,128]{2,1,0:T(8,128)}, f32[1,392,128]{2,1,0:T(8,128)}, u32[]{:S(2)}, u32[]{:S(2)}) collective-permute-start(f32[1,392,128]{2,1,0:T(8,128)} %get-tuple-element.41), channel_id=1, source_target_pairs={{0,1},{1,0},{2,3},{3,2},{4,5},{5,4},{6,7},{7,6},{8,9},{9,8},{10,11... | collective-permute-start | bytes 602120 | tf_op jit(solution)/shard_map/ppermute | solution.py:583
  52.9 22.6 %collective-permute-start.9 = (f32[4,128,512]{2,1,0:T(8,128)}, f32[4,128,512]{2,1,0:T(8,128)}, u32[]{:S(2)}, u32[]{:S(2)}) collective-permute-start(f32[4,128,512]{2,1,0:T(8,128)} %get-tuple-element.43.own_ref), channel_id=1, source_target_pairs={{0,1},{1,0},{2,3},{3,2},{4,5},{5,4},{6,7},{7,6},{8,9},{9,8},{10,11... | collective-permute-start | bytes 3145736 | tf_op jit(solution)/shard_map/ppermute | solution.py:603
  53.4 13.5 %collective-permute-start.3 = (f32[1,392,128]{2,1,0:T(8,128)}, f32[1,392,128]{2,1,0:T(8,128)}, u32[]{:S(2)}, u32[]{:S(2)}) collective-permute-start(f32[1,392,128]{2,1,0:T(8,128)} %get-tuple-element.36), channel_id=1, source_target_pairs={{0,6},{1,7},{8,14},{9,15},{16,22},{17,23},{24,30},{25,31}} | collective-permute-start | bytes 602120 | tf_op jit(solution)/shard_map/ppermute | solution.py:580
  60.3 9.6 %collective-permute-start.2 = (f32[1,392,128]{2,1,0:T(8,128)}, f32[1,392,128]{2,1,0:T(8,128)}, u32[]{:S(2)}, u32[]{:S(2)}) collective-permute-start(f32[1,392,128]{2,1,0:T(8,128)} %get-tuple-element.36), channel_id=1, source_target_pairs={{0,4},{1,5},{2,6},{3,7},{8,12},{9,13},{10,14},{11,15},{16,20},{17,... | collective-permute-start | bytes 602120 | tf_op jit(solution)/shard_map/ppermute | solution.py:580
  65.0 8.4 %collective-permute-start.1 = (f32[1,392,128]{2,1,0:T(8,128)}, f32[1,392,128]{2,1,0:T(8,128)}, u32[]{:S(2)}, u32[]{:S(2)}) collective-permute-start(f32[1,392,128]{2,1,0:T(8,128)} %get-tuple-element.36), channel_id=1, source_target_pairs={{0,2},{1,3},{2,4},{3,5},{4,6},{5,7},{8,10},{9,11},{10,12},{11,13},... | collective-permute-start | bytes 602120 | tf_op jit(solution)/shard_map/ppermute | solution.py:580
  75.5 6.4 %collective-permute-start.4 = (f32[1,392,128]{2,1,0:T(8,128)}, f32[1,392,128]{2,1,0:T(8,128)}, u32[]{:S(2)}, u32[]{:S(2)}) collective-permute-start(f32[1,392,128]{2,1,0:T(8,128)} %get-tuple-element.37), channel_id=1, source_target_pairs={{0,1},{1,0},{2,3},{3,2},{4,5},{5,4},{6,7},{7,6},{8,9},{9,8},{10,11... | collective-permute-start | bytes 602120 | tf_op jit(solution)/shard_map/ppermute | solution.py:583
  93.5 3.5 %collective-permute-start.11 = (f32[4,128,512]{2,1,0:T(8,128)}, f32[4,128,512]{2,1,0:T(8,128)}, u32[]{:S(2)}, u32[]{:S(2)}) collective-permute-start(f32[4,128,512]{2,1,0:T(8,128)} %solve_heads.5.own_ref), channel_id=1, source_target_pairs={{0,1},{1,0},{2,3},{3,2},{4,5},{5,4},{6,7},{7,6},{8,9},{9,8},{10,11... | collective-permute-start | bytes 3145736 | tf_op jit(solution)/shard_map/ppermute | solution.py:603
  94.0 15.1 %collective-permute-start.12 = (f32[2,4,64,256]{3,2,1,0:T(8,128)}, f32[2,4,64,256]{3,2,1,0:T(8,128)}, u32[]{:S(2)}, u32[]{:S(2)}) collective-permute-start(f32[2,4,64,256]{3,2,1,0:T(8,128)} %get-tuple-element.46), channel_id=1, source_target_pairs={{0,8},{8,0},{16,24},{24,16},{1,9},{9,1},{17,25},{25,17},{2,10},{10... | collective-permute-start | bytes 1572872 | tf_op jit(solution)/shard_map/ppermute | solution.py:618
  95.5 15.1 %collective-permute-start.13 = (f32[2,4,64,256]{3,2,1,0:T(8,128)}, f32[2,4,64,256]{3,2,1,0:T(8,128)}, u32[]{:S(2)}, u32[]{:S(2)}) collective-permute-start(f32[2,4,64,256]{3,2,1,0:T(8,128)} %get-tuple-element.48), channel_id=1, source_target_pairs={{0,16},{8,24},{16,0},{24,8},{1,17},{9,25},{17,1},{25,9},{2,18},{10... | collective-permute-start | bytes 1572872 | tf_op jit(solution)/shard_map/ppermute | solution.py:618
  103.3 17.1 %collective-permute-start.19 = (f32[2,4,64,256]{3,2,1,0:T(8,128)}, f32[2,4,64,256]{3,2,1,0:T(8,128)}, u32[]{:S(2)}, u32[]{:S(2)}) collective-permute-start(f32[2,4,64,256]{3,2,1,0:T(8,128)} %get-tuple-element.55), channel_id=1, source_target_pairs={{0,8},{8,0},{16,24},{24,16},{1,9},{9,1},{17,25},{25,17},{2,10},{10... | collective-permute-start | bytes 1572872 | tf_op jit(solution)/shard_map/ppermute | solution.py:618
  104.4 17.4 %collective-permute-start.20 = (f32[2,4,64,256]{3,2,1,0:T(8,128)}, f32[2,4,64,256]{3,2,1,0:T(8,128)}, u32[]{:S(2)}, u32[]{:S(2)}) collective-permute-start(f32[2,4,64,256]{3,2,1,0:T(8,128)} %get-tuple-element.57), channel_id=1, source_target_pairs={{0,16},{8,24},{16,0},{24,8},{1,17},{9,25},{17,1},{25,9},{2,18},{10... | collective-permute-start | bytes 1572872 | tf_op jit(solution)/shard_map/ppermute | solution.py:618
  112.6 14.9 %collective-permute-start.14 = (f32[1,4,64,256]{3,2,1,0:T(8,128)}, f32[1,4,64,256]{3,2,1,0:T(8,128)}, u32[]{:S(2)}, u32[]{:S(2)}) collective-permute-start(f32[1,4,64,256]{3,2,1,0:T(8,128)} %get-tuple-element.49), channel_id=1, source_target_pairs={{0,16},{8,24},{16,0},{24,8},{1,17},{9,25},{17,1},{25,9},{2,18},{10... | collective-permute-start | bytes 786440 | tf_op jit(solution)/shard_map/ppermute | solution.py:618
  114.1 13.3 %collective-permute-start.15 = (f32[1,4,64,256]{3,2,1,0:T(8,128)}, f32[1,4,64,256]{3,2,1,0:T(8,128)}, u32[]{:S(2)}, u32[]{:S(2)}) collective-permute-start(f32[1,4,64,256]{3,2,1,0:T(8,128)} %get-tuple-element.50), channel_id=1, source_target_pairs={{0,8},{8,0},{16,24},{24,16},{1,9},{9,1},{17,25},{25,17},{2,10},{10... | collective-permute-start | bytes 786440 | tf_op jit(solution)/shard_map/ppermute | solution.py:618
  123.8 14.5 %collective-permute-start.21 = (f32[1,4,64,256]{3,2,1,0:T(8,128)}, f32[1,4,64,256]{3,2,1,0:T(8,128)}, u32[]{:S(2)}, u32[]{:S(2)}) collective-permute-start(f32[1,4,64,256]{3,2,1,0:T(8,128)} %get-tuple-element.58), channel_id=1, source_target_pairs={{0,16},{8,24},{16,0},{24,8},{1,17},{9,25},{17,1},{25,9},{2,18},{10... | collective-permute-start | bytes 786440 | tf_op jit(solution)/shard_map/ppermute | solution.py:618
  125.4 13.0 %collective-permute-start.22 = (f32[1,4,64,256]{3,2,1,0:T(8,128)}, f32[1,4,64,256]{3,2,1,0:T(8,128)}, u32[]{:S(2)}, u32[]{:S(2)}) collective-permute-start(f32[1,4,64,256]{3,2,1,0:T(8,128)} %get-tuple-element.59), channel_id=1, source_target_pairs={{0,8},{8,0},{16,24},{24,16},{1,9},{9,1},{17,25},{25,17},{2,10},{10... | collective-permute-start | bytes 786440 | tf_op jit(solution)/shard_map/ppermute | solution.py:618
  129.6 13.9 %collective-permute-start.16 = (f32[128,256]{1,0:T(8,128)}, f32[128,256]{1,0:T(8,128)}, u32[]{:S(2)}, u32[]{:S(2)}) collective-permute-start(f32[128,256]{1,0:T(8,128)} %get-tuple-element.52), channel_id=1, source_target_pairs={{0,2},{1,3},{2,0},{3,1},{4,6},{5,7},{6,4},{7,5},{8,10},{9,11},{10,... | collective-permute-start | bytes 393224 | tf_op jit(solution)/shard_map/ppermute | solution.py:625
  135.0 23.3 %collective-permute-start.17 = (f32[128,256]{1,0:T(8,128)}, f32[128,256]{1,0:T(8,128)}, u32[]{:S(2)}, u32[]{:S(2)}) collective-permute-start(f32[128,256]{1,0:T(8,128)} %get-tuple-element.53), channel_id=1, source_target_pairs={{0,4},{1,5},{2,6},{3,7},{4,0},{5,1},{6,2},{7,3},{8,12},{9,13},{10,... | collective-permute-start | bytes 393224 | tf_op jit(solution)/shard_map/ppermute | solution.py:625
  136.9 21.4 %collective-permute-start.18 = (f32[128,256]{1,0:T(8,128)}, f32[128,256]{1,0:T(8,128)}, u32[]{:S(2)}, u32[]{:S(2)}) collective-permute-start(f32[128,256]{1,0:T(8,128)} %get-tuple-element.54), channel_id=1, source_target_pairs={{0,6},{1,7},{2,4},{3,5},{4,2},{5,3},{6,0},{7,1},{8,14},{9,15},{10,... | collective-permute-start | bytes 393224 | tf_op jit(solution)/shard_map/ppermute | solution.py:625
  140.6 17.8 %collective-permute-start.23 = (f32[128,256]{1,0:T(8,128)}, f32[128,256]{1,0:T(8,128)}, u32[]{:S(2)}, u32[]{:S(2)}) collective-permute-start(f32[128,256]{1,0:T(8,128)} %get-tuple-element.61), channel_id=1, source_target_pairs={{0,2},{1,3},{2,0},{3,1},{4,6},{5,7},{6,4},{7,5},{8,10},{9,11},{10,... | collective-permute-start | bytes 393224 | tf_op jit(solution)/shard_map/ppermute | solution.py:625
  141.1 17.2 %collective-permute-start.24 = (f32[128,256]{1,0:T(8,128)}, f32[128,256]{1,0:T(8,128)}, u32[]{:S(2)}, u32[]{:S(2)}) collective-permute-start(f32[128,256]{1,0:T(8,128)} %get-tuple-element.62), channel_id=1, source_target_pairs={{0,4},{1,5},{2,6},{3,7},{4,0},{5,1},{6,2},{7,3},{8,12},{9,13},{10,... | collective-permute-start | bytes 393224 | tf_op jit(solution)/shard_map/ppermute | solution.py:625
  143.5 14.8 %collective-permute-start.25 = (f32[128,256]{1,0:T(8,128)}, f32[128,256]{1,0:T(8,128)}, u32[]{:S(2)}, u32[]{:S(2)}) collective-permute-start(f32[128,256]{1,0:T(8,128)} %get-tuple-element.63), channel_id=1, source_target_pairs={{0,6},{1,7},{2,4},{3,5},{4,2},{5,3},{6,0},{7,1},{8,14},{9,15},{10,... | collective-permute-start | bytes 393224 | tf_op jit(solution)/shard_map/ppermute | solution.py:625

commit v11 on v10

--- a/solution.py
+++ b/solution.py
@@ -72,18 +72,9 @@
     return local, jnp.exp(offset - jnp.concatenate(full, axis=1)), jnp.exp(offset)
 
 
-def states_kernel(half, per, keys_hbm, values_hbm, decay_ref, near_ref, away_ref, table_ref, work_ref, held_ref, done):
-    rows, dim = keys_hbm.shape[0], SUB
+def states_kernel(half, per, keys_ref, values_ref, decay_ref, near_ref, away_ref, table_ref, work_ref):
+    rows, dim = keys_ref.shape[0], SUB
     core = lax.axis_index("seq") % 2
-    copies = []
-    for slot in range(2 * half):
-        block = 1 - core if slot < half else core
-        group = block * half + slot % half
-        column = pl.ds(pl.multiple_of(group * per * dim, per * dim), per * dim)
-        for which, source in enumerate((keys_hbm, values_hbm)):
-            target = held_ref.at[which, slot]
-            copies.append(pltpu.make_async_copy(source.at[:, column], target, done.at[which, slot]))
-            copies[-1].start()
     row_at = lax.broadcasted_iota(jnp.int32, (dim, dim), 0)
     column_at = lax.broadcasted_iota(jnp.int32, (dim, dim), 1)
     local, tails, total = decay_tables(decay_ref)
@@ -93,15 +84,13 @@
     for slot in range(2 * half):
         out, block = (away_ref, 1 - core) if slot < half else (near_ref, core)
         i = slot % half
-        copies[2 * slot].wait()
-        copies[2 * slot + 1].wait()
         for k in range(per):
             head = (block * half + i) * per + k
-            column = slice(k * dim, (k + 1) * dim)
-            key = held_ref[0, slot, :, column]
+            column = pl.ds(pl.multiple_of(head * dim, dim), dim)
+            key = keys_ref[:, column]
             tail = work_ref[0, pl.ds(head, 1), :]
             key_turned = key.astype(F32).T
-            value_turned = held_ref[1, slot, :, column].astype(F32).T
+            value_turned = values_ref[:, column].astype(F32).T
             work_ref[1, pl.ds(head, 1), :] = jnp.sum(key_turned * key_turned, axis=0, keepdims=True)
             high, low = split(jnp.concatenate([key_turned * tail, value_turned * tail], axis=0))
             state = dot(high, key) + dot(low, key)
@@ -135,13 +124,9 @@
     return pl.pallas_call(
         functools.partial(states_kernel, half, per),
         out_shape=[state, state, table],
-        in_specs=[pl.BlockSpec(memory_space=pl.ANY)] * 2 + [whole(decay)],
+        in_specs=[whole(a) for a in (keys, values, decay)],
         out_specs=[whole(state), whole(state), whole(table)],
-        scratch_shapes=[
-            pltpu.VMEM((3, heads, rows), F32),
-            pltpu.VMEM((2, 2 * half, rows, per * dim), keys.dtype),
-            pltpu.SemaphoreType.DMA((2, 2 * half)),
-        ],
+        scratch_shapes=[pltpu.VMEM((3, heads, rows), F32)],
         grid=(1,),
         compiler_params=FULL,
         cost_estimate=pl.CostEstimate(

time: 161 us -> 161 us (level)
  no operation moved by 1% of the time
where the time goes in v11:
time: 161 us; the launch traced here: 160 us
  Pallas kernels  77 us (48%)
  starting transfers between devices  50.7 us (31%)
  waiting for transfers between devices  25 us (16%)
  matrix products  6.18 us (4%)
    pallas_call x4, Pallas kernels, solve_heads(): pl.pallas_call(functools.partial(solve_kernel, with_query, with_gradient,...  38.5 us
    ppermute x6, starting transfers between devices, program(): sent.append(lax.ppermute(chip_state, 'seq', pairs))  25.5 us
    ppermute x6, starting transfers between devices, program(): finished[-1].append(lax.ppermute(other_block, 'seq', pairs))  13.9 us
    ppermute x8, waiting for transfers between devices, program(): sums[index].append(lax.ppermute(sends[index], 'dp', pairs))  13.4 us
    pallas_call x2, Pallas kernels, gradient_blocks(): pl.pallas_call(functools.partial(gradient_kernel, order), out_shape=[out]...  12.6 us
    ppermute x6, waiting for transfers between devices, program(): sent.append(lax.ppermute(chip_state, 'seq', pairs))  9.84 us
    ppermute x8, starting transfers between devices, program(): sums[index].append(lax.ppermute(sends[index], 'dp', pairs))  9.75 us
    pallas_call x3, Pallas kernels, combine(): pl.pallas_call(kernel, out_shape=[out] * outs, in_specs=[whole(a) for a i...  6.21 us
  transfers between devices with their start and end apart: 26, of which 9 were waited for; matrix products, arithmetic and copies ran while one was open for 4% of the time, Pallas kernels for 35%

profile of v11, /device:TPU:0, one launch (start us, length us, event | category | flops | bytes accessed | tf_op | source)
XLA Modules:
  0.0 160.2 jit_solution(2548766477595065945)
XLA Ops:
  0.6 5.0 %local_states.1 = (f32[2,1,392,128]{3,2,1,0:T(8,128)}, f32[2,1,392,128]{3,2,1,0:T(8,128)}, f32[2,8,512]{2,1,0:T(8,128)}) custom-call(bf16[512,1024]{1,0:T(8,128)(2,1)} %bitcast.15, bf16[512,1024]{1,0:T(8,128)(2,1)} %bitcast.20, f32[8,512]{1,0:T(8,128)} %bitcast.26), custom_call_target="tpu_custom_call" | custom-call | flops 536870912 | bytes 4194304 | tf_op jit(solution)/shard_map/local_states/pallas_call | solution.py:124
  5.6 0.5 collective-permute-start
  6.2 1.7 %collective-permute-done.came_ref = f32[2,1,392,128]{3,2,1,0:T(8,128)} collective-permute-done((f32[2,1,392,128]{3,2,1,0:T(8,128)}, f32[2,1,392,128]{3,2,1,0:T(8,128)}, u32[]{:S(2)}, u32[]{:S(2)}) %collective-permute-start) | collective-permute-done | bytes 401440 | tf_op jit(solution)/shard_map/ppermute | solution.py:557
  7.9 1.9 %shard_map.86 = (f32[1,392,128]{2,1,0:T(8,128)}, f32[1,392,128]{2,1,0:T(8,128)}) custom-call(f32[2,1,392,128]{3,2,1,0:T(8,128)} %get-tuple-element.34.own_ref, f32[2,1,392,128]{3,2,1,0:T(8,128)} %collective-permute-done.came_ref), custom_call_target="tpu_custom_call" | custom-call | bytes 1605632 | tf_op jit(solution)/shard_map/pallas_call | solution.py:169
  9.8 7.5 %collective-permute-start.7 = (f32[1,392,128]{2,1,0:T(8,128)}, f32[1,392,128]{2,1,0:T(8,128)}, u32[]{:S(2)}, u32[]{:S(2)}) collective-permute-start(f32[1,392,128]{2,1,0:T(8,128)} %get-tuple-element.39), channel_id=1, source_target_pairs={{0,6},{1,7},{8,14},{9,15},{16,22},{17,23},{24,30},{25,31}} | collective-permute-start | bytes 602120 | tf_op jit(solution)/shard_map/ppermute | solution.py:565
  17.3 2.0 %collective-permute-start.6 = (f32[1,392,128]{2,1,0:T(8,128)}, f32[1,392,128]{2,1,0:T(8,128)}, u32[]{:S(2)}, u32[]{:S(2)}) collective-permute-start(f32[1,392,128]{2,1,0:T(8,128)} %get-tuple-element.39), channel_id=1, source_target_pairs={{0,4},{1,5},{2,6},{3,7},{8,12},{9,13},{10,14},{11,15},{16,20},{17,... | collective-permute-start | bytes 602120 | tf_op jit(solution)/shard_map/ppermute | solution.py:565
  19.3 2.5 %collective-permute-start.5 = (f32[1,392,128]{2,1,0:T(8,128)}, f32[1,392,128]{2,1,0:T(8,128)}, u32[]{:S(2)}, u32[]{:S(2)}) collective-permute-start(f32[1,392,128]{2,1,0:T(8,128)} %get-tuple-element.39), channel_id=1, source_target_pairs={{0,2},{1,3},{2,4},{3,5},{4,6},{5,7},{8,10},{9,11},{10,12},{11,13},... | collective-permute-start | bytes 602120 | tf_op jit(solution)/shard_map/ppermute | solution.py:565
  21.7 0.7 pad_add_fusion.place_ref.core_ref
  22.4 4.3 %pick_columns.1 = f32[4,512,256]{2,1,0:T(8,128)} custom-call(s32[3]{0:T(128)} %pad_add_fusion.place_ref.core_ref, bf16[512,2048]{1,0:T(8,128)(2,1)} %bitcast.12), custom_call_target="tpu_custom_call" | custom-call | bytes 3145728 | tf_op jit(solution)/shard_map/pick_columns/pallas_call | solution.py:369
  26.7 3.5 %collective-permute-done.5.refs_0_ = f32[1,392,128]{2,1,0:T(8,128)} collective-permute-done((f32[1,392,128]{2,1,0:T(8,128)}, f32[1,392,128]{2,1,0:T(8,128)}, u32[]{:S(2)}, u32[]{:S(2)}) %collective-permute-start.5) | collective-permute-done | bytes 200736 | tf_op jit(solution)/shard_map/ppermute | solution.py:565
  30.1 2.1 %shard_map.88 = (f32[1,392,128]{2,1,0:T(8,128)}, f32[1,392,128]{2,1,0:T(8,128)}) custom-call(f32[2,1,392,128]{3,2,1,0:T(8,128)} %get-tuple-element.34.own_ref, f32[2,1,392,128]{3,2,1,0:T(8,128)} %collective-permute-done.came_ref, f32[1,392,128]{2,1,0:T(8,128)} %collective-permute-done.5.refs_0_, f32[1,392,128]{2,1,0:T(8,128)} %collective-permute-done.6.refs_1_, ...), custom_call_target="tpu_custom_call" | custom-call | bytes 2809856 | tf_op jit(solution)/shard_map/pallas_call | solution.py:169
  32.3 6.2 %convolution_convert_fusion.refs_0_ = bf16[512,1024]{1,0:T(8,128)(2,1)} fusion(bf16[2048,1024]{1,0:T(8,128)(2,1)} %param.8, bf16[1,512,2048]{2,1,0:T(8,128)(2,1)} %param.7), kind=kOutput, calls=%fused_computation | convolution fusion | flops 2148007936 | bytes 7340032 | tf_op jit(solution)/shard_map/dot_general | solution.py:572
  38.5 14.2 %solve_heads.4 = (bf16[512,1024]{1,0:T(8,128)(2,1)}, f32[4,128,512]{2,1,0:T(8,128)}) custom-call(s32[3]{0:T(128)} %pad_add_fusion.place_ref.core_ref, f32[8]{0:T(128)} %regular_ref.7, bf16[512,1024]{1,0:T(8,128)(2,1)} %convolution_convert_fusion.refs_0_, bf16[512,1024]{1,0:T(8,128)(2,1)} %bitcast.27, bf16[512,1024]{1,0:T(8,128)(2,1)} %bitcast.16, ...), custom_call_target="tpu_custom_call" | custom-call | flops 2684354560 | bytes 3670016 | tf_op jit(solution)/shard_map/solve_heads/pallas_call | solution.py:347
  53.2 6.9 %collective-permute-start.3 = (f32[1,392,128]{2,1,0:T(8,128)}, f32[1,392,128]{2,1,0:T(8,128)}, u32[]{:S(2)}, u32[]{:S(2)}) collective-permute-start(f32[1,392,128]{2,1,0:T(8,128)} %get-tuple-element.36), channel_id=1, source_target_pairs={{0,6},{1,7},{8,14},{9,15},{16,22},{17,23},{24,30},{25,31}} | collective-permute-start | bytes 602120 | tf_op jit(solution)/shard_map/ppermute | solution.py:565
  60.1 4.7 %collective-permute-start.2 = (f32[1,392,128]{2,1,0:T(8,128)}, f32[1,392,128]{2,1,0:T(8,128)}, u32[]{:S(2)}, u32[]{:S(2)}) collective-permute-start(f32[1,392,128]{2,1,0:T(8,128)} %get-tuple-element.36), channel_id=1, source_target_pairs={{0,4},{1,5},{2,6},{3,7},{8,12},{9,13},{10,14},{11,15},{16,20},{17,... | collective-permute-start | bytes 602120 | tf_op jit(solution)/shard_map/ppermute | solution.py:565
  64.7 2.0 %collective-permute-start.1 = (f32[1,392,128]{2,1,0:T(8,128)}, f32[1,392,128]{2,1,0:T(8,128)}, u32[]{:S(2)}, u32[]{:S(2)}) collective-permute-start(f32[1,392,128]{2,1,0:T(8,128)} %get-tuple-element.36), channel_id=1, source_target_pairs={{0,2},{1,3},{2,4},{3,5},{4,6},{5,7},{8,10},{9,11},{10,12},{11,13},... | collective-permute-start | bytes 602120 | tf_op jit(solution)/shard_map/ppermute | solution.py:565
  66.7 3.0 %collective-permute-done.2.refs_1_ = f32[1,392,128]{2,1,0:T(8,128)} collective-permute-done((f32[1,392,128]{2,1,0:T(8,128)}, f32[1,392,128]{2,1,0:T(8,128)}, u32[]{:S(2)}, u32[]{:S(2)}) %collective-permute-start.2) | collective-permute-done | bytes 200736 | tf_op jit(solution)/shard_map/ppermute | solution.py:565
  69.7 3.4 %collective-permute-done.1.refs_0_ = f32[1,392,128]{2,1,0:T(8,128)} collective-permute-done((f32[1,392,128]{2,1,0:T(8,128)}, f32[1,392,128]{2,1,0:T(8,128)}, u32[]{:S(2)}, u32[]{:S(2)}) %collective-permute-start.1) | collective-permute-done | bytes 200736 | tf_op jit(solution)/shard_map/ppermute | solution.py:565
  73.1 2.1 %shard_map.87 = (f32[1,392,128]{2,1,0:T(8,128)}, f32[1,392,128]{2,1,0:T(8,128)}) custom-call(f32[2,1,392,128]{3,2,1,0:T(8,128)} %get-tuple-element.34.own_ref, f32[2,1,392,128]{3,2,1,0:T(8,128)} %collective-permute-done.came_ref, f32[1,392,128]{2,1,0:T(8,128)} %collective-permute-done.1.refs_0_, f32[1,392,128]{2,1,0:T(8,128)} %collective-permute-done.2.refs_1_, ...), custom_call_target="tpu_custom_call" | custom-call | bytes 2809856 | tf_op jit(solution)/shard_map/pallas_call | solution.py:169
  75.3 6.4 %gradient_blocks.2 = (f32[2,4,64,256]{3,2,1,0:T(8,128)}, f32[2,4,64,256]{3,2,1,0:T(8,128)}, f32[2,4,64,256]{3,2,1,0:T(8,128)}, f32[2,4,64,256]{3,2,1,0:T(8,128)}) custom-call(s32[3]{0:T(128)} %pad_add_fusion.place_ref.core_ref, f32[4,128,512]{2,1,0:T(8,128)} %get-tuple-element.43.own_ref, f32[4,128,512]{2,1,0:T(8,128)} %collective-permute-done.9.far_ref, ...), custom_call_target="tpu_custom_call" | custom-call | flops 1073741824 | bytes 6291456 | tf_op jit(solution)/shard_map/gradient_blocks/pallas_call | solution.py:415
  81.6 11.6 %solve_heads.5.own_ref = f32[4,128,512]{2,1,0:T(8,128)} custom-call(s32[3]{0:T(128)} %pad_add_fusion.place_ref.core_ref, f32[8]{0:T(128)} %regular_ref.7, bf16[512,1024]{1,0:T(8,128)(2,1)} %bitcast.28, bf16[512,1024]{1,0:T(8,128)(2,1)} %bitcast.17, bf16[512,1024]{1,0:T(8,128)(2,1)} %bitcast.22, f32[2,8,512]{2,1,0:T(8,128)} %get-tuple-element.33.refs_4_.refs_3_, ...), custom_call_target="tpu_custom_call" | custom-call | flops 2684354560 | bytes 3670016 | tf_op jit(solution)/shard_map/solve_heads/pallas_call | solution.py:347
  93.8 1.5 collective-permute-start.12
  95.3 1.5 collective-permute-start.13
  96.8 6.3 %gradient_blocks.3 = (f32[2,4,64,256]{3,2,1,0:T(8,128)}, f32[2,4,64,256]{3,2,1,0:T(8,128)}, f32[2,4,64,256]{3,2,1,0:T(8,128)}, f32[2,4,64,256]{3,2,1,0:T(8,128)}) custom-call(s32[3]{0:T(128)} %pad_add_fusion.place_ref.core_ref, f32[4,128,512]{2,1,0:T(8,128)} %solve_heads.5.own_ref, f32[4,128,512]{2,1,0:T(8,128)} %collective-permute-done.11.far_ref, ...), custom_call_target="tpu_custom_call" | custom-call | flops 1073741824 | bytes 6291456 | tf_op jit(solution)/shard_map/gradient_blocks/pallas_call | solution.py:415
  103.0 1.1 collective-permute-start.19
  104.2 1.5 collective-permute-start.20
  105.7 3.2 %collective-permute-done.12.refs_1_ = f32[2,4,64,256]{3,2,1,0:T(8,128)} collective-permute-done((f32[2,4,64,256]{3,2,1,0:T(8,128)}, f32[2,4,64,256]{3,2,1,0:T(8,128)}, u32[]{:S(2)}, u32[]{:S(2)}) %collective-permute-start.12) | collective-permute-done | bytes 524320 | tf_op jit(solution)/shard_map/ppermute | solution.py:603
  108.9 1.5 collective-permute-done.13.refs_3_.refs_4_
  110.4 2.0 %sum_blocks.2 = (f32[1,4,64,256]{3,2,1,0:T(8,128)}, f32[1,4,64,256]{3,2,1,0:T(8,128)}) custom-call(f32[2,4,64,256]{3,2,1,0:T(8,128)} %get-tuple-element.44.refs_6_.refs_0_, f32[2,4,64,256]{3,2,1,0:T(8,128)} %collective-permute-done.12.refs_1_, f32[2,4,64,256]{3,2,1,0:T(8,128)} %get-tuple-element.47.refs_2_.refs_3_, ...), custom_call_target="tpu_custom_call" | custom-call | bytes 1572864 | tf_op jit(solution)/shard_map/sum_blocks/pallas_call | solution.py:454
  112.4 1.5 collective-permute-start.14
  113.9 0.5 collective-permute-start.15
  114.4 5.7 %collective-permute-done.19.refs_1_ = f32[2,4,64,256]{3,2,1,0:T(8,128)} collective-permute-done((f32[2,4,64,256]{3,2,1,0:T(8,128)}, f32[2,4,64,256]{3,2,1,0:T(8,128)}, u32[]{:S(2)}, u32[]{:S(2)}) %collective-permute-start.19) | collective-permute-done | bytes 524320 | tf_op jit(solution)/shard_map/ppermute | solution.py:603
  120.1 1.5 collective-permute-done.20.refs_3_.refs_4_
  121.6 2.0 %sum_blocks.3 = (f32[1,4,64,256]{3,2,1,0:T(8,128)}, f32[1,4,64,256]{3,2,1,0:T(8,128)}) custom-call(f32[2,4,64,256]{3,2,1,0:T(8,128)} %get-tuple-element.45.refs_6_.refs_0_, f32[2,4,64,256]{3,2,1,0:T(8,128)} %collective-permute-done.19.refs_1_, f32[2,4,64,256]{3,2,1,0:T(8,128)} %get-tuple-element.56.refs_2_.refs_3_, ...), custom_call_target="tpu_custom_call" | custom-call | bytes 1572864 | tf_op jit(solution)/shard_map/sum_blocks/pallas_call | solution.py:454
  123.6 1.5 collective-permute-start.21
  125.1 0.5 collective-permute-start.22
  125.7 1.6 collective-permute-done.14.refs_2_
  127.2 2.1 %merge_blocks.2 = (f32[128,256]{1,0:T(8,128)}, f32[128,256]{1,0:T(8,128)}, f32[128,256]{1,0:T(8,128)}, f32[128,256]{1,0:T(8,128)}) custom-call(f32[2,4,64,256]{3,2,1,0:T(8,128)} %get-tuple-element.44.refs_6_.refs_0_, f32[2,4,64,256]{3,2,1,0:T(8,128)} %collective-permute-done.12.refs_1_, f32[1,4,64,256]{3,2,1,0:T(8,128)} %collective-permute-done.14.refs_2_, ...), custom_call_target="tpu_custom_call" | custom-call | bytes 2097152 | tf_op jit(solution)/shard_map/merge_blocks/pallas_call | solution.py:486
  129.4 5.4 %collective-permute-start.16 = (f32[128,256]{1,0:T(8,128)}, f32[128,256]{1,0:T(8,128)}, u32[]{:S(2)}, u32[]{:S(2)}) collective-permute-start(f32[128,256]{1,0:T(8,128)} %get-tuple-element.52), channel_id=1, source_target_pairs={{0,2},{1,3},{2,0},{3,1},{4,6},{5,7},{6,4},{7,5},{8,10},{9,11},{10,... | collective-permute-start | bytes 393224 | tf_op jit(solution)/shard_map/ppermute | solution.py:610
  134.8 1.9 %collective-permute-start.17 = (f32[128,256]{1,0:T(8,128)}, f32[128,256]{1,0:T(8,128)}, u32[]{:S(2)}, u32[]{:S(2)}) collective-permute-start(f32[128,256]{1,0:T(8,128)} %get-tuple-element.53), channel_id=1, source_target_pairs={{0,4},{1,5},{2,6},{3,7},{4,0},{5,1},{6,2},{7,3},{8,12},{9,13},{10,... | collective-permute-start | bytes 393224 | tf_op jit(solution)/shard_map/ppermute | solution.py:610
  136.7 1.4 collective-permute-start.18
  138.2 2.2 %merge_blocks.3 = (f32[128,256]{1,0:T(8,128)}, f32[128,256]{1,0:T(8,128)}, f32[128,256]{1,0:T(8,128)}, f32[128,256]{1,0:T(8,128)}) custom-call(f32[2,4,64,256]{3,2,1,0:T(8,128)} %get-tuple-element.45.refs_6_.refs_0_, f32[2,4,64,256]{3,2,1,0:T(8,128)} %collective-permute-done.19.refs_1_, f32[1,4,64,256]{3,2,1,0:T(8,128)} %collective-permute-done.21.refs_2_, ...), custom_call_target="tpu_custom_call" | custom-call | bytes 2097152 | tf_op jit(solution)/shard_map/merge_blocks/pallas_call | solution.py:486
  140.3 0.6 collective-permute-start.23
  140.9 2.4 %collective-permute-start.24 = (f32[128,256]{1,0:T(8,128)}, f32[128,256]{1,0:T(8,128)}, u32[]{:S(2)}, u32[]{:S(2)}) collective-permute-start(f32[128,256]{1,0:T(8,128)} %get-tuple-element.62), channel_id=1, source_target_pairs={{0,4},{1,5},{2,6},{3,7},{4,0},{5,1},{6,2},{7,3},{8,12},{9,13},{10,... | collective-permute-start | bytes 393224 | tf_op jit(solution)/shard_map/ppermute | solution.py:610
  143.3 2.2 %collective-permute-start.25 = (f32[128,256]{1,0:T(8,128)}, f32[128,256]{1,0:T(8,128)}, u32[]{:S(2)}, u32[]{:S(2)}) collective-permute-start(f32[128,256]{1,0:T(8,128)} %get-tuple-element.63), channel_id=1, source_target_pairs={{0,6},{1,7},{2,4},{3,5},{4,2},{5,3},{6,0},{7,1},{8,14},{9,15},{10,... | collective-permute-start | bytes 393224 | tf_op jit(solution)/shard_map/ppermute | solution.py:610
  145.4 6.3 %solve_heads.6.refs_5_ = bf16[512,1024]{1,0:T(8,128)(2,1)} custom-call(s32[3]{0:T(128)} %pad_add_fusion.place_ref.core_ref, f32[8]{0:T(128)} %regular_ref.7, bf16[512,1024]{1,0:T(8,128)(2,1)} %convolution_convert_fusion.refs_0_, bf16[512,1024]{1,0:T(8,128)(2,1)} %bitcast.18, bf16[512,1024]{1,0:T(8,128)(2,1)} %bitcast.23, ...), custom_call_target="tpu_custom_call", output_to_operand_aliasing={{}: (7, {})} | custom-call | flops 1342177280 | bytes 1835008 | tf_op jit(solution)/shard_map/solve_heads/pallas_call | solution.py:347
  151.8 6.3 %solve_heads.7 = bf16[512,1024]{1,0:T(8,128)(2,1)} custom-call(s32[3]{0:T(128)} %pad_add_fusion.place_ref.core_ref, f32[8]{0:T(128)} %regular_ref.7, bf16[512,1024]{1,0:T(8,128)(2,1)} %convolution_convert_fusion.refs_0_, bf16[512,1024]{1,0:T(8,128)(2,1)} %bitcast.19, bf16[512,1024]{1,0:T(8,128)(2,1)} %bitcast.24, ...), custom_call_target="tpu_custom_call", output_to_operand_aliasing={{}: (7, {})} | custom-call | flops 1342177280 | bytes 1835008 | tf_op jit(solution)/shard_map/solve_heads/pallas_call | solution.py:347
  158.1 2.0 %finish.1 = f32[256,256]{1,0:T(8,128)} custom-call(f32[128,256]{1,0:T(8,128)} %get-tuple-element.51.refs_0_, f32[128,256]{1,0:T(8,128)} %collective-permute-done.16.refs_1_, f32[128,256]{1,0:T(8,128)} %collective-permute-done.17.refs_2_, f32[128,256]{1,0:T(8,128)} %collective-permute-done.18.refs_3_, f32[128,256]{1,0:T(8,128)} %get-tuple-element.60.refs_4_, ...), custom_call_target="tpu_custom_call" | custom-call | bytes 1310720 | tf_op jit(solution)/shard_map/finish/pallas_call | solution.py:514
  (22 shorter events, 1.1 us)
Async XLA Ops:
  5.6 2.2 %collective-permute-start = (f32[2,1,392,128]{3,2,1,0:T(8,128)}, f32[2,1,392,128]{3,2,1,0:T(8,128)}, u32[]{:S(2)}, u32[]{:S(2)}) collective-permute-start(f32[2,1,392,128]{3,2,1,0:T(8,128)} %get-tuple-element.35), channel_id=1, source_target_pairs={{0,1},{1,0},{2,3},{3,2},{4,5},{5,4},{6,7},{7,6},{8,9},{9,8},{10,11... | collective-permute-start | bytes 1204232 | tf_op jit(solution)/shard_map/ppermute | solution.py:557
  9.8 16.9 %collective-permute-start.7 = (f32[1,392,128]{2,1,0:T(8,128)}, f32[1,392,128]{2,1,0:T(8,128)}, u32[]{:S(2)}, u32[]{:S(2)}) collective-permute-start(f32[1,392,128]{2,1,0:T(8,128)} %get-tuple-element.39), channel_id=1, source_target_pairs={{0,6},{1,7},{8,14},{9,15},{16,22},{17,23},{24,30},{25,31}} | collective-permute-start | bytes 602120 | tf_op jit(solution)/shard_map/ppermute | solution.py:565
  17.3 9.4 %collective-permute-start.6 = (f32[1,392,128]{2,1,0:T(8,128)}, f32[1,392,128]{2,1,0:T(8,128)}, u32[]{:S(2)}, u32[]{:S(2)}) collective-permute-start(f32[1,392,128]{2,1,0:T(8,128)} %get-tuple-element.39), channel_id=1, source_target_pairs={{0,4},{1,5},{2,6},{3,7},{8,12},{9,13},{10,14},{11,15},{16,20},{17,... | collective-permute-start | bytes 602120 | tf_op jit(solution)/shard_map/ppermute | solution.py:565
  19.3 10.9 %collective-permute-start.5 = (f32[1,392,128]{2,1,0:T(8,128)}, f32[1,392,128]{2,1,0:T(8,128)}, u32[]{:S(2)}, u32[]{:S(2)}) collective-permute-start(f32[1,392,128]{2,1,0:T(8,128)} %get-tuple-element.39), channel_id=1, source_target_pairs={{0,2},{1,3},{2,4},{3,5},{4,6},{5,7},{8,10},{9,11},{10,12},{11,13},... | collective-permute-start | bytes 602120 | tf_op jit(solution)/shard_map/ppermute | solution.py:565
  26.7 48.6 %collective-permute-start.10 = (f32[4,512,256]{2,1,0:T(8,128)}, f32[4,512,256]{2,1,0:T(8,128)}, u32[]{:S(2)}, u32[]{:S(2)}) collective-permute-start(f32[4,512,256]{2,1,0:T(8,128)} %pick_columns.1), channel_id=1, source_target_pairs={{0,1},{1,0},{2,3},{3,2},{4,5},{5,4},{6,7},{7,6},{8,9},{9,8},{10,11... | collective-permute-start | bytes 6291464 | tf_op jit(solution)/shard_map/ppermute | solution.py:571
  32.3 6.2 %collective-permute-start.8 = (f32[1,392,128]{2,1,0:T(8,128)}, f32[1,392,128]{2,1,0:T(8,128)}, u32[]{:S(2)}, u32[]{:S(2)}) collective-permute-start(f32[1,392,128]{2,1,0:T(8,128)} %get-tuple-element.41), channel_id=1, source_target_pairs={{0,1},{1,0},{2,3},{3,2},{4,5},{5,4},{6,7},{7,6},{8,9},{9,8},{10,11... | collective-permute-start | bytes 602120 | tf_op jit(solution)/shard_map/ppermute | solution.py:568
  52.7 22.6 %collective-permute-start.9 = (f32[4,128,512]{2,1,0:T(8,128)}, f32[4,128,512]{2,1,0:T(8,128)}, u32[]{:S(2)}, u32[]{:S(2)}) collective-permute-start(f32[4,128,512]{2,1,0:T(8,128)} %get-tuple-element.43.own_ref), channel_id=1, source_target_pairs={{0,1},{1,0},{2,3},{3,2},{4,5},{5,4},{6,7},{7,6},{8,9},{9,8},{10,11... | collective-permute-start | bytes 3145736 | tf_op jit(solution)/shard_map/ppermute | solution.py:588
  53.2 13.5 %collective-permute-start.3 = (f32[1,392,128]{2,1,0:T(8,128)}, f32[1,392,128]{2,1,0:T(8,128)}, u32[]{:S(2)}, u32[]{:S(2)}) collective-permute-start(f32[1,392,128]{2,1,0:T(8,128)} %get-tuple-element.36), channel_id=1, source_target_pairs={{0,6},{1,7},{8,14},{9,15},{16,22},{17,23},{24,30},{25,31}} | collective-permute-start | bytes 602120 | tf_op jit(solution)/shard_map/ppermute | solution.py:565
  60.1 9.6 %collective-permute-start.2 = (f32[1,392,128]{2,1,0:T(8,128)}, f32[1,392,128]{2,1,0:T(8,128)}, u32[]{:S(2)}, u32[]{:S(2)}) collective-permute-start(f32[1,392,128]{2,1,0:T(8,128)} %get-tuple-element.36), channel_id=1, source_target_pairs={{0,4},{1,5},{2,6},{3,7},{8,12},{9,13},{10,14},{11,15},{16,20},{17,... | collective-permute-start | bytes 602120 | tf_op jit(solution)/shard_map/ppermute | solution.py:565
  64.7 8.4 %collective-permute-start.1 = (f32[1,392,128]{2,1,0:T(8,128)}, f32[1,392,128]{2,1,0:T(8,128)}, u32[]{:S(2)}, u32[]{:S(2)}) collective-permute-start(f32[1,392,128]{2,1,0:T(8,128)} %get-tuple-element.36), channel_id=1, source_target_pairs={{0,2},{1,3},{2,4},{3,5},{4,6},{5,7},{8,10},{9,11},{10,12},{11,13},... | collective-permute-start | bytes 602120 | tf_op jit(solution)/shard_map/ppermute | solution.py:565
  75.2 6.4 %collective-permute-start.4 = (f32[1,392,128]{2,1,0:T(8,128)}, f32[1,392,128]{2,1,0:T(8,128)}, u32[]{:S(2)}, u32[]{:S(2)}) collective-permute-start(f32[1,392,128]{2,1,0:T(8,128)} %get-tuple-element.37), channel_id=1, source_target_pairs={{0,1},{1,0},{2,3},{3,2},{4,5},{5,4},{6,7},{7,6},{8,9},{9,8},{10,11... | collective-permute-start | bytes 602120 | tf_op jit(solution)/shard_map/ppermute | solution.py:568
  93.3 3.5 %collective-permute-start.11 = (f32[4,128,512]{2,1,0:T(8,128)}, f32[4,128,512]{2,1,0:T(8,128)}, u32[]{:S(2)}, u32[]{:S(2)}) collective-permute-start(f32[4,128,512]{2,1,0:T(8,128)} %solve_heads.5.own_ref), channel_id=1, source_target_pairs={{0,1},{1,0},{2,3},{3,2},{4,5},{5,4},{6,7},{7,6},{8,9},{9,8},{10,11... | collective-permute-start | bytes 3145736 | tf_op jit(solution)/shard_map/ppermute | solution.py:588
  93.8 15.1 %collective-permute-start.12 = (f32[2,4,64,256]{3,2,1,0:T(8,128)}, f32[2,4,64,256]{3,2,1,0:T(8,128)}, u32[]{:S(2)}, u32[]{:S(2)}) collective-permute-start(f32[2,4,64,256]{3,2,1,0:T(8,128)} %get-tuple-element.46), channel_id=1, source_target_pairs={{0,8},{8,0},{16,24},{24,16},{1,9},{9,1},{17,25},{25,17},{2,10},{10... | collective-permute-start | bytes 1572872 | tf_op jit(solution)/shard_map/ppermute | solution.py:603
  95.3 15.1 %collective-permute-start.13 = (f32[2,4,64,256]{3,2,1,0:T(8,128)}, f32[2,4,64,256]{3,2,1,0:T(8,128)}, u32[]{:S(2)}, u32[]{:S(2)}) collective-permute-start(f32[2,4,64,256]{3,2,1,0:T(8,128)} %get-tuple-element.48), channel_id=1, source_target_pairs={{0,16},{8,24},{16,0},{24,8},{1,17},{9,25},{17,1},{25,9},{2,18},{10... | collective-permute-start | bytes 1572872 | tf_op jit(solution)/shard_map/ppermute | solution.py:603
  103.0 17.1 %collective-permute-start.19 = (f32[2,4,64,256]{3,2,1,0:T(8,128)}, f32[2,4,64,256]{3,2,1,0:T(8,128)}, u32[]{:S(2)}, u32[]{:S(2)}) collective-permute-start(f32[2,4,64,256]{3,2,1,0:T(8,128)} %get-tuple-element.55), channel_id=1, source_target_pairs={{0,8},{8,0},{16,24},{24,16},{1,9},{9,1},{17,25},{25,17},{2,10},{10... | collective-permute-start | bytes 1572872 | tf_op jit(solution)/shard_map/ppermute | solution.py:603
  104.2 17.4 %collective-permute-start.20 = (f32[2,4,64,256]{3,2,1,0:T(8,128)}, f32[2,4,64,256]{3,2,1,0:T(8,128)}, u32[]{:S(2)}, u32[]{:S(2)}) collective-permute-start(f32[2,4,64,256]{3,2,1,0:T(8,128)} %get-tuple-element.57), channel_id=1, source_target_pairs={{0,16},{8,24},{16,0},{24,8},{1,17},{9,25},{17,1},{25,9},{2,18},{10... | collective-permute-start | bytes 1572872 | tf_op jit(solution)/shard_map/ppermute | solution.py:603
  112.4 14.9 %collective-permute-start.14 = (f32[1,4,64,256]{3,2,1,0:T(8,128)}, f32[1,4,64,256]{3,2,1,0:T(8,128)}, u32[]{:S(2)}, u32[]{:S(2)}) collective-permute-start(f32[1,4,64,256]{3,2,1,0:T(8,128)} %get-tuple-element.49), channel_id=1, source_target_pairs={{0,16},{8,24},{16,0},{24,8},{1,17},{9,25},{17,1},{25,9},{2,18},{10... | collective-permute-start | bytes 786440 | tf_op jit(solution)/shard_map/ppermute | solution.py:603
  113.9 13.3 %collective-permute-start.15 = (f32[1,4,64,256]{3,2,1,0:T(8,128)}, f32[1,4,64,256]{3,2,1,0:T(8,128)}, u32[]{:S(2)}, u32[]{:S(2)}) collective-permute-start(f32[1,4,64,256]{3,2,1,0:T(8,128)} %get-tuple-element.50), channel_id=1, source_target_pairs={{0,8},{8,0},{16,24},{24,16},{1,9},{9,1},{17,25},{25,17},{2,10},{10... | collective-permute-start | bytes 786440 | tf_op jit(solution)/shard_map/ppermute | solution.py:603
  123.6 14.5 %collective-permute-start.21 = (f32[1,4,64,256]{3,2,1,0:T(8,128)}, f32[1,4,64,256]{3,2,1,0:T(8,128)}, u32[]{:S(2)}, u32[]{:S(2)}) collective-permute-start(f32[1,4,64,256]{3,2,1,0:T(8,128)} %get-tuple-element.58), channel_id=1, source_target_pairs={{0,16},{8,24},{16,0},{24,8},{1,17},{9,25},{17,1},{25,9},{2,18},{10... | collective-permute-start | bytes 786440 | tf_op jit(solution)/shard_map/ppermute | solution.py:603
  125.1 13.0 %collective-permute-start.22 = (f32[1,4,64,256]{3,2,1,0:T(8,128)}, f32[1,4,64,256]{3,2,1,0:T(8,128)}, u32[]{:S(2)}, u32[]{:S(2)}) collective-permute-start(f32[1,4,64,256]{3,2,1,0:T(8,128)} %get-tuple-element.59), channel_id=1, source_target_pairs={{0,8},{8,0},{16,24},{24,16},{1,9},{9,1},{17,25},{25,17},{2,10},{10... | collective-permute-start | bytes 786440 | tf_op jit(solution)/shard_map/ppermute | solution.py:603
  129.4 13.9 %collective-permute-start.16 = (f32[128,256]{1,0:T(8,128)}, f32[128,256]{1,0:T(8,128)}, u32[]{:S(2)}, u32[]{:S(2)}) collective-permute-start(f32[128,256]{1,0:T(8,128)} %get-tuple-element.52), channel_id=1, source_target_pairs={{0,2},{1,3},{2,0},{3,1},{4,6},{5,7},{6,4},{7,5},{8,10},{9,11},{10,... | collective-permute-start | bytes 393224 | tf_op jit(solution)/shard_map/ppermute | solution.py:610
  134.8 23.3 %collective-permute-start.17 = (f32[128,256]{1,0:T(8,128)}, f32[128,256]{1,0:T(8,128)}, u32[]{:S(2)}, u32[]{:S(2)}) collective-permute-start(f32[128,256]{1,0:T(8,128)} %get-tuple-element.53), channel_id=1, source_target_pairs={{0,4},{1,5},{2,6},{3,7},{4,0},{5,1},{6,2},{7,3},{8,12},{9,13},{10,... | collective-permute-start | bytes 393224 | tf_op jit(solution)/shard_map/ppermute | solution.py:610
  136.7 21.4 %collective-permute-start.18 = (f32[128,256]{1,0:T(8,128)}, f32[128,256]{1,0:T(8,128)}, u32[]{:S(2)}, u32[]{:S(2)}) collective-permute-start(f32[128,256]{1,0:T(8,128)} %get-tuple-element.54), channel_id=1, source_target_pairs={{0,6},{1,7},{2,4},{3,5},{4,2},{5,3},{6,0},{7,1},{8,14},{9,15},{10,... | collective-permute-start | bytes 393224 | tf_op jit(solution)/shard_map/ppermute | solution.py:610
  140.3 17.8 %collective-permute-start.23 = (f32[128,256]{1,0:T(8,128)}, f32[128,256]{1,0:T(8,128)}, u32[]{:S(2)}, u32[]{:S(2)}) collective-permute-start(f32[128,256]{1,0:T(8,128)} %get-tuple-element.61), channel_id=1, source_target_pairs={{0,2},{1,3},{2,0},{3,1},{4,6},{5,7},{6,4},{7,5},{8,10},{9,11},{10,... | collective-permute-start | bytes 393224 | tf_op jit(solution)/shard_map/ppermute | solution.py:610
  140.9 17.2 %collective-permute-start.24 = (f32[128,256]{1,0:T(8,128)}, f32[128,256]{1,0:T(8,128)}, u32[]{:S(2)}, u32[]{:S(2)}) collective-permute-start(f32[128,256]{1,0:T(8,128)} %get-tuple-element.62), channel_id=1, source_target_pairs={{0,4},{1,5},{2,6},{3,7},{4,0},{5,1},{6,2},{7,3},{8,12},{9,13},{10,... | collective-permute-start | bytes 393224 | tf_op jit(solution)/shard_map/ppermute | solution.py:610
  143.3 14.8 %collective-permute-start.25 = (f32[128,256]{1,0:T(8,128)}, f32[128,256]{1,0:T(8,128)}, u32[]{:S(2)}, u32[]{:S(2)}) collective-permute-start(f32[128,256]{1,0:T(8,128)} %get-tuple-element.63), channel_id=1, source_target_pairs={{0,6},{1,7},{2,4},{3,5},{4,2},{5,3},{6,0},{7,1},{8,14},{9,15},{10,... | collective-permute-start | bytes 393224 | tf_op jit(solution)/shard_map/ppermute | solution.py:610

commit v12 on v11

--- a/solution.py
+++ b/solution.py
@@ -185,7 +185,8 @@
     g_ref = refs.pop(0) if with_gradient else None
     k_ref, v_ref, rows_ref = refs[:3]
     state_refs, refs = refs[3 : 3 + len(bounds)], refs[3 + len(bounds) :]
-    turned_ref = refs.pop() if with_gradient else None
+    if with_gradient:
+        half_ref, turned_ref = refs.pop(), refs.pop()
     mixed_ref = refs.pop() if with_query else None
     rows, dim = k_ref.shape
     pieces = range(rows // SUB)
@@ -290,7 +291,9 @@
 
     if with_gradient:
         for c in pieces:
-            turned_ref[0, :, place[c]] = solution[c][-SUB:].T.astype(BF16).astype(F32)
+            turned = solution[c][-SUB:].T.astype(BF16)
+            half_ref[0, :, place[c]] = turned
+            turned_ref[0, :, place[c]] = turned.astype(F32)
     for c in pieces if with_query else ():
         high, low = split(solution[c][0:SUB])
         memory_high, memory_low = split(memory[c].T)
@@ -342,8 +345,8 @@
         shapes.append(jax.ShapeDtypeStruct((rows, columns), BF16))
         out_specs.append(wide_spec)
     if with_gradient:
-        shapes.append(jax.ShapeDtypeStruct((count, dim, rows), F32))
-        out_specs.append(pl.BlockSpec((1, dim, rows), lambda step, *_: (step, 0, 0)))
+        shapes += [jax.ShapeDtypeStruct((count, dim, rows), kind) for kind in (F32, BF16)]
+        out_specs += [pl.BlockSpec((1, dim, rows), lambda step, *_: (step, 0, 0))] * 2
     return pl.pallas_call(
         functools.partial(solve_kernel, with_query, with_gradient, bounds, head_of),
         out_shape=shapes,
@@ -392,8 +395,8 @@
     def _():
         for i in range(half):
             near, away = (core * half + i) ^ group, ((1 - core) * half + i) ^ group
-            left_ref[near, :, 0:rows] = own_ref[i].astype(BF16)
-            left_ref[away, :, 0:rows] = own_ref[half + i].astype(BF16)
+            left_ref[near, :, 0:rows] = own_ref[i]
+            left_ref[away, :, 0:rows] = own_ref[half + i]
             left_ref[near, :, rows:] = far_ref[half + i].astype(BF16)
             left_ref[away, :, rows:] = far_ref[i].astype(BF16)
 
@@ -582,11 +585,11 @@
         results = solve_heads(
             place, k, 0, per, regular, queries if joint else None, grads, keys, values, table, states, mixed, after
         )
-        turned = results[-1]
+        turned, own_rows = results[-2:]
         if joint:
             mixed = results[0]
         far = lax.ppermute(turned, "seq", partner)
-        products.append(gradient_blocks(place, turned, far, tokens, other, order))
+        products.append(gradient_blocks(place, own_rows, far, tokens, other, order))
     for side in range(2):
         after = products[-1][0] if side == 0 else None
         (mixed,) = solve_heads(

time: 161 us -> 161 us (level)
  transfers between devices with their start and end apart: 26 -> 26, of which waited for: 9 -> 10; matrix products, arithmetic and copies ran while one was open for 4% -> 4% of each run, Pallas kernels for 35% -> 35%
where the time goes in v12:
time: 161 us; the launch traced here: 160 us
  Pallas kernels  76.8 us (48%)
  starting transfers between devices  50.6 us (31%)
  waiting for transfers between devices  25.2 us (16%)
  matrix products  6.13 us (4%)
    pallas_call x4, Pallas kernels, solve_heads(): pl.pallas_call(functools.partial(solve_kernel, with_query, with_gradient,...  38.6 us
    ppermute x6, starting transfers between devices, program(): sent.append(lax.ppermute(chip_state, 'seq', pairs))  25.4 us
    ppermute x6, starting transfers between devices, program(): finished[-1].append(lax.ppermute(other_block, 'seq', pairs))  13.8 us
    ppermute x8, waiting for transfers between devices, program(): sums[index].append(lax.ppermute(sends[index], 'dp', pairs))  13.5 us
    pallas_call x2, Pallas kernels, gradient_blocks(): pl.pallas_call(functools.partial(gradient_kernel, order), out_shape=[out]...  12.3 us
    ppermute x6, waiting for transfers between devices, program(): sent.append(lax.ppermute(chip_state, 'seq', pairs))  9.95 us
    ppermute x8, starting transfers between devices, program(): sums[index].append(lax.ppermute(sends[index], 'dp', pairs))  9.75 us
    pallas_call x3, Pallas kernels, combine(): pl.pallas_call(kernel, out_shape=[out] * outs, in_specs=[whole(a) for a i...  6.21 us
  transfers between devices with their start and end apart: 26, of which 10 were waited for; matrix products, arithmetic and copies ran while one was open for 4% of the time, Pallas kernels for 35%

profile of v12, /device:TPU:0, one launch (start us, length us, event | category | flops | bytes accessed | tf_op | source)
XLA Modules:
  0.0 160.1 jit_solution(12174421696702635826)
XLA Ops:
  0.6 5.0 %local_states.1 = (f32[2,1,392,128]{3,2,1,0:T(8,128)}, f32[2,1,392,128]{3,2,1,0:T(8,128)}, f32[2,8,512]{2,1,0:T(8,128)}) custom-call(bf16[512,1024]{1,0:T(8,128)(2,1)} %bitcast.15, bf16[512,1024]{1,0:T(8,128)(2,1)} %bitcast.20, f32[8,512]{1,0:T(8,128)} %bitcast.26), custom_call_target="tpu_custom_call" | custom-call | flops 536870912 | bytes 4194304 | tf_op jit(solution)/shard_map/local_states/pallas_call | solution.py:124
  6.2 1.7 %collective-permute-done.came_ref = f32[2,1,392,128]{3,2,1,0:T(8,128)} collective-permute-done((f32[2,1,392,128]{3,2,1,0:T(8,128)}, f32[2,1,392,128]{3,2,1,0:T(8,128)}, u32[]{:S(2)}, u32[]{:S(2)}) %collective-permute-start) | collective-permute-done | bytes 401440 | tf_op jit(solution)/shard_map/ppermute | solution.py:560
  7.9 1.9 %shard_map.86 = (f32[1,392,128]{2,1,0:T(8,128)}, f32[1,392,128]{2,1,0:T(8,128)}) custom-call(f32[2,1,392,128]{3,2,1,0:T(8,128)} %get-tuple-element.37.own_ref, f32[2,1,392,128]{3,2,1,0:T(8,128)} %collective-permute-done.came_ref), custom_call_target="tpu_custom_call" | custom-call | bytes 1605632 | tf_op jit(solution)/shard_map/pallas_call | solution.py:169
  9.8 7.5 %collective-permute-start.7 = (f32[1,392,128]{2,1,0:T(8,128)}, f32[1,392,128]{2,1,0:T(8,128)}, u32[]{:S(2)}, u32[]{:S(2)}) collective-permute-start(f32[1,392,128]{2,1,0:T(8,128)} %get-tuple-element.42), channel_id=1, source_target_pairs={{0,6},{1,7},{8,14},{9,15},{16,22},{17,23},{24,30},{25,31}} | collective-permute-start | bytes 602120 | tf_op jit(solution)/shard_map/ppermute | solution.py:568
  17.3 2.0 %collective-permute-start.6 = (f32[1,392,128]{2,1,0:T(8,128)}, f32[1,392,128]{2,1,0:T(8,128)}, u32[]{:S(2)}, u32[]{:S(2)}) collective-permute-start(f32[1,392,128]{2,1,0:T(8,128)} %get-tuple-element.42), channel_id=1, source_target_pairs={{0,4},{1,5},{2,6},{3,7},{8,12},{9,13},{10,14},{11,15},{16,20},{17,... | collective-permute-start | bytes 602120 | tf_op jit(solution)/shard_map/ppermute | solution.py:568
  19.2 2.5 %collective-permute-start.5 = (f32[1,392,128]{2,1,0:T(8,128)}, f32[1,392,128]{2,1,0:T(8,128)}, u32[]{:S(2)}, u32[]{:S(2)}) collective-permute-start(f32[1,392,128]{2,1,0:T(8,128)} %get-tuple-element.42), channel_id=1, source_target_pairs={{0,2},{1,3},{2,4},{3,5},{4,6},{5,7},{8,10},{9,11},{10,12},{11,13},... | collective-permute-start | bytes 602120 | tf_op jit(solution)/shard_map/ppermute | solution.py:568
  21.7 0.6 pad_add_fusion.place_ref.core_ref
  22.3 4.3 %pick_columns.1 = f32[4,512,256]{2,1,0:T(8,128)} custom-call(s32[3]{0:T(128)} %pad_add_fusion.place_ref.core_ref, bf16[512,2048]{1,0:T(8,128)(2,1)} %bitcast.12), custom_call_target="tpu_custom_call" | custom-call | bytes 3145728 | tf_op jit(solution)/shard_map/pick_columns/pallas_call | solution.py:372
  26.7 3.5 %collective-permute-done.5.refs_0_ = f32[1,392,128]{2,1,0:T(8,128)} collective-permute-done((f32[1,392,128]{2,1,0:T(8,128)}, f32[1,392,128]{2,1,0:T(8,128)}, u32[]{:S(2)}, u32[]{:S(2)}) %collective-permute-start.5) | collective-permute-done | bytes 200736 | tf_op jit(solution)/shard_map/ppermute | solution.py:568
  30.1 2.1 %shard_map.88 = (f32[1,392,128]{2,1,0:T(8,128)}, f32[1,392,128]{2,1,0:T(8,128)}) custom-call(f32[2,1,392,128]{3,2,1,0:T(8,128)} %get-tuple-element.37.own_ref, f32[2,1,392,128]{3,2,1,0:T(8,128)} %collective-permute-done.came_ref, f32[1,392,128]{2,1,0:T(8,128)} %collective-permute-done.5.refs_0_, f32[1,392,128]{2,1,0:T(8,128)} %collective-permute-done.6.refs_1_, ...), custom_call_target="tpu_custom_call" | custom-call | bytes 2809856 | tf_op jit(solution)/shard_map/pallas_call | solution.py:169
  32.3 6.1 %convolution_convert_fusion.refs_0_ = bf16[512,1024]{1,0:T(8,128)(2,1)} fusion(bf16[2048,1024]{1,0:T(8,128)(2,1)} %param.8, bf16[1,512,2048]{2,1,0:T(8,128)(2,1)} %param.7), kind=kOutput, calls=%fused_computation | convolution fusion | flops 2148007936 | bytes 7340032 | tf_op jit(solution)/shard_map/dot_general | solution.py:575
  38.4 14.3 %solve_heads.4 = (bf16[512,1024]{1,0:T(8,128)(2,1)}, f32[4,128,512]{2,1,0:T(8,128)}, bf16[4,128,512]{2,1,0:T(8,128)(2,1)}) custom-call(s32[3]{0:T(128)} %pad_add_fusion.place_ref.core_ref, f32[8]{0:T(128)} %regular_ref.7, bf16[512,1024]{1,0:T(8,128)(2,1)} %convolution_convert_fusion.refs_0_, bf16[512,1024]{1,0:T(8,128)(2,1)} %bitcast.27, ...), custom_call_target="tpu_custom_call" | custom-call | flops 2684354560 | bytes 3670016 | tf_op jit(solution)/shard_map/solve_heads/pallas_call | solution.py:350
  52.7 0.6 collective-permute-start.9
  53.3 6.9 %collective-permute-start.3 = (f32[1,392,128]{2,1,0:T(8,128)}, f32[1,392,128]{2,1,0:T(8,128)}, u32[]{:S(2)}, u32[]{:S(2)}) collective-permute-start(f32[1,392,128]{2,1,0:T(8,128)} %get-tuple-element.39), channel_id=1, source_target_pairs={{0,6},{1,7},{8,14},{9,15},{16,22},{17,23},{24,30},{25,31}} | collective-permute-start | bytes 602120 | tf_op jit(solution)/shard_map/ppermute | solution.py:568
  60.2 4.6 %collective-permute-start.2 = (f32[1,392,128]{2,1,0:T(8,128)}, f32[1,392,128]{2,1,0:T(8,128)}, u32[]{:S(2)}, u32[]{:S(2)}) collective-permute-start(f32[1,392,128]{2,1,0:T(8,128)} %get-tuple-element.39), channel_id=1, source_target_pairs={{0,4},{1,5},{2,6},{3,7},{8,12},{9,13},{10,14},{11,15},{16,20},{17,... | collective-permute-start | bytes 602120 | tf_op jit(solution)/shard_map/ppermute | solution.py:568
  64.8 2.0 %collective-permute-start.1 = (f32[1,392,128]{2,1,0:T(8,128)}, f32[1,392,128]{2,1,0:T(8,128)}, u32[]{:S(2)}, u32[]{:S(2)}) collective-permute-start(f32[1,392,128]{2,1,0:T(8,128)} %get-tuple-element.39), channel_id=1, source_target_pairs={{0,2},{1,3},{2,4},{3,5},{4,6},{5,7},{8,10},{9,11},{10,12},{11,13},... | collective-permute-start | bytes 602120 | tf_op jit(solution)/shard_map/ppermute | solution.py:568
  66.8 3.0 %collective-permute-done.2.refs_1_ = f32[1,392,128]{2,1,0:T(8,128)} collective-permute-done((f32[1,392,128]{2,1,0:T(8,128)}, f32[1,392,128]{2,1,0:T(8,128)}, u32[]{:S(2)}, u32[]{:S(2)}) %collective-permute-start.2) | collective-permute-done | bytes 200736 | tf_op jit(solution)/shard_map/ppermute | solution.py:568
  69.8 3.4 %collective-permute-done.1.refs_0_ = f32[1,392,128]{2,1,0:T(8,128)} collective-permute-done((f32[1,392,128]{2,1,0:T(8,128)}, f32[1,392,128]{2,1,0:T(8,128)}, u32[]{:S(2)}, u32[]{:S(2)}) %collective-permute-start.1) | collective-permute-done | bytes 200736 | tf_op jit(solution)/shard_map/ppermute | solution.py:568
  73.2 2.1 %shard_map.87 = (f32[1,392,128]{2,1,0:T(8,128)}, f32[1,392,128]{2,1,0:T(8,128)}) custom-call(f32[2,1,392,128]{3,2,1,0:T(8,128)} %get-tuple-element.37.own_ref, f32[2,1,392,128]{3,2,1,0:T(8,128)} %collective-permute-done.came_ref, f32[1,392,128]{2,1,0:T(8,128)} %collective-permute-done.1.refs_0_, f32[1,392,128]{2,1,0:T(8,128)} %collective-permute-done.2.refs_1_, ...), custom_call_target="tpu_custom_call" | custom-call | bytes 2809856 | tf_op jit(solution)/shard_map/pallas_call | solution.py:169
  75.4 6.2 %gradient_blocks.2 = (f32[2,4,64,256]{3,2,1,0:T(8,128)}, f32[2,4,64,256]{3,2,1,0:T(8,128)}, f32[2,4,64,256]{3,2,1,0:T(8,128)}, f32[2,4,64,256]{3,2,1,0:T(8,128)}) custom-call(s32[3]{0:T(128)} %pad_add_fusion.place_ref.core_ref, bf16[4,128,512]{2,1,0:T(8,128)(2,1)} %get-tuple-element.46.own_ref, f32[4,128,512]{2,1,0:T(8,128)} %collective-permute-done.9.far_ref, ...), custom_call_target="tpu_custom_call" | custom-call | flops 1073741824 | bytes 6291456 | tf_op jit(solution)/shard_map/gradient_blocks/pallas_call | solution.py:418
  81.5 11.7 %solve_heads.5 = (f32[4,128,512]{2,1,0:T(8,128)}, bf16[4,128,512]{2,1,0:T(8,128)(2,1)}) custom-call(s32[3]{0:T(128)} %pad_add_fusion.place_ref.core_ref, f32[8]{0:T(128)} %regular_ref.7, bf16[512,1024]{1,0:T(8,128)(2,1)} %bitcast.28, bf16[512,1024]{1,0:T(8,128)(2,1)} %bitcast.17, bf16[512,1024]{1,0:T(8,128)(2,1)} %bitcast.22, ...), custom_call_target="tpu_custom_call" | custom-call | flops 2684354560 | bytes 3670016 | tf_op jit(solution)/shard_map/solve_heads/pallas_call | solution.py:350
  93.7 1.5 collective-permute-start.12
  95.2 1.5 collective-permute-start.13
  96.8 6.1 %gradient_blocks.3 = (f32[2,4,64,256]{3,2,1,0:T(8,128)}, f32[2,4,64,256]{3,2,1,0:T(8,128)}, f32[2,4,64,256]{3,2,1,0:T(8,128)}, f32[2,4,64,256]{3,2,1,0:T(8,128)}) custom-call(s32[3]{0:T(128)} %pad_add_fusion.place_ref.core_ref, bf16[4,128,512]{2,1,0:T(8,128)(2,1)} %get-tuple-element.49.own_ref, f32[4,128,512]{2,1,0:T(8,128)} %collective-permute-done.11.far_ref, ...), custom_call_target="tpu_custom_call" | custom-call | flops 1073741824 | bytes 6291456 | tf_op jit(solution)/shard_map/gradient_blocks/pallas_call | solution.py:418
  102.9 1.1 collective-permute-start.19
  104.0 1.5 collective-permute-start.20
  105.5 3.3 %collective-permute-done.12.refs_1_ = f32[2,4,64,256]{3,2,1,0:T(8,128)} collective-permute-done((f32[2,4,64,256]{3,2,1,0:T(8,128)}, f32[2,4,64,256]{3,2,1,0:T(8,128)}, u32[]{:S(2)}, u32[]{:S(2)}) %collective-permute-start.12) | collective-permute-done | bytes 524320 | tf_op jit(solution)/shard_map/ppermute | solution.py:606
  108.9 1.5 collective-permute-done.13.refs_3_.refs_4_
  110.4 2.0 %sum_blocks.2 = (f32[1,4,64,256]{3,2,1,0:T(8,128)}, f32[1,4,64,256]{3,2,1,0:T(8,128)}) custom-call(f32[2,4,64,256]{3,2,1,0:T(8,128)} %get-tuple-element.48.refs_6_.refs_0_, f32[2,4,64,256]{3,2,1,0:T(8,128)} %collective-permute-done.12.refs_1_, f32[2,4,64,256]{3,2,1,0:T(8,128)} %get-tuple-element.53.refs_2_.refs_3_, ...), custom_call_target="tpu_custom_call" | custom-call | bytes 1572864 | tf_op jit(solution)/shard_map/sum_blocks/pallas_call | solution.py:457
  112.4 1.5 collective-permute-start.14
  113.9 0.5 collective-permute-start.15
  114.4 5.7 %collective-permute-done.19.refs_1_ = f32[2,4,64,256]{3,2,1,0:T(8,128)} collective-permute-done((f32[2,4,64,256]{3,2,1,0:T(8,128)}, f32[2,4,64,256]{3,2,1,0:T(8,128)}, u32[]{:S(2)}, u32[]{:S(2)}) %collective-permute-start.19) | collective-permute-done | bytes 524320 | tf_op jit(solution)/shard_map/ppermute | solution.py:606
  120.1 1.5 collective-permute-done.20.refs_3_.refs_4_
  121.6 2.0 %sum_blocks.3 = (f32[1,4,64,256]{3,2,1,0:T(8,128)}, f32[1,4,64,256]{3,2,1,0:T(8,128)}) custom-call(f32[2,4,64,256]{3,2,1,0:T(8,128)} %get-tuple-element.51.refs_6_.refs_0_, f32[2,4,64,256]{3,2,1,0:T(8,128)} %collective-permute-done.19.refs_1_, f32[2,4,64,256]{3,2,1,0:T(8,128)} %get-tuple-element.62.refs_2_.refs_3_, ...), custom_call_target="tpu_custom_call" | custom-call | bytes 1572864 | tf_op jit(solution)/shard_map/sum_blocks/pallas_call | solution.py:457
  123.6 1.5 collective-permute-start.21
  125.1 0.5 collective-permute-start.22
  125.7 1.5 collective-permute-done.14.refs_2_
  127.2 2.2 %merge_blocks.2 = (f32[128,256]{1,0:T(8,128)}, f32[128,256]{1,0:T(8,128)}, f32[128,256]{1,0:T(8,128)}, f32[128,256]{1,0:T(8,128)}) custom-call(f32[2,4,64,256]{3,2,1,0:T(8,128)} %get-tuple-element.48.refs_6_.refs_0_, f32[2,4,64,256]{3,2,1,0:T(8,128)} %collective-permute-done.12.refs_1_, f32[1,4,64,256]{3,2,1,0:T(8,128)} %collective-permute-done.14.refs_2_, ...), custom_call_target="tpu_custom_call" | custom-call | bytes 2097152 | tf_op jit(solution)/shard_map/merge_blocks/pallas_call | solution.py:489
  129.4 5.4 %collective-permute-start.16 = (f32[128,256]{1,0:T(8,128)}, f32[128,256]{1,0:T(8,128)}, u32[]{:S(2)}, u32[]{:S(2)}) collective-permute-start(f32[128,256]{1,0:T(8,128)} %get-tuple-element.58), channel_id=1, source_target_pairs={{0,2},{1,3},{2,0},{3,1},{4,6},{5,7},{6,4},{7,5},{8,10},{9,11},{10,... | collective-permute-start | bytes 393224 | tf_op jit(solution)/shard_map/ppermute | solution.py:613
  134.8 1.9 %collective-permute-start.17 = (f32[128,256]{1,0:T(8,128)}, f32[128,256]{1,0:T(8,128)}, u32[]{:S(2)}, u32[]{:S(2)}) collective-permute-start(f32[128,256]{1,0:T(8,128)} %get-tuple-element.59), channel_id=1, source_target_pairs={{0,4},{1,5},{2,6},{3,7},{4,0},{5,1},{6,2},{7,3},{8,12},{9,13},{10,... | collective-permute-start | bytes 393224 | tf_op jit(solution)/shard_map/ppermute | solution.py:613
  136.7 1.4 collective-permute-start.18
  138.2 2.2 %merge_blocks.3 = (f32[128,256]{1,0:T(8,128)}, f32[128,256]{1,0:T(8,128)}, f32[128,256]{1,0:T(8,128)}, f32[128,256]{1,0:T(8,128)}) custom-call(f32[2,4,64,256]{3,2,1,0:T(8,128)} %get-tuple-element.51.refs_6_.refs_0_, f32[2,4,64,256]{3,2,1,0:T(8,128)} %collective-permute-done.19.refs_1_, f32[1,4,64,256]{3,2,1,0:T(8,128)} %collective-permute-done.21.refs_2_, ...), custom_call_target="tpu_custom_call" | custom-call | bytes 2097152 | tf_op jit(solution)/shard_map/merge_blocks/pallas_call | solution.py:489
  140.3 0.6 collective-permute-start.23
  140.9 2.4 %collective-permute-start.24 = (f32[128,256]{1,0:T(8,128)}, f32[128,256]{1,0:T(8,128)}, u32[]{:S(2)}, u32[]{:S(2)}) collective-permute-start(f32[128,256]{1,0:T(8,128)} %get-tuple-element.68), channel_id=1, source_target_pairs={{0,4},{1,5},{2,6},{3,7},{4,0},{5,1},{6,2},{7,3},{8,12},{9,13},{10,... | collective-permute-start | bytes 393224 | tf_op jit(solution)/shard_map/ppermute | solution.py:613
  143.3 2.1 %collective-permute-start.25 = (f32[128,256]{1,0:T(8,128)}, f32[128,256]{1,0:T(8,128)}, u32[]{:S(2)}, u32[]{:S(2)}) collective-permute-start(f32[128,256]{1,0:T(8,128)} %get-tuple-element.69), channel_id=1, source_target_pairs={{0,6},{1,7},{2,4},{3,5},{4,2},{5,3},{6,0},{7,1},{8,14},{9,15},{10,... | collective-permute-start | bytes 393224 | tf_op jit(solution)/shard_map/ppermute | solution.py:613
  145.4 6.3 %solve_heads.6.refs_5_ = bf16[512,1024]{1,0:T(8,128)(2,1)} custom-call(s32[3]{0:T(128)} %pad_add_fusion.place_ref.core_ref, f32[8]{0:T(128)} %regular_ref.7, bf16[512,1024]{1,0:T(8,128)(2,1)} %convolution_convert_fusion.refs_0_, bf16[512,1024]{1,0:T(8,128)(2,1)} %bitcast.18, bf16[512,1024]{1,0:T(8,128)(2,1)} %bitcast.23, ...), custom_call_target="tpu_custom_call", output_to_operand_aliasing={{}: (7, {})} | custom-call | flops 1342177280 | bytes 1835008 | tf_op jit(solution)/shard_map/solve_heads/pallas_call | solution.py:350
  151.7 6.3 %solve_heads.7 = bf16[512,1024]{1,0:T(8,128)(2,1)} custom-call(s32[3]{0:T(128)} %pad_add_fusion.place_ref.core_ref, f32[8]{0:T(128)} %regular_ref.7, bf16[512,1024]{1,0:T(8,128)(2,1)} %convolution_convert_fusion.refs_0_, bf16[512,1024]{1,0:T(8,128)(2,1)} %bitcast.19, bf16[512,1024]{1,0:T(8,128)(2,1)} %bitcast.24, ...), custom_call_target="tpu_custom_call", output_to_operand_aliasing={{}: (7, {})} | custom-call | flops 1342177280 | bytes 1835008 | tf_op jit(solution)/shard_map/solve_heads/pallas_call | solution.py:350
  158.1 2.0 %finish.1 = f32[256,256]{1,0:T(8,128)} custom-call(f32[128,256]{1,0:T(8,128)} %get-tuple-element.57.refs_0_, f32[128,256]{1,0:T(8,128)} %collective-permute-done.16.refs_1_, f32[128,256]{1,0:T(8,128)} %collective-permute-done.17.refs_2_, f32[128,256]{1,0:T(8,128)} %collective-permute-done.18.refs_3_, f32[128,256]{1,0:T(8,128)} %get-tuple-element.66.refs_4_, ...), custom_call_target="tpu_custom_call" | custom-call | bytes 1310720 | tf_op jit(solution)/shard_map/finish/pallas_call | solution.py:517
  (22 shorter events, 1.1 us)
Async XLA Ops:
  5.6 2.2 %collective-permute-start = (f32[2,1,392,128]{3,2,1,0:T(8,128)}, f32[2,1,392,128]{3,2,1,0:T(8,128)}, u32[]{:S(2)}, u32[]{:S(2)}) collective-permute-start(f32[2,1,392,128]{3,2,1,0:T(8,128)} %get-tuple-element.38), channel_id=1, source_target_pairs={{0,1},{1,0},{2,3},{3,2},{4,5},{5,4},{6,7},{7,6},{8,9},{9,8},{10,11... | collective-permute-start | bytes 1204232 | tf_op jit(solution)/shard_map/ppermute | solution.py:560
  9.8 16.8 %collective-permute-start.7 = (f32[1,392,128]{2,1,0:T(8,128)}, f32[1,392,128]{2,1,0:T(8,128)}, u32[]{:S(2)}, u32[]{:S(2)}) collective-permute-start(f32[1,392,128]{2,1,0:T(8,128)} %get-tuple-element.42), channel_id=1, source_target_pairs={{0,6},{1,7},{8,14},{9,15},{16,22},{17,23},{24,30},{25,31}} | collective-permute-start | bytes 602120 | tf_op jit(solution)/shard_map/ppermute | solution.py:568
  17.3 9.4 %collective-permute-start.6 = (f32[1,392,128]{2,1,0:T(8,128)}, f32[1,392,128]{2,1,0:T(8,128)}, u32[]{:S(2)}, u32[]{:S(2)}) collective-permute-start(f32[1,392,128]{2,1,0:T(8,128)} %get-tuple-element.42), channel_id=1, source_target_pairs={{0,4},{1,5},{2,6},{3,7},{8,12},{9,13},{10,14},{11,15},{16,20},{17,... | collective-permute-start | bytes 602120 | tf_op jit(solution)/shard_map/ppermute | solution.py:568
  19.2 10.9 %collective-permute-start.5 = (f32[1,392,128]{2,1,0:T(8,128)}, f32[1,392,128]{2,1,0:T(8,128)}, u32[]{:S(2)}, u32[]{:S(2)}) collective-permute-start(f32[1,392,128]{2,1,0:T(8,128)} %get-tuple-element.42), channel_id=1, source_target_pairs={{0,2},{1,3},{2,4},{3,5},{4,6},{5,7},{8,10},{9,11},{10,12},{11,13},... | collective-permute-start | bytes 602120 | tf_op jit(solution)/shard_map/ppermute | solution.py:568
  26.6 48.8 %collective-permute-start.10 = (f32[4,512,256]{2,1,0:T(8,128)}, f32[4,512,256]{2,1,0:T(8,128)}, u32[]{:S(2)}, u32[]{:S(2)}) collective-permute-start(f32[4,512,256]{2,1,0:T(8,128)} %pick_columns.1), channel_id=1, source_target_pairs={{0,1},{1,0},{2,3},{3,2},{4,5},{5,4},{6,7},{7,6},{8,9},{9,8},{10,11... | collective-permute-start | bytes 6291464 | tf_op jit(solution)/shard_map/ppermute | solution.py:574
  32.3 6.1 %collective-permute-start.8 = (f32[1,392,128]{2,1,0:T(8,128)}, f32[1,392,128]{2,1,0:T(8,128)}, u32[]{:S(2)}, u32[]{:S(2)}) collective-permute-start(f32[1,392,128]{2,1,0:T(8,128)} %get-tuple-element.44), channel_id=1, source_target_pairs={{0,1},{1,0},{2,3},{3,2},{4,5},{5,4},{6,7},{7,6},{8,9},{9,8},{10,11... | collective-permute-start | bytes 602120 | tf_op jit(solution)/shard_map/ppermute | solution.py:571
  52.7 22.7 %collective-permute-start.9 = (f32[4,128,512]{2,1,0:T(8,128)}, f32[4,128,512]{2,1,0:T(8,128)}, u32[]{:S(2)}, u32[]{:S(2)}) collective-permute-start(f32[4,128,512]{2,1,0:T(8,128)} %get-tuple-element.47), channel_id=1, source_target_pairs={{0,1},{1,0},{2,3},{3,2},{4,5},{5,4},{6,7},{7,6},{8,9},{9,8},{10,11... | collective-permute-start | bytes 3145736 | tf_op jit(solution)/shard_map/ppermute | solution.py:591
  53.3 13.5 %collective-permute-start.3 = (f32[1,392,128]{2,1,0:T(8,128)}, f32[1,392,128]{2,1,0:T(8,128)}, u32[]{:S(2)}, u32[]{:S(2)}) collective-permute-start(f32[1,392,128]{2,1,0:T(8,128)} %get-tuple-element.39), channel_id=1, source_target_pairs={{0,6},{1,7},{8,14},{9,15},{16,22},{17,23},{24,30},{25,31}} | collective-permute-start | bytes 602120 | tf_op jit(solution)/shard_map/ppermute | solution.py:568
  60.2 9.6 %collective-permute-start.2 = (f32[1,392,128]{2,1,0:T(8,128)}, f32[1,392,128]{2,1,0:T(8,128)}, u32[]{:S(2)}, u32[]{:S(2)}) collective-permute-start(f32[1,392,128]{2,1,0:T(8,128)} %get-tuple-element.39), channel_id=1, source_target_pairs={{0,4},{1,5},{2,6},{3,7},{8,12},{9,13},{10,14},{11,15},{16,20},{17,... | collective-permute-start | bytes 602120 | tf_op jit(solution)/shard_map/ppermute | solution.py:568
  64.8 8.4 %collective-permute-start.1 = (f32[1,392,128]{2,1,0:T(8,128)}, f32[1,392,128]{2,1,0:T(8,128)}, u32[]{:S(2)}, u32[]{:S(2)}) collective-permute-start(f32[1,392,128]{2,1,0:T(8,128)} %get-tuple-element.39), channel_id=1, source_target_pairs={{0,2},{1,3},{2,4},{3,5},{4,6},{5,7},{8,10},{9,11},{10,12},{11,13},... | collective-permute-start | bytes 602120 | tf_op jit(solution)/shard_map/ppermute | solution.py:568
  75.4 6.2 %collective-permute-start.4 = (f32[1,392,128]{2,1,0:T(8,128)}, f32[1,392,128]{2,1,0:T(8,128)}, u32[]{:S(2)}, u32[]{:S(2)}) collective-permute-start(f32[1,392,128]{2,1,0:T(8,128)} %get-tuple-element.40), channel_id=1, source_target_pairs={{0,1},{1,0},{2,3},{3,2},{4,5},{5,4},{6,7},{7,6},{8,9},{9,8},{10,11... | collective-permute-start | bytes 602120 | tf_op jit(solution)/shard_map/ppermute | solution.py:571
  93.3 3.5 %collective-permute-start.11 = (f32[4,128,512]{2,1,0:T(8,128)}, f32[4,128,512]{2,1,0:T(8,128)}, u32[]{:S(2)}, u32[]{:S(2)}) collective-permute-start(f32[4,128,512]{2,1,0:T(8,128)} %get-tuple-element.50), channel_id=1, source_target_pairs={{0,1},{1,0},{2,3},{3,2},{4,5},{5,4},{6,7},{7,6},{8,9},{9,8},{10,11... | collective-permute-start | bytes 3145736 | tf_op jit(solution)/shard_map/ppermute | solution.py:591
  93.7 15.1 %collective-permute-start.12 = (f32[2,4,64,256]{3,2,1,0:T(8,128)}, f32[2,4,64,256]{3,2,1,0:T(8,128)}, u32[]{:S(2)}, u32[]{:S(2)}) collective-permute-start(f32[2,4,64,256]{3,2,1,0:T(8,128)} %get-tuple-element.52), channel_id=1, source_target_pairs={{0,8},{8,0},{16,24},{24,16},{1,9},{9,1},{17,25},{25,17},{2,10},{10... | collective-permute-start | bytes 1572872 | tf_op jit(solution)/shard_map/ppermute | solution.py:606
  95.2 15.1 %collective-permute-start.13 = (f32[2,4,64,256]{3,2,1,0:T(8,128)}, f32[2,4,64,256]{3,2,1,0:T(8,128)}, u32[]{:S(2)}, u32[]{:S(2)}) collective-permute-start(f32[2,4,64,256]{3,2,1,0:T(8,128)} %get-tuple-element.54), channel_id=1, source_target_pairs={{0,16},{8,24},{16,0},{24,8},{1,17},{9,25},{17,1},{25,9},{2,18},{10... | collective-permute-start | bytes 1572872 | tf_op jit(solution)/shard_map/ppermute | solution.py:606
  102.9 17.2 %collective-permute-start.19 = (f32[2,4,64,256]{3,2,1,0:T(8,128)}, f32[2,4,64,256]{3,2,1,0:T(8,128)}, u32[]{:S(2)}, u32[]{:S(2)}) collective-permute-start(f32[2,4,64,256]{3,2,1,0:T(8,128)} %get-tuple-element.61), channel_id=1, source_target_pairs={{0,8},{8,0},{16,24},{24,16},{1,9},{9,1},{17,25},{25,17},{2,10},{10... | collective-permute-start | bytes 1572872 | tf_op jit(solution)/shard_map/ppermute | solution.py:606
  104.0 17.6 %collective-permute-start.20 = (f32[2,4,64,256]{3,2,1,0:T(8,128)}, f32[2,4,64,256]{3,2,1,0:T(8,128)}, u32[]{:S(2)}, u32[]{:S(2)}) collective-permute-start(f32[2,4,64,256]{3,2,1,0:T(8,128)} %get-tuple-element.63), channel_id=1, source_target_pairs={{0,16},{8,24},{16,0},{24,8},{1,17},{9,25},{17,1},{25,9},{2,18},{10... | collective-permute-start | bytes 1572872 | tf_op jit(solution)/shard_map/ppermute | solution.py:606
  112.4 14.8 %collective-permute-start.14 = (f32[1,4,64,256]{3,2,1,0:T(8,128)}, f32[1,4,64,256]{3,2,1,0:T(8,128)}, u32[]{:S(2)}, u32[]{:S(2)}) collective-permute-start(f32[1,4,64,256]{3,2,1,0:T(8,128)} %get-tuple-element.55), channel_id=1, source_target_pairs={{0,16},{8,24},{16,0},{24,8},{1,17},{9,25},{17,1},{25,9},{2,18},{10... | collective-permute-start | bytes 786440 | tf_op jit(solution)/shard_map/ppermute | solution.py:606
  113.9 13.3 %collective-permute-start.15 = (f32[1,4,64,256]{3,2,1,0:T(8,128)}, f32[1,4,64,256]{3,2,1,0:T(8,128)}, u32[]{:S(2)}, u32[]{:S(2)}) collective-permute-start(f32[1,4,64,256]{3,2,1,0:T(8,128)} %get-tuple-element.56), channel_id=1, source_target_pairs={{0,8},{8,0},{16,24},{24,16},{1,9},{9,1},{17,25},{25,17},{2,10},{10... | collective-permute-start | bytes 786440 | tf_op jit(solution)/shard_map/ppermute | solution.py:606
  123.6 14.5 %collective-permute-start.21 = (f32[1,4,64,256]{3,2,1,0:T(8,128)}, f32[1,4,64,256]{3,2,1,0:T(8,128)}, u32[]{:S(2)}, u32[]{:S(2)}) collective-permute-start(f32[1,4,64,256]{3,2,1,0:T(8,128)} %get-tuple-element.64), channel_id=1, source_target_pairs={{0,16},{8,24},{16,0},{24,8},{1,17},{9,25},{17,1},{25,9},{2,18},{10... | collective-permute-start | bytes 786440 | tf_op jit(solution)/shard_map/ppermute | solution.py:606
  125.1 13.0 %collective-permute-start.22 = (f32[1,4,64,256]{3,2,1,0:T(8,128)}, f32[1,4,64,256]{3,2,1,0:T(8,128)}, u32[]{:S(2)}, u32[]{:S(2)}) collective-permute-start(f32[1,4,64,256]{3,2,1,0:T(8,128)} %get-tuple-element.65), channel_id=1, source_target_pairs={{0,8},{8,0},{16,24},{24,16},{1,9},{9,1},{17,25},{25,17},{2,10},{10... | collective-permute-start | bytes 786440 | tf_op jit(solution)/shard_map/ppermute | solution.py:606
  129.4 13.9 %collective-permute-start.16 = (f32[128,256]{1,0:T(8,128)}, f32[128,256]{1,0:T(8,128)}, u32[]{:S(2)}, u32[]{:S(2)}) collective-permute-start(f32[128,256]{1,0:T(8,128)} %get-tuple-element.58), channel_id=1, source_target_pairs={{0,2},{1,3},{2,0},{3,1},{4,6},{5,7},{6,4},{7,5},{8,10},{9,11},{10,... | collective-permute-start | bytes 393224 | tf_op jit(solution)/shard_map/ppermute | solution.py:613
  134.8 23.3 %collective-permute-start.17 = (f32[128,256]{1,0:T(8,128)}, f32[128,256]{1,0:T(8,128)}, u32[]{:S(2)}, u32[]{:S(2)}) collective-permute-start(f32[128,256]{1,0:T(8,128)} %get-tuple-element.59), channel_id=1, source_target_pairs={{0,4},{1,5},{2,6},{3,7},{4,0},{5,1},{6,2},{7,3},{8,12},{9,13},{10,... | collective-permute-start | bytes 393224 | tf_op jit(solution)/shard_map/ppermute | solution.py:613
  136.7 21.3 %collective-permute-start.18 = (f32[128,256]{1,0:T(8,128)}, f32[128,256]{1,0:T(8,128)}, u32[]{:S(2)}, u32[]{:S(2)}) collective-permute-start(f32[128,256]{1,0:T(8,128)} %get-tuple-element.60), channel_id=1, source_target_pairs={{0,6},{1,7},{2,4},{3,5},{4,2},{5,3},{6,0},{7,1},{8,14},{9,15},{10,... | collective-permute-start | bytes 393224 | tf_op jit(solution)/shard_map/ppermute | solution.py:613
  140.3 17.7 %collective-permute-start.23 = (f32[128,256]{1,0:T(8,128)}, f32[128,256]{1,0:T(8,128)}, u32[]{:S(2)}, u32[]{:S(2)}) collective-permute-start(f32[128,256]{1,0:T(8,128)} %get-tuple-element.67), channel_id=1, source_target_pairs={{0,2},{1,3},{2,0},{3,1},{4,6},{5,7},{6,4},{7,5},{8,10},{9,11},{10,... | collective-permute-start | bytes 393224 | tf_op jit(solution)/shard_map/ppermute | solution.py:613
  140.9 17.1 %collective-permute-start.24 = (f32[128,256]{1,0:T(8,128)}, f32[128,256]{1,0:T(8,128)}, u32[]{:S(2)}, u32[]{:S(2)}) collective-permute-start(f32[128,256]{1,0:T(8,128)} %get-tuple-element.68), channel_id=1, source_target_pairs={{0,4},{1,5},{2,6},{3,7},{4,0},{5,1},{6,2},{7,3},{8,12},{9,13},{10,... | collective-permute-start | bytes 393224 | tf_op jit(solution)/shard_map/ppermute | solution.py:613
  143.3 14.8 %collective-permute-start.25 = (f32[128,256]{1,0:T(8,128)}, f32[128,256]{1,0:T(8,128)}, u32[]{:S(2)}, u32[]{:S(2)}) collective-permute-start(f32[128,256]{1,0:T(8,128)} %get-tuple-element.69), channel_id=1, source_target_pairs={{0,6},{1,7},{2,4},{3,5},{4,2},{5,3},{6,0},{7,1},{8,14},{9,15},{10,... | collective-permute-start | bytes 393224 | tf_op jit(solution)/shard_map/ppermute | solution.py:613
